TPU v7x, 32 devices: a whole 2x2x4 slice. The times are simulated.
32 devices in a mesh: fsdp: 8 (over y, x, core), seq: 4 (over z).
Axes of the slice: x: 2, y: 2, z: 4, core: 2. Of those that a mesh axis runs over, the one named last changes fastest.
Arguments:
- tokens: bfloat16 [8, 2, 2048, 768], P('fsdp', None, 'seq'), may hold values from -6 to 6
- doc_lengths: int32 [8, 2, 8], P('fsdp'), may hold values from 1 to 1024, 2048 in all within a row
- qkv_weight: bfloat16 [768, 2304], P('fsdp'), may hold values from -0.21875 to 0.21875
- q_bias: bfloat16 [768], P('fsdp'), may hold values from -1.5 to 1.5
- v_bias: bfloat16 [768], P('fsdp'), may hold values from -0.25 to 0.25
- out_weight: bfloat16 [768, 768], P('fsdp'), may hold values from -1.25 to 1.25
- out_bias: bfloat16 [768], P('fsdp'), may hold values from -1.5 to 1.5
- norm1_gain: bfloat16 [768], P('fsdp'), may hold values from 0.25 to 1.75
- norm1_bias: bfloat16 [768], P('fsdp'), may hold values from -1.5 to 1.5
- ff_in_weight: bfloat16 [768, 3072], P('fsdp'), may hold values from -0.21875 to 0.21875
- ff_in_bias: bfloat16 [3072], P('fsdp'), may hold values from -2.5 to 2.5
- ff_out_weight: bfloat16 [3072, 768], P('fsdp'), may hold values from -0.109375 to 0.109375
- ff_out_bias: bfloat16 [768], P('fsdp'), may hold values from -1.5 to 1.5
- norm2_gain: bfloat16 [768], P('fsdp'), may hold values from 0.25 to 1.75
- norm2_bias: bfloat16 [768], P('fsdp'), may hold values from -1.5 to 1.5
- out_cotangent: bfloat16 [8, 2, 2048, 768], P('fsdp', None, 'seq'), may hold values from -6 to 6
Outputs:
- output: bfloat16 [8, 2, 2048, 768], P('fsdp', None, 'seq')
- input_grad: float32 [8, 2, 2048, 768], P('fsdp', None, 'seq')
- qkv_weight_grad: float32 [768, 2304], P('fsdp')
- q_bias_grad: float32 [768], P('fsdp')
- v_bias_grad: float32 [768], P('fsdp')
- out_weight_grad: float32 [768, 768], P('fsdp')
- out_bias_grad: float32 [768], P('fsdp')
- norm1_gain_grad: float32 [768], P('fsdp')
- norm1_bias_grad: float32 [768], P('fsdp')
- ff_in_weight_grad: float32 [768, 3072], P('fsdp')
- ff_in_bias_grad: float32 [3072], P('fsdp')
- ff_out_weight_grad: float32 [3072, 768], P('fsdp')
- ff_out_bias_grad: float32 [768], P('fsdp')
- norm2_gain_grad: float32 [768], P('fsdp')
- norm2_bias_grad: float32 [768], P('fsdp')
Inputs may be any that keep to these rules, and one draw needn't show every extreme that they name: `doc_lengths`: the 8 lengths of a stretch sum to 2048; in every stretch the longest is exactly 1024 tokens.
All inputs are finite; a program needn't handle non-finite values.
Results may differ from a plain program's by a relative error of at most 0.017.
Values may be sent and summed in bfloat16 or wider, within the bound.
A program may use at most 192 MiB of HBM per device.

v0:
```python
import math

import jax
import jax.numpy as jnp
from jax import lax
from jax.sharding import PartitionSpec as P

HEAD_DIM = 64
BLOCK = 512


EPS = 1e-05
NEG = -1e30


def norm_forward(resid, gain, shift):
    mean = jnp.mean(resid, axis=-1, keepdims=True)
    centered = resid - mean
    inv = lax.rsqrt(jnp.mean(centered * centered, axis=-1, keepdims=True) + EPS)
    normed = centered * inv
    return (normed * gain + shift, normed, inv)


def norm_backward(grad, normed, inv, gain):
    scaled = grad * gain
    return inv * (
        scaled
        - jnp.mean(scaled, axis=-1, keepdims=True)
        - normed * jnp.mean(scaled * normed, axis=-1, keepdims=True)
    )


def contract_rows(left, right):
    return lax.dot_general(
        left, right, (((0,), (0,)), ((), ())), preferred_element_type=jnp.float32
    )


def contract_cols(left, right):
    return lax.dot_general(
        left, right, (((1,), (1,)), ((), ())), preferred_element_type=jnp.float32
    )


def gelu_slope(pre):
    cdf = 0.5 * (1.0 + lax.erf(pre * (1.0 / math.sqrt(2.0))))
    density = jnp.exp(-0.5 * pre * pre) * (1.0 / math.sqrt(2.0 * math.pi))
    return cdf + pre * density


def doc_ids(lengths, count):
    ends = jnp.cumsum(lengths)
    places = jnp.arange(count, dtype=jnp.int32)
    return jnp.sum((places[:, None] >= ends[None, :]).astype(jnp.int32), axis=1)


def block_scores(qblock, sblock, keys, seg, scale):
    raw = jnp.einsum("qgd,kgd->gqk", qblock, keys, preferred_element_type=jnp.float32) * scale
    same = sblock[:, None] == seg[None, :]
    return jnp.where(same[None], raw, NEG)


def per_device(
    tokens,
    doc_lengths,
    qkv_weight,
    q_bias,
    v_bias,
    out_weight,
    out_bias,
    norm1_gain,
    norm1_bias,
    ff_in_weight,
    ff_in_bias,
    ff_out_weight,
    ff_out_bias,
    norm2_gain,
    norm2_bias,
    out_cotangent,
):
    gathered = (
        lax.all_gather(qkv_weight, "fsdp", axis=0, tiled=True),
        lax.all_gather(q_bias, "fsdp", axis=0, tiled=True),
        lax.all_gather(v_bias, "fsdp", axis=0, tiled=True),
        lax.all_gather(out_weight, "fsdp", axis=0, tiled=True),
        lax.all_gather(out_bias, "fsdp", axis=0, tiled=True),
        lax.all_gather(norm1_gain, "fsdp", axis=0, tiled=True),
        lax.all_gather(norm1_bias, "fsdp", axis=0, tiled=True),
        lax.all_gather(ff_in_weight, "fsdp", axis=0, tiled=True),
        lax.all_gather(ff_in_bias, "fsdp", axis=0, tiled=True),
        lax.all_gather(ff_out_weight, "fsdp", axis=0, tiled=True),
        lax.all_gather(ff_out_bias, "fsdp", axis=0, tiled=True),
        lax.all_gather(norm2_gain, "fsdp", axis=0, tiled=True),
        lax.all_gather(norm2_bias, "fsdp", axis=0, tiled=True),
    )
    (
        w_qkv,
        bias_q,
        bias_v,
        w_out,
        bias_out,
        gain_one,
        shift_one,
        w_in,
        bias_in,
        w_down,
        bias_down,
        gain_two,
        shift_two,
    ) = gathered
    bias_out32 = bias_out.astype(jnp.float32)
    gain_one32 = gain_one.astype(jnp.float32)
    shift_one32 = shift_one.astype(jnp.float32)
    bias_in32 = bias_in.astype(jnp.float32)
    bias_down32 = bias_down.astype(jnp.float32)
    gain_two32 = gain_two.astype(jnp.float32)
    shift_two32 = shift_two.astype(jnp.float32)
    nseq = lax.axis_size("seq")
    rows = tokens.shape[2]
    width = tokens.shape[3]
    stretch = rows * nseq
    group_width = width // nseq
    heads_dev = group_width // HEAD_DIM
    scale = HEAD_DIM ** (-0.5)
    blocks = stretch // BLOCK
    proj_bias = jnp.concatenate(
        [bias_q.astype(jnp.float32), jnp.zeros((width,), jnp.float32), bias_v.astype(jnp.float32)]
    )
    totals = None
    outputs = []
    input_grads = []
    for micro in range(tokens.shape[1]):
        x_in = tokens[0, micro]
        seg = doc_ids(doc_lengths[0, micro], stretch)
        proj = (jnp.dot(x_in, w_qkv, preferred_element_type=jnp.float32) + proj_bias).astype(
            jnp.bfloat16
        )
        heads = lax.all_to_all(
            proj.reshape(rows, 3, nseq, group_width), "seq", split_axis=2, concat_axis=0, tiled=True
        )
        heads = heads.reshape(stretch, 3, heads_dev, HEAD_DIM)
        queries = heads[:, 0]
        keys = heads[:, 1]
        values = heads[:, 2]
        qblocks = queries.reshape(blocks, BLOCK, heads_dev, HEAD_DIM)
        sblocks = seg.reshape(blocks, BLOCK)

        def attend(item):
            qblock, sblock = item
            masked = block_scores(qblock, sblock, keys, seg, scale)
            top = jnp.max(masked, axis=-1, keepdims=True)
            expd = jnp.exp(masked - top)
            total = jnp.sum(expd, axis=-1, keepdims=True)
            probs = (expd / total).astype(jnp.bfloat16)
            ctx = jnp.einsum("gqk,kgd->qgd", probs, values, preferred_element_type=jnp.float32)
            return (ctx.astype(jnp.bfloat16), (top + jnp.log(total))[..., 0])

        ctx_blocks, lse_blocks = lax.map(attend, (qblocks, sblocks))
        context = lax.all_to_all(
            ctx_blocks.reshape(stretch, 1, group_width),
            "seq",
            split_axis=0,
            concat_axis=1,
            tiled=True,
        )
        context = context.reshape(rows, width)
        attn = jnp.dot(context, w_out, preferred_element_type=jnp.float32) + bias_out32
        resid_one = x_in.astype(jnp.float32) + attn
        hidden, normed_one, inv_one = norm_forward(resid_one, gain_one32, shift_one32)
        hidden_low = hidden.astype(jnp.bfloat16)
        pre = jnp.dot(hidden_low, w_in, preferred_element_type=jnp.float32) + bias_in32
        act_low = jax.nn.gelu(pre, approximate=False).astype(jnp.bfloat16)
        resid_two = (
            hidden + jnp.dot(act_low, w_down, preferred_element_type=jnp.float32) + bias_down32
        )
        result, normed_two, inv_two = norm_forward(resid_two, gain_two32, shift_two32)
        outputs.append(result.astype(jnp.bfloat16))
        grad_out = out_cotangent[0, micro].astype(jnp.float32)
        gain_two_grad = jnp.sum(grad_out * normed_two, axis=0)
        shift_two_grad = jnp.sum(grad_out, axis=0)
        grad_two = norm_backward(grad_out, normed_two, inv_two, gain_two32)
        grad_down = grad_two.astype(jnp.bfloat16)
        down_grad = contract_rows(act_low, grad_down)
        down_bias_grad = jnp.sum(grad_down.astype(jnp.float32), axis=0)
        grad_pre = (contract_cols(grad_down, w_down) * gelu_slope(pre)).astype(jnp.bfloat16)
        in_grad = contract_rows(hidden_low, grad_pre)
        in_bias_grad = jnp.sum(grad_pre.astype(jnp.float32), axis=0)
        grad_hidden = grad_two + contract_cols(grad_pre, w_in)
        gain_one_grad = jnp.sum(grad_hidden * normed_one, axis=0)
        shift_one_grad = jnp.sum(grad_hidden, axis=0)
        grad_one = norm_backward(grad_hidden, normed_one, inv_one, gain_one32)
        grad_attn = grad_one.astype(jnp.bfloat16)
        attn_grad = contract_rows(context, grad_attn)
        attn_bias_grad = jnp.sum(grad_attn.astype(jnp.float32), axis=0)
        grad_context = contract_cols(grad_attn, w_out).astype(jnp.bfloat16)
        grad_heads = lax.all_to_all(
            grad_context.reshape(rows, nseq, group_width),
            "seq",
            split_axis=1,
            concat_axis=0,
            tiled=True,
        )
        grad_heads = grad_heads.reshape(blocks, BLOCK, heads_dev, HEAD_DIM)

        def back(carry, item):
            keys_acc, values_acc = carry
            qblock, sblock, lse_block, grad_block = item
            masked = block_scores(qblock, sblock, keys, seg, scale)
            probs = jnp.exp(masked - lse_block[..., None])
            probs_low = probs.astype(jnp.bfloat16)
            values_acc = values_acc + jnp.einsum(
                "gqk,qgd->kgd", probs_low, grad_block, preferred_element_type=jnp.float32
            )
            grad_probs = jnp.einsum(
                "qgd,kgd->gqk", grad_block, values, preferred_element_type=jnp.float32
            )
            delta = jnp.sum(probs * grad_probs, axis=-1, keepdims=True)
            grad_scores = (probs * (grad_probs - delta)).astype(jnp.bfloat16)
            grad_q = (
                jnp.einsum("gqk,kgd->qgd", grad_scores, keys, preferred_element_type=jnp.float32)
                * scale
            )
            keys_acc = (
                keys_acc
                + jnp.einsum(
                    "gqk,qgd->kgd", grad_scores, qblock, preferred_element_type=jnp.float32
                )
                * scale
            )
            return ((keys_acc, values_acc), grad_q)

        empty = jnp.zeros((stretch, heads_dev, HEAD_DIM), jnp.float32)
        (grad_keys, grad_values), grad_queries = lax.scan(
            back, (empty, empty), (qblocks, sblocks, lse_blocks, grad_heads)
        )
        grad_stack = jnp.stack(
            [grad_queries.reshape(stretch, heads_dev, HEAD_DIM), grad_keys, grad_values], 1
        )
        grad_stack = grad_stack.astype(jnp.bfloat16).reshape(stretch, 3, 1, group_width)
        grad_proj = lax.all_to_all(
            grad_stack, "seq", split_axis=0, concat_axis=2, tiled=True
        ).reshape(rows, 3 * width)
        qkv_grad = contract_rows(x_in, grad_proj)
        column_sums = jnp.sum(grad_proj.astype(jnp.float32), axis=0)
        input_grads.append(grad_one + contract_cols(grad_proj, w_qkv))
        terms = (
            qkv_grad,
            column_sums[:width],
            column_sums[2 * width :],
            attn_grad,
            attn_bias_grad,
            gain_one_grad,
            shift_one_grad,
            in_grad,
            in_bias_grad,
            down_grad,
            down_bias_grad,
            gain_two_grad,
            shift_two_grad,
        )
        if totals is None:
            totals = terms
        else:
            totals = tuple((a + b for a, b in zip(totals, terms)))
    shards = (
        lax.psum_scatter(totals[0], "fsdp", scatter_dimension=0, tiled=True),
        lax.psum_scatter(totals[1], "fsdp", scatter_dimension=0, tiled=True),
        lax.psum_scatter(totals[2], "fsdp", scatter_dimension=0, tiled=True),
        lax.psum_scatter(totals[3], "fsdp", scatter_dimension=0, tiled=True),
        lax.psum_scatter(totals[4], "fsdp", scatter_dimension=0, tiled=True),
        lax.psum_scatter(totals[5], "fsdp", scatter_dimension=0, tiled=True),
        lax.psum_scatter(totals[6], "fsdp", scatter_dimension=0, tiled=True),
        lax.psum_scatter(totals[7], "fsdp", scatter_dimension=0, tiled=True),
        lax.psum_scatter(totals[8], "fsdp", scatter_dimension=0, tiled=True),
        lax.psum_scatter(totals[9], "fsdp", scatter_dimension=0, tiled=True),
        lax.psum_scatter(totals[10], "fsdp", scatter_dimension=0, tiled=True),
        lax.psum_scatter(totals[11], "fsdp", scatter_dimension=0, tiled=True),
        lax.psum_scatter(totals[12], "fsdp", scatter_dimension=0, tiled=True),
    )
    final = (
        lax.psum(shards[0].astype(jnp.bfloat16), "seq").astype(jnp.float32),
        lax.psum(shards[1].astype(jnp.bfloat16), "seq").astype(jnp.float32),
        lax.psum(shards[2].astype(jnp.bfloat16), "seq").astype(jnp.float32),
        lax.psum(shards[3].astype(jnp.bfloat16), "seq").astype(jnp.float32),
        lax.psum(shards[4].astype(jnp.bfloat16), "seq").astype(jnp.float32),
        lax.psum(shards[5].astype(jnp.bfloat16), "seq").astype(jnp.float32),
        lax.psum(shards[6].astype(jnp.bfloat16), "seq").astype(jnp.float32),
        lax.psum(shards[7].astype(jnp.bfloat16), "seq").astype(jnp.float32),
        lax.psum(shards[8].astype(jnp.bfloat16), "seq").astype(jnp.float32),
        lax.psum(shards[9].astype(jnp.bfloat16), "seq").astype(jnp.float32),
        lax.psum(shards[10].astype(jnp.bfloat16), "seq").astype(jnp.float32),
        lax.psum(shards[11].astype(jnp.bfloat16), "seq").astype(jnp.float32),
        lax.psum(shards[12].astype(jnp.bfloat16), "seq").astype(jnp.float32),
    )
    output = jnp.stack(outputs)[None]
    input_grad = jnp.stack(input_grads)[None]
    return (
        output,
        input_grad,
        final[0],
        final[1],
        final[2],
        final[3],
        final[4],
        final[5],
        final[6],
        final[7],
        final[8],
        final[9],
        final[10],
        final[11],
        final[12],
    )


def solution(mesh):
    placed = (
        P("fsdp", None, "seq", None),
        P("fsdp", None, None),
        P("fsdp", None),
        P("fsdp"),
        P("fsdp"),
        P("fsdp", None),
        P("fsdp"),
        P("fsdp"),
        P("fsdp"),
        P("fsdp", None),
        P("fsdp"),
        P("fsdp", None),
        P("fsdp"),
        P("fsdp"),
        P("fsdp"),
        P("fsdp", None, "seq", None),
    )
    return jax.shard_map(
        per_device,
        mesh=mesh,
        in_specs=placed,
        out_specs=(
            P("fsdp", None, "seq", None),
            P("fsdp", None, "seq", None),
            P("fsdp", None),
            P("fsdp"),
            P("fsdp"),
            P("fsdp", None),
            P("fsdp"),
            P("fsdp"),
            P("fsdp"),
            P("fsdp", None),
            P("fsdp"),
            P("fsdp", None),
            P("fsdp"),
            P("fsdp"),
            P("fsdp"),
        ),
        check_vma=False,
    )
```

profile of v0, /device:TPU:9, one launch (start us, length us, event | category | flops | bytes accessed | tf_op | source)
XLA Modules:
  0.0 1104.4 jit_solution(3628686376557271715)
XLA Ops:
  16.6 22.1 %all-reduce.18 = (bf16[768]{0:T(1024)(128)(2,1)S(1)}, bf16[768]{0:T(1024)(128)(2,1)S(1)}, bf16[768]{0:T(1024)(128)(2,1)}, bf16[768]{0:T(1024)(128)(2,1)}, bf16[7...) all-reduce(bf16[768]{0:T(1024)(128)(2,1)S(1)} %dynamic-update-slice, ...), channel_id=1, replica_groups=mesh['fsdp'=8,'seq'=4] {'fsdp'}, use_global_device_ids=true, to_apply=%add.1 | all-reduce | flops 6144 | bytes 24576
  38.7 6.8 all-gather.6.cloned.1.call-done
  76.3 34.5 %all-to-all-done = bf16[512,3,4,192]{0,3,1,2:T(8,128)(2,1)S(1)} async-done(((bf16[512,3,4,192]{0,3,1,2:T(8,128)(2,1)}), bf16[512,3,4,192]{0,3,1,2:T(8,128)(2,1)S(1)}, u32[]{:S(2)}, u32[]{:S(2)}) %all-to-all-start) | async-done | bytes 2359328 | tf_op jit(solution)/shard_map/all_to_all | solution.py:138
  110.8 7.7 all-to-all-start.2
  130.2 80.7 %while.54 = (s32[]{:T(128)}, bf16[4,512,3,64]{1,3,2,0:T(8,128)(2,1)S(1)}, f32[4,3,512]{2,1,0:T(4,128)S(1)}, s32[4,512]{1,0:T(4,128)S(1)}, s32[2048]{0:T(1024)S(1...) while((s32[]{:T(128)}, ...), condition=%wide.region_5.6_spmd, body=%wide.region_2.5_spmd.sunk | while | flops 844200448 | bytes 43982956 | solution.py:158
  136.9 6.8 fusion.258
  143.7 6.7 fusion.259
  157.1 6.8 fusion.258
  163.9 6.7 fusion.259
  177.2 6.8 fusion.258
  184.0 6.7 fusion.259
  197.4 6.8 fusion.258
  204.2 6.7 fusion.259
  235.0 83.5 %while.55 = (s32[]{:T(128)}, bf16[4,512,3,64]{1,3,2,0:T(8,128)(2,1)S(1)}, f32[4,3,512]{2,1,0:T(4,128)S(1)}, s32[4,512]{1,0:T(4,128)}, s32[2048]{0:T(1024)S(1)}, ...) while((s32[]{:T(128)}, ...), condition=%wide.region_15.16_spmd, body=%wide.region_12.15_spmd.sunk | while | flops 844200448 | bytes 43982956 | solution.py:158
  242.4 6.8 fusion.263
  249.1 6.7 fusion.264
  263.2 6.8 fusion.263
  270.0 6.7 fusion.264
  284.1 6.8 fusion.263
  290.9 6.7 fusion.264
  305.0 6.8 fusion.263
  311.7 6.7 fusion.264
  333.3 11.7 %all-gather = bf16[8,1,384]{2,1,0:T(2,128)(2,1)S(1)} all-gather(bf16[1,1,384]{2,1,0:T(2,128)(2,1)S(1)} %reshape.552), channel_id=1, replica_groups=mesh['fsdp'=8,'seq'=4] {'fsdp'}, dimensions={0}, use_global_device_ids=true | all-gather | bytes 6912 | tf_op jit(solution)/shard_map/all_gather | solution.py:90
  371.4 31.5 %fusion.86 = (bf16[512,3072]{1,0:T(8,128)(2,1)}, bf16[512,3072]{1,0:T(8,128)(2,1)}, f32[512,3072]{1,0:T(8,128)}) fusion(f32[3072]{0:T(1024)S(1)} %bitcast.381, f32[512,3072]{1,0:T(8,128)S(1)} %fusion.160, bf16[768,3072]{1,0:T(8,128)(2,1)S(1)} %copy-done.75, f32[512,768]{1,0:T(8,128)S(1)} %copy-done.35, f32[768]{0:T(1024)S(1)} %convert_element_type.256, ...), kind=kOutput, calls=%fused_computation.109 | convolution fusion | flops 2625503232 | bytes 25188352 | tf_op jit(solution)/shard_map/dot_general | solution.py:171
  426.6 7.1 convert_reduce_fusion
  464.7 9.0 fusion.162
  477.8 8.9 convolution_add_fusion.1
  492.3 154.1 %while.56 = (s32[]{:T(128)}, f32[2048,3,64]{0,2,1:T(8,128)}, f32[2048,3,64]{0,2,1:T(8,128)}, bf16[4,512,3,64]{1,3,2,0:T(8,128)(2,1)}, bf16[4,512,3,64]{1,3,2,0:T...) while((s32[]{:T(128)}, f32[2048,3,64]{0,2,1:T(8,128)}, ...), condition=%wide.region_26.27_spmd.clone, body=%wide.region_24.26_spmd.clone.sunk | while | flops 2063563264 | bytes 229043040 | solution.py:233
  499.2 7.7 multiply_reduce_fusion.14
  519.0 6.8 fusion.277
  538.1 6.8 multiply_reduce_fusion.14
  575.7 7.6 multiply_reduce_fusion.14
  595.3 7.0 fusion.277
  614.6 6.8 multiply_reduce_fusion.14
  627.6 6.6 fusion.275
  661.4 149.0 %while.57 = (s32[]{:T(128)}, f32[2048,3,64]{0,2,1:T(8,128)}, f32[2048,3,64]{0,2,1:T(8,128)}, bf16[4,512,3,64]{1,3,2,0:T(8,128)(2,1)}, bf16[4,512,3,64]{1,3,2,0:T...) while((s32[]{:T(128)}, f32[2048,3,64]{0,2,1:T(8,128)}, ...), condition=%wide.region_33.34_spmd.clone, body=%wide.region_31.33_spmd.clone.sunk | while | flops 2063563264 | bytes 229043040 | solution.py:233
  668.0 6.7 multiply_reduce_fusion.15
  704.9 6.7 multiply_reduce_fusion.15
  742.1 6.7 multiply_reduce_fusion.15
  779.4 6.7 multiply_reduce_fusion.15
  824.3 7.4 copy.217
  831.8 81.4 %all-to-all-done.7 = bf16[2048,3,1,192]{3,1,2,0:T(4,128)(2,1)} async-done(((bf16[2048,3,1,192]{3,1,2,0:T(4,128)(2,1)}), bf16[2048,3,1,192]{3,1,2,0:T(4,128)(2,1)}, u32[]{:S(2)}, u32[]{:S(2)}) %all-to-all-start.7) | async-done | bytes 2359328 | tf_op jit(solution)/shard_map/all_to_all | solution.py:240
  913.2 7.2 copy.218
  932.2 8.0 copy.219
  955.3 52.1 %reduce-scatter.13.cloned.1.call-done = f32[96,2304]{1,0:T(8,128)} async-done(((f32[768,2304]{1,0:T(8,128)}), f32[96,2304]{1,0:T(8,128)}) %reduce-scatter.13.cloned.1.call-update) | async-done | bytes 884752
  1011.1 22.1 %all-reduce.17 = (bf16[768]{0:T(1024)(128)(2,1)S(1)}, bf16[768]{0:T(1024)(128)(2,1)S(1)}, bf16[768]{0:T(1024)(128)(2,1)S(1)}, bf16[768]{0:T(1024)(128)(2,1)S(1)}...) all-reduce(f32[768]{0:T(1024)S(1)} %add.343, ...), channel_id=3, replica_groups=mesh['fsdp'=8,'seq'=4] {'fsdp'}, use_global_device_ids=true, to_apply=%region_38.39.clone | all-reduce | flops 9216 | bytes 55296
  1033.9 8.4 all-reduce.19
  1056.3 34.8 %all-reduce.23.cloned.1.call-done = (bf16[96,2304]{0,1:T(8,128)(2,1)}, bf16[96,768]{1,0:T(8,128)(2,1)}, bf16[96,3072]{1,0:T(8,128)(2,1)}, bf16[384,768]{1,0:T(8,128)(2,1)}) async-done(((bf16[96,2304]{0,1:T(8,128)(2,1)}, bf16[96,768]{1,0:T(8,128)(2,1)}, bf16[96,3072]{1,0:T(8,128)(2,1)}, bf16[384,768]{1,0:T(8,128)(2,1)}), (bf16[96,2304]{0,1:T(8,128)(2,1)}, bf16[96,768]{1,0:T(8,128)(2,1)}, ...) | async-done | bytes 1769488 | tf_op jit(solution)/shard_map/psum | solution.py:281
  (553 shorter events, 540.9 us)
Async XLA Ops:
  7.2 38.3 %all-gather.6.cloned.1.call-start = ((), (), s32[]{:S(2)}) async-start(), calls=%async_computation.12 | async-start | bytes 3981312 | tf_op jit(solution)/shard_map/all_gather | solution.py:82
  55.7 55.1 %all-to-all-start = ((bf16[512,3,4,192]{0,3,1,2:T(8,128)(2,1)}), bf16[512,3,4,192]{0,3,1,2:T(8,128)(2,1)S(1)}, u32[]{:S(2)}, u32[]{:S(2)}) async-start(bf16[512,3,4,192]{0,3,1,2:T(8,128)(2,1)} %copy.187), calls=%async_computation | async-start | bytes 4718592 | tf_op jit(solution)/shard_map/all_to_all | solution.py:138
  60.4 293.2 %all-gather.8.cloned.1.call-start = ((), (), s32[]{:S(2)}) async-start(), calls=%async_computation.13 | async-start | bytes 1327104 | tf_op jit(solution)/shard_map/all_gather | solution.py:85
  61.2 302.7 %all-gather.10.cloned.1.call-start = ((), (), s32[]{:S(2)}) async-start(), calls=%async_computation.14 | async-start | bytes 5308416 | tf_op jit(solution)/shard_map/all_gather | solution.py:89
  110.8 110.1 %all-to-all-start.2 = ((bf16[512,3,4,192]{0,3,1,2:T(8,128)(2,1)}), bf16[512,3,4,192]{0,3,1,2:T(8,128)(2,1)}, u32[]{:S(2)}, u32[]{:S(2)}) async-start(bf16[512,3,4,192]{0,3,1,2:T(8,128)(2,1)} %copy.195), calls=%async_computation.2 | async-start | bytes 4718592 | tf_op jit(solution)/shard_map/all_to_all | solution.py:138
  210.9 7.6 copy-start.9
  211.0 7.6 copy-start.15
  211.0 7.6 copy-start.21
  220.9 107.1 %all-to-all-start.1 = ((bf16[4,2,49152]{2,1,0:T(2,128)(2,1)}), bf16[4,2,49152]{2,1,0:T(2,128)(2,1)}, u32[]{:S(2)}, u32[]{:S(2)}) async-start(bf16[4,2,49152]{2,1,0:T(2,128)(2,1)} %reshape.582), calls=%async_computation.1 | async-start | bytes 1572864 | tf_op jit(solution)/shard_map/all_to_all | solution.py:159
  324.1 9.1 copy-start.72
  324.1 9.1 copy-start.71
  324.1 9.1 copy-start.70
  324.1 9.1 copy-start.74
  324.1 20.8 %copy-start.69 = (bf16[768]{0:T(1024)(128)(2,1)S(1)}, bf16[768]{0:T(1024)(128)(2,1)}, u32[]{:S(2)}) copy-start(bf16[768]{0:T(1024)(128)(2,1)} %get-tuple-element.795) | copy-start | bytes 4612
  324.1 20.8 %copy-start.68 = (bf16[768]{0:T(1024)(128)(2,1)S(1)}, bf16[768]{0:T(1024)(128)(2,1)}, u32[]{:S(2)}) copy-start(bf16[768]{0:T(1024)(128)(2,1)} %get-tuple-element.796) | copy-start | bytes 4612
  324.1 20.8 %copy-start.67 = (bf16[768]{0:T(1024)(128)(2,1)S(1)}, bf16[768]{0:T(1024)(128)(2,1)}, u32[]{:S(2)}) copy-start(bf16[768]{0:T(1024)(128)(2,1)} %get-tuple-element.797) | copy-start | bytes 4612
  328.0 29.4 %all-to-all-start.3 = ((bf16[4,2,49152]{2,1,0:T(2,128)(2,1)}), bf16[4,2,49152]{2,1,0:T(2,128)(2,1)S(1)}, u32[]{:S(2)}, u32[]{:S(2)}) async-start(bf16[4,2,49152]{2,1,0:T(2,128)(2,1)} %reshape.584), calls=%async_computation.3 | async-start | bytes 1572864 | tf_op jit(solution)/shard_map/all_to_all | solution.py:159
  332.6 70.4 %all-gather.12.cloned.1.call-start = ((), (), s32[]{:S(2)}) async-start(), calls=%async_computation.15 | async-start | bytes 5308416 | tf_op jit(solution)/shard_map/all_gather | solution.py:91
  333.1 612.9 %reduce-scatter.7.cloned.1.call-start = ((), (), s32[]{:S(2)}) async-start(), calls=%async_computation.16 | async-start | bytes 2654208 | tf_op jit(solution)/shard_map/reduce_scatter | solution.py:269
  409.1 8.6 slice-start.2
  409.5 8.2 slice-start.3
  414.8 8.2 slice-start
  442.8 507.8 %reduce-scatter.11.cloned.1.call-start = ((), (), s32[]{:S(2)}) async-start(), calls=%async_computation.18 | async-start | bytes 10616832 | tf_op jit(solution)/shard_map/reduce_scatter | solution.py:275
  460.2 26.5 %all-to-all-start.4 = ((bf16[512,4,192]{0,2,1:T(8,128)(2,1)}), bf16[512,4,192]{0,2,1:T(8,128)(2,1)}, u32[]{:S(2)}, u32[]{:S(2)}) async-start(bf16[512,4,192]{0,2,1:T(8,128)(2,1)} %bitcast.36), calls=%async_computation.4 | async-start | bytes 1572864 | tf_op jit(solution)/shard_map/all_to_all | solution.py:196
  464.7 9.0 copy-start.25
  464.7 488.2 %reduce-scatter.9.cloned.1.call-start = ((), (), s32[]{:S(2)}) async-start(), calls=%async_computation.17 | async-start | bytes 10616832 | tf_op jit(solution)/shard_map/reduce_scatter | solution.py:273
  464.7 9.0 copy-start.78
  486.7 168.7 %all-to-all-start.6 = ((bf16[512,4,192]{0,2,1:T(8,128)(2,1)}), bf16[512,4,192]{0,2,1:T(8,128)(2,1)}, u32[]{:S(2)}, u32[]{:S(2)}) async-start(bf16[512,4,192]{0,2,1:T(8,128)(2,1)} %bitcast.47), calls=%async_computation.6 | async-start | bytes 1572864 | tf_op jit(solution)/shard_map/all_to_all | solution.py:196
  495.5 11.3 %copy-start = (f32[3,512,2048]{2,1,0:T(8,128)}, f32[3,512,2048]{2,1,0:T(8,128)S(1)}, u32[]{:S(2)}) copy-start(f32[3,512,2048]{2,1,0:T(8,128)S(1)} %fusion.274) | copy-start | bytes 37748740 | tf_op jit(solution)/shard_map/while
  513.0 12.8 %copy-start.1 = (f32[3,512,2048]{2,1,0:T(8,128)S(1)}, f32[3,512,2048]{2,1,0:T(8,128)}, u32[]{:S(2)}) copy-start(f32[3,512,2048]{2,1,0:T(8,128)} %copy-done) | copy-start | bytes 37748740 | tf_op jit(solution)/shard_map/while
  534.4 10.5 copy-start
  551.1 12.4 %copy-start.1 = (f32[3,512,2048]{2,1,0:T(8,128)S(1)}, f32[3,512,2048]{2,1,0:T(8,128)}, u32[]{:S(2)}) copy-start(f32[3,512,2048]{2,1,0:T(8,128)} %copy-done) | copy-start | bytes 37748740 | tf_op jit(solution)/shard_map/while
  572.0 11.2 %copy-start = (f32[3,512,2048]{2,1,0:T(8,128)}, f32[3,512,2048]{2,1,0:T(8,128)S(1)}, u32[]{:S(2)}) copy-start(f32[3,512,2048]{2,1,0:T(8,128)S(1)} %fusion.274) | copy-start | bytes 37748740 | tf_op jit(solution)/shard_map/while
  589.5 12.8 %copy-start.1 = (f32[3,512,2048]{2,1,0:T(8,128)S(1)}, f32[3,512,2048]{2,1,0:T(8,128)}, u32[]{:S(2)}) copy-start(f32[3,512,2048]{2,1,0:T(8,128)} %copy-done) | copy-start | bytes 37748740 | tf_op jit(solution)/shard_map/while
  610.9 10.5 copy-start
  627.6 13.0 %copy-start.1 = (f32[3,512,2048]{2,1,0:T(8,128)S(1)}, f32[3,512,2048]{2,1,0:T(8,128)}, u32[]{:S(2)}) copy-start(f32[3,512,2048]{2,1,0:T(8,128)} %copy-done) | copy-start | bytes 37748740 | tf_op jit(solution)/shard_map/while
  655.4 164.0 %all-to-all-start.5 = ((bf16[2048,3,1,192]{3,1,2,0:T(4,128)(2,1)}), bf16[2048,3,1,192]{3,1,2,0:T(4,128)(2,1)}, u32[]{:S(2)}, u32[]{:S(2)}) async-start(bf16[2048,3,1,192]{3,1,2,0:T(4,128)(2,1)} %copy.205), calls=%async_computation.5 | async-start | bytes 8388608 | tf_op jit(solution)/shard_map/all_to_all | solution.py:240
  664.4 10.4 copy-start.2
  680.9 11.7 %copy-start.3 = (f32[3,512,2048]{2,1,0:T(8,128)S(1)}, f32[3,512,2048]{2,1,0:T(8,128)}, u32[]{:S(2)}) copy-start(f32[3,512,2048]{2,1,0:T(8,128)} %copy-done.2) | copy-start | bytes 37748740 | tf_op jit(solution)/shard_map/while
  701.2 10.4 copy-start.2
  717.7 12.2 %copy-start.3 = (f32[3,512,2048]{2,1,0:T(8,128)S(1)}, f32[3,512,2048]{2,1,0:T(8,128)}, u32[]{:S(2)}) copy-start(f32[3,512,2048]{2,1,0:T(8,128)} %copy-done.2) | copy-start | bytes 37748740 | tf_op jit(solution)/shard_map/while
  738.4 10.4 copy-start.2
  755.0 12.2 %copy-start.3 = (f32[3,512,2048]{2,1,0:T(8,128)S(1)}, f32[3,512,2048]{2,1,0:T(8,128)}, u32[]{:S(2)}) copy-start(f32[3,512,2048]{2,1,0:T(8,128)} %copy-done.2) | copy-start | bytes 37748740 | tf_op jit(solution)/shard_map/while
  775.7 10.4 copy-start.2
  792.2 12.2 %copy-start.3 = (f32[3,512,2048]{2,1,0:T(8,128)S(1)}, f32[3,512,2048]{2,1,0:T(8,128)}, u32[]{:S(2)}) copy-start(f32[3,512,2048]{2,1,0:T(8,128)} %copy-done.2) | copy-start | bytes 37748740 | tf_op jit(solution)/shard_map/while
  819.4 93.8 %all-to-all-start.7 = ((bf16[2048,3,1,192]{3,1,2,0:T(4,128)(2,1)}), bf16[2048,3,1,192]{3,1,2,0:T(4,128)(2,1)}, u32[]{:S(2)}, u32[]{:S(2)}) async-start(bf16[2048,3,1,192]{3,1,2,0:T(4,128)(2,1)} %copy.211), calls=%async_computation.7 | async-start | bytes 8388608 | tf_op jit(solution)/shard_map/all_to_all | solution.py:240
  824.3 183.1 %reduce-scatter.13.cloned.1.call-start = ((), (), s32[]{:S(2)}) async-start(), calls=%async_computation.19 | async-start | bytes 7962624
  940.3 150.8 %all-reduce.23.cloned.1.call-start = ((), (), s32[]{:S(2)}) async-start(), calls=%async_computation.20 | async-start | bytes 3833856 | tf_op jit(solution)/shard_map/psum | solution.py:281
  (90 other events, 399.4 us)
Sparse Core Ops, SparseCore 0:
  9.9 35.6 all-gather.5
  63.1 24.3 all-gather.7
  89.4 38.7 all-gather.9
  334.9 41.2 all-gather.11
  442.9 41.8 reduce-scatter.6
  488.2 76.8 reduce-scatter.10
  568.5 76.8 reduce-scatter.8
  940.4 66.8 reduce-scatter.12
  1011.2 79.8 all-reduce.22
where the time goes:
time: 1120 us; the launch traced here: 1100 us
  matrix products  449 us (40%)
  waiting for transfers between devices  212 us (19%)
  other arithmetic  165 us (15%)
  local copies, waits for them, and re-layouts  153 us (14%)
  blocking collectives  64.2 us (6%)
  starting transfers between devices  41.3 us (4%)
  between operations  17.7 us (2%)
    all_to_all x2, waiting for transfers between devices, per_device(): lax.all_to_all(grad_stack, 'seq', split_axis=0, concat_axis=2, tiled=True)  81.4 us
    dot_general x16, matrix products, block_scores(): jnp.einsum('qgd,kgd->gqk', qblock, keys, preferred_element_type=jnp.float32)  70 us
    dot_general x8, matrix products, back(): jnp.einsum('qgd,kgd->gqk', grad_block, values, preferred_element_type=jnp...  55.6 us
    unnamed x10, waiting for transfers between devices  54.8 us
    reduce_sum x8, other arithmetic, attend(): total = jnp.sum(expd, axis=-1, keepdims=True)  54.1 us
    dot_general x8, matrix products, attend(): jnp.einsum('gqk,kgd->qgd', probs, values, preferred_element_type=jnp.floa...  53.5 us
    dot_general x8, matrix products, back(): jnp.einsum('gqk,kgd->qgd', grad_scores, keys, preferred_element_type=jnp....  52.1 us
    convert_element_type x8, other arithmetic, back(): grad_scores = (probs * (grad_probs - delta)).astype(jnp.bfloat16)  49.4 us
  transfers between devices with their start and end apart: 17, of which 5 were waited for; matrix products, arithmetic and copies ran while one was open for 62% of the time, Pallas kernels for 0%

commit v1 on v0

v1 whole, which is shorter than its diff:
```python
import functools
import math

import jax
import jax.numpy as jnp
from jax import lax
from jax.experimental import pallas as pl
from jax.experimental.pallas import tpu as pltpu
from jax.sharding import Mesh
from jax.sharding import PartitionSpec as P

HEAD_DIM = 64
LANES = 128
NEG = -1e30
TILE = 256
NT = (((1,), (1,)), ((), ()))
NN = (((1,), (0,)), ((), ()))
TN = (((0,), (0,)), ((), ()))


def mm(left, right, dims):
    return lax.dot_general(left, right, dims, preferred_element_type=jnp.float32)


def key_tiles(ends_ref, first, last, tile, total):
    low = jnp.int32(0)
    high = jnp.int32(total)
    for doc in reversed(range(ends_ref.shape[0])):
        end = ends_ref[doc]
        low = jnp.maximum(low, jnp.where(end <= first, end, 0))
        high = jnp.minimum(high, jnp.where(end > last, end, total))
    return low // tile, (high + tile - 1) // tile


def lane_halves(x, fill):
    lane = lax.broadcasted_iota(jnp.int32, x.shape, 1)
    fill = jnp.full_like(x, fill)
    return jnp.where(lane < HEAD_DIM, x, fill), jnp.where(lane < HEAD_DIM, fill, x)


def piece_copies(halves, columns, place, scratch, slot, sems, run, mask, inbound):
    copies = []
    pieces = halves[0].shape[0] // run
    for half, ref in enumerate(halves):
        for part in range(pieces):
            index = half * pieces + part
            natural = pl.multiple_of(jnp.bitwise_xor(mask, index) * run, run)
            outer = ref.at[pl.ds(part * run, run), pl.ds(columns, LANES)]
            inner = scratch.at[place, pl.ds(natural, run), :]
            ends = (outer, inner) if inbound else (inner, outer)
            copies.append(pltpu.make_async_copy(ends[0], ends[1], sems.at[slot, index]))
    return copies


def forward_kernel(run, mask_ref, ends_ref, own, sib, seg_col, seg_row, ctx_own, ctx_sib, lse_ref, qkv, out, acc, top, sems, out_sems):
    total = qkv.shape[1]
    pairs = out.shape[0]
    width = pairs * LANES
    mask = mask_ref[0]

    def loads(pair):
        copies = []
        for kind in range(3):
            copies += piece_copies(
                (own, sib), kind * width + pair * LANES, kind * pairs + pair, qkv, kind * pairs + pair, sems, run, mask, True
            )
        return copies

    for pair in range(pairs):
        for copy in loads(pair):
            copy.start()

    for pair in range(pairs):
        for copy in loads(pair):
            copy.wait()

        @pl.loop(0, total // TILE)
        def _(block):
            rows = pl.multiple_of(block * TILE, TILE)
            q_heads = lane_halves(qkv[pair, pl.ds(rows, TILE), :], 0.0)
            segq = seg_col[pl.ds(rows, TILE), :]
            segq = jnp.concatenate([segq] * (TILE // LANES), axis=1)
            first, after = key_tiles(ends_ref, rows, rows + TILE - 1, TILE, total)
            acc[...] = jnp.zeros_like(acc)
            top[...] = jnp.full_like(top, NEG)

            @pl.loop(first, after)
            def _(step):
                at = pl.multiple_of(step * TILE, TILE)
                keys = qkv[pairs + pair, pl.ds(at, TILE), :]
                v_heads = lane_halves(qkv[2 * pairs + pair, pl.ds(at, TILE), :], 1.0)
                same = segq == seg_row[:, pl.ds(at, TILE)]
                for head in range(2):
                    scores = jnp.where(same, mm(q_heads[head], keys, NT), NEG)
                    old = top[head]
                    new = jnp.maximum(old, jnp.max(scores, axis=1, keepdims=True))
                    top[head] = new
                    probs = jnp.exp(scores - jnp.concatenate([new] * (TILE // LANES), axis=1)).astype(jnp.bfloat16)
                    acc[head] = acc[head] * jnp.exp(old - new) + mm(probs, v_heads[head], NN)

            lane = lax.broadcasted_iota(jnp.int32, (TILE, LANES), 1)
            sum_a = acc[0][:, HEAD_DIM : HEAD_DIM + 1]
            sum_b = acc[1][:, 0:1]
            out[pair, pl.ds(rows, TILE), :] = jnp.where(lane < HEAD_DIM, acc[0] / sum_a, acc[1] / sum_b).astype(jnp.bfloat16)
            lse_a = (top[0] + jnp.log(sum_a)).T
            lse_b = (top[1] + jnp.log(sum_b)).T
            lse_ref[2 * pair, :, pl.ds(rows, TILE)] = lse_a[0:8]
            lse_ref[2 * pair + 1, :, pl.ds(rows, TILE)] = lse_b[0:8]

        for copy in piece_copies((ctx_own, ctx_sib), pair * LANES, pair, out, pair, out_sems, run, mask, False):
            copy.start()
    for pair in range(pairs):
        for copy in piece_copies((ctx_own, ctx_sib), pair * LANES, pair, out, pair, out_sems, run, mask, False):
            copy.wait()


def attend_forward(mask, ends, own, sib, seg_col, seg_row, run):
    half, columns = own.shape
    total = 2 * half
    pairs = columns // (3 * LANES)
    pieces = total // run
    any_spec = pl.BlockSpec(memory_space=pl.ANY)
    vmem = pl.BlockSpec(memory_space=pltpu.VMEM)
    smem = pl.BlockSpec(memory_space=pltpu.SMEM)
    return pl.pallas_call(
        functools.partial(forward_kernel, run),
        out_shape=(
            jax.ShapeDtypeStruct((half, pairs * LANES), jnp.bfloat16),
            jax.ShapeDtypeStruct((half, pairs * LANES), jnp.bfloat16),
            jax.ShapeDtypeStruct((2 * pairs, 8, total), jnp.float32),
        ),
        in_specs=[smem, smem, any_spec, any_spec, vmem, vmem],
        out_specs=(any_spec, any_spec, vmem),
        scratch_shapes=[
            pltpu.VMEM((3 * pairs, total, LANES), jnp.bfloat16),
            pltpu.VMEM((pairs, total, LANES), jnp.bfloat16),
            pltpu.VMEM((2, TILE, LANES), jnp.float32),
            pltpu.VMEM((2, TILE, LANES), jnp.float32),
            pltpu.SemaphoreType.DMA((3 * pairs, pieces)),
            pltpu.SemaphoreType.DMA((pairs, pieces)),
        ],
        compiler_params=pltpu.CompilerParams(vmem_limit_bytes=40 << 20),
        name="attend_forward",
    )(mask, ends, own, sib, seg_col, seg_row)


def backward_kernel(
    run, mask_ref, ends_ref, own, sib, ctx_own, ctx_sib, dctx_own, dctx_sib, seg_col, seg_row, lse_ref,
    d_own, d_sib, qkv, ctx, dctx, out, delta, dq, dkv, sems, out_sems
):
    total = qkv.shape[1]
    pairs = ctx.shape[0]
    width = pairs * LANES
    mask = mask_ref[0]

    def loads(pair):
        copies = []
        for kind in range(3):
            copies += piece_copies(
                (own, sib), kind * width + pair * LANES, kind * pairs + pair, qkv, kind * pairs + pair, sems, run, mask, True
            )
        copies += piece_copies((ctx_own, ctx_sib), pair * LANES, pair, ctx, 3 * pairs + pair, sems, run, mask, True)
        copies += piece_copies((dctx_own, dctx_sib), pair * LANES, pair, dctx, 4 * pairs + pair, sems, run, mask, True)
        return copies

    def stores(pair):
        copies = []
        for kind in range(3):
            copies += piece_copies(
                (d_own, d_sib), kind * width + pair * LANES, kind * pairs + pair, out, kind * pairs + pair, out_sems, run, mask, False
            )
        return copies

    for pair in range(pairs):
        for copy in loads(pair):
            copy.start()

    for pair in range(pairs):
        for copy in loads(pair):
            copy.wait()

        @pl.loop(0, total // TILE)
        def _(block):
            rows = pl.multiple_of(block * TILE, TILE)
            product = ctx[pair, pl.ds(rows, TILE), :].astype(jnp.float32) * dctx[pair, pl.ds(rows, TILE), :].astype(jnp.float32)
            product = product.T
            for head in range(2):
                part = jnp.sum(product[head * HEAD_DIM : (head + 1) * HEAD_DIM], axis=0, keepdims=True)
                delta[head, :, pl.ds(rows, TILE)] = jnp.broadcast_to(part, (8, TILE))
            dq[pl.ds(rows, TILE), :] = jnp.zeros((TILE, LANES), jnp.float32)

        @pl.loop(0, total // TILE)
        def _(block):
            rows = pl.multiple_of(block * TILE, TILE)
            k_heads = lane_halves(qkv[pairs + pair, pl.ds(rows, TILE), :], 0.0)
            v_heads = lane_halves(qkv[2 * pairs + pair, pl.ds(rows, TILE), :], 0.0)
            segk = seg_col[pl.ds(rows, TILE), :]
            segk = jnp.concatenate([segk] * (TILE // LANES), axis=1)
            first, after = key_tiles(ends_ref, rows, rows + TILE - 1, TILE, total)
            dkv[...] = jnp.zeros_like(dkv)

            @pl.loop(first, after)
            def _(step):
                at = pl.multiple_of(step * TILE, TILE)
                queries = qkv[pair, pl.ds(at, TILE), :]
                grads = dctx[pair, pl.ds(at, TILE), :]
                q_heads = lane_halves(queries, 0.0)
                g_heads = lane_halves(grads, 0.0)
                same = segk == seg_row[:, pl.ds(at, TILE)]
                for head in range(2):
                    scores = mm(k_heads[head], queries, NT)
                    lse = lse_ref[2 * pair + head, 0:1, pl.ds(at, TILE)]
                    probs = jnp.exp(jnp.where(same, scores - lse, NEG))
                    dprobs = mm(v_heads[head], grads, NT)
                    dscores = (probs * (dprobs - delta[head, 0:1, pl.ds(at, TILE)])).astype(jnp.bfloat16)
                    dkv[1] += mm(probs.astype(jnp.bfloat16), g_heads[head], NN)
                    dkv[0] += mm(dscores, q_heads[head], NN)
                    dq[pl.ds(at, TILE), :] += mm(dscores, k_heads[head], TN)

            out[pairs + pair, pl.ds(rows, TILE), :] = dkv[0].astype(jnp.bfloat16)
            out[2 * pairs + pair, pl.ds(rows, TILE), :] = dkv[1].astype(jnp.bfloat16)

        out[pair] = (dq[...] * HEAD_DIM**-0.5).astype(jnp.bfloat16)
        for copy in stores(pair):
            copy.start()
    for pair in range(pairs):
        for copy in stores(pair):
            copy.wait()


def attend_backward(mask, ends, own, sib, ctx_own, ctx_sib, dctx_own, dctx_sib, seg_col, seg_row, lse, run):
    half, columns = own.shape
    total = 2 * half
    pairs = columns // (3 * LANES)
    pieces = total // run
    any_spec = pl.BlockSpec(memory_space=pl.ANY)
    vmem = pl.BlockSpec(memory_space=pltpu.VMEM)
    smem = pl.BlockSpec(memory_space=pltpu.SMEM)
    return pl.pallas_call(
        functools.partial(backward_kernel, run),
        out_shape=(
            jax.ShapeDtypeStruct((half, columns), jnp.bfloat16),
            jax.ShapeDtypeStruct((half, columns), jnp.bfloat16),
        ),
        in_specs=[smem, smem] + [any_spec] * 6 + [vmem] * 3,
        out_specs=(any_spec, any_spec),
        scratch_shapes=[
            pltpu.VMEM((3 * pairs, total, LANES), jnp.bfloat16),
            pltpu.VMEM((pairs, total, LANES), jnp.bfloat16),
            pltpu.VMEM((pairs, total, LANES), jnp.bfloat16),
            pltpu.VMEM((3 * pairs, total, LANES), jnp.bfloat16),
            pltpu.VMEM((2, 8, total), jnp.float32),
            pltpu.VMEM((total, LANES), jnp.float32),
            pltpu.VMEM((2, TILE, LANES), jnp.float32),
            pltpu.SemaphoreType.DMA((5 * pairs, pieces)),
            pltpu.SemaphoreType.DMA((3 * pairs, pieces)),
        ],
        compiler_params=pltpu.CompilerParams(vmem_limit_bytes=48 << 20),
        name="attend_backward",
    )(mask, ends, own, sib, ctx_own, ctx_sib, dctx_own, dctx_sib, seg_col, seg_row, lse)


EPS = 1e-05


def norm_forward(resid, gain, shift):
    mean = jnp.mean(resid, axis=-1, keepdims=True)
    centered = resid - mean
    inv = lax.rsqrt(jnp.mean(centered * centered, axis=-1, keepdims=True) + EPS)
    normed = centered * inv
    return (normed * gain + shift, normed, inv)


def norm_backward(grad, normed, inv, gain):
    scaled = grad * gain
    return inv * (
        scaled
        - jnp.mean(scaled, axis=-1, keepdims=True)
        - normed * jnp.mean(scaled * normed, axis=-1, keepdims=True)
    )


def gelu_slope(pre):
    cdf = 0.5 * (1.0 + lax.erf(pre * (1.0 / math.sqrt(2.0))))
    density = jnp.exp(-0.5 * pre * pre) * (1.0 / math.sqrt(2.0 * math.pi))
    return cdf + pre * density


def doc_ids(ends, count):
    places = jnp.arange(count, dtype=jnp.int32)
    return jnp.sum((places[:, None] >= ends[None, :]).astype(jnp.int32), axis=1)


CORES = 2


def routes(nseq):
    first, second = [], []
    for core in range(CORES):
        for z in range(nseq):
            source = core * nseq + z
            first.append((source, (z // 2) * nseq + 2 * core + z % 2))
            second.append((source, (z // 2) * nseq + 2 * core + 1 - z % 2))
    return first, second


def swap(x):
    return lax.ppermute(x, "core", [(0, 1), (1, 0)])


def either(core, own, other, axis):
    return jnp.where(core == 0, jnp.concatenate([own, other], axis), jnp.concatenate([other, own], axis))


def per_device(
    tokens, doc_lengths, qkv_weight, q_bias, v_bias, out_weight, out_bias, norm1_gain, norm1_bias,
    ff_in_weight, ff_in_bias, ff_out_weight, ff_out_bias, norm2_gain, norm2_bias, out_cotangent,
):
    bf16, f32 = jnp.bfloat16, jnp.float32
    fsdp = ("xy", "core")
    nseq = lax.axis_size("seq")
    planes = lax.axis_size("xy")
    shards = planes * CORES
    core = lax.axis_index("core")
    odd = lax.axis_index("seq") % 2
    micro, run, width = tokens.shape[1:]
    assert micro == 2 and nseq == 4
    stretch = run * nseq
    mine = width // CORES
    rows = width // shards
    first, second = routes(nseq)
    back = [[(b, a) for a, b in route] for route in (first, second)]

    def spread(x):
        halves = [lax.dynamic_index_in_dim(x[0], which, 0, keepdims=False) for which in (odd, 1 - odd)]
        return [lax.ppermute(h, ("core", "seq"), r) for h, r in zip(halves, (first, second))]

    def collect(x):
        got = [lax.ppermute(x[i * run : (i + 1) * run], ("core", "seq"), back[i]) for i in range(2)]
        return jnp.where(odd == 0, jnp.stack(got), jnp.stack(got[::-1]))[None]

    pieces = spread(tokens)
    lengths = jnp.stack([doc_lengths[0], swap(doc_lengths[0])])
    z = lax.axis_index("seq")
    theirs = jnp.where(z // 2 == core, lengths[0], lengths[1])
    ends = jnp.cumsum(lax.dynamic_index_in_dim(theirs, odd, 0, keepdims=False)).astype(jnp.int32)
    seg = doc_ids(ends, stretch)
    seg_col = jnp.broadcast_to(seg[:, None], (stretch, LANES))
    seg_row = seg[None]
    mask = (odd + 2 * core).astype(jnp.int32)[None]

    small = [q_bias, v_bias, out_bias, norm1_gain, norm1_bias, ff_out_bias, norm2_gain, norm2_bias, ff_in_bias]
    vector = jnp.concatenate(small)
    packed = jnp.zeros((16, 3 * width), bf16).at[0, : vector.shape[0]].set(vector)
    packed = jnp.concatenate([qkv_weight, packed], axis=0)
    packed = lax.all_gather(packed, fsdp, axis=0, tiled=False)
    w_qkv = packed[:, :rows].reshape(width, 3, CORES, mine)
    w_mine = lax.dynamic_index_in_dim(w_qkv, core, 2, keepdims=False).reshape(width, 3 * mine)
    vectors = packed[:, rows, : vector.shape[0]].astype(f32)
    bias_q, bias_v, bias_out, gain_one, shift_one, bias_down, gain_two, shift_two = [
        vectors[:, i * rows : (i + 1) * rows].reshape(width) for i in range(8)
    ]
    bias_in = vectors[:, 8 * rows :].reshape(-1)
    w_out = lax.all_gather(out_weight, fsdp, axis=0, tiled=True)
    w_in = lax.all_gather(ff_in_weight, fsdp, axis=0, tiled=True)
    w_down = lax.all_gather(ff_out_weight, fsdp, axis=0, tiled=True)

    own_slice = lambda v: lax.dynamic_slice_in_dim(v, core * mine, mine, 0)
    bias_mine = jnp.concatenate([own_slice(bias_q), jnp.zeros((mine,), f32), own_slice(bias_v)])
    scale = jnp.concatenate([jnp.full((mine,), HEAD_DIM**-0.5, f32), jnp.ones((2 * mine,), f32)])
    x_own = jnp.concatenate(pieces)
    x_sib = jnp.concatenate([swap(p) for p in pieces])
    projected = [((mm(x, w_mine, NN) + bias_mine) * scale).astype(bf16) for x in (x_own, x_sib)]
    ctx_own, ctx_sib, lse = attend_forward(mask, ends, *projected, seg_col, seg_row, run)
    ctx_far = swap(ctx_sib)

    wo_own = lax.dynamic_slice_in_dim(w_out, core * mine, mine, 0)
    wo_far = lax.dynamic_slice_in_dim(w_out, (1 - core) * mine, mine, 0)
    attn = mm(ctx_own, wo_own, NN) + mm(ctx_far, wo_far, NN) + bias_out
    hidden, normed_one, inv_one = norm_forward(x_own.astype(f32) + attn, gain_one, shift_one)
    hidden_low = hidden.astype(bf16)
    pre = mm(hidden_low, w_in, NN) + bias_in
    act_low = jax.nn.gelu(pre, approximate=False).astype(bf16)
    resid_two = hidden + mm(act_low, w_down, NN) + bias_down
    result, normed_two, inv_two = norm_forward(resid_two, gain_two, shift_two)
    output = collect(result.astype(bf16))

    grad_out = jnp.concatenate(spread(out_cotangent)).astype(f32)
    gain_two_grad = jnp.sum(grad_out * normed_two, axis=0)
    shift_two_grad = jnp.sum(grad_out, axis=0)
    grad_two = norm_backward(grad_out, normed_two, inv_two, gain_two)
    grad_down = grad_two.astype(bf16)
    down_grad = mm(act_low, grad_down, TN).astype(bf16)
    down_grad = lax.psum_scatter(down_grad, fsdp, scatter_dimension=0, tiled=True)
    down_grad = lax.psum(down_grad, "seq").astype(f32)
    down_bias_grad = jnp.sum(grad_down.astype(f32), axis=0)
    grad_pre = (mm(grad_down, w_down, NT) * gelu_slope(pre)).astype(bf16)
    in_grad = mm(hidden_low, grad_pre, TN).astype(bf16)
    in_grad = lax.psum_scatter(in_grad, fsdp, scatter_dimension=0, tiled=True)
    in_grad = lax.psum(in_grad, "seq").astype(f32)
    in_bias_grad = jnp.sum(grad_pre.astype(f32), axis=0)
    grad_hidden = grad_two + mm(grad_pre, w_in, NT)
    gain_one_grad = jnp.sum(grad_hidden * normed_one, axis=0)
    shift_one_grad = jnp.sum(grad_hidden, axis=0)
    grad_one = norm_backward(grad_hidden, normed_one, inv_one, gain_one)
    grad_attn = grad_one.astype(bf16)
    dctx_far = swap(mm(grad_attn, wo_far, NT).astype(bf16))
    dctx_own = mm(grad_attn, wo_own, NT).astype(bf16)
    out_bias_grad = jnp.sum(grad_attn.astype(f32), axis=0)
    out_grad = [mm(c, grad_attn, TN).astype(bf16) for c in (ctx_own, ctx_far)]
    out_grad = lax.psum_scatter(either(core, *out_grad, 0), fsdp, scatter_dimension=0, tiled=True)
    out_grad = lax.psum(out_grad, "seq").astype(f32)

    d_own, d_sib = attend_backward(
        mask, ends, *projected, ctx_own, ctx_sib, dctx_own, dctx_far, seg_col, seg_row, lse, run
    )
    grad_far = swap(mm(d_sib, w_mine, NT).astype(bf16))
    input_grad = grad_one + mm(d_own, w_mine, NT) + grad_far.astype(f32)
    input_grad = collect(input_grad.astype(bf16)).astype(f32)

    qkv_grad = (mm(x_own, d_own, TN) + mm(x_sib, d_sib, TN)).astype(bf16)
    columns = jnp.sum(d_own.astype(f32), axis=0) + jnp.sum(d_sib.astype(f32), axis=0)
    none = jnp.zeros((mine,), f32)
    q_bias_grad = either(core, columns[:mine], none, 0)
    v_bias_grad = either(core, columns[2 * mine :], none, 0)
    small = [q_bias_grad, v_bias_grad, out_bias_grad, gain_one_grad, shift_one_grad, down_bias_grad,
             gain_two_grad, shift_two_grad, in_bias_grad]
    vector = jnp.concatenate([v.reshape(shards, -1) for v in small], axis=1).astype(bf16)
    vector = vector.reshape(planes, CORES, -1)
    vector = jnp.pad(vector, ((0, 0), (0, 16 - CORES), (0, 3 * mine - vector.shape[2])))
    packed = jnp.concatenate([qkv_grad.reshape(planes, CORES * rows, 3 * mine), vector], axis=1)
    packed = lax.psum_scatter(packed.reshape(-1, 3 * mine), "xy", scatter_dimension=0, tiled=True)
    packed = lax.psum(packed, "seq")
    block = packed[: CORES * rows].reshape(CORES, rows, 3 * mine)
    tail = packed[CORES * rows : CORES * rows + CORES]
    pick = lambda v, which: lax.dynamic_index_in_dim(v, which, 0, keepdims=False)
    block_far, tail_far = swap(pick(block, 1 - core)), swap(pick(tail, 1 - core))
    own_block = pick(block, core).reshape(rows, 3, 1, mine)
    qkv_final = either(core, own_block, block_far.reshape(rows, 3, 1, mine), 2).reshape(rows, 3 * width).astype(f32)
    tail = pick(tail, core).astype(f32) + tail_far.astype(f32)
    g = [tail[i * rows : (i + 1) * rows] for i in range(8)]
    return (
        output, input_grad, qkv_final, g[0], g[1], out_grad, g[2], g[3], g[4], in_grad,
        tail[8 * rows : 8 * rows + ff_in_bias.shape[0]], down_grad, g[5], g[6], g[7],
    )


def solution(mesh):
    fsdp, nseq = mesh.shape["fsdp"], mesh.shape["seq"]
    fine = Mesh(mesh.devices.reshape(fsdp // CORES, CORES, nseq), ("xy", "core", "seq"))
    shard = ("xy", "core")
    stream, matrix, vector = P(shard, None, "seq", None), P(shard, None), P(shard)
    return jax.shard_map(
        per_device,
        mesh=fine,
        in_specs=(
            stream, P(shard, None, None), matrix, vector, vector, matrix, vector, vector, vector,
            matrix, vector, matrix, vector, vector, vector, stream,
        ),
        out_specs=(
            stream, stream, matrix, vector, vector, matrix, vector, vector, vector,
            matrix, vector, matrix, vector, vector, vector,
        ),
        check_vma=False,
    )
```

time: 1120 us -> 674 us (0.60)
  matrix products: 449 us -> 124 us
  Pallas kernels: 0 us -> 171 us
  other arithmetic: 165 us -> 28.7 us
  local copies, waits for them, and re-layouts: 153 us -> 71.3 us
  blocking collectives: 64.2 us -> 0 us
  starting transfers between devices: 41.3 us -> 22.7 us
  waiting for transfers between devices: 212 us -> 229 us
    dot_general x80 -> x18, matrix products: 449 us -> 124 us  [mm(): lax.dot_general(left, right, dims, preferred_element_type=jnp.float32)]
    pallas_call x0 -> x2, Pallas kernels: none -> 171 us  [the longest x1 88.3 us: attend_backward(): pl.pallas_call(functools.partial(backward_kernel, run), out_shape=(jax.Sh...]
    all_to_all x8 -> x0, waiting for transfers between devices: 116 us -> none  [the longest x2 81.4 us: per_device(): lax.all_to_all(grad_stack, 'seq', split_axis=0, concat_axis=2, tiled=True)]
    reduce_scatter x3, waiting for transfers between devices: 0.02 us -> 113 us  [the longest x1 57.3 us: per_device(): in_grad = lax.psum_scatter(in_grad, fsdp, scatter_dimension=0, tiled=True)]
    ppermute x0 -> x16, waiting for transfers between devices: none -> 99.7 us  [the longest x4 65.3 us: collect(): lax.ppermute(x[i * run:(i + 1) * run], ('core', 'seq'), back[i])]
    reduce_sum x12 -> x4, other arithmetic: 62.1 us -> 6.68 us  [the longest x1 2.17 us: per_device(): jnp.sum(d_sib.astype(f32), axis=0)]
    convert_element_type x32 -> x8, other arithmetic: 65.6 us -> 10.9 us  [the longest x2 6.91 us: per_device(): input_grad = collect(input_grad.astype(bf16)).astype(f32)]
    unnamed x10, waiting for transfers between devices: 54.8 us -> 1.49 us
  transfers between devices with their start and end apart: 17 -> 25, of which waited for: 5 -> 7; matrix products, arithmetic and copies ran while one was open for 62% -> 26% of each run, Pallas kernels for 0% -> 26%
where the time goes in v1:
time: 674 us; the launch traced here: 661 us
  waiting for transfers between devices  229 us (34%)
  Pallas kernels  171 us (25%)
  matrix products  124 us (18%)
  local copies, waits for them, and re-layouts  71.3 us (11%)
  other arithmetic  28.7 us (4%)
  starting transfers between devices  22.7 us (3%)
  between operations  14.9 us (2%)
    dot_general x18, matrix products, mm(): lax.dot_general(left, right, dims, preferred_element_type=jnp.float32)  124 us
    pallas_call x1, Pallas kernels, attend_backward(): pl.pallas_call(functools.partial(backward_kernel, run), out_shape=(jax.Sh...  88.3 us
    pallas_call x1, Pallas kernels, attend_forward(): pl.pallas_call(functools.partial(forward_kernel, run), out_shape=(jax.Sha...  82.3 us
    ppermute x4, waiting for transfers between devices, collect(): lax.ppermute(x[i * run:(i + 1) * run], ('core', 'seq'), back[i])  65.3 us
    reduce_scatter x1, waiting for transfers between devices, per_device(): in_grad = lax.psum_scatter(in_grad, fsdp, scatter_dimension=0, tiled=True)  57.3 us
    reduce_scatter x1, waiting for transfers between devices, per_device(): lax.psum_scatter(down_grad, fsdp, scatter_dimension=0, tiled=True)  55.4 us
    ppermute x4, waiting for transfers between devices, spread(): lax.ppermute(h, ('core', 'seq'), r)  34.4 us
    dynamic_slice x2, local copies, waits for them, and re-layouts, per_device(): lax.dynamic_index_in_dim(w_qkv, core, 2, keepdims=False)  19.1 us
  transfers between devices with their start and end apart: 25, of which 7 were waited for; matrix products, arithmetic and copies ran while one was open for 26% of the time, Pallas kernels for 26%

profile of v1, /device:TPU:9, one launch (start us, length us, event | category | flops | bytes accessed | tf_op | source)
XLA Modules:
  0.0 661.0 jit_solution(16594873737122987197)
XLA Ops:
  7.2 6.1 concatenate.99
  13.3 1.8 fusion.34
  16.8 2.1 constant_dynamic-slice_fusion.2
  20.0 4.8 collective-permute-start
  25.9 22.5 %collective-permute-done = bf16[512,768]{0,1:T(8,128)(2,1)} collective-permute-done((bf16[512,768]{0,1:T(8,128)(2,1)}, bf16[512,768]{0,1:T(8,128)(2,1)}, u32[]{:S(2)}, u32[]{:S(2)}) %collective-permute-start) | collective-permute-done | bytes 786464 | tf_op jit(solution)/shard_map/ppermute | solution.py:336
  50.2 5.5 collective-permute-start.8
  56.8 11.9 %collective-permute-done.1 = bf16[512,768]{0,1:T(8,128)(2,1)} collective-permute-done((bf16[512,768]{0,1:T(8,128)(2,1)}, bf16[512,768]{0,1:T(8,128)(2,1)}, u32[]{:S(2)}, u32[]{:S(2)}) %collective-permute-start.1) | collective-permute-done | bytes 786464 | tf_op jit(solution)/shard_map/ppermute | solution.py:336
  71.5 2.7 constant_dynamic-update-slice_fusion.3
  74.2 2.1 constant_dynamic-update-slice_fusion.2
  76.2 4.0 slice.132
  81.6 7.9 %reshape.343 = bf16[768,3,2,384]{3,2,1,0:T(2,128)(2,1)} reshape(bf16[8,96,2304]{2,1,0:T(8,128)(2,1)} %slice.132) | data formatting | bytes 7077888 | tf_op jit(solution)/shard_map/reshape | solution.py:357
  89.5 7.6 %constant_dynamic-slice_fusion.3 = bf16[768,3,1,384]{3,2,1,0:T(2,128)(2,1)} fusion(bf16[768,3,2,384]{3,2,1,0:T(2,128)(2,1)} %reshape.343, s32[]{:T(128)S(6)} %select_n.113), kind=kLoop, calls=%fused_computation.108 | loop fusion | bytes 3538948 | tf_op jit(solution)/shard_map/jit(dynamic_index_in_dim)/dynamic_slice | solution.py:358
  97.0 11.5 %copy.89 = bf16[768,3,1,384]{0,3,1,2:T(8,128)(2,1)} copy(bf16[768,3,1,384]{3,2,1,0:T(2,128)(2,1)} %constant_dynamic-slice_fusion.3) | data formatting | bytes 3538944 | tf_op jit(solution)/shard_map/jit(dynamic_index_in_dim)/dynamic_slice | solution.py:358
  108.6 4.3 multiply_convert_fusion.sib
  112.9 2.3 multiply_convert_fusion.1.own
  115.6 82.3 %attend_forward.1 = (bf16[1024,384]{1,0:T(8,128)(2,1)S(1)}, bf16[1024,384]{1,0:T(8,128)(2,1)}, f32[6,8,2048]{2,1,0:T(8,128)S(1)}) custom-call(s32[1]{0:T(128)} %bitcast.2.mask_ref, s32[8]{0:T(128)S(1)} %bitcast.59, bf16[1024,1152]{1,0:T(8,128)(2,1)S(1)} %multiply_convert_fusion.1.own, bf16[1024,1152]{1,0:T(8,128)(2,1)S(1)} %multiply_convert_fusion.sib, ...), custom_call_target="tpu_custom_call" | custom-call | tf_op jit(solution)/shard_map/attend_forward/pallas_call | solution.py:125
  201.1 2.3 fusion.32
  203.4 2.4 fusion.57
  205.8 1.6 copy-done.6
  207.9 39.6 %fusion.2 = (bf16[1024,3072]{1,0:T(8,128)(2,1)}, f32[1024,3072]{1,0:T(8,128)}) fusion(f32[3072]{0:T(1024)S(1)} %add.201, bf16[768,3072]{1,0:T(8,128)(2,1)} %all-gather.8.cloned.1.call-done, f32[1024,768]{0,1:T(8,128)} %copy-done.6, f32[768]{0:T(1024)S(1)} %add.198, f32[768]{0:T(1024)S(1)} %mul.166, f32[1024]{0:T(1024)S(1)} %add_rsqrt_fusion.1, ...), kind=kOutput, calls=%fused_computation.4 | convolution fusion | flops 5043388416 | bytes 26765312 | tf_op jit(solution)/shard_map/dot_general | solution.py:22
  247.5 9.4 %fusion.58 = (f32[1024]{0:T(1024)S(1)}, f32[1024,768]{0,1:T(8,128)S(1)}) fusion(f32[768]{0:T(1024)S(1)} %add.205, bf16[1024,3072]{1,0:T(8,128)(2,1)} %get-tuple-element.173, bf16[3072,768]{1,0:T(8,128)(2,1)} %all-gather.10.cloned.1.call-done, f32[768]{0:T(1024)S(1)} %add.198, f32[768]{0:T(1024)S(1)} %mul.166, f32[1024]{0:T(1024)S(1)} %add_rsqrt_fusion.1, ...), kind=kOutput, calls=%fused_computation.130 | convolution fusion | flops 4837342208 | bytes 17323008 | tf_op jit(solution)/shard_map/dot_general | solution.py:22
  257.4 2.6 fusion.24
  261.4 12.4 %fusion.59 = (bf16[3072]{0:T(1024)(128)(2,1)S(1)}, bf16[1024,3072]{1,0:T(8,128)(2,1)S(1)}) fusion(f32[1024,3072]{1,0:T(8,128)} %get-tuple-element.174, f32[3072]{0:T(1024)S(1)} %add.201, bf16[1024,768]{0,1:T(8,128)(2,1)S(1)} %get-tuple-element.139, bf16[3072,768]{1,0:T(8,128)(2,1)S(1)} %bitcast.79), kind=kOutput, calls=%fused_computation.131 | convolution fusion | flops 4869583872 | bytes 25184256 | tf_op jit(solution)/shard_map/dot_general | solution.py:22
  273.8 6.6 multiply_reduce_fusion
  282.6 1.9 convolution_convert_fusion.3
  285.6 2.0 convolution_convert_fusion.5
  289.5 2.6 convolution_convert_fusion.4.dctx_own
  292.1 88.3 %attend_backward.1 = (bf16[1024,1152]{1,0:T(8,128)(2,1)}, bf16[1024,1152]{1,0:T(8,128)(2,1)}) custom-call(s32[1]{0:T(128)} %bitcast.2.mask_ref, s32[8]{0:T(128)S(1)} %bitcast.60, bf16[1024,1152]{1,0:T(8,128)(2,1)} %copy-done.1, bf16[1024,1152]{1,0:T(8,128)(2,1)} %copy-done, bf16[1024,384]{1,0:T(8,128)(2,1)S(1)} %copy-done.3, ...), custom_call_target="tpu_custom_call" | custom-call | tf_op jit(solution)/shard_map/attend_backward/pallas_call | solution.py:239
  380.5 2.2 convert_reduce_fusion
  382.6 2.1 convert_reduce_fusion.1
  385.1 4.0 fusion.61
  389.1 3.6 fusion.20
  394.8 9.9 %convolution_convert_fusion = bf16[3072,768]{1,0:T(8,128)(2,1)} fusion(bf16[1024,3072]{1,0:T(8,128)(2,1)} %get-tuple-element.173, bf16[1024,768]{0,1:T(8,128)(2,1)S(1)} %copy-done.18), kind=kOutput, calls=%fused_computation.26 | convolution fusion | flops 4834197504 | bytes 12582912 | tf_op jit(solution)/shard_map/dot_general | solution.py:22
  404.8 10.0 %convolution_convert_fusion.1 = bf16[768,3072]{1,0:T(8,128)(2,1)} fusion(bf16[1024,3072]{1,0:T(8,128)(2,1)} %copy-done.28, f32[1024,768]{0,1:T(8,128)} %copy-done.6, f32[768]{0:T(1024)S(1)} %add.198, f32[768]{0:T(1024)S(1)} %mul.166, f32[1024]{0:T(1024)S(1)} %add_rsqrt_fusion.1, f32[1024]{0:T(1024)S(1)} %broadcast_multiply_fusion.5), kind=kOutput, calls=%fused_computation.27 | convolution fusion | flops 4838129664 | bytes 14170112 | tf_op jit(solution)/shard_map/dot_general | solution.py:22
  415.0 5.7 convolution_convert_fusion.2
  422.3 2.4 collective-permute-start.7
  424.7 1.9 collective-permute-start.6
  426.7 3.9 fusion.60
  430.6 55.4 %reduce-scatter.11.cloned.1.call-done = bf16[384,768]{1,0:T(8,128)(2,1)} async-done(((bf16[3072,768]{1,0:T(8,128)(2,1)}), bf16[384,768]{1,0:T(8,128)(2,1)}) %reduce-scatter.11.cloned.1.call-update) | async-done | bytes 589840 | tf_op jit(solution)/shard_map/reduce_scatter | solution.py:394
  485.9 57.3 %reduce-scatter.9.cloned.1.call-done = bf16[96,3072]{1,0:T(8,128)(2,1)} async-done(((bf16[768,3072]{1,0:T(8,128)(2,1)}), bf16[96,3072]{1,0:T(8,128)(2,1)}) %reduce-scatter.9.cloned.1.call-update) | async-done | bytes 589840 | tf_op jit(solution)/shard_map/reduce_scatter | solution.py:399
  543.2 5.0 add_convert_fusion
  549.5 4.7 collective-permute-start.12
  554.3 2.3 maximum_select_fusion
  558.1 44.0 %collective-permute-done.12 = bf16[512,768]{0,1:T(8,128)(2,1)S(1)} collective-permute-done((bf16[512,768]{0,1:T(8,128)(2,1)}, bf16[512,768]{0,1:T(8,128)(2,1)S(1)}, u32[]{:S(2)}, u32[]{:S(2)}) %collective-permute-start.12) | collective-permute-done | bytes 786464 | tf_op jit(solution)/shard_map/ppermute | solution.py:339
  602.2 21.2 %collective-permute-done.13 = bf16[512,768]{0,1:T(8,128)(2,1)S(1)} collective-permute-done((bf16[512,768]{0,1:T(8,128)(2,1)}, bf16[512,768]{0,1:T(8,128)(2,1)S(1)}, u32[]{:S(2)}, u32[]{:S(2)}) %collective-permute-start.13) | collective-permute-done | bytes 786464 | tf_op jit(solution)/shard_map/ppermute | solution.py:339
  623.4 1.9 fusion.27
  625.3 3.5 copy.102
  628.9 15.3 %all-reduce.9.cloned.1.call-done = (bf16[208,1152]{1,0:T(8,128)(2,1)}, bf16[96,768]{1,0:T(8,128)(2,1)}, bf16[96,3072]{1,0:T(8,128)(2,1)}, bf16[384,768]{1,0:T(8,128)(2,1)}) async-done(((bf16[208,1152]{1,0:T(8,128)(2,1)}, bf16[96,768]{1,0:T(8,128)(2,1)}, bf16[96,3072]{1,0:T(8,128)(2,1)}, bf16[384,768]{1,0:T(8,128)(2,1)}), (bf16[208,1152]{1,0:T(8,128)(2,1)}, bf16[96,768]{1,0:T(8,128)(2,1)}, ...) | async-done | bytes 1806352 | tf_op jit(solution)/shard_map/psum | solution.py:433
  (196 shorter events, 38.8 us)
Async XLA Ops:
  7.2 69.0 %all-gather.12.cloned.1.call-start = ((), (), s32[]{:S(2)}) async-start(), calls=%async_computation.10 | async-start | bytes 4644864 | tf_op jit(solution)/shard_map/all_gather | solution.py:356
  15.2 185.8 %all-gather.6.cloned.1.call-start = ((), (), s32[]{:S(2)}) async-start(), calls=%async_computation.4 | async-start | bytes 1327104 | tf_op jit(solution)/shard_map/all_gather | solution.py:364
  16.0 191.9 %all-gather.8.cloned.1.call-start = ((), (), s32[]{:S(2)}) async-start(), calls=%async_computation.5 | async-start | bytes 5308416 | tf_op jit(solution)/shard_map/all_gather | solution.py:365
  16.7 230.8 %all-gather.10.cloned.1.call-start = ((), (), s32[]{:S(2)}) async-start(), calls=%async_computation.6 | async-start | bytes 5308416 | tf_op jit(solution)/shard_map/all_gather | solution.py:366
  18.8 29.7 %copy-start.25 = (s32[1,2,8]{2,1,0:T(2,128)S(1)}, s32[1,2,8]{2,1,0:T(2,128)}, u32[]{:S(2)}) copy-start(s32[1,2,8]{2,1,0:T(2,128)} %param.19) | copy-start | bytes 196
  20.0 28.5 %collective-permute-start = (bf16[512,768]{0,1:T(8,128)(2,1)}, bf16[512,768]{0,1:T(8,128)(2,1)}, u32[]{:S(2)}, u32[]{:S(2)}) collective-permute-start(bf16[512,768]{0,1:T(8,128)(2,1)} %bitcast.72), channel_id=1, source_target_pairs={{0,0},{1,1},{2,4},{3,5},{4,2},{5,3},{6,6},{7,7},{8,8},{9,9},{10,12... | collective-permute-start | bytes 2359304 | tf_op jit(solution)/shard_map/ppermute | solution.py:336
  25.9 42.7 %collective-permute-start.1 = (bf16[512,768]{0,1:T(8,128)(2,1)}, bf16[512,768]{0,1:T(8,128)(2,1)}, u32[]{:S(2)}, u32[]{:S(2)}) collective-permute-start(bf16[512,768]{0,1:T(8,128)(2,1)} %bitcast.1), channel_id=1, source_target_pairs={{0,1},{1,0},{2,5},{3,4},{4,3},{5,2},{6,7},{7,6},{8,9},{9,8},{10,13... | collective-permute-start | bytes 2359304 | tf_op jit(solution)/shard_map/ppermute | solution.py:336
  48.5 23.0 %collective-permute-start.3 = (bf16[512,768]{0,1:T(8,128)(2,1)}, bf16[512,768]{0,1:T(8,128)(2,1)}, u32[]{:S(2)}, u32[]{:S(2)}) collective-permute-start(bf16[512,768]{0,1:T(8,128)(2,1)} %collective-permute-done), channel_id=1, source_target_pairs={{0,4},{4,0},{1,5},{5,1},{2,6},{6,2},{3,7},{7,3},{8,12},{12,8},{9,1... | collective-permute-start | bytes 2359304 | tf_op jit(solution)/shard_map/ppermute | solution.py:308
  48.5 20.2 %collective-permute-start.2 = (s32[2,8]{1,0:T(2,128)S(1)}, s32[2,8]{1,0:T(2,128)S(1)}, u32[]{:S(2)}, u32[]{:S(2)}) collective-permute-start(s32[2,8]{1,0:T(2,128)S(1)} %bitcast.75), channel_id=1, source_target_pairs={{0,4},{4,0},{1,5},{5,1},{2,6},{6,2},{3,7},{7,3},{8,12},{12,8},{9,1... | collective-permute-start | bytes 200 | tf_op jit(solution)/shard_map/ppermute | solution.py:308
  50.2 150.0 %collective-permute-start.8 = (bf16[512,768]{0,1:T(8,128)(2,1)}, bf16[512,768]{0,1:T(8,128)(2,1)S(1)}, u32[]{:S(2)}, u32[]{:S(2)}) collective-permute-start(bf16[512,768]{0,1:T(8,128)(2,1)} %bitcast.11), channel_id=1, source_target_pairs={{0,0},{1,1},{2,4},{3,5},{4,2},{5,3},{6,6},{7,7},{8,8},{9,9},{10,12... | collective-permute-start | bytes 2359304 | tf_op jit(solution)/shard_map/ppermute | solution.py:336
  56.8 143.5 %collective-permute-start.9 = (bf16[512,768]{0,1:T(8,128)(2,1)}, bf16[512,768]{0,1:T(8,128)(2,1)S(1)}, u32[]{:S(2)}, u32[]{:S(2)}) collective-permute-start(bf16[512,768]{0,1:T(8,128)(2,1)} %bitcast.12), channel_id=1, source_target_pairs={{0,1},{1,0},{2,5},{3,4},{4,3},{5,2},{6,7},{7,6},{8,9},{9,8},{10,13... | collective-permute-start | bytes 2359304 | tf_op jit(solution)/shard_map/ppermute | solution.py:336
  68.7 5.5 collective-permute-start.4
  71.5 41.4 %copy-start.10 = (bf16[1024,768]{0,1:T(8,128)(2,1)}, bf16[1024,768]{0,1:T(8,128)(2,1)S(1)}, u32[]{:S(2)}) copy-start(bf16[1024,768]{0,1:T(8,128)(2,1)S(1)} %constant_dynamic-update-slice_fusion) | copy-start | bytes 4718596
  97.0 11.5 %copy-start.27 = (f32[1152]{0:T(1024)S(1)}, f32[1152]{0:T(1024)}, u32[]{:S(2)}) copy-start(f32[1152]{0:T(1024)} %constant.155.clone.1) | copy-start | bytes 13828
  108.6 4.4 copy-start.15
  115.2 82.7 %copy-start.1 = (bf16[1024,1152]{1,0:T(8,128)(2,1)}, bf16[1024,1152]{1,0:T(8,128)(2,1)S(1)}, u32[]{:S(2)}) copy-start(bf16[1024,1152]{1,0:T(8,128)(2,1)S(1)} %multiply_convert_fusion.1.own) | copy-start | bytes 7077892
  199.5 3.8 collective-permute-start.5
  200.1 230.5 %reduce-scatter.7.cloned.1.call-start = ((), (), s32[]{:S(2)}) async-start(), calls=%async_computation.7 | async-start | bytes 1327104 | tf_op jit(solution)/shard_map/reduce_scatter | solution.py:411
  257.0 4.4 slice-start.2
  257.4 4.0 slice-start.3
  260.0 13.8 %slice-start = ((s8[4718592]{0:T(1024)(128)(4,1)}), s8[4194304]{0:T(1024)(128)(4,1)S(1)}, s32[]{:S(2)}) async-start(s8[4718592]{0:T(1024)(128)(4,1)} %bitcast.76), calls=%async_computation.13 | async-start | bytes 8388608
  261.3 12.4 %copy-start.17 = (bf16[1024,768]{0,1:T(8,128)(2,1)}, bf16[1024,768]{0,1:T(8,128)(2,1)S(1)}, u32[]{:S(2)}) copy-start(bf16[1024,768]{0,1:T(8,128)(2,1)S(1)} %get-tuple-element.139) | copy-start | bytes 4718596
  261.4 12.4 %copy-start.7 = (f32[1024,768]{0,1:T(8,128)S(1)}, f32[1024,768]{0,1:T(8,128)}, u32[]{:S(2)}) copy-start(f32[1024,768]{0,1:T(8,128)} %copy-done.6) | copy-start | bytes 9437188
  261.4 12.4 %slice-start.1 = ((s8[4718592]{0:T(1024)(128)(4,1)}), s8[524288]{0:T(1024)(128)(4,1)S(1)}, s32[]{:S(2)}) async-start(s8[4718592]{0:T(1024)(128)(4,1)} %bitcast.76), calls=%async_computation.14 | async-start | bytes 1048576
  273.8 6.6 %copy-start.28 = (bf16[1024,3072]{1,0:T(8,128)(2,1)}, bf16[1024,3072]{1,0:T(8,128)(2,1)S(1)}, u32[]{:S(2)}) copy-start(bf16[1024,3072]{1,0:T(8,128)(2,1)S(1)} %get-tuple-element.179) | copy-start | bytes 18874372
  282.1 3.4 copy-start.19
  284.5 7.6 %collective-permute-start.10 = (bf16[1024,384]{1,0:T(8,128)(2,1)}, bf16[1024,384]{1,0:T(8,128)(2,1)S(1)}, u32[]{:S(2)}, u32[]{:S(2)}) collective-permute-start(bf16[1024,384]{1,0:T(8,128)(2,1)} %convolution_convert_fusion.3), channel_id=1, source_target_pairs={{0,4},{4,0},{1,5},{5,1},{2,6},{6,2},{3,7},{7,3},{8,12},{12,8},{9,1... | collective-permute-start | bytes 2359304 | tf_op jit(solution)/shard_map/ppermute | solution.py:308
  289.0 3.1 copy-start.5
  289.0 141.5 %reduce-scatter.13.cloned.1.call-start = ((), (), s32[]{:S(2)}) async-start(), calls=%async_computation.11 | async-start | bytes 2396160
  380.4 4.4 copy-start.26
  380.4 4.6 copy-start.12
  385.0 4.0 copy-start.14
  394.1 91.8 %reduce-scatter.11.cloned.1.call-start = ((), (), s32[]{:S(2)}) async-start(), calls=%async_computation.9 | async-start | bytes 5308416 | tf_op jit(solution)/shard_map/reduce_scatter | solution.py:394
  404.7 138.4 %reduce-scatter.9.cloned.1.call-start = ((), (), s32[]{:S(2)}) async-start(), calls=%async_computation.8 | async-start | bytes 5308416 | tf_op jit(solution)/shard_map/reduce_scatter | solution.py:399
  414.8 6.3 copy-start.9
  414.8 229.4 %all-reduce.9.cloned.1.call-start = ((), (), s32[]{:S(2)}) async-start(), calls=%async_computation.12 | async-start | bytes 3612672 | tf_op jit(solution)/shard_map/psum | solution.py:433
  415.0 11.6 %copy-start.16 = (bf16[768,3,1,384]{0,3,1,2:T(8,128)(2,1)S(1)}, bf16[768,3,1,384]{0,3,1,2:T(8,128)(2,1)}, u32[]{:S(2)}) copy-start(bf16[768,3,1,384]{0,3,1,2:T(8,128)(2,1)} %copy.89) | copy-start | bytes 5308420
  420.8 5.9 copy-start.13
  420.8 122.5 %collective-permute-start.11 = (bf16[1024,768]{0,1:T(8,128)(2,1)}, bf16[1024,768]{0,1:T(8,128)(2,1)S(1)}, u32[]{:S(2)}, u32[]{:S(2)}) collective-permute-start(bf16[1024,768]{0,1:T(8,128)(2,1)} %convolution_convert_fusion.2), channel_id=1, source_target_pairs={{0,4},{4,0},{1,5},{5,1},{2,6},{6,2},{3,7},{7,3},{8,12},{12,8},{9,1... | collective-permute-start | bytes 4718600 | tf_op jit(solution)/shard_map/ppermute | solution.py:308
  422.3 132.0 %collective-permute-start.7 = (bf16[512,768]{0,1:T(8,128)(2,1)}, bf16[512,768]{0,1:T(8,128)(2,1)}, u32[]{:S(2)}, u32[]{:S(2)}) collective-permute-start(bf16[512,768]{0,1:T(8,128)(2,1)} %get-tuple-element.148), channel_id=1, source_target_pairs={{1,0},{0,1},{5,2},{4,3},{3,4},{2,5},{7,6},{6,7},{9,8},{8,9},{13,10... | collective-permute-start | bytes 2359304 | tf_op jit(solution)/shard_map/ppermute | solution.py:339
  424.7 129.6 %collective-permute-start.6 = (bf16[512,768]{0,1:T(8,128)(2,1)}, bf16[512,768]{0,1:T(8,128)(2,1)}, u32[]{:S(2)}, u32[]{:S(2)}) collective-permute-start(bf16[512,768]{0,1:T(8,128)(2,1)} %get-tuple-element.147), channel_id=1, source_target_pairs={{0,0},{1,1},{4,2},{5,3},{2,4},{3,5},{6,6},{7,7},{8,8},{9,9},{12,10... | collective-permute-start | bytes 2359304 | tf_op jit(solution)/shard_map/ppermute | solution.py:339
  549.5 52.7 %collective-permute-start.12 = (bf16[512,768]{0,1:T(8,128)(2,1)}, bf16[512,768]{0,1:T(8,128)(2,1)S(1)}, u32[]{:S(2)}, u32[]{:S(2)}) collective-permute-start(bf16[512,768]{0,1:T(8,128)(2,1)} %get-tuple-element.143), channel_id=1, source_target_pairs={{0,0},{1,1},{4,2},{5,3},{2,4},{3,5},{6,6},{7,7},{8,8},{9,9},{12,10... | collective-permute-start | bytes 2359304 | tf_op jit(solution)/shard_map/ppermute | solution.py:339
  554.2 69.2 %collective-permute-start.13 = (bf16[512,768]{0,1:T(8,128)(2,1)}, bf16[512,768]{0,1:T(8,128)(2,1)S(1)}, u32[]{:S(2)}, u32[]{:S(2)}) collective-permute-start(bf16[512,768]{0,1:T(8,128)(2,1)} %get-tuple-element.144), channel_id=1, source_target_pairs={{1,0},{0,1},{5,2},{4,3},{3,4},{2,5},{7,6},{6,7},{9,8},{8,9},{13,10... | collective-permute-start | bytes 2359304 | tf_op jit(solution)/shard_map/ppermute | solution.py:339
  644.2 3.4 copy-start.23
  644.2 4.6 copy-start.22
  645.0 4.8 copy-start.24
  646.1 4.5 collective-permute-start.15
  647.4 4.4 collective-permute-start.14
  (10 other events, 18.0 us)
Sparse Core Ops, SparseCore 0:
  15.3 37.8 all-gather.11
  55.1 24.0 all-gather.5
  81.1 38.7 all-gather.7
  200.2 40.1 all-gather.9
  289.2 37.1 reduce-scatter.6
  394.2 34.4 reduce-scatter.12
  432.1 53.7 reduce-scatter.10
  489.4 53.7 reduce-scatter.8
  545.8 98.2 all-reduce.8

commit v2 on v1

--- a/solution.py
+++ b/solution.py
@@ -55,14 +55,13 @@
 def forward_kernel(run, mask_ref, ends_ref, own, sib, seg_col, seg_row, ctx_own, ctx_sib, lse_ref, qkv, out, acc, top, sems, out_sems):
     total = qkv.shape[1]
     pairs = out.shape[0]
-    width = pairs * LANES
     mask = mask_ref[0]
 
     def loads(pair):
         copies = []
         for kind in range(3):
             copies += piece_copies(
-                (own, sib), kind * width + pair * LANES, kind * pairs + pair, qkv, kind * pairs + pair, sems, run, mask, True
+                (own, sib), (3 * pair + kind) * LANES, kind * pairs + pair, qkv, kind * pairs + pair, sems, run, mask, True
             )
         return copies
 
@@ -140,123 +139,104 @@
             pltpu.SemaphoreType.DMA((pairs, pieces)),
         ],
         compiler_params=pltpu.CompilerParams(vmem_limit_bytes=40 << 20),
+        cost_estimate=pl.CostEstimate(flops=50_000_000_000, bytes_accessed=8_000_000, transcendentals=0),
         name="attend_forward",
     )(mask, ends, own, sib, seg_col, seg_row)
 
 
 def backward_kernel(
-    run, mask_ref, ends_ref, own, sib, ctx_own, ctx_sib, dctx_own, dctx_sib, seg_col, seg_row, lse_ref,
-    d_own, d_sib, qkv, ctx, dctx, out, delta, dq, dkv, sems, out_sems
+    run, pair, mask_ref, ends_ref, own, sib, ctx_own, ctx_sib, dctx_own, dctx_sib, seg_col, seg_row, lse_ref,
+    d_own, d_sib, qkv, ctx, out, delta, dq, dkv, sems, out_sems
 ):
     total = qkv.shape[1]
-    pairs = ctx.shape[0]
-    width = pairs * LANES
     mask = mask_ref[0]
-
-    def loads(pair):
-        copies = []
-        for kind in range(3):
-            copies += piece_copies(
-                (own, sib), kind * width + pair * LANES, kind * pairs + pair, qkv, kind * pairs + pair, sems, run, mask, True
-            )
-        copies += piece_copies((ctx_own, ctx_sib), pair * LANES, pair, ctx, 3 * pairs + pair, sems, run, mask, True)
-        copies += piece_copies((dctx_own, dctx_sib), pair * LANES, pair, dctx, 4 * pairs + pair, sems, run, mask, True)
-        return copies
-
-    def stores(pair):
-        copies = []
-        for kind in range(3):
-            copies += piece_copies(
-                (d_own, d_sib), kind * width + pair * LANES, kind * pairs + pair, out, kind * pairs + pair, out_sems, run, mask, False
-            )
-        return copies
-
-    for pair in range(pairs):
-        for copy in loads(pair):
-            copy.start()
-
-    for pair in range(pairs):
-        for copy in loads(pair):
-            copy.wait()
-
-        @pl.loop(0, total // TILE)
-        def _(block):
-            rows = pl.multiple_of(block * TILE, TILE)
-            product = ctx[pair, pl.ds(rows, TILE), :].astype(jnp.float32) * dctx[pair, pl.ds(rows, TILE), :].astype(jnp.float32)
-            product = product.T
+    loads, stores = [], []
+    for kind in range(3):
+        loads += piece_copies((own, sib), (3 * pair + kind) * LANES, kind, qkv, kind, sems, run, mask, True)
+        stores += piece_copies((d_own, d_sib), kind * LANES, kind, out, kind, out_sems, run, mask, False)
+    loads += piece_copies((ctx_own, ctx_sib), pair * LANES, 0, ctx, 3, sems, run, mask, True)
+    loads += piece_copies((dctx_own, dctx_sib), pair * LANES, 1, ctx, 4, sems, run, mask, True)
+    for copy in loads:
+        copy.start()
+    for copy in loads:
+        copy.wait()
+
+    @pl.loop(0, total // TILE)
+    def _(block):
+        rows = pl.multiple_of(block * TILE, TILE)
+        product = ctx[0, pl.ds(rows, TILE), :].astype(jnp.float32) * ctx[1, pl.ds(rows, TILE), :].astype(jnp.float32)
+        product = product.T
+        for head in range(2):
+            part = jnp.sum(product[head * HEAD_DIM : (head + 1) * HEAD_DIM], axis=0, keepdims=True)
+            delta[head, :, pl.ds(rows, TILE)] = jnp.broadcast_to(part, (8, TILE))
+        dq[pl.ds(rows, TILE), :] = jnp.zeros((TILE, LANES), jnp.float32)
+
+    @pl.loop(0, total // TILE)
+    def _(block):
+        rows = pl.multiple_of(block * TILE, TILE)
+        k_heads = lane_halves(qkv[1, pl.ds(rows, TILE), :], 0.0)
+        v_heads = lane_halves(qkv[2, pl.ds(rows, TILE), :], 0.0)
+        segk = seg_col[pl.ds(rows, TILE), :]
+        segk = jnp.concatenate([segk] * (TILE // LANES), axis=1)
+        first, after = key_tiles(ends_ref, rows, rows + TILE - 1, TILE, total)
+        dkv[...] = jnp.zeros_like(dkv)
+
+        @pl.loop(first, after)
+        def _(step):
+            at = pl.multiple_of(step * TILE, TILE)
+            queries = qkv[0, pl.ds(at, TILE), :]
+            grads = ctx[1, pl.ds(at, TILE), :]
+            q_heads = lane_halves(queries, 0.0)
+            g_heads = lane_halves(grads, 0.0)
+            same = segk == seg_row[:, pl.ds(at, TILE)]
             for head in range(2):
-                part = jnp.sum(product[head * HEAD_DIM : (head + 1) * HEAD_DIM], axis=0, keepdims=True)
-                delta[head, :, pl.ds(rows, TILE)] = jnp.broadcast_to(part, (8, TILE))
-            dq[pl.ds(rows, TILE), :] = jnp.zeros((TILE, LANES), jnp.float32)
-
-        @pl.loop(0, total // TILE)
-        def _(block):
-            rows = pl.multiple_of(block * TILE, TILE)
-            k_heads = lane_halves(qkv[pairs + pair, pl.ds(rows, TILE), :], 0.0)
-            v_heads = lane_halves(qkv[2 * pairs + pair, pl.ds(rows, TILE), :], 0.0)
-            segk = seg_col[pl.ds(rows, TILE), :]
-            segk = jnp.concatenate([segk] * (TILE // LANES), axis=1)
-            first, after = key_tiles(ends_ref, rows, rows + TILE - 1, TILE, total)
-            dkv[...] = jnp.zeros_like(dkv)
-
-            @pl.loop(first, after)
-            def _(step):
-                at = pl.multiple_of(step * TILE, TILE)
-                queries = qkv[pair, pl.ds(at, TILE), :]
-                grads = dctx[pair, pl.ds(at, TILE), :]
-                q_heads = lane_halves(queries, 0.0)
-                g_heads = lane_halves(grads, 0.0)
-                same = segk == seg_row[:, pl.ds(at, TILE)]
-                for head in range(2):
-                    scores = mm(k_heads[head], queries, NT)
-                    lse = lse_ref[2 * pair + head, 0:1, pl.ds(at, TILE)]
-                    probs = jnp.exp(jnp.where(same, scores - lse, NEG))
-                    dprobs = mm(v_heads[head], grads, NT)
-                    dscores = (probs * (dprobs - delta[head, 0:1, pl.ds(at, TILE)])).astype(jnp.bfloat16)
-                    dkv[1] += mm(probs.astype(jnp.bfloat16), g_heads[head], NN)
-                    dkv[0] += mm(dscores, q_heads[head], NN)
-                    dq[pl.ds(at, TILE), :] += mm(dscores, k_heads[head], TN)
-
-            out[pairs + pair, pl.ds(rows, TILE), :] = dkv[0].astype(jnp.bfloat16)
-            out[2 * pairs + pair, pl.ds(rows, TILE), :] = dkv[1].astype(jnp.bfloat16)
-
-        out[pair] = (dq[...] * HEAD_DIM**-0.5).astype(jnp.bfloat16)
-        for copy in stores(pair):
-            copy.start()
-    for pair in range(pairs):
-        for copy in stores(pair):
-            copy.wait()
-
-
-def attend_backward(mask, ends, own, sib, ctx_own, ctx_sib, dctx_own, dctx_sib, seg_col, seg_row, lse, run):
-    half, columns = own.shape
+                scores = mm(k_heads[head], queries, NT)
+                lse = lse_ref[2 * pair + head, 0:1, pl.ds(at, TILE)]
+                probs = jnp.exp(jnp.where(same, scores - lse, NEG))
+                dprobs = mm(v_heads[head], grads, NT)
+                dscores = (probs * (dprobs - delta[head, 0:1, pl.ds(at, TILE)])).astype(jnp.bfloat16)
+                dkv[1] += mm(probs.astype(jnp.bfloat16), g_heads[head], NN)
+                dkv[0] += mm(dscores, q_heads[head], NN)
+                dq[pl.ds(at, TILE), :] += mm(dscores, k_heads[head], TN)
+
+        out[1, pl.ds(rows, TILE), :] = dkv[0].astype(jnp.bfloat16)
+        out[2, pl.ds(rows, TILE), :] = dkv[1].astype(jnp.bfloat16)
+
+    out[0] = (dq[...] * HEAD_DIM**-0.5).astype(jnp.bfloat16)
+    for copy in stores:
+        copy.start()
+    for copy in stores:
+        copy.wait()
+
+
+def attend_backward(pair, mask, ends, own, sib, ctx_own, ctx_sib, dctx_own, dctx_sib, seg_col, seg_row, lse, run):
+    half = own.shape[0]
     total = 2 * half
-    pairs = columns // (3 * LANES)
     pieces = total // run
     any_spec = pl.BlockSpec(memory_space=pl.ANY)
     vmem = pl.BlockSpec(memory_space=pltpu.VMEM)
     smem = pl.BlockSpec(memory_space=pltpu.SMEM)
     return pl.pallas_call(
-        functools.partial(backward_kernel, run),
+        functools.partial(backward_kernel, run, pair),
         out_shape=(
-            jax.ShapeDtypeStruct((half, columns), jnp.bfloat16),
-            jax.ShapeDtypeStruct((half, columns), jnp.bfloat16),
+            jax.ShapeDtypeStruct((half, 3 * LANES), jnp.bfloat16),
+            jax.ShapeDtypeStruct((half, 3 * LANES), jnp.bfloat16),
         ),
         in_specs=[smem, smem] + [any_spec] * 6 + [vmem] * 3,
         out_specs=(any_spec, any_spec),
         scratch_shapes=[
-            pltpu.VMEM((3 * pairs, total, LANES), jnp.bfloat16),
-            pltpu.VMEM((pairs, total, LANES), jnp.bfloat16),
-            pltpu.VMEM((pairs, total, LANES), jnp.bfloat16),
-            pltpu.VMEM((3 * pairs, total, LANES), jnp.bfloat16),
+            pltpu.VMEM((3, total, LANES), jnp.bfloat16),
+            pltpu.VMEM((2, total, LANES), jnp.bfloat16),
+            pltpu.VMEM((3, total, LANES), jnp.bfloat16),
             pltpu.VMEM((2, 8, total), jnp.float32),
             pltpu.VMEM((total, LANES), jnp.float32),
             pltpu.VMEM((2, TILE, LANES), jnp.float32),
-            pltpu.SemaphoreType.DMA((5 * pairs, pieces)),
-            pltpu.SemaphoreType.DMA((3 * pairs, pieces)),
+            pltpu.SemaphoreType.DMA((5, pieces)),
+            pltpu.SemaphoreType.DMA((3, pieces)),
         ],
-        compiler_params=pltpu.CompilerParams(vmem_limit_bytes=48 << 20),
-        name="attend_backward",
+        compiler_params=pltpu.CompilerParams(vmem_limit_bytes=24 << 20),
+        cost_estimate=pl.CostEstimate(flops=20_000_000_000, bytes_accessed=8_000_000, transcendentals=0),
+        name=f"attend_backward_{pair}",
     )(mask, ends, own, sib, ctx_own, ctx_sib, dctx_own, dctx_sib, seg_col, seg_row, lse)
 
 
@@ -306,6 +286,73 @@
 
 def swap(x):
     return lax.ppermute(x, "core", [(0, 1), (1, 0)])
+
+
+def after(value, *done):
+    return lax.optimization_barrier((value, done))[0]
+
+
+def pick(value, which, axis=0):
+    return lax.dynamic_index_in_dim(value, which, axis, keepdims=False)
+
+
+def total(keep, received):
+    return (keep.astype(jnp.float32) + received.astype(jnp.float32)).astype(jnp.bfloat16)
+
+
+class Halving:
+    def __init__(self, blocks, planes):
+        bits = planes.bit_length() - 1
+        rows = blocks.shape[1]
+        self.planes = planes
+        self.orders = (list(range(bits)), list(range(bits))[::-1])
+        self.left = [list(range(bits))[::-1] for _ in range(2)]
+        parts = (blocks[:, : rows // 2], blocks[:, rows // 2 :])
+        self.parts = [p.reshape((2,) * bits + p.shape[1:]) for p in parts]
+        self.steps = bits
+
+    def send(self, step):
+        place = lax.axis_index("xy")
+        self.keep, self.received, self.sent = [], [], []
+        for half in range(2):
+            bit = self.orders[half][step]
+            axis = self.left[half].index(bit)
+            mine = (place >> bit) % 2
+            self.left[half].remove(bit)
+            out = pick(self.parts[half], 1 - mine, axis)
+            self.keep.append(pick(self.parts[half], mine, axis))
+            self.sent.append(out)
+            self.received.append(lax.ppermute(out, "xy", [(i, i ^ (1 << bit)) for i in range(self.planes)]))
+
+    def add(self, *done):
+        self.parts = [total(k, after(r, *done)) for k, r in zip(self.keep, self.received)]
+
+    def result(self):
+        return jnp.concatenate(self.parts)
+
+
+class Spread:
+    def __init__(self, value, nseq):
+        self.nseq, self.rows = nseq, value.shape[0] // nseq
+        self.me = lax.axis_index("seq")
+        quarter = lambda which: lax.dynamic_slice_in_dim(value, (which % nseq) * self.rows, self.rows, 0)
+        self.keep = quarter(self.me)
+        self.received = [self.shift(quarter(self.me + d), d) for d in range(1, nseq)]
+
+    def shift(self, value, distance):
+        return lax.ppermute(value, "seq", [(i, (i + distance) % self.nseq) for i in range(self.nseq)])
+
+    def add(self, *done):
+        parts = [self.keep] + [after(r, *done) for r in self.received]
+        self.keep = sum(p.astype(jnp.float32) for p in parts).astype(jnp.bfloat16)
+        self.received = [self.shift(self.keep, d) for d in range(1, self.nseq)]
+
+    def result(self):
+        whole = jnp.zeros((self.nseq * self.rows,) + self.keep.shape[1:], jnp.bfloat16)
+        for d, part in enumerate([self.keep] + self.received):
+            start = ((self.me - d) % self.nseq) * self.rows
+            whole = lax.dynamic_update_slice_in_dim(whole, part, start, 0)
+        return whole
 
 
 def either(core, own, other, axis):
@@ -349,14 +396,14 @@
     seg_row = seg[None]
     mask = (odd + 2 * core).astype(jnp.int32)[None]
 
+    pairs = mine // LANES
+    own_columns = qkv_weight.reshape(rows, 3, CORES, pairs, LANES)
+    own_columns = jnp.moveaxis(own_columns, (2, 3), (0, 2)).reshape(CORES, rows, 3 * mine)
+    kept = pick(own_columns, core)
+    w_mine = either(core, kept, swap(pick(own_columns, 1 - core)), 0)
+    w_mine = lax.all_gather(w_mine, "xy", axis=0, tiled=True)
     small = [q_bias, v_bias, out_bias, norm1_gain, norm1_bias, ff_out_bias, norm2_gain, norm2_bias, ff_in_bias]
-    vector = jnp.concatenate(small)
-    packed = jnp.zeros((16, 3 * width), bf16).at[0, : vector.shape[0]].set(vector)
-    packed = jnp.concatenate([qkv_weight, packed], axis=0)
-    packed = lax.all_gather(packed, fsdp, axis=0, tiled=False)
-    w_qkv = packed[:, :rows].reshape(width, 3, CORES, mine)
-    w_mine = lax.dynamic_index_in_dim(w_qkv, core, 2, keepdims=False).reshape(width, 3 * mine)
-    vectors = packed[:, rows, : vector.shape[0]].astype(f32)
+    vectors = lax.all_gather(jnp.concatenate(small)[None, None], fsdp, axis=0, tiled=True)[:, 0].astype(f32)
     bias_q, bias_v, bias_out, gain_one, shift_one, bias_down, gain_two, shift_two = [
         vectors[:, i * rows : (i + 1) * rows].reshape(width) for i in range(8)
     ]
@@ -365,9 +412,10 @@
     w_in = lax.all_gather(ff_in_weight, fsdp, axis=0, tiled=True)
     w_down = lax.all_gather(ff_out_weight, fsdp, axis=0, tiled=True)
 
-    own_slice = lambda v: lax.dynamic_slice_in_dim(v, core * mine, mine, 0)
-    bias_mine = jnp.concatenate([own_slice(bias_q), jnp.zeros((mine,), f32), own_slice(bias_v)])
-    scale = jnp.concatenate([jnp.full((mine,), HEAD_DIM**-0.5, f32), jnp.ones((2 * mine,), f32)])
+    own_slice = lambda v: lax.dynamic_slice_in_dim(v, core * mine, mine, 0).reshape(pairs, LANES)
+    one = jnp.ones((pairs, LANES), f32)
+    bias_mine = jnp.stack([own_slice(bias_q), 0.0 * one, own_slice(bias_v)], axis=1).reshape(-1)
+    scale = jnp.stack([HEAD_DIM**-0.5 * one, one, one], axis=1).reshape(-1)
     x_own = jnp.concatenate(pieces)
     x_sib = jnp.concatenate([swap(p) for p in pieces])
     projected = [((mm(x, w_mine, NN) + bias_mine) * scale).astype(bf16) for x in (x_own, x_sib)]
@@ -390,14 +438,14 @@
     shift_two_grad = jnp.sum(grad_out, axis=0)
     grad_two = norm_backward(grad_out, normed_two, inv_two, gain_two)
     grad_down = grad_two.astype(bf16)
-    down_grad = mm(act_low, grad_down, TN).astype(bf16)
-    down_grad = lax.psum_scatter(down_grad, fsdp, scatter_dimension=0, tiled=True)
-    down_grad = lax.psum(down_grad, "seq").astype(f32)
+
+    def cores(blocks):
+        return pick(blocks, core, 1), swap(pick(blocks, 1 - core, 1))
+
+    down_grad = cores(mm(act_low, grad_down, TN).astype(bf16).reshape(planes, CORES, -1, width))
     down_bias_grad = jnp.sum(grad_down.astype(f32), axis=0)
     grad_pre = (mm(grad_down, w_down, NT) * gelu_slope(pre)).astype(bf16)
-    in_grad = mm(hidden_low, grad_pre, TN).astype(bf16)
-    in_grad = lax.psum_scatter(in_grad, fsdp, scatter_dimension=0, tiled=True)
-    in_grad = lax.psum(in_grad, "seq").astype(f32)
+    in_grad = cores(mm(hidden_low, grad_pre, TN).astype(bf16).reshape(planes, CORES, rows, -1))
     in_bias_grad = jnp.sum(grad_pre.astype(f32), axis=0)
     grad_hidden = grad_two + mm(grad_pre, w_in, NT)
     gain_one_grad = jnp.sum(grad_hidden * normed_one, axis=0)
@@ -408,40 +456,97 @@
     dctx_own = mm(grad_attn, wo_own, NT).astype(bf16)
     out_bias_grad = jnp.sum(grad_attn.astype(f32), axis=0)
     out_grad = [mm(c, grad_attn, TN).astype(bf16) for c in (ctx_own, ctx_far)]
-    out_grad = lax.psum_scatter(either(core, *out_grad, 0), fsdp, scatter_dimension=0, tiled=True)
-    out_grad = lax.psum(out_grad, "seq").astype(f32)
-
-    d_own, d_sib = attend_backward(
-        mask, ends, *projected, ctx_own, ctx_sib, dctx_own, dctx_far, seg_col, seg_row, lse, run
-    )
-    grad_far = swap(mm(d_sib, w_mine, NT).astype(bf16))
-    input_grad = grad_one + mm(d_own, w_mine, NT) + grad_far.astype(f32)
+    out_grad = cores(either(core, *out_grad, 0).reshape(planes, CORES, rows, width))
+    small = [out_bias_grad, gain_one_grad, shift_one_grad, down_bias_grad, gain_two_grad, shift_two_grad, in_bias_grad]
+    vector = jnp.concatenate([v.reshape(shards, -1) for v in small], axis=1).astype(bf16)
+    lines = -(-vector.shape[1] // width)
+    vector = jnp.pad(vector, ((0, 0), (0, lines * width - vector.shape[1])))
+    vector = jnp.pad(vector.reshape(shards, lines, width), ((0, 0), (0, 32 - lines), (0, 0)))
+    vector = cores(vector.reshape(planes, CORES, 32, width))
+    inner = in_grad[0].shape[2] // width
+    joined = []
+    for which in range(2):
+        wide = in_grad[which]
+        wide = [wide[:, :, i * width : (i + 1) * width] for i in range(inner)]
+        joined.append(jnp.concatenate([down_grad[which]] + wide + [out_grad[which], vector[which]], axis=1))
+    early = Halving(total(*joined), planes)
+    early.send(0)
+
+    def attend(pair, *ready):
+        held = after(mask, *ready)
+        return attend_backward(
+            pair, held, ends, *projected, ctx_own, ctx_sib, dctx_own, dctx_far, seg_col, seg_row, lse, run
+        )
+
+    def weight_sums(grads):
+        near = jnp.concatenate([g[0] for g in grads], axis=1)
+        far = jnp.concatenate([g[1] for g in grads], axis=1)
+        matrix = (mm(x_own, near, TN) + mm(x_sib, far, TN)).astype(bf16)
+        column = (jnp.sum(near.astype(f32), axis=0) + jnp.sum(far.astype(f32), axis=0)).astype(bf16)
+        column = jnp.pad(column[None], ((0, 63), (0, 0)))
+        column = jnp.broadcast_to(column, (planes,) + column.shape)
+        return jnp.concatenate([matrix.reshape(planes, CORES * rows, -1), column], axis=1)
+
+    grads = [attend(0, *early.sent)]
+    sent = []
+    for pair in range(1, pairs):
+        if len(early.left[0]):
+            early.add(grads[-1][0])
+            early.send(early.steps - len(early.left[0]))
+            sent = early.sent
+        if pair == pairs - 1:
+            first_sums = Halving(weight_sums(grads), planes)
+            first_sums.send(0)
+            sent = sent + first_sums.sent
+        grads.append(attend(pair, *sent))
+    while len(early.left[0]):
+        early.add(grads[-1][0])
+        early.send(early.steps - len(early.left[0]))
+    early.add(grads[-1][0])
+    early_sum = Spread(early.result(), nseq)
+
+    near = jnp.concatenate([g[0] for g in grads], axis=1)
+    far = jnp.concatenate([g[1] for g in grads], axis=1)
+    grad_far = swap(mm(far, w_mine, NT).astype(bf16))
+    last_sums = Halving(weight_sums(grads[-1:]), planes)
+    last_sums.send(0)
+    input_grad = grad_one + mm(near, w_mine, NT) + grad_far.astype(f32)
     input_grad = collect(input_grad.astype(bf16)).astype(f32)
-
-    qkv_grad = (mm(x_own, d_own, TN) + mm(x_sib, d_sib, TN)).astype(bf16)
-    columns = jnp.sum(d_own.astype(f32), axis=0) + jnp.sum(d_sib.astype(f32), axis=0)
-    none = jnp.zeros((mine,), f32)
-    q_bias_grad = either(core, columns[:mine], none, 0)
-    v_bias_grad = either(core, columns[2 * mine :], none, 0)
-    small = [q_bias_grad, v_bias_grad, out_bias_grad, gain_one_grad, shift_one_grad, down_bias_grad,
-             gain_two_grad, shift_two_grad, in_bias_grad]
-    vector = jnp.concatenate([v.reshape(shards, -1) for v in small], axis=1).astype(bf16)
-    vector = vector.reshape(planes, CORES, -1)
-    vector = jnp.pad(vector, ((0, 0), (0, 16 - CORES), (0, 3 * mine - vector.shape[2])))
-    packed = jnp.concatenate([qkv_grad.reshape(planes, CORES * rows, 3 * mine), vector], axis=1)
-    packed = lax.psum_scatter(packed.reshape(-1, 3 * mine), "xy", scatter_dimension=0, tiled=True)
-    packed = lax.psum(packed, "seq")
-    block = packed[: CORES * rows].reshape(CORES, rows, 3 * mine)
-    tail = packed[CORES * rows : CORES * rows + CORES]
-    pick = lambda v, which: lax.dynamic_index_in_dim(v, which, 0, keepdims=False)
-    block_far, tail_far = swap(pick(block, 1 - core)), swap(pick(tail, 1 - core))
-    own_block = pick(block, core).reshape(rows, 3, 1, mine)
-    qkv_final = either(core, own_block, block_far.reshape(rows, 3, 1, mine), 2).reshape(rows, 3 * width).astype(f32)
-    tail = pick(tail, core).astype(f32) + tail_far.astype(f32)
-    g = [tail[i * rows : (i + 1) * rows] for i in range(8)]
+    for step in range(last_sums.steps):
+        for sums in (first_sums, last_sums):
+            sums.add()
+            if step + 1 < sums.steps:
+                sums.send(step + 1)
+    qkv_sum = Spread(jnp.concatenate([first_sums.result(), last_sums.result()], axis=1), nseq)
+    early_sum.add()
+    qkv_sum.add()
+    early_total = early_sum.result()
+    qkv_total = qkv_sum.result()
+
+    down_rows = down_grad[0].shape[1]
+    down_final = early_total[:down_rows].astype(f32)
+    wide = [early_total[down_rows + i * rows : down_rows + (i + 1) * rows] for i in range(inner)]
+    in_final = jnp.concatenate(wide, axis=1).astype(f32)
+    at = down_rows + inner * rows
+    out_final = early_total[at : at + rows].astype(f32)
+    at = at + rows
+    line = early_total[at : at + lines].reshape(-1).astype(f32)
+    out_bias_final, g1, b1, down_bias_final, g2, b2 = [line[i * rows : (i + 1) * rows] for i in range(6)]
+    in_bias_final = line[6 * rows : 6 * rows + ff_in_bias.shape[0]]
+
+    part = qkv_total
+    column = part[CORES * rows]
+    other = swap(jnp.concatenate([lax.dynamic_slice_in_dim(part, (1 - core) * rows, rows, 0), part[CORES * rows : CORES * rows + 16]]))
+    own_block = lax.dynamic_slice_in_dim(part, core * rows, rows, 0)
+    spread_out = lambda v: jnp.moveaxis(v.reshape(-1, pairs, 3, LANES), 2, 1).reshape(-1, 3, 1, mine)
+    qkv_final = either(core, spread_out(own_block), spread_out(other[:rows]), 2).reshape(rows, 3 * width).astype(f32)
+    sums = either(core, spread_out(column), spread_out(other[rows]), 2).reshape(3, width)
+    shard = lax.axis_index("xy") * CORES + core
+    q_final = lax.dynamic_slice_in_dim(sums[0], shard * rows, rows, 0).astype(f32)
+    v_final = lax.dynamic_slice_in_dim(sums[2], shard * rows, rows, 0).astype(f32)
     return (
-        output, input_grad, qkv_final, g[0], g[1], out_grad, g[2], g[3], g[4], in_grad,
-        tail[8 * rows : 8 * rows + ff_in_bias.shape[0]], down_grad, g[5], g[6], g[7],
+        output, input_grad, qkv_final, q_final, v_final, out_final, out_bias_final, g1, b1, in_final,
+        in_bias_final, down_final, down_bias_final, g2, b2,
     )
 
 

time: 674 us -> 669 us (level)
  waiting for transfers between devices: 229 us -> 138 us
  starting transfers between devices: 22.7 us -> 69.1 us
  local copies, waits for them, and re-layouts: 71.3 us -> 89.8 us
  other arithmetic: 28.7 us -> 39.3 us
  blocking collectives: 0 us -> 9.36 us
    reduce_scatter x3 -> x0, waiting for transfers between devices: 113 us -> none  [the longest x1 57.3 us: per_device(): in_grad = lax.psum_scatter(in_grad, fsdp, scatter_dimension=0, tiled=True)]
    ppermute x0 -> x24, waiting for transfers between devices: none -> 66.2 us  [the longest x12 61.5 us: shift(): lax.ppermute(value, 'seq', [(i, (i + distance) % self.nseq) for i in rang...]
    ppermute x0 -> x24, starting transfers between devices: none -> 34.3 us  [the longest x12 21.8 us: shift(): lax.ppermute(value, 'seq', [(i, (i + distance) % self.nseq) for i in rang...]
    dynamic_slice x6 -> x4, local copies, waits for them, and re-layouts: 19.3 us -> 0.25 us  [the longest x2 0.15 us: per_device(): lax.dynamic_slice_in_dim(v, core * mine, mine, 0).reshape(pairs, LANES)]
    ppermute x4, waiting for transfers between devices: 34.4 us -> 16.9 us  [spread(): lax.ppermute(h, ('core', 'seq'), r)]
    unnamed x71 -> x130, local copies, waits for them, and re-layouts: 14.1 us -> 29.8 us
    psum x1 -> x0, waiting for transfers between devices: 15.3 us -> none  [per_device(): packed = lax.psum(packed, 'seq')]
    ppermute x4, waiting for transfers between devices: 65.3 us -> 52.4 us  [collect(): lax.ppermute(x[i * run:(i + 1) * run], ('core', 'seq'), back[i])]
  transfers between devices with their start and end apart: 25 -> 48, of which waited for: 7 -> 17; matrix products, arithmetic and copies ran while one was open for 26% -> 25% of each run, Pallas kernels for 26% -> 21%
where the time goes in v2:
time: 669 us; the launch traced here: 659 us
  Pallas kernels  171 us (26%)
  waiting for transfers between devices  138 us (21%)
  matrix products  127 us (19%)
  local copies, waits for them, and re-layouts  89.8 us (13%)
  starting transfers between devices  69.1 us (10%)
  other arithmetic  39.3 us (6%)
  between operations  15.6 us (2%)
  blocking collectives  9.36 us (1%)
    dot_general x20, matrix products, mm(): lax.dot_general(left, right, dims, preferred_element_type=jnp.float32)  127 us
    pallas_call x3, Pallas kernels, attend_backward(): pl.pallas_call(functools.partial(backward_kernel, run, pair), out_shape=(...  88.9 us
    pallas_call x1, Pallas kernels, attend_forward(): pl.pallas_call(functools.partial(forward_kernel, run), out_shape=(jax.Sha...  81.6 us
    ppermute x12, waiting for transfers between devices, shift(): lax.ppermute(value, 'seq', [(i, (i + distance) % self.nseq) for i in rang...  61.5 us
    ppermute x4, waiting for transfers between devices, collect(): lax.ppermute(x[i * run:(i + 1) * run], ('core', 'seq'), back[i])  52.4 us
    unnamed x130, local copies, waits for them, and re-layouts  29.8 us
    ppermute x12, starting transfers between devices, shift(): lax.ppermute(value, 'seq', [(i, (i + distance) % self.nseq) for i in rang...  21.8 us
    ppermute x4, waiting for transfers between devices, spread(): lax.ppermute(h, ('core', 'seq'), r)  16.9 us
  transfers between devices with their start and end apart: 48, of which 17 were waited for; matrix products, arithmetic and copies ran while one was open for 25% of the time, Pallas kernels for 21%

profile of v2, /device:TPU:9, one launch (start us, length us, event | category | flops | bytes accessed | tf_op | source)
XLA Modules:
  0.0 658.8 jit_solution(13274198173436919606)
XLA Ops:
  17.1 4.5 collective-permute-start
  22.8 3.3 collective-permute-start.2
  27.3 2.6 collective-permute-start.10
  31.1 3.4 collective-permute-start.9
  34.6 9.4 %all-gather.1 = bf16[8,1,1152]{2,1,0:T(2,128)(2,1)S(1)} all-gather(bf16[1,1,1152]{2,1,0:T(2,128)(2,1)S(1)} %reshape.516), channel_id=2, replica_groups=mesh['xy'=4,'core'=2,'seq'=4] {'xy','core'}, dimensions={0}, use_global_device_ids=true | all-gather | bytes 20736 | tf_op jit(solution)/shard_map/all_gather | solution.py:406
  45.4 16.8 %collective-permute-done.1 = bf16[512,768]{0,1:T(8,128)(2,1)} collective-permute-done((bf16[512,768]{0,1:T(8,128)(2,1)}, bf16[512,768]{0,1:T(8,128)(2,1)}, u32[]{:S(2)}, u32[]{:S(2)}) %collective-permute-start.1) | collective-permute-done | bytes 786464 | tf_op jit(solution)/shard_map/ppermute | solution.py:383
  68.7 4.4 multiply_convert_fusion.sib
  73.1 4.5 multiply_convert_fusion.1.own
  78.0 81.6 %attend_forward.1 = (bf16[1024,384]{1,0:T(8,128)(2,1)S(1)}, bf16[1024,384]{1,0:T(8,128)(2,1)S(1)}, f32[6,8,2048]{2,1,0:T(8,128)S(1)}) custom-call(s32[1]{0:T(128)} %bitcast.2.mask_ref, s32[8]{0:T(128)S(1)} %bitcast.163, bf16[1024,1152]{1,0:T(8,128)(2,1)S(1)} %multiply_convert_fusion.1.own, bf16[1024,1152]{1,0:T(8,128)(2,1)S(1)} %multiply_convert_fusion.sib, ...), custom_call_target="tpu_custom_call" | custom-call | flops 49999998976 | bytes 8000000 | tf_op jit(solution)/shard_map/attend_forward/pallas_call | solution.py:124
  176.8 3.0 fusion.86
  181.9 46.6 %fusion.2 = (bf16[1024,3072]{1,0:T(8,128)(2,1)}, f32[1024,3072]{1,0:T(8,128)}) fusion(f32[3072]{0:T(1024)S(1)} %copy-done.33, bf16[768,3072]{1,0:T(8,128)(2,1)} %all-gather.11.cloned.1.call-done, f32[1024,768]{0,1:T(8,128)} %copy-done.8, f32[768]{0:T(1024)S(1)} %copy-done.34, f32[768]{0:T(1024)S(1)} %copy-done.22, f32[1024]{0:T(1024)S(1)} %add_rsqrt_fusion.1, ...), kind=kOutput, calls=%fused_computation.4 | convolution fusion | flops 5043388416 | bytes 26765312 | tf_op jit(solution)/shard_map/dot_general | solution.py:22
  228.5 9.4 %fusion.87 = (f32[1024]{0:T(1024)S(1)}, f32[1024,768]{0,1:T(8,128)S(1)}) fusion(f32[768]{0:T(1024)S(1)} %copy-done.35, bf16[1024,3072]{1,0:T(8,128)(2,1)} %get-tuple-element.187, bf16[3072,768]{1,0:T(8,128)(2,1)} %all-gather.13.cloned.1.call-done, f32[768]{0:T(1024)S(1)} %copy-done.34, f32[768]{0:T(1024)S(1)} %copy-done.22, f32[1024]{0:T(1024)S(1)} %add_rsqrt_fusion.1, ...), kind=kOutput, calls=%fused_computation.239 | convolution fusion | flops 4837342208 | bytes 17323008 | tf_op jit(solution)/shard_map/dot_general | solution.py:22
  238.6 3.2 fusion.22
  243.7 6.9 %convolution_convert_fusion.1 = bf16[3072,768]{1,0:T(8,128)(2,1)} fusion(bf16[1024,3072]{1,0:T(8,128)(2,1)S(1)} %bitcast.206, bf16[1024,768]{0,1:T(8,128)(2,1)S(1)} %get-tuple-element.136), kind=kOutput, calls=%fused_computation.28 | convolution fusion | flops 4834197504 | bytes 12582912 | tf_op jit(solution)/shard_map/dot_general | solution.py:22
  250.6 12.5 %fusion.88 = (bf16[3072]{0:T(1024)(128)(2,1)}, bf16[1024,3072]{1,0:T(8,128)(2,1)S(1)}) fusion(f32[1024,3072]{1,0:T(8,128)} %get-tuple-element.188, f32[3072]{0:T(1024)S(1)} %copy-done.33, bf16[1024,768]{0,1:T(8,128)(2,1)S(1)} %get-tuple-element.136, bf16[3072,768]{1,0:T(8,128)(2,1)S(1)} %bitcast.204), kind=kOutput, calls=%fused_computation.240 | convolution fusion | flops 4869583872 | bytes 25184256 | tf_op jit(solution)/shard_map/dot_general | solution.py:22
  263.2 5.9 convolution_convert_fusion
  269.1 2.6 dynamic-slice_bitcast_fusion.2
  271.7 7.2 %multiply_reduce_fusion = (bf16[768]{0:T(1024)(128)(2,1)}, f32[1024]{0:T(1024)S(1)}, f32[1024]{0:T(1024)S(1)}, bf16[768]{0:T(1024)(128)(2,1)}, f32[1024,768]{0,1:T(8,128)S(1)}) fusion(f32[1024,768]{0,1:T(8,128)S(1)} %copy-done.9, f32[1024]{0:T(1024)S(1)} %add_rsqrt_fusion.1, f32[1024]{0:T(1024)S(1)} %broadcast_multiply_fusion.5, f32[768]{0:T(1024)S(1)} %copy-done.22, ...), kind=kOutput, calls=%fused_computation.43 | convolution fusion | flops 4848349184 | bytes 22062080 | tf_op jit(solution)/shard_map/dot_general | solution.py:22
  298.2 3.4 dynamic-slice_bitcast_fusion.1
  303.8 7.6 %collective-permute-start.8 = (bf16[512,768]{0,1:T(8,128)(2,1)S(1)}, bf16[512,768]{0,1:T(8,128)(2,1)S(1)}, u32[]{:S(2)}, u32[]{:S(2)}) collective-permute-start(bf16[512,768]{0,1:T(8,128)(2,1)S(1)} %get-tuple-element.149), channel_id=1, source_target_pairs={{1,0},{0,1},{5,2},{4,3},{3,4},{2,5},{7,6},{6,7},{9,8},{8,9},{13,10... | collective-permute-start | bytes 2359304 | tf_op jit(solution)/shard_map/ppermute | solution.py:386
  320.4 21.1 %collective-permute-done.8 = bf16[512,768]{0,1:T(8,128)(2,1)S(1)} collective-permute-done((bf16[512,768]{0,1:T(8,128)(2,1)S(1)}, bf16[512,768]{0,1:T(8,128)(2,1)S(1)}, u32[]{:S(2)}, u32[]{:S(2)}) %collective-permute-start.8) | collective-permute-done | bytes 786464 | tf_op jit(solution)/shard_map/ppermute | solution.py:386
  342.9 2.7 copy.99
  345.6 3.2 constant_dynamic-update-slice_fusion.6
  360.2 5.5 add_convert_fusion
  368.9 29.6 %attend_backward_0.1 = (bf16[1024,384]{1,0:T(8,128)(2,1)S(1)}, bf16[1024,384]{1,0:T(8,128)(2,1)S(1)}) custom-call(s32[1]{0:T(128)} %bitcast.2.mask_ref, s32[8]{0:T(128)S(1)} %bitcast.164, bf16[1024,1152]{1,0:T(8,128)(2,1)S(1)} %copy-done.7, bf16[1024,1152]{1,0:T(8,128)(2,1)S(1)} %copy-done.5, bf16[1024,384]{1,0:T(8,128)(2,1)S(1)} %copy-done.1, ...), custom_call_target="tpu_custom_call" | custom-call | flops 20000000000 | bytes 8000000 | tf_op jit(solution)/shard_map/attend_backward_0/pallas_call | solution.py:219
  399.5 29.6 %attend_backward_1.1 = (bf16[1024,384]{1,0:T(8,128)(2,1)S(1)}, bf16[1024,384]{1,0:T(8,128)(2,1)S(1)}) custom-call(s32[1]{0:T(128)} %bitcast.2.mask_ref, s32[8]{0:T(128)S(1)} %bitcast.165, bf16[1024,1152]{1,0:T(8,128)(2,1)S(1)} %copy-done.7, bf16[1024,1152]{1,0:T(8,128)(2,1)S(1)} %copy-done.5, bf16[1024,384]{1,0:T(8,128)(2,1)S(1)} %copy-done.1, ...), custom_call_target="tpu_custom_call" | custom-call | flops 20000000000 | bytes 8000000 | tf_op jit(solution)/shard_map/attend_backward_1/pallas_call | solution.py:219
  429.2 2.8 fusion.89
  434.8 2.8 add_convert_fusion.3
  438.1 29.8 %attend_backward_2.1 = (bf16[1024,384]{1,0:T(8,128)(2,1)S(1)}, bf16[1024,384]{1,0:T(8,128)(2,1)S(1)}) custom-call(s32[1]{0:T(128)} %bitcast.2.mask_ref, s32[8]{0:T(128)S(1)} %bitcast.166, bf16[1024,1152]{1,0:T(8,128)(2,1)S(1)} %copy-done.7, bf16[1024,1152]{1,0:T(8,128)(2,1)S(1)} %copy-done.5, bf16[1024,384]{1,0:T(8,128)(2,1)S(1)} %copy-done.1, ...), custom_call_target="tpu_custom_call" | custom-call | flops 20000000000 | bytes 8000000 | tf_op jit(solution)/shard_map/attend_backward_2/pallas_call | solution.py:219
  470.6 2.5 fusion.44
  475.0 3.4 fusion.38
  480.1 3.9 fusion.26
  485.4 3.1 collective-permute-start.18
  493.3 2.4 collective-permute-done.22
  496.8 5.8 collective-permute-start.29
  506.3 3.2 collective-permute-done.30
  512.2 2.9 collective-permute-start.38
  517.6 34.3 %collective-permute-done.33 = bf16[64,1152]{1,0:T(8,128)(2,1)S(1)} collective-permute-done((bf16[64,1152]{1,0:T(8,128)(2,1)S(1)}, bf16[64,1152]{1,0:T(8,128)(2,1)S(1)}, u32[]{:S(2)}, u32[]{:S(2)}) %collective-permute-start.33) | collective-permute-done | bytes 147488 | tf_op jit(solution)/shard_map/ppermute | solution.py:343
  551.9 2.8 collective-permute-start.34
  557.6 3.8 collective-permute-start.35
  567.5 3.3 collective-permute-start.42
  576.3 2.8 reshape.509
  581.3 16.0 %collective-permute-done.42 = bf16[224,768]{1,0:T(8,128)(2,1)} collective-permute-done((bf16[224,768]{1,0:T(8,128)(2,1)}, bf16[224,768]{1,0:T(8,128)(2,1)}, u32[]{:S(2)}, u32[]{:S(2)}) %collective-permute-start.42) | collective-permute-done | bytes 344096 | tf_op jit(solution)/shard_map/ppermute | solution.py:343
  598.3 3.5 collective-permute-done.43
  604.3 5.4 add_convert_fusion.1
  615.0 14.7 %collective-permute-done.19 = bf16[512,768]{0,1:T(8,128)(2,1)S(1)} collective-permute-done((bf16[512,768]{0,1:T(8,128)(2,1)S(1)}, bf16[512,768]{0,1:T(8,128)(2,1)S(1)}, u32[]{:S(2)}, u32[]{:S(2)}) %collective-permute-start.19) | collective-permute-done | bytes 786464 | tf_op jit(solution)/shard_map/ppermute | solution.py:386
  629.7 16.6 %collective-permute-done.20 = bf16[512,768]{0,1:T(8,128)(2,1)S(1)} collective-permute-done((bf16[512,768]{0,1:T(8,128)(2,1)S(1)}, bf16[512,768]{0,1:T(8,128)(2,1)S(1)}, u32[]{:S(2)}, u32[]{:S(2)}) %collective-permute-start.20) | collective-permute-done | bytes 786464 | tf_op jit(solution)/shard_map/ppermute | solution.py:386
  648.2 3.5 copy.100
  (370 shorter events, 143.5 us)
Async XLA Ops:
  7.2 61.5 %all-gather.7.cloned.1.call-start = ((), (), s32[]{:S(2)}) async-start(), calls=%async_computation | async-start | bytes 2211840 | tf_op jit(solution)/shard_map/all_gather | solution.py:404
  9.5 1.8 collective-permute-start.3
  12.2 162.3 %all-gather.9.cloned.1.call-start = ((), (), s32[]{:S(2)}) async-start(), calls=%async_computation.1 | async-start | bytes 1327104 | tf_op jit(solution)/shard_map/all_gather | solution.py:411
  13.0 168.8 %all-gather.11.cloned.1.call-start = ((), (), s32[]{:S(2)}) async-start(), calls=%async_computation.2 | async-start | bytes 5308416 | tf_op jit(solution)/shard_map/all_gather | solution.py:412
  13.7 214.8 %all-gather.13.cloned.1.call-start = ((), (), s32[]{:S(2)}) async-start(), calls=%async_computation.3 | async-start | bytes 5308416 | tf_op jit(solution)/shard_map/all_gather | solution.py:413
  17.1 28.1 %collective-permute-start = (bf16[512,768]{0,1:T(8,128)(2,1)}, bf16[512,768]{0,1:T(8,128)(2,1)}, u32[]{:S(2)}, u32[]{:S(2)}) collective-permute-start(bf16[512,768]{0,1:T(8,128)(2,1)} %bitcast.193), channel_id=1, source_target_pairs={{0,0},{1,1},{2,4},{3,5},{4,2},{5,3},{6,6},{7,7},{8,8},{9,9},{10,12... | collective-permute-start | bytes 2359304 | tf_op jit(solution)/shard_map/ppermute | solution.py:383
  22.8 39.4 %collective-permute-start.1 = (bf16[512,768]{0,1:T(8,128)(2,1)}, bf16[512,768]{0,1:T(8,128)(2,1)}, u32[]{:S(2)}, u32[]{:S(2)}) collective-permute-start(bf16[512,768]{0,1:T(8,128)(2,1)} %bitcast.1), channel_id=1, source_target_pairs={{0,1},{1,0},{2,5},{3,4},{4,3},{5,2},{6,7},{7,6},{8,9},{9,8},{10,13... | collective-permute-start | bytes 2359304 | tf_op jit(solution)/shard_map/ppermute | solution.py:383
  22.8 39.4 %collective-permute-start.2 = (s32[2,8]{1,0:T(2,128)S(1)}, s32[2,8]{1,0:T(2,128)S(1)}, u32[]{:S(2)}, u32[]{:S(2)}) collective-permute-start(s32[2,8]{1,0:T(2,128)S(1)} %bitcast.200), channel_id=1, source_target_pairs={{0,4},{4,0},{1,5},{5,1},{2,6},{6,2},{3,7},{7,3},{8,12},{12,8},{9,1... | collective-permute-start | bytes 200 | tf_op jit(solution)/shard_map/ppermute | solution.py:288
  27.3 143.9 %collective-permute-start.10 = (bf16[512,768]{0,1:T(8,128)(2,1)}, bf16[512,768]{0,1:T(8,128)(2,1)S(1)}, u32[]{:S(2)}, u32[]{:S(2)}) collective-permute-start(bf16[512,768]{0,1:T(8,128)(2,1)} %bitcast.13), channel_id=1, source_target_pairs={{0,1},{1,0},{2,5},{3,4},{4,3},{5,2},{6,7},{7,6},{8,9},{9,8},{10,13... | collective-permute-start | bytes 2359304 | tf_op jit(solution)/shard_map/ppermute | solution.py:383
  31.1 139.3 %collective-permute-start.9 = (bf16[512,768]{0,1:T(8,128)(2,1)}, bf16[512,768]{0,1:T(8,128)(2,1)S(1)}, u32[]{:S(2)}, u32[]{:S(2)}) collective-permute-start(bf16[512,768]{0,1:T(8,128)(2,1)} %bitcast.12), channel_id=1, source_target_pairs={{0,0},{1,1},{2,4},{3,5},{4,2},{5,3},{6,6},{7,7},{8,8},{9,9},{10,12... | collective-permute-start | bytes 2359304 | tf_op jit(solution)/shard_map/ppermute | solution.py:383
  45.3 21.4 %collective-permute-start.4 = (bf16[512,768]{0,1:T(8,128)(2,1)}, bf16[512,768]{0,1:T(8,128)(2,1)S(1)}, u32[]{:S(2)}, u32[]{:S(2)}) collective-permute-start(bf16[512,768]{0,1:T(8,128)(2,1)} %collective-permute-done), channel_id=1, source_target_pairs={{0,4},{4,0},{1,5},{5,1},{2,6},{6,2},{3,7},{7,3},{8,12},{12,8},{9,1... | collective-permute-start | bytes 2359304 | tf_op jit(solution)/shard_map/ppermute | solution.py:288
  62.1 5.6 collective-permute-start.5
  159.7 17.1 %collective-permute-start.6 = (bf16[1024,384]{1,0:T(8,128)(2,1)S(1)}, bf16[1024,384]{1,0:T(8,128)(2,1)}, u32[]{:S(2)}, u32[]{:S(2)}) collective-permute-start(bf16[1024,384]{1,0:T(8,128)(2,1)S(1)} %get-tuple-element.32.ctx_sib), channel_id=1, source_target_pairs={{0,4},{4,0},{1,5},{5,1},{2,6},{6,2},{3,7},{7,3},{8,12},{12,8},{9,1... | collective-permute-start | bytes 2359304 | tf_op jit(solution)/shard_map/ppermute | solution.py:288
  297.7 60.8 %collective-permute-start.14 = (bf16[4,32,768]{2,1,0:T(8,128)(2,1)}, bf16[4,32,768]{2,1,0:T(8,128)(2,1)}, u32[]{:S(2)}, u32[]{:S(2)}) collective-permute-start(bf16[4,32,768]{2,1,0:T(8,128)(2,1)} %dynamic-slice_bitcast_fusion.16), channel_id=1, source_target_pairs={{0,4},{4,0},{1,5},{5,1},{2,6},{6,2},{3,7},{7,3},{8,12},{12,8},{9,1... | collective-permute-start | bytes 589832 | tf_op jit(solution)/shard_map/ppermute | solution.py:288
  297.9 51.0 %collective-permute-start.12 = (bf16[4,96,3072]{2,1,0:T(8,128)(2,1)}, bf16[4,96,3072]{2,1,0:T(8,128)(2,1)}, u32[]{:S(2)}, u32[]{:S(2)}) collective-permute-start(bf16[4,96,3072]{2,1,0:T(8,128)(2,1)} %get-tuple-element.142), channel_id=1, source_target_pairs={{0,4},{4,0},{1,5},{5,1},{2,6},{6,2},{3,7},{7,3},{8,12},{12,8},{9,1... | collective-permute-start | bytes 7077896 | tf_op jit(solution)/shard_map/ppermute | solution.py:288
  301.7 44.0 %collective-permute-start.11 = (bf16[4,384,768]{2,1,0:T(8,128)(2,1)}, bf16[4,384,768]{2,1,0:T(8,128)(2,1)}, u32[]{:S(2)}, u32[]{:S(2)}) collective-permute-start(bf16[4,384,768]{2,1,0:T(8,128)(2,1)} %dynamic-slice_bitcast_fusion.1), channel_id=1, source_target_pairs={{0,4},{4,0},{1,5},{5,1},{2,6},{6,2},{3,7},{7,3},{8,12},{12,8},{9,1... | collective-permute-start | bytes 7077896 | tf_op jit(solution)/shard_map/ppermute | solution.py:288
  301.9 18.4 %collective-permute-start.7 = (bf16[512,768]{0,1:T(8,128)(2,1)S(1)}, bf16[512,768]{0,1:T(8,128)(2,1)S(1)}, u32[]{:S(2)}, u32[]{:S(2)}) collective-permute-start(bf16[512,768]{0,1:T(8,128)(2,1)S(1)} %get-tuple-element.148), channel_id=1, source_target_pairs={{0,0},{1,1},{4,2},{5,3},{2,4},{3,5},{6,6},{7,7},{8,8},{9,9},{12,10... | collective-permute-start | bytes 2359304 | tf_op jit(solution)/shard_map/ppermute | solution.py:386
  303.8 37.7 %collective-permute-start.8 = (bf16[512,768]{0,1:T(8,128)(2,1)S(1)}, bf16[512,768]{0,1:T(8,128)(2,1)S(1)}, u32[]{:S(2)}, u32[]{:S(2)}) collective-permute-start(bf16[512,768]{0,1:T(8,128)(2,1)S(1)} %get-tuple-element.149), channel_id=1, source_target_pairs={{1,0},{0,1},{5,2},{4,3},{3,4},{2,5},{7,6},{6,7},{9,8},{8,9},{13,10... | collective-permute-start | bytes 2359304 | tf_op jit(solution)/shard_map/ppermute | solution.py:386
  320.4 36.3 %collective-permute-start.13 = (bf16[4,96,768]{2,1,0:T(8,128)(2,1)}, bf16[4,96,768]{2,1,0:T(8,128)(2,1)}, u32[]{:S(2)}, u32[]{:S(2)}) collective-permute-start(bf16[4,96,768]{2,1,0:T(8,128)(2,1)} %dynamic-slice_bitcast_fusion.7), channel_id=1, source_target_pairs={{0,4},{4,0},{1,5},{5,1},{2,6},{6,2},{3,7},{7,3},{8,12},{12,8},{9,1... | collective-permute-start | bytes 1769480 | tf_op jit(solution)/shard_map/ppermute | solution.py:288
  341.5 27.4 %collective-permute-start.15 = (bf16[1024,384]{1,0:T(8,128)(2,1)}, bf16[1024,384]{1,0:T(8,128)(2,1)S(1)}, u32[]{:S(2)}, u32[]{:S(2)}) collective-permute-start(bf16[1024,384]{1,0:T(8,128)(2,1)} %convolution_convert_fusion.2), channel_id=1, source_target_pairs={{0,4},{4,0},{1,5},{5,1},{2,6},{6,2},{3,7},{7,3},{8,12},{12,8},{9,1... | collective-permute-start | bytes 2359304 | tf_op jit(solution)/shard_map/ppermute | solution.py:288
  366.1 32.5 %collective-permute-start.17 = (bf16[2,448,768]{2,1,0:T(8,128)(2,1)S(1)}, bf16[2,448,768]{2,1,0:T(8,128)(2,1)S(1)}, u32[]{:S(2)}, u32[]{:S(2)}) collective-permute-start(bf16[2,448,768]{2,1,0:T(8,128)(2,1)S(1)} %dynamic-slice_bitcast_fusion.3), channel_id=1, source_target_pairs={{0,16},{8,24},{16,0},{24,8},{1,17},{9,25},{17,1},{25,9},{2,18},{10... | collective-permute-start | bytes 4128776 | tf_op jit(solution)/shard_map/ppermute | solution.py:325
  367.0 32.1 %collective-permute-start.16 = (bf16[2,448,768]{2,1,0:T(8,128)(2,1)S(1)}, bf16[2,448,768]{2,1,0:T(8,128)(2,1)S(1)}, u32[]{:S(2)}, u32[]{:S(2)}) collective-permute-start(bf16[2,448,768]{2,1,0:T(8,128)(2,1)S(1)} %dynamic-slice_bitcast_fusion.4), channel_id=1, source_target_pairs={{0,8},{8,0},{16,24},{24,16},{1,9},{9,1},{17,25},{25,17},{2,10},{10... | collective-permute-start | bytes 4128776 | tf_op jit(solution)/shard_map/ppermute | solution.py:325
  432.3 70.3 %collective-permute-start.37 = (bf16[448,768]{1,0:T(8,128)(2,1)S(1)}, bf16[448,768]{1,0:T(8,128)(2,1)S(1)}, u32[]{:S(2)}, u32[]{:S(2)}) collective-permute-start(bf16[448,768]{1,0:T(8,128)(2,1)S(1)} %dynamic-slice_bitcast_fusion.5), channel_id=1, source_target_pairs={{0,8},{8,0},{16,24},{24,16},{1,9},{9,1},{17,25},{25,17},{2,10},{10... | collective-permute-start | bytes 2064392 | tf_op jit(solution)/shard_map/ppermute | solution.py:325
  433.1 70.7 %collective-permute-start.36 = (bf16[448,768]{1,0:T(8,128)(2,1)S(1)}, bf16[448,768]{1,0:T(8,128)(2,1)S(1)}, u32[]{:S(2)}, u32[]{:S(2)}) collective-permute-start(bf16[448,768]{1,0:T(8,128)(2,1)S(1)} %dynamic-slice_bitcast_fusion.6), channel_id=1, source_target_pairs={{0,16},{8,24},{16,0},{24,8},{1,17},{9,25},{17,1},{25,9},{2,18},{10... | collective-permute-start | bytes 2064392 | tf_op jit(solution)/shard_map/ppermute | solution.py:325
  437.9 50.7 %collective-permute-start.21 = (bf16[2,128,768]{2,1,0:T(8,128)(2,1)S(1)}, bf16[2,128,768]{2,1,0:T(8,128)(2,1)S(1)}, u32[]{:S(2)}, u32[]{:S(2)}) collective-permute-start(bf16[2,128,768]{2,1,0:T(8,128)(2,1)S(1)} %dynamic-slice_bitcast_fusion.9), channel_id=1, source_target_pairs={{0,8},{8,0},{16,24},{24,16},{1,9},{9,1},{17,25},{25,17},{2,10},{10... | collective-permute-start | bytes 1179656 | tf_op jit(solution)/shard_map/ppermute | solution.py:325
  473.3 5.4 collective-permute-start.25
  474.8 5.1 collective-permute-start.27
  478.7 5.3 collective-permute-start.26
  480.0 5.4 collective-permute-start.28
  484.0 7.0 %collective-permute-start.23 = (bf16[2,128,768]{2,1,0:T(8,128)(2,1)S(1)}, bf16[2,128,768]{2,1,0:T(8,128)(2,1)S(1)}, u32[]{:S(2)}, u32[]{:S(2)}) collective-permute-start(bf16[2,128,768]{2,1,0:T(8,128)(2,1)S(1)} %dynamic-slice_bitcast_fusion.8), channel_id=1, source_target_pairs={{0,16},{8,24},{16,0},{24,8},{1,17},{9,25},{17,1},{25,9},{2,18},{10... | collective-permute-start | bytes 1179656 | tf_op jit(solution)/shard_map/ppermute | solution.py:325
  485.4 118.8 %collective-permute-start.18 = (bf16[1024,768]{0,1:T(8,128)(2,1)}, bf16[1024,768]{0,1:T(8,128)(2,1)}, u32[]{:S(2)}, u32[]{:S(2)}) collective-permute-start(bf16[1024,768]{0,1:T(8,128)(2,1)} %fusion.38), channel_id=1, source_target_pairs={{0,4},{4,0},{1,5},{5,1},{2,6},{6,2},{3,7},{7,3},{8,12},{12,8},{9,1... | collective-permute-start | bytes 4718600 | tf_op jit(solution)/shard_map/ppermute | solution.py:288
  488.8 7.0 %collective-permute-start.22 = (bf16[128,768]{1,0:T(8,128)(2,1)S(1)}, bf16[128,768]{1,0:T(8,128)(2,1)S(1)}, u32[]{:S(2)}, u32[]{:S(2)}) collective-permute-start(bf16[128,768]{1,0:T(8,128)(2,1)S(1)} %dynamic-slice_bitcast_fusion.15), channel_id=1, source_target_pairs={{0,16},{8,24},{16,0},{24,8},{1,17},{9,25},{17,1},{25,9},{2,18},{10... | collective-permute-start | bytes 589832 | tf_op jit(solution)/shard_map/ppermute | solution.py:325
  491.1 5.5 collective-permute-start.24
  496.8 9.4 %collective-permute-start.29 = (bf16[64,1152]{1,0:T(8,128)(2,1)S(1)}, bf16[64,1152]{1,0:T(8,128)(2,1)S(1)}, u32[]{:S(2)}, u32[]{:S(2)}) collective-permute-start(bf16[64,1152]{1,0:T(8,128)(2,1)S(1)} %get-tuple-element.164), channel_id=1, source_target_pairs={{0,1},{1,2},{2,3},{3,0},{4,5},{5,6},{6,7},{7,4},{8,9},{9,10},{10,1... | collective-permute-start | bytes 442376 | tf_op jit(solution)/shard_map/ppermute | solution.py:343
  502.6 6.8 %collective-permute-start.30 = (bf16[64,1152]{1,0:T(8,128)(2,1)S(1)}, bf16[64,1152]{1,0:T(8,128)(2,1)S(1)}, u32[]{:S(2)}, u32[]{:S(2)}) collective-permute-start(bf16[64,1152]{1,0:T(8,128)(2,1)S(1)} %get-tuple-element.166), channel_id=1, source_target_pairs={{0,2},{1,3},{2,0},{3,1},{4,6},{5,7},{6,4},{7,5},{8,10},{9,11},{10,... | collective-permute-start | bytes 442376 | tf_op jit(solution)/shard_map/ppermute | solution.py:343
  502.6 7.1 %collective-permute-start.31 = (bf16[64,1152]{1,0:T(8,128)(2,1)S(1)}, bf16[64,1152]{1,0:T(8,128)(2,1)S(1)}, u32[]{:S(2)}, u32[]{:S(2)}) collective-permute-start(bf16[64,1152]{1,0:T(8,128)(2,1)S(1)} %get-tuple-element.165), channel_id=1, source_target_pairs={{0,3},{1,0},{2,1},{3,2},{4,7},{5,4},{6,5},{7,6},{8,11},{9,8},{10,9... | collective-permute-start | bytes 442376 | tf_op jit(solution)/shard_map/ppermute | solution.py:343
  509.8 6.5 collective-permute-start.32
  512.2 49.6 %collective-permute-start.38 = (bf16[224,768]{1,0:T(8,128)(2,1)}, bf16[224,768]{1,0:T(8,128)(2,1)S(1)}, u32[]{:S(2)}, u32[]{:S(2)}) collective-permute-start(bf16[224,768]{1,0:T(8,128)(2,1)} %get-tuple-element.157), channel_id=1, source_target_pairs={{0,1},{1,2},{2,3},{3,0},{4,5},{5,6},{6,7},{7,4},{8,9},{9,10},{10,1... | collective-permute-start | bytes 1032200 | tf_op jit(solution)/shard_map/ppermute | solution.py:343
  515.2 46.7 %collective-permute-start.39 = (bf16[224,768]{1,0:T(8,128)(2,1)S(1)}, bf16[224,768]{1,0:T(8,128)(2,1)S(1)}, u32[]{:S(2)}, u32[]{:S(2)}) collective-permute-start(bf16[224,768]{1,0:T(8,128)(2,1)S(1)} %get-tuple-element.158), channel_id=1, source_target_pairs={{0,2},{1,3},{2,0},{3,1},{4,6},{5,7},{6,4},{7,5},{8,10},{9,11},{10,... | collective-permute-start | bytes 1032200 | tf_op jit(solution)/shard_map/ppermute | solution.py:343
  515.7 47.6 %collective-permute-start.40 = (bf16[224,768]{1,0:T(8,128)(2,1)S(1)}, bf16[224,768]{1,0:T(8,128)(2,1)}, u32[]{:S(2)}, u32[]{:S(2)}) collective-permute-start(bf16[224,768]{1,0:T(8,128)(2,1)S(1)} %get-tuple-element.159), channel_id=1, source_target_pairs={{0,3},{1,0},{2,1},{3,2},{4,7},{5,4},{6,5},{7,6},{8,11},{9,8},{10,9... | collective-permute-start | bytes 1032200 | tf_op jit(solution)/shard_map/ppermute | solution.py:343
  516.4 35.5 %collective-permute-start.33 = (bf16[64,1152]{1,0:T(8,128)(2,1)S(1)}, bf16[64,1152]{1,0:T(8,128)(2,1)S(1)}, u32[]{:S(2)}, u32[]{:S(2)}) collective-permute-start(bf16[64,1152]{1,0:T(8,128)(2,1)S(1)} %get-tuple-element.134), channel_id=1, source_target_pairs={{0,2},{1,3},{2,0},{3,1},{4,6},{5,7},{6,4},{7,5},{8,10},{9,11},{10,... | collective-permute-start | bytes 442376 | tf_op jit(solution)/shard_map/ppermute | solution.py:343
  551.9 4.9 collective-permute-start.34
  557.6 14.8 %collective-permute-start.35 = (bf16[112,1152]{1,0:T(8,128)(2,1)}, bf16[112,1152]{1,0:T(8,128)(2,1)}, u32[]{:S(2)}, u32[]{:S(2)}) collective-permute-start(bf16[112,1152]{1,0:T(8,128)(2,1)} %pad_maximum_fusion.3), channel_id=1, source_target_pairs={{0,4},{4,0},{1,5},{5,1},{2,6},{6,2},{3,7},{7,3},{8,12},{12,8},{9,1... | collective-permute-start | bytes 774152 | tf_op jit(solution)/shard_map/ppermute | solution.py:288
  565.8 14.5 %collective-permute-start.41 = (bf16[224,768]{1,0:T(8,128)(2,1)}, bf16[224,768]{1,0:T(8,128)(2,1)}, u32[]{:S(2)}, u32[]{:S(2)}) collective-permute-start(bf16[224,768]{1,0:T(8,128)(2,1)} %get-tuple-element.132), channel_id=1, source_target_pairs={{0,1},{1,2},{2,3},{3,0},{4,5},{5,6},{6,7},{7,4},{8,9},{9,10},{10,1... | collective-permute-start | bytes 1032200 | tf_op jit(solution)/shard_map/ppermute | solution.py:343
  567.5 29.9 %collective-permute-start.42 = (bf16[224,768]{1,0:T(8,128)(2,1)}, bf16[224,768]{1,0:T(8,128)(2,1)}, u32[]{:S(2)}, u32[]{:S(2)}) collective-permute-start(bf16[224,768]{1,0:T(8,128)(2,1)} %get-tuple-element.132), channel_id=1, source_target_pairs={{0,2},{1,3},{2,0},{3,1},{4,6},{5,7},{6,4},{7,5},{8,10},{9,11},{10,... | collective-permute-start | bytes 1032200 | tf_op jit(solution)/shard_map/ppermute | solution.py:343
  570.7 31.1 %collective-permute-start.43 = (bf16[224,768]{1,0:T(8,128)(2,1)}, bf16[224,768]{1,0:T(8,128)(2,1)}, u32[]{:S(2)}, u32[]{:S(2)}) collective-permute-start(bf16[224,768]{1,0:T(8,128)(2,1)} %get-tuple-element.132), channel_id=1, source_target_pairs={{0,3},{1,0},{2,1},{3,2},{4,7},{5,4},{6,5},{7,6},{8,11},{9,8},{10,9... | collective-permute-start | bytes 1032200 | tf_op jit(solution)/shard_map/ppermute | solution.py:343
  609.8 19.9 %collective-permute-start.19 = (bf16[512,768]{0,1:T(8,128)(2,1)S(1)}, bf16[512,768]{0,1:T(8,128)(2,1)S(1)}, u32[]{:S(2)}, u32[]{:S(2)}) collective-permute-start(bf16[512,768]{0,1:T(8,128)(2,1)S(1)} %get-tuple-element.144), channel_id=1, source_target_pairs={{0,0},{1,1},{4,2},{5,3},{2,4},{3,5},{6,6},{7,7},{8,8},{9,9},{12,10... | collective-permute-start | bytes 2359304 | tf_op jit(solution)/shard_map/ppermute | solution.py:386
  612.1 34.2 %collective-permute-start.20 = (bf16[512,768]{0,1:T(8,128)(2,1)S(1)}, bf16[512,768]{0,1:T(8,128)(2,1)S(1)}, u32[]{:S(2)}, u32[]{:S(2)}) collective-permute-start(bf16[512,768]{0,1:T(8,128)(2,1)S(1)} %get-tuple-element.145), channel_id=1, source_target_pairs={{1,0},{0,1},{5,2},{4,3},{3,4},{2,5},{7,6},{6,7},{9,8},{8,9},{13,10... | collective-permute-start | bytes 2359304 | tf_op jit(solution)/shard_map/ppermute | solution.py:386
  (55 other events, 793.6 us)
Sparse Core Ops, SparseCore 0:
  12.4 33.3 all-gather.6
  47.6 24.4 all-gather.8
  74.0 38.7 all-gather.10
  160.4 44.2 all-gather.12

commit v3 on v2

--- a/solution.py
+++ b/solution.py
@@ -13,6 +13,9 @@
 LANES = 128
 NEG = -1e30
 TILE = 256
+VALUE_ROWS = HEAD_DIM + 16
+KEY_TILES = 2
+QUERY_TILES = 2
 NT = (((1,), (1,)), ((), ()))
 NN = (((1,), (0,)), ((), ()))
 TN = (((0,), (0,)), ((), ()))
@@ -30,6 +33,11 @@
         low = jnp.maximum(low, jnp.where(end <= first, end, 0))
         high = jnp.minimum(high, jnp.where(end > last, end, total))
     return low // tile, (high + tile - 1) // tile
+
+
+def spans(first, after, count, tiles):
+    steps = (after - first + count - 1) // count
+    return jnp.minimum(first, tiles - steps * count), steps
 
 
 def lane_halves(x, fill):
@@ -52,7 +60,7 @@
     return copies
 
 
-def forward_kernel(run, mask_ref, ends_ref, own, sib, seg_col, seg_row, ctx_own, ctx_sib, lse_ref, qkv, out, acc, top, sems, out_sems):
+def forward_kernel(run, mask_ref, ends_ref, own, sib, seg_col, seg_row, ctx_own, ctx_sib, lse_ref, qkv, out, turned, acc, top, sems, out_sems):
     total = qkv.shape[1]
     pairs = out.shape[0]
     mask = mask_ref[0]
@@ -69,43 +77,56 @@
         for copy in loads(pair):
             copy.start()
 
+    for head in range(2 * pairs):
+        turned[head, HEAD_DIM:, :] = jnp.ones((VALUE_ROWS - HEAD_DIM, total), jnp.bfloat16)
     for pair in range(pairs):
         for copy in loads(pair):
             copy.wait()
+    heads = [(pair, head) for pair in range(pairs) for head in range(2)]
+    if True:
 
         @pl.loop(0, total // TILE)
         def _(block):
             rows = pl.multiple_of(block * TILE, TILE)
-            q_heads = lane_halves(qkv[pair, pl.ds(rows, TILE), :], 0.0)
-            segq = seg_col[pl.ds(rows, TILE), :]
-            segq = jnp.concatenate([segq] * (TILE // LANES), axis=1)
+            for pair in range(pairs):
+                values = qkv[2 * pairs + pair, pl.ds(rows, TILE), :].astype(jnp.float32).T.astype(jnp.bfloat16)
+                for head in range(2):
+                    turned[2 * pair + head, :HEAD_DIM, pl.ds(rows, TILE)] = values[head * HEAD_DIM : (head + 1) * HEAD_DIM]
+
+        @pl.loop(0, total // TILE)
+        def _(block):
+            rows = pl.multiple_of(block * TILE, TILE)
+            q_heads = sum([list(lane_halves(qkv[pair, pl.ds(rows, TILE), :], 0.0)) for pair in range(pairs)], [])
+            segq = seg_row[:, pl.ds(rows, TILE)]
             first, after = key_tiles(ends_ref, rows, rows + TILE - 1, TILE, total)
             acc[...] = jnp.zeros_like(acc)
             top[...] = jnp.full_like(top, NEG)
 
-            @pl.loop(first, after)
+            first, steps = spans(first, after, KEY_TILES, total // TILE)
+
+            @pl.loop(0, steps)
             def _(step):
-                at = pl.multiple_of(step * TILE, TILE)
-                keys = qkv[pairs + pair, pl.ds(at, TILE), :]
-                v_heads = lane_halves(qkv[2 * pairs + pair, pl.ds(at, TILE), :], 1.0)
-                same = segq == seg_row[:, pl.ds(at, TILE)]
-                for head in range(2):
-                    scores = jnp.where(same, mm(q_heads[head], keys, NT), NEG)
-                    old = top[head]
-                    new = jnp.maximum(old, jnp.max(scores, axis=1, keepdims=True))
-                    top[head] = new
-                    probs = jnp.exp(scores - jnp.concatenate([new] * (TILE // LANES), axis=1)).astype(jnp.bfloat16)
-                    acc[head] = acc[head] * jnp.exp(old - new) + mm(probs, v_heads[head], NN)
-
-            lane = lax.broadcasted_iota(jnp.int32, (TILE, LANES), 1)
-            sum_a = acc[0][:, HEAD_DIM : HEAD_DIM + 1]
-            sum_b = acc[1][:, 0:1]
-            out[pair, pl.ds(rows, TILE), :] = jnp.where(lane < HEAD_DIM, acc[0] / sum_a, acc[1] / sum_b).astype(jnp.bfloat16)
-            lse_a = (top[0] + jnp.log(sum_a)).T
-            lse_b = (top[1] + jnp.log(sum_b)).T
-            lse_ref[2 * pair, :, pl.ds(rows, TILE)] = lse_a[0:8]
-            lse_ref[2 * pair + 1, :, pl.ds(rows, TILE)] = lse_b[0:8]
-
+                at = pl.multiple_of((first + step * KEY_TILES) * TILE, TILE)
+                keys = [qkv[pairs + pair, pl.ds(at, KEY_TILES * TILE), :] for pair in range(pairs)]
+                segk = seg_col[pl.ds(at, KEY_TILES * TILE), :]
+                same = jnp.concatenate([segk] * (TILE // LANES), axis=1) == segq
+                for head in range(2 * pairs):
+                    scores = jnp.where(same, mm(keys[head // 2], q_heads[head], NT), NEG)
+                    old = top[head, 0:1]
+                    new = jnp.maximum(old, jnp.max(scores, axis=0, keepdims=True))
+                    probs = jnp.exp(scores - new).astype(jnp.bfloat16)
+                    acc[head] = acc[head] * jnp.exp(old - new) + mm(turned[head, :, pl.ds(at, KEY_TILES * TILE)], probs, NN)
+                    top[head] = jnp.broadcast_to(new, (8, TILE))
+
+            for pair in range(pairs):
+                parts = []
+                for head in (2 * pair, 2 * pair + 1):
+                    weight = acc[head, HEAD_DIM : HEAD_DIM + 1]
+                    parts.append(acc[head, :HEAD_DIM] / weight)
+                    lse_ref[head, :, pl.ds(rows, TILE)] = top[head] + jnp.log(acc[head, HEAD_DIM : HEAD_DIM + 8])
+                out[pair, pl.ds(rows, TILE), :] = jnp.concatenate(parts, axis=0).T.astype(jnp.bfloat16)
+
+    for pair in range(pairs):
         for copy in piece_copies((ctx_own, ctx_sib), pair * LANES, pair, out, pair, out_sems, run, mask, False):
             copy.start()
     for pair in range(pairs):
@@ -133,8 +154,9 @@
         scratch_shapes=[
             pltpu.VMEM((3 * pairs, total, LANES), jnp.bfloat16),
             pltpu.VMEM((pairs, total, LANES), jnp.bfloat16),
-            pltpu.VMEM((2, TILE, LANES), jnp.float32),
-            pltpu.VMEM((2, TILE, LANES), jnp.float32),
+            pltpu.VMEM((2 * pairs, VALUE_ROWS, total), jnp.bfloat16),
+            pltpu.VMEM((2 * pairs, VALUE_ROWS, TILE), jnp.float32),
+            pltpu.VMEM((2 * pairs, 8, TILE), jnp.float32),
             pltpu.SemaphoreType.DMA((3 * pairs, pieces)),
             pltpu.SemaphoreType.DMA((pairs, pieces)),
         ],
@@ -146,7 +168,7 @@
 
 def backward_kernel(
     run, pair, mask_ref, ends_ref, own, sib, ctx_own, ctx_sib, dctx_own, dctx_sib, seg_col, seg_row, lse_ref,
-    d_own, d_sib, qkv, ctx, out, delta, dq, dkv, sems, out_sems
+    d_own, d_sib, qkv, ctx, out, turned, delta, dq, dkv, sems, out_sems
 ):
     total = qkv.shape[1]
     mask = mask_ref[0]
@@ -169,7 +191,8 @@
         for head in range(2):
             part = jnp.sum(product[head * HEAD_DIM : (head + 1) * HEAD_DIM], axis=0, keepdims=True)
             delta[head, :, pl.ds(rows, TILE)] = jnp.broadcast_to(part, (8, TILE))
-        dq[pl.ds(rows, TILE), :] = jnp.zeros((TILE, LANES), jnp.float32)
+        turned[:, pl.ds(rows, TILE)] = qkv[1, pl.ds(rows, TILE), :].astype(jnp.float32).T.astype(jnp.bfloat16)
+        dq[:, pl.ds(rows, TILE)] = jnp.zeros((LANES, TILE), jnp.float32)
 
     @pl.loop(0, total // TILE)
     def _(block):
@@ -181,28 +204,35 @@
         first, after = key_tiles(ends_ref, rows, rows + TILE - 1, TILE, total)
         dkv[...] = jnp.zeros_like(dkv)
 
-        @pl.loop(first, after)
+        first, steps = spans(first, after, QUERY_TILES, total // TILE)
+
+        @pl.loop(0, steps)
         def _(step):
-            at = pl.multiple_of(step * TILE, TILE)
-            queries = qkv[0, pl.ds(at, TILE), :]
-            grads = ctx[1, pl.ds(at, TILE), :]
+            at = pl.multiple_of((first + step * QUERY_TILES) * TILE, TILE)
+            span = pl.ds(at, QUERY_TILES * TILE)
+            queries = qkv[0, span, :]
+            grads = ctx[1, span, :]
             q_heads = lane_halves(queries, 0.0)
             g_heads = lane_halves(grads, 0.0)
-            same = segk == seg_row[:, pl.ds(at, TILE)]
+            same = jnp.concatenate([segk] * QUERY_TILES, axis=1) == seg_row[:, span]
             for head in range(2):
                 scores = mm(k_heads[head], queries, NT)
-                lse = lse_ref[2 * pair + head, 0:1, pl.ds(at, TILE)]
-                probs = jnp.exp(jnp.where(same, scores - lse, NEG))
+                probs = jnp.exp(jnp.where(same, scores - lse_ref[2 * pair + head, 0:1, span], NEG))
                 dprobs = mm(v_heads[head], grads, NT)
-                dscores = (probs * (dprobs - delta[head, 0:1, pl.ds(at, TILE)])).astype(jnp.bfloat16)
+                dscores = (probs * (dprobs - delta[head, 0:1, span])).astype(jnp.bfloat16)
                 dkv[1] += mm(probs.astype(jnp.bfloat16), g_heads[head], NN)
                 dkv[0] += mm(dscores, q_heads[head], NN)
-                dq[pl.ds(at, TILE), :] += mm(dscores, k_heads[head], TN)
+                lanes = slice(head * HEAD_DIM, (head + 1) * HEAD_DIM)
+                dq[lanes, span] += mm(turned[lanes, pl.ds(rows, TILE)], dscores, NN)
 
         out[1, pl.ds(rows, TILE), :] = dkv[0].astype(jnp.bfloat16)
         out[2, pl.ds(rows, TILE), :] = dkv[1].astype(jnp.bfloat16)
 
-    out[0] = (dq[...] * HEAD_DIM**-0.5).astype(jnp.bfloat16)
+    @pl.loop(0, total // TILE)
+    def _(block):
+        rows = pl.multiple_of(block * TILE, TILE)
+        out[0, pl.ds(rows, TILE), :] = (dq[:, pl.ds(rows, TILE)].T * HEAD_DIM**-0.5).astype(jnp.bfloat16)
+
     for copy in stores:
         copy.start()
     for copy in stores:
@@ -228,8 +258,9 @@
             pltpu.VMEM((3, total, LANES), jnp.bfloat16),
             pltpu.VMEM((2, total, LANES), jnp.bfloat16),
             pltpu.VMEM((3, total, LANES), jnp.bfloat16),
+            pltpu.VMEM((LANES, total), jnp.bfloat16),
             pltpu.VMEM((2, 8, total), jnp.float32),
-            pltpu.VMEM((total, LANES), jnp.float32),
+            pltpu.VMEM((LANES, total), jnp.float32),
             pltpu.VMEM((2, TILE, LANES), jnp.float32),
             pltpu.SemaphoreType.DMA((5, pieces)),
             pltpu.SemaphoreType.DMA((3, pieces)),
@@ -337,7 +368,8 @@
         self.me = lax.axis_index("seq")
         quarter = lambda which: lax.dynamic_slice_in_dim(value, (which % nseq) * self.rows, self.rows, 0)
         self.keep = quarter(self.me)
-        self.received = [self.shift(quarter(self.me + d), d) for d in range(1, nseq)]
+        self.sent = [quarter(self.me + d) for d in range(1, nseq)]
+        self.received = [self.shift(q, d) for d, q in enumerate(self.sent, 1)]
 
     def shift(self, value, distance):
         return lax.ppermute(value, "seq", [(i, (i + distance) % self.nseq) for i in range(self.nseq)])
@@ -471,6 +503,18 @@
         joined.append(jnp.concatenate([down_grad[which]] + wide + [out_grad[which], vector[which]], axis=1))
     early = Halving(total(*joined), planes)
     early.send(0)
+    progress = [early]
+
+    def advance(*done):
+        if len(progress) > 1:
+            return []
+        early.add(*done)
+        step = early.steps - len(early.left[0])
+        if step < early.steps:
+            early.send(step)
+            return early.sent
+        progress.append(Spread(early.result(), nseq))
+        return progress[1].sent
 
     def attend(pair, *ready):
         held = after(mask, *ready)
@@ -488,38 +532,33 @@
         return jnp.concatenate([matrix.reshape(planes, CORES * rows, -1), column], axis=1)
 
     grads = [attend(0, *early.sent)]
-    sent = []
     for pair in range(1, pairs):
-        if len(early.left[0]):
-            early.add(grads[-1][0])
-            early.send(early.steps - len(early.left[0]))
-            sent = early.sent
+        sent = advance(grads[-1][0])
         if pair == pairs - 1:
             first_sums = Halving(weight_sums(grads), planes)
             first_sums.send(0)
             sent = sent + first_sums.sent
         grads.append(attend(pair, *sent))
-    while len(early.left[0]):
-        early.add(grads[-1][0])
-        early.send(early.steps - len(early.left[0]))
-    early.add(grads[-1][0])
-    early_sum = Spread(early.result(), nseq)
+    while len(progress) == 1:
+        advance(grads[-1][0])
+    early_sum = progress[1]
 
     near = jnp.concatenate([g[0] for g in grads], axis=1)
     far = jnp.concatenate([g[1] for g in grads], axis=1)
     grad_far = swap(mm(far, w_mine, NT).astype(bf16))
-    last_sums = Halving(weight_sums(grads[-1:]), planes)
+    early_sum.add(grads[-1][0])
+    input_grad = (grad_one + mm(near, w_mine, NT) + grad_far.astype(f32)).astype(bf16)
+    returned = [lax.ppermute(input_grad[i * run : (i + 1) * run], ("core", "seq"), back[i]) for i in range(2)]
+    last_sums = Halving(after(weight_sums(grads[-1:]), input_grad), planes)
     last_sums.send(0)
-    input_grad = grad_one + mm(near, w_mine, NT) + grad_far.astype(f32)
-    input_grad = collect(input_grad.astype(bf16)).astype(f32)
     for step in range(last_sums.steps):
         for sums in (first_sums, last_sums):
             sums.add()
             if step + 1 < sums.steps:
                 sums.send(step + 1)
     qkv_sum = Spread(jnp.concatenate([first_sums.result(), last_sums.result()], axis=1), nseq)
-    early_sum.add()
-    qkv_sum.add()
+    qkv_sum.add(*returned)
+    input_grad = jnp.where(odd == 0, jnp.stack(returned), jnp.stack(returned[::-1]))[None].astype(f32)
     early_total = early_sum.result()
     qkv_total = qkv_sum.result()
 

time: 669 us -> 581 us (0.87)
  Pallas kernels: 171 us -> 126 us
  local copies, waits for them, and re-layouts: 89.8 us -> 60.1 us
  matrix products: 127 us -> 112 us
    pallas_call x3, Pallas kernels: 88.9 us -> 58.9 us  [attend_backward(): pl.pallas_call(functools.partial(backward_kernel, run, pair), out_shape=(...]
    ppermute x4 -> x2, waiting for transfers between devices: 52.4 us -> 27.4 us  [collect(): lax.ppermute(x[i * run:(i + 1) * run], ('core', 'seq'), back[i])]
    dot_general x20, matrix products: 127 us -> 112 us  [mm(): lax.dot_general(left, right, dims, preferred_element_type=jnp.float32)]
    pallas_call x1, Pallas kernels: 81.6 us -> 66.7 us  [attend_forward(): pl.pallas_call(functools.partial(forward_kernel, run), out_shape=(jax.Sha...]
    ppermute x12, waiting for transfers between devices: 4.66 us -> 19.2 us  [send(): lax.ppermute(out, 'xy', [(i, i ^ 1 << bit) for i in range(self.planes)])]
    ppermute x12, starting transfers between devices: 12.5 us -> 25.4 us  [send(): lax.ppermute(out, 'xy', [(i, i ^ 1 << bit) for i in range(self.planes)])]
    ppermute x12, waiting for transfers between devices: 61.5 us -> 74.1 us  [shift(): lax.ppermute(value, 'seq', [(i, (i + distance) % self.nseq) for i in rang...]
    ppermute x4 -> x2, starting transfers between devices: 11.9 us -> 2.39 us  [collect(): lax.ppermute(x[i * run:(i + 1) * run], ('core', 'seq'), back[i])]
  transfers between devices with their start and end apart: 48 -> 48, of which waited for: 17 -> 19; matrix products, arithmetic and copies ran while one was open for 25% -> 23% of each run, Pallas kernels for 21% -> 19%
where the time goes in v3:
time: 581 us; the launch traced here: 570 us
  waiting for transfers between devices  141 us (24%)
  Pallas kernels  126 us (22%)
  matrix products  112 us (19%)
  starting transfers between devices  64.1 us (11%)
  local copies, waits for them, and re-layouts  60.1 us (10%)
  other arithmetic  43 us (7%)
  between operations  15.7 us (3%)
  blocking collectives  9.34 us (2%)
    dot_general x20, matrix products, mm(): lax.dot_general(left, right, dims, preferred_element_type=jnp.float32)  112 us
    ppermute x12, waiting for transfers between devices, shift(): lax.ppermute(value, 'seq', [(i, (i + distance) % self.nseq) for i in rang...  74.1 us
    pallas_call x1, Pallas kernels, attend_forward(): pl.pallas_call(functools.partial(forward_kernel, run), out_shape=(jax.Sha...  66.7 us
    pallas_call x3, Pallas kernels, attend_backward(): pl.pallas_call(functools.partial(backward_kernel, run, pair), out_shape=(...  58.9 us
    ppermute x2, waiting for transfers between devices, collect(): lax.ppermute(x[i * run:(i + 1) * run], ('core', 'seq'), back[i])  27.4 us
    unnamed x178, local copies, waits for them, and re-layouts  26.7 us
    ppermute x12, starting transfers between devices, send(): lax.ppermute(out, 'xy', [(i, i ^ 1 << bit) for i in range(self.planes)])  25.4 us
    ppermute x12, waiting for transfers between devices, send(): lax.ppermute(out, 'xy', [(i, i ^ 1 << bit) for i in range(self.planes)])  19.2 us
  transfers between devices with their start and end apart: 48, of which 19 were waited for; matrix products, arithmetic and copies ran while one was open for 23% of the time, Pallas kernels for 19%

profile of v3, /device:TPU:9, one launch (start us, length us, event | category | flops | bytes accessed | tf_op | source)
XLA Modules:
  0.0 570.4 jit_solution(13244963082323957992)
XLA Ops:
  17.1 4.5 collective-permute-start
  22.0 3.4 collective-permute-start.2
  26.6 2.5 collective-permute-start.10
  30.3 3.4 collective-permute-start.9
  33.8 9.3 %all-gather.1 = bf16[8,1,1152]{2,1,0:T(2,128)(2,1)S(1)} all-gather(bf16[1,1,1152]{2,1,0:T(2,128)(2,1)S(1)} %reshape.516), channel_id=2, replica_groups=mesh['xy'=4,'core'=2,'seq'=4] {'xy','core'}, dimensions={0}, use_global_device_ids=true | all-gather | bytes 20736 | tf_op jit(solution)/shard_map/all_gather | solution.py:438
  44.4 16.7 %collective-permute-done.1 = bf16[512,768]{0,1:T(8,128)(2,1)} collective-permute-done((bf16[512,768]{0,1:T(8,128)(2,1)S(1)}, bf16[512,768]{0,1:T(8,128)(2,1)}, u32[]{:S(2)}, u32[]{:S(2)}) %collective-permute-start.1) | collective-permute-done | bytes 786464 | tf_op jit(solution)/shard_map/ppermute | solution.py:415
  63.9 2.7 constant_dynamic-update-slice_fusion.3
  68.7 4.4 multiply_convert_fusion.sib
  75.8 66.7 %attend_forward.1 = (bf16[1024,384]{1,0:T(8,128)(2,1)S(1)}, bf16[1024,384]{1,0:T(8,128)(2,1)S(1)}, f32[6,8,2048]{2,1,0:T(8,128)S(1)}) custom-call(s32[1]{0:T(128)} %bitcast.2.mask_ref, s32[8]{0:T(128)S(1)} %bitcast.163, bf16[1024,1152]{1,0:T(8,128)(2,1)S(1)} %multiply_convert_fusion.1.own, bf16[1024,1152]{1,0:T(8,128)(2,1)S(1)} %multiply_convert_fusion.sib, ...), custom_call_target="tpu_custom_call" | custom-call | flops 49999998976 | bytes 8000000 | tf_op jit(solution)/shard_map/attend_forward/pallas_call | solution.py:145
  147.6 2.4 fusion.86
  150.5 38.5 %fusion.2 = (bf16[1024,3072]{1,0:T(8,128)(2,1)}, f32[1024,3072]{1,0:T(8,128)}) fusion(f32[3072]{0:T(1024)S(1)} %add.429, bf16[768,3072]{1,0:T(8,128)(2,1)} %all-gather.11.cloned.1.call-done, f32[1024,768]{0,1:T(8,128)S(1)} %get-tuple-element.200, f32[768]{0:T(1024)S(1)} %add.426, f32[768]{0:T(1024)S(1)} %mul.223, f32[1024]{0:T(1024)S(1)} %add_rsqrt_fusion.1, ...), kind=kOutput, calls=%fused_computation.4 | convolution fusion | flops 5043388416 | bytes 26765312 | tf_op jit(solution)/shard_map/dot_general | solution.py:25
  189.5 8.9 %fusion.87 = (f32[1024]{0:T(1024)S(1)}, f32[1024,768]{0,1:T(8,128)S(1)}) fusion(f32[768]{0:T(1024)S(1)} %add.433, bf16[1024,3072]{1,0:T(8,128)(2,1)} %get-tuple-element.201, bf16[3072,768]{1,0:T(8,128)(2,1)} %all-gather.13.cloned.1.call-done, f32[768]{0:T(1024)S(1)} %add.426, f32[768]{0:T(1024)S(1)} %mul.223, f32[1024]{0:T(1024)S(1)} %add_rsqrt_fusion.1, ...), kind=kOutput, calls=%fused_computation.239 | convolution fusion | flops 4837342208 | bytes 17323008 | tf_op jit(solution)/shard_map/dot_general | solution.py:25
  199.8 2.6 fusion.22
  203.7 6.9 %convolution_convert_fusion.1 = bf16[3072,768]{1,0:T(8,128)(2,1)} fusion(bf16[1024,3072]{1,0:T(8,128)(2,1)S(1)} %bitcast.207, bf16[1024,768]{0,1:T(8,128)(2,1)S(1)} %get-tuple-element.150), kind=kOutput, calls=%fused_computation.28 | convolution fusion | flops 4834197504 | bytes 12582912 | tf_op jit(solution)/shard_map/dot_general | solution.py:25
  210.6 11.9 %fusion.88 = (bf16[3072]{0:T(1024)(128)(2,1)S(1)}, bf16[1024,3072]{1,0:T(8,128)(2,1)S(1)}) fusion(f32[1024,3072]{1,0:T(8,128)} %get-tuple-element.202, f32[3072]{0:T(1024)S(1)} %add.429, bf16[1024,768]{0,1:T(8,128)(2,1)S(1)} %get-tuple-element.150, bf16[3072,768]{1,0:T(8,128)(2,1)S(1)} %bitcast.205), kind=kOutput, calls=%fused_computation.240 | convolution fusion | flops 4869583872 | bytes 25184256 | tf_op jit(solution)/shard_map/dot_general | solution.py:25
  222.5 5.8 %convolution_convert_fusion = bf16[768,3072]{1,0:T(8,128)(2,1)S(1)} fusion(bf16[1024,3072]{1,0:T(8,128)(2,1)S(1)} %get-tuple-element.207, f32[1024,768]{0,1:T(8,128)S(1)} %get-tuple-element.200, f32[768]{0:T(1024)S(1)} %add.426, f32[768]{0:T(1024)S(1)} %mul.223, f32[1024]{0:T(1024)S(1)} %add_rsqrt_fusion.1, f32[1024]{0:T(1024)S(1)} %broadcast_multiply_fusion.5), kind=kOutput, calls=%fused_computation.27 | convolution fusion | flops 4838129664 | bytes 14170112 | tf_op jit(solution)/shard_map/dot_general | solution.py:25
  228.3 2.6 dynamic-slice_bitcast_fusion.2
  230.9 6.6 %multiply_reduce_fusion = (bf16[768]{0:T(1024)(128)(2,1)S(1)}, f32[1024]{0:T(1024)S(1)}, f32[1024]{0:T(1024)S(1)}, bf16[768]{0:T(1024)(128)(2,1)S(1)}, f32[1024,768]{0,1:T(8,128)S(1)}) fusion(f32[1024,768]{0,1:T(8,128)S(1)} %get-tuple-element.200, f32[1024]{0:T(1024)S(1)} %add_rsqrt_fusion.1, f32[1024]{0:T(1024)S(1)} %broadcast_multiply_fusion.5, ...), kind=kOutput, calls=%fused_computation.43 | convolution fusion | flops 4848349184 | bytes 22062080 | tf_op jit(solution)/shard_map/dot_general | solution.py:25
  237.6 4.2 fusion.77
  268.8 5.5 add_convert_fusion
  276.0 8.6 %collective-permute-start.16 = (bf16[2,448,768]{2,1,0:T(8,128)(2,1)S(1)}, bf16[2,448,768]{2,1,0:T(8,128)(2,1)S(1)}, u32[]{:S(2)}, u32[]{:S(2)}) collective-permute-start(bf16[2,448,768]{2,1,0:T(8,128)(2,1)S(1)} %dynamic-slice_bitcast_fusion.4), channel_id=1, source_target_pairs={{0,8},{8,0},{16,24},{24,16},{1,9},{9,1},{17,25},{25,17},{2,10},{10... | collective-permute-start | bytes 4128776 | tf_op jit(solution)/shard_map/ppermute | solution.py:356
  284.6 19.6 %attend_backward_0.1 = (bf16[1024,384]{1,0:T(8,128)(2,1)S(1)}, bf16[1024,384]{1,0:T(8,128)(2,1)S(1)}) custom-call(s32[1]{0:T(128)} %bitcast.2.mask_ref, s32[8]{0:T(128)S(1)} %bitcast.164, bf16[1024,1152]{1,0:T(8,128)(2,1)S(1)} %copy-done.23, bf16[1024,1152]{1,0:T(8,128)(2,1)S(1)} %copy-done.20, bf16[1024,384]{1,0:T(8,128)(2,1)S(1)} %copy-done.1, ...), custom_call_target="tpu_custom_call" | custom-call | flops 20000000000 | bytes 8000000 | tf_op jit(solution)/shard_map/attend_backward_0/pallas_call | solution.py:249
  307.7 6.4 %collective-permute-done.16 = bf16[2,448,768]{2,1,0:T(8,128)(2,1)S(1)} collective-permute-done((bf16[2,448,768]{2,1,0:T(8,128)(2,1)S(1)}, bf16[2,448,768]{2,1,0:T(8,128)(2,1)S(1)}, u32[]{:S(2)}, u32[]{:S(2)}) %collective-permute-start.16) | collective-permute-done | bytes 1376288 | tf_op jit(solution)/shard_map/ppermute | solution.py:356
  315.5 19.6 %attend_backward_1.1 = (bf16[1024,384]{1,0:T(8,128)(2,1)S(1)}, bf16[1024,384]{1,0:T(8,128)(2,1)S(1)}) custom-call(s32[1]{0:T(128)} %bitcast.2.mask_ref, s32[8]{0:T(128)S(1)} %bitcast.165, bf16[1024,1152]{1,0:T(8,128)(2,1)S(1)} %copy-done.23, bf16[1024,1152]{1,0:T(8,128)(2,1)S(1)} %copy-done.20, bf16[1024,384]{1,0:T(8,128)(2,1)S(1)} %copy-done.1, ...), custom_call_target="tpu_custom_call" | custom-call | flops 20000000000 | bytes 8000000 | tf_op jit(solution)/shard_map/attend_backward_1/pallas_call | solution.py:249
  337.5 2.8 add_convert_fusion.3
  340.6 2.5 collective-permute-start.23
  343.0 2.9 collective-permute-start.25
  351.9 2.8 collective-permute-start.24
  356.9 17.8 %collective-permute-done.7 = bf16[512,768]{0,1:T(8,128)(2,1)} collective-permute-done((bf16[512,768]{0,1:T(8,128)(2,1)}, bf16[512,768]{0,1:T(8,128)(2,1)}, u32[]{:S(2)}, u32[]{:S(2)}) %collective-permute-start.7) | collective-permute-done | bytes 786464 | tf_op jit(solution)/shard_map/ppermute | solution.py:418
  374.6 9.6 %collective-permute-done.8 = bf16[512,768]{0,1:T(8,128)(2,1)} collective-permute-done((bf16[512,768]{0,1:T(8,128)(2,1)}, bf16[512,768]{0,1:T(8,128)(2,1)}, u32[]{:S(2)}, u32[]{:S(2)}) %collective-permute-start.8) | collective-permute-done | bytes 786464 | tf_op jit(solution)/shard_map/ppermute | solution.py:418
  384.3 3.3 maximum_select_fusion
  387.6 2.6 copy.99
  397.3 6.8 %collective-permute-done.18 = bf16[448,768]{1,0:T(8,128)(2,1)S(1)} collective-permute-done((bf16[448,768]{1,0:T(8,128)(2,1)}, bf16[448,768]{1,0:T(8,128)(2,1)S(1)}, u32[]{:S(2)}, u32[]{:S(2)}) %collective-permute-start.18) | collective-permute-done | bytes 688160 | tf_op jit(solution)/shard_map/ppermute | solution.py:356
  408.4 19.6 %attend_backward_2.1 = (bf16[1024,384]{1,0:T(8,128)(2,1)S(1)}, bf16[1024,384]{1,0:T(8,128)(2,1)S(1)}) custom-call(s32[1]{0:T(128)} %bitcast.2.mask_ref, s32[8]{0:T(128)S(1)} %bitcast.166, bf16[1024,1152]{1,0:T(8,128)(2,1)S(1)} %copy-done.24, bf16[1024,1152]{1,0:T(8,128)(2,1)S(1)} %copy-done.21, bf16[1024,384]{1,0:T(8,128)(2,1)S(1)} %copy-done.1, ...), custom_call_target="tpu_custom_call" | custom-call | flops 20000000000 | bytes 8000000 | tf_op jit(solution)/shard_map/attend_backward_2/pallas_call | solution.py:249
  429.8 3.4 fusion.38
  433.9 3.8 fusion.26
  438.0 2.4 fusion.44
  441.0 2.7 collective-permute-start.41
  446.6 4.8 collective-permute-done.41
  451.5 21.7 %collective-permute-done.42 = bf16[224,768]{1,0:T(8,128)(2,1)S(1)} collective-permute-done((bf16[224,768]{1,0:T(8,128)(2,1)S(1)}, bf16[224,768]{1,0:T(8,128)(2,1)S(1)}, u32[]{:S(2)}, u32[]{:S(2)}) %collective-permute-start.42) | collective-permute-done | bytes 344096 | tf_op jit(solution)/shard_map/ppermute | solution.py:375
  479.7 3.6 add_convert_fusion.1
  485.6 4.3 collective-permute-start.21
  495.6 3.4 collective-permute-start.32
  501.2 33.3 %collective-permute-done.31 = bf16[64,1152]{1,0:T(8,128)(2,1)S(1)} collective-permute-done((bf16[64,1152]{1,0:T(8,128)(2,1)S(1)}, bf16[64,1152]{1,0:T(8,128)(2,1)S(1)}, u32[]{:S(2)}, u32[]{:S(2)}) %collective-permute-start.31) | collective-permute-done | bytes 147488 | tf_op jit(solution)/shard_map/ppermute | solution.py:375
  537.2 2.5 collective-permute-start.35
  541.2 8.5 %collective-permute-done.35 = bf16[64,1152]{1,0:T(8,128)(2,1)S(1)} collective-permute-done((bf16[64,1152]{1,0:T(8,128)(2,1)S(1)}, bf16[64,1152]{1,0:T(8,128)(2,1)S(1)}, u32[]{:S(2)}, u32[]{:S(2)}) %collective-permute-start.35) | collective-permute-done | bytes 147488 | tf_op jit(solution)/shard_map/ppermute | solution.py:375
  549.8 3.0 collective-permute-done.36
  554.4 2.4 copy.100
  (420 shorter events, 120.4 us)
Async XLA Ops:
  7.2 61.5 %all-gather.7.cloned.1.call-start = ((), (), s32[]{:S(2)}) async-start(), calls=%async_computation | async-start | bytes 2211840 | tf_op jit(solution)/shard_map/all_gather | solution.py:436
  9.5 1.8 collective-permute-start.3
  12.2 133.1 %all-gather.9.cloned.1.call-start = ((), (), s32[]{:S(2)}) async-start(), calls=%async_computation.1 | async-start | bytes 1327104 | tf_op jit(solution)/shard_map/all_gather | solution.py:443
  13.0 137.5 %all-gather.11.cloned.1.call-start = ((), (), s32[]{:S(2)}) async-start(), calls=%async_computation.2 | async-start | bytes 5308416 | tf_op jit(solution)/shard_map/all_gather | solution.py:444
  13.7 175.7 %all-gather.13.cloned.1.call-start = ((), (), s32[]{:S(2)}) async-start(), calls=%async_computation.3 | async-start | bytes 5308416 | tf_op jit(solution)/shard_map/all_gather | solution.py:445
  17.1 27.1 %collective-permute-start = (bf16[512,768]{0,1:T(8,128)(2,1)}, bf16[512,768]{0,1:T(8,128)(2,1)}, u32[]{:S(2)}, u32[]{:S(2)}) collective-permute-start(bf16[512,768]{0,1:T(8,128)(2,1)} %bitcast.195), channel_id=1, source_target_pairs={{0,0},{1,1},{2,4},{3,5},{4,2},{5,3},{6,6},{7,7},{8,8},{9,9},{10,12... | collective-permute-start | bytes 2359304 | tf_op jit(solution)/shard_map/ppermute | solution.py:415
  21.9 39.1 %collective-permute-start.1 = (bf16[512,768]{0,1:T(8,128)(2,1)S(1)}, bf16[512,768]{0,1:T(8,128)(2,1)}, u32[]{:S(2)}, u32[]{:S(2)}) collective-permute-start(bf16[512,768]{0,1:T(8,128)(2,1)S(1)} %bitcast.194), channel_id=1, source_target_pairs={{0,1},{1,0},{2,5},{3,4},{4,3},{5,2},{6,7},{7,6},{8,9},{9,8},{10,13... | collective-permute-start | bytes 2359304 | tf_op jit(solution)/shard_map/ppermute | solution.py:415
  22.0 39.0 %collective-permute-start.2 = (s32[2,8]{1,0:T(2,128)S(1)}, s32[2,8]{1,0:T(2,128)S(1)}, u32[]{:S(2)}, u32[]{:S(2)}) collective-permute-start(s32[2,8]{1,0:T(2,128)S(1)} %bitcast.201), channel_id=1, source_target_pairs={{0,4},{4,0},{1,5},{5,1},{2,6},{6,2},{3,7},{7,3},{8,12},{12,8},{9,1... | collective-permute-start | bytes 200 | tf_op jit(solution)/shard_map/ppermute | solution.py:319
  26.6 117.9 %collective-permute-start.10 = (bf16[512,768]{0,1:T(8,128)(2,1)}, bf16[512,768]{0,1:T(8,128)(2,1)S(1)}, u32[]{:S(2)}, u32[]{:S(2)}) collective-permute-start(bf16[512,768]{0,1:T(8,128)(2,1)} %bitcast.13), channel_id=1, source_target_pairs={{0,1},{1,0},{2,5},{3,4},{4,3},{5,2},{6,7},{7,6},{8,9},{9,8},{10,13... | collective-permute-start | bytes 2359304 | tf_op jit(solution)/shard_map/ppermute | solution.py:415
  30.3 114.0 %collective-permute-start.9 = (bf16[512,768]{0,1:T(8,128)(2,1)}, bf16[512,768]{0,1:T(8,128)(2,1)S(1)}, u32[]{:S(2)}, u32[]{:S(2)}) collective-permute-start(bf16[512,768]{0,1:T(8,128)(2,1)} %bitcast.12), channel_id=1, source_target_pairs={{0,0},{1,1},{2,4},{3,5},{4,2},{5,3},{6,6},{7,7},{8,8},{9,9},{10,12... | collective-permute-start | bytes 2359304 | tf_op jit(solution)/shard_map/ppermute | solution.py:415
  44.3 19.6 %collective-permute-start.4 = (bf16[512,768]{0,1:T(8,128)(2,1)}, bf16[512,768]{0,1:T(8,128)(2,1)}, u32[]{:S(2)}, u32[]{:S(2)}) collective-permute-start(bf16[512,768]{0,1:T(8,128)(2,1)} %collective-permute-done), channel_id=1, source_target_pairs={{0,4},{4,0},{1,5},{5,1},{2,6},{6,2},{3,7},{7,3},{8,12},{12,8},{9,1... | collective-permute-start | bytes 2359304 | tf_op jit(solution)/shard_map/ppermute | solution.py:319
  61.0 5.5 collective-permute-start.5
  143.2 4.4 collective-permute-start.6
  245.4 22.7 %collective-permute-start.14 = (bf16[4,32,768]{2,1,0:T(8,128)(2,1)S(1)}, bf16[4,32,768]{2,1,0:T(8,128)(2,1)S(1)}, u32[]{:S(2)}, u32[]{:S(2)}) collective-permute-start(bf16[4,32,768]{2,1,0:T(8,128)(2,1)S(1)} %dynamic-slice_bitcast_fusion.16), channel_id=1, source_target_pairs={{0,4},{4,0},{1,5},{5,1},{2,6},{6,2},{3,7},{7,3},{8,12},{12,8},{9,1... | collective-permute-start | bytes 589832 | tf_op jit(solution)/shard_map/ppermute | solution.py:319
  245.7 17.9 %collective-permute-start.12 = (bf16[4,96,3072]{2,1,0:T(8,128)(2,1)S(1)}, bf16[4,96,3072]{2,1,0:T(8,128)(2,1)S(1)}, u32[]{:S(2)}, u32[]{:S(2)}) collective-permute-start(bf16[4,96,3072]{2,1,0:T(8,128)(2,1)S(1)} %copy-done.46), channel_id=1, source_target_pairs={{0,4},{4,0},{1,5},{5,1},{2,6},{6,2},{3,7},{7,3},{8,12},{12,8},{9,1... | collective-permute-start | bytes 7077896 | tf_op jit(solution)/shard_map/ppermute | solution.py:319
  247.9 14.0 %collective-permute-start.11 = (bf16[4,384,768]{2,1,0:T(8,128)(2,1)S(1)}, bf16[4,384,768]{2,1,0:T(8,128)(2,1)S(1)}, u32[]{:S(2)}, u32[]{:S(2)}) collective-permute-start(bf16[4,384,768]{2,1,0:T(8,128)(2,1)S(1)} %dynamic-slice_bitcast_fusion.1), channel_id=1, source_target_pairs={{0,4},{4,0},{1,5},{5,1},{2,6},{6,2},{3,7},{7,3},{8,12},{12,8},{9,1... | collective-permute-start | bytes 7077896 | tf_op jit(solution)/shard_map/ppermute | solution.py:319
  250.9 16.3 %collective-permute-start.13 = (bf16[4,96,768]{2,1,0:T(8,128)(2,1)S(1)}, bf16[4,96,768]{2,1,0:T(8,128)(2,1)S(1)}, u32[]{:S(2)}, u32[]{:S(2)}) collective-permute-start(bf16[4,96,768]{2,1,0:T(8,128)(2,1)S(1)} %dynamic-slice_bitcast_fusion.7), channel_id=1, source_target_pairs={{0,4},{4,0},{1,5},{5,1},{2,6},{6,2},{3,7},{7,3},{8,12},{12,8},{9,1... | collective-permute-start | bytes 1769480 | tf_op jit(solution)/shard_map/ppermute | solution.py:319
  253.2 31.4 %collective-permute-start.15 = (bf16[1024,384]{1,0:T(8,128)(2,1)}, bf16[1024,384]{1,0:T(8,128)(2,1)S(1)}, u32[]{:S(2)}, u32[]{:S(2)}) collective-permute-start(bf16[1024,384]{1,0:T(8,128)(2,1)} %convolution_convert_fusion.2), channel_id=1, source_target_pairs={{0,4},{4,0},{1,5},{5,1},{2,6},{6,2},{3,7},{7,3},{8,12},{12,8},{9,1... | collective-permute-start | bytes 2359304 | tf_op jit(solution)/shard_map/ppermute | solution.py:319
  274.8 31.6 %collective-permute-start.17 = (bf16[2,448,768]{2,1,0:T(8,128)(2,1)S(1)}, bf16[2,448,768]{2,1,0:T(8,128)(2,1)S(1)}, u32[]{:S(2)}, u32[]{:S(2)}) collective-permute-start(bf16[2,448,768]{2,1,0:T(8,128)(2,1)S(1)} %dynamic-slice_bitcast_fusion.3), channel_id=1, source_target_pairs={{0,16},{8,24},{16,0},{24,8},{1,17},{9,25},{17,1},{25,9},{2,18},{10... | collective-permute-start | bytes 4128776 | tf_op jit(solution)/shard_map/ppermute | solution.py:356
  276.0 38.2 %collective-permute-start.16 = (bf16[2,448,768]{2,1,0:T(8,128)(2,1)S(1)}, bf16[2,448,768]{2,1,0:T(8,128)(2,1)S(1)}, u32[]{:S(2)}, u32[]{:S(2)}) collective-permute-start(bf16[2,448,768]{2,1,0:T(8,128)(2,1)S(1)} %dynamic-slice_bitcast_fusion.4), channel_id=1, source_target_pairs={{0,8},{8,0},{16,24},{24,16},{1,9},{9,1},{17,25},{25,17},{2,10},{10... | collective-permute-start | bytes 4128776 | tf_op jit(solution)/shard_map/ppermute | solution.py:356
  340.6 10.5 %collective-permute-start.23 = (bf16[2,128,768]{2,1,0:T(8,128)(2,1)S(1)}, bf16[2,128,768]{2,1,0:T(8,128)(2,1)S(1)}, u32[]{:S(2)}, u32[]{:S(2)}) collective-permute-start(bf16[2,128,768]{2,1,0:T(8,128)(2,1)S(1)} %dynamic-slice_bitcast_fusion.9), channel_id=1, source_target_pairs={{0,8},{8,0},{16,24},{24,16},{1,9},{9,1},{17,25},{25,17},{2,10},{10... | collective-permute-start | bytes 1179656 | tf_op jit(solution)/shard_map/ppermute | solution.py:356
  343.0 11.7 %collective-permute-start.25 = (bf16[2,128,768]{2,1,0:T(8,128)(2,1)S(1)}, bf16[2,128,768]{2,1,0:T(8,128)(2,1)S(1)}, u32[]{:S(2)}, u32[]{:S(2)}) collective-permute-start(bf16[2,128,768]{2,1,0:T(8,128)(2,1)S(1)} %dynamic-slice_bitcast_fusion.8), channel_id=1, source_target_pairs={{0,16},{8,24},{16,0},{24,8},{1,17},{9,25},{17,1},{25,9},{2,18},{10... | collective-permute-start | bytes 1179656 | tf_op jit(solution)/shard_map/ppermute | solution.py:356
  347.2 27.5 %collective-permute-start.7 = (bf16[512,768]{0,1:T(8,128)(2,1)}, bf16[512,768]{0,1:T(8,128)(2,1)}, u32[]{:S(2)}, u32[]{:S(2)}) collective-permute-start(bf16[512,768]{0,1:T(8,128)(2,1)} %get-tuple-element.162), channel_id=1, source_target_pairs={{0,0},{1,1},{4,2},{5,3},{2,4},{3,5},{6,6},{7,7},{8,8},{9,9},{12,10... | collective-permute-start | bytes 2359304 | tf_op jit(solution)/shard_map/ppermute | solution.py:418
  349.5 34.8 %collective-permute-start.8 = (bf16[512,768]{0,1:T(8,128)(2,1)}, bf16[512,768]{0,1:T(8,128)(2,1)}, u32[]{:S(2)}, u32[]{:S(2)}) collective-permute-start(bf16[512,768]{0,1:T(8,128)(2,1)} %get-tuple-element.163), channel_id=1, source_target_pairs={{1,0},{0,1},{5,2},{4,3},{3,4},{2,5},{7,6},{6,7},{9,8},{8,9},{13,10... | collective-permute-start | bytes 2359304 | tf_op jit(solution)/shard_map/ppermute | solution.py:418
  349.6 46.1 %collective-permute-start.19 = (bf16[448,768]{1,0:T(8,128)(2,1)}, bf16[448,768]{1,0:T(8,128)(2,1)}, u32[]{:S(2)}, u32[]{:S(2)}) collective-permute-start(bf16[448,768]{1,0:T(8,128)(2,1)} %dynamic-slice_bitcast_fusion.5), channel_id=1, source_target_pairs={{0,8},{8,0},{16,24},{24,16},{1,9},{9,1},{17,25},{25,17},{2,10},{10... | collective-permute-start | bytes 2064392 | tf_op jit(solution)/shard_map/ppermute | solution.py:356
  351.9 40.0 %collective-permute-start.24 = (bf16[128,768]{1,0:T(8,128)(2,1)}, bf16[128,768]{1,0:T(8,128)(2,1)}, u32[]{:S(2)}, u32[]{:S(2)}) collective-permute-start(bf16[128,768]{1,0:T(8,128)(2,1)} %dynamic-slice_bitcast_fusion.15), channel_id=1, source_target_pairs={{0,16},{8,24},{16,0},{24,8},{1,17},{9,25},{17,1},{25,9},{2,18},{10... | collective-permute-start | bytes 589832 | tf_op jit(solution)/shard_map/ppermute | solution.py:356
  355.7 36.3 %collective-permute-start.26 = (bf16[128,768]{1,0:T(8,128)(2,1)}, bf16[128,768]{1,0:T(8,128)(2,1)}, u32[]{:S(2)}, u32[]{:S(2)}) collective-permute-start(bf16[128,768]{1,0:T(8,128)(2,1)} %dynamic-slice_bitcast_fusion.14), channel_id=1, source_target_pairs={{0,8},{8,0},{16,24},{24,16},{1,9},{9,1},{17,25},{25,17},{2,10},{10... | collective-permute-start | bytes 589832 | tf_op jit(solution)/shard_map/ppermute | solution.py:356
  390.2 14.0 %collective-permute-start.18 = (bf16[448,768]{1,0:T(8,128)(2,1)}, bf16[448,768]{1,0:T(8,128)(2,1)S(1)}, u32[]{:S(2)}, u32[]{:S(2)}) collective-permute-start(bf16[448,768]{1,0:T(8,128)(2,1)} %dynamic-slice_bitcast_fusion.6), channel_id=1, source_target_pairs={{0,16},{8,24},{16,0},{24,8},{1,17},{9,25},{17,1},{25,9},{2,18},{10... | collective-permute-start | bytes 2064392 | tf_op jit(solution)/shard_map/ppermute | solution.py:356
  406.8 33.6 %collective-permute-start.38 = (bf16[224,768]{1,0:T(8,128)(2,1)S(1)}, bf16[224,768]{1,0:T(8,128)(2,1)S(1)}, u32[]{:S(2)}, u32[]{:S(2)}) collective-permute-start(bf16[224,768]{1,0:T(8,128)(2,1)S(1)} %get-tuple-element.172), channel_id=1, source_target_pairs={{0,1},{1,2},{2,3},{3,0},{4,5},{5,6},{6,7},{7,4},{8,9},{9,10},{10,1... | collective-permute-start | bytes 1032200 | tf_op jit(solution)/shard_map/ppermute | solution.py:375
  406.9 33.5 %collective-permute-start.39 = (bf16[224,768]{1,0:T(8,128)(2,1)S(1)}, bf16[224,768]{1,0:T(8,128)(2,1)S(1)}, u32[]{:S(2)}, u32[]{:S(2)}) collective-permute-start(bf16[224,768]{1,0:T(8,128)(2,1)S(1)} %get-tuple-element.173), channel_id=1, source_target_pairs={{0,2},{1,3},{2,0},{3,1},{4,6},{5,7},{6,4},{7,5},{8,10},{9,11},{10,... | collective-permute-start | bytes 1032200 | tf_op jit(solution)/shard_map/ppermute | solution.py:375
  407.0 33.4 %collective-permute-start.40 = (bf16[224,768]{1,0:T(8,128)(2,1)S(1)}, bf16[224,768]{1,0:T(8,128)(2,1)S(1)}, u32[]{:S(2)}, u32[]{:S(2)}) collective-permute-start(bf16[224,768]{1,0:T(8,128)(2,1)S(1)} %get-tuple-element.171), channel_id=1, source_target_pairs={{0,3},{1,0},{2,1},{3,2},{4,7},{5,4},{6,5},{7,6},{8,11},{9,8},{10,9... | collective-permute-start | bytes 1032200 | tf_op jit(solution)/shard_map/ppermute | solution.py:375
  433.1 46.5 %collective-permute-start.20 = (bf16[1024,768]{0,1:T(8,128)(2,1)}, bf16[1024,768]{0,1:T(8,128)(2,1)}, u32[]{:S(2)}, u32[]{:S(2)}) collective-permute-start(bf16[1024,768]{0,1:T(8,128)(2,1)} %fusion.38), channel_id=1, source_target_pairs={{0,4},{4,0},{1,5},{5,1},{2,6},{6,2},{3,7},{7,3},{8,12},{12,8},{9,1... | collective-permute-start | bytes 4718600 | tf_op jit(solution)/shard_map/ppermute | solution.py:319
  441.0 10.5 %collective-permute-start.41 = (bf16[224,768]{1,0:T(8,128)(2,1)S(1)}, bf16[224,768]{1,0:T(8,128)(2,1)S(1)}, u32[]{:S(2)}, u32[]{:S(2)}) collective-permute-start(bf16[224,768]{1,0:T(8,128)(2,1)S(1)} %get-tuple-element.146), channel_id=1, source_target_pairs={{0,1},{1,2},{2,3},{3,0},{4,5},{5,6},{6,7},{7,4},{8,9},{9,10},{10,1... | collective-permute-start | bytes 1032200 | tf_op jit(solution)/shard_map/ppermute | solution.py:375
  443.7 29.5 %collective-permute-start.42 = (bf16[224,768]{1,0:T(8,128)(2,1)S(1)}, bf16[224,768]{1,0:T(8,128)(2,1)S(1)}, u32[]{:S(2)}, u32[]{:S(2)}) collective-permute-start(bf16[224,768]{1,0:T(8,128)(2,1)S(1)} %get-tuple-element.146), channel_id=1, source_target_pairs={{0,2},{1,3},{2,0},{3,1},{4,6},{5,7},{6,4},{7,5},{8,10},{9,11},{10,... | collective-permute-start | bytes 1032200 | tf_op jit(solution)/shard_map/ppermute | solution.py:375
  445.4 29.0 %collective-permute-start.43 = (bf16[224,768]{1,0:T(8,128)(2,1)S(1)}, bf16[224,768]{1,0:T(8,128)(2,1)S(1)}, u32[]{:S(2)}, u32[]{:S(2)}) collective-permute-start(bf16[224,768]{1,0:T(8,128)(2,1)S(1)} %get-tuple-element.146), channel_id=1, source_target_pairs={{0,3},{1,0},{2,1},{3,2},{4,7},{5,4},{6,5},{7,6},{8,11},{9,8},{10,9... | collective-permute-start | bytes 1032200 | tf_op jit(solution)/shard_map/ppermute | solution.py:375
  483.4 6.5 %collective-permute-start.27 = (bf16[2,128,384]{2,1,0:T(8,128)(2,1)S(1)}, bf16[2,128,384]{2,1,0:T(8,128)(2,1)S(1)}, u32[]{:S(2)}, u32[]{:S(2)}) collective-permute-start(bf16[2,128,384]{2,1,0:T(8,128)(2,1)S(1)} %dynamic-slice_bitcast_fusion.13), channel_id=1, source_target_pairs={{0,8},{8,0},{16,24},{24,16},{1,9},{9,1},{17,25},{25,17},{2,10},{10... | collective-permute-start | bytes 589832 | tf_op jit(solution)/shard_map/ppermute | solution.py:356
  484.8 6.6 %collective-permute-start.29 = (bf16[2,128,384]{2,1,0:T(8,128)(2,1)S(1)}, bf16[2,128,384]{2,1,0:T(8,128)(2,1)S(1)}, u32[]{:S(2)}, u32[]{:S(2)}) collective-permute-start(bf16[2,128,384]{2,1,0:T(8,128)(2,1)S(1)} %dynamic-slice_bitcast_fusion.12), channel_id=1, source_target_pairs={{0,16},{8,24},{16,0},{24,8},{1,17},{9,25},{17,1},{25,9},{2,18},{10... | collective-permute-start | bytes 589832 | tf_op jit(solution)/shard_map/ppermute | solution.py:356
  485.6 49.0 %collective-permute-start.21 = (bf16[512,768]{0,1:T(8,128)(2,1)S(1)}, bf16[512,768]{0,1:T(8,128)(2,1)S(1)}, u32[]{:S(2)}, u32[]{:S(2)}) collective-permute-start(bf16[512,768]{0,1:T(8,128)(2,1)S(1)} %get-tuple-element.158), channel_id=1, source_target_pairs={{0,0},{1,1},{4,2},{5,3},{2,4},{3,5},{6,6},{7,7},{8,8},{9,9},{12,10... | collective-permute-start | bytes 2359304 | tf_op jit(solution)/shard_map/ppermute | solution.py:551
  489.9 44.6 %collective-permute-start.22 = (bf16[512,768]{0,1:T(8,128)(2,1)S(1)}, bf16[512,768]{0,1:T(8,128)(2,1)S(1)}, u32[]{:S(2)}, u32[]{:S(2)}) collective-permute-start(bf16[512,768]{0,1:T(8,128)(2,1)S(1)} %get-tuple-element.159), channel_id=1, source_target_pairs={{1,0},{0,1},{5,2},{4,3},{3,4},{2,5},{7,6},{6,7},{9,8},{8,9},{13,10... | collective-permute-start | bytes 2359304 | tf_op jit(solution)/shard_map/ppermute | solution.py:551
  490.1 3.8 collective-permute-start.28
  491.5 3.8 collective-permute-start.30
  495.5 39.0 %collective-permute-start.31 = (bf16[64,1152]{1,0:T(8,128)(2,1)S(1)}, bf16[64,1152]{1,0:T(8,128)(2,1)S(1)}, u32[]{:S(2)}, u32[]{:S(2)}) collective-permute-start(bf16[64,1152]{1,0:T(8,128)(2,1)S(1)} %get-tuple-element.180), channel_id=1, source_target_pairs={{0,1},{1,2},{2,3},{3,0},{4,5},{5,6},{6,7},{7,4},{8,9},{9,10},{10,1... | collective-permute-start | bytes 442376 | tf_op jit(solution)/shard_map/ppermute | solution.py:375
  495.6 40.5 %collective-permute-start.32 = (bf16[64,1152]{1,0:T(8,128)(2,1)S(1)}, bf16[64,1152]{1,0:T(8,128)(2,1)S(1)}, u32[]{:S(2)}, u32[]{:S(2)}) collective-permute-start(bf16[64,1152]{1,0:T(8,128)(2,1)S(1)} %get-tuple-element.182), channel_id=1, source_target_pairs={{0,2},{1,3},{2,0},{3,1},{4,6},{5,7},{6,4},{7,5},{8,10},{9,11},{10,... | collective-permute-start | bytes 442376 | tf_op jit(solution)/shard_map/ppermute | solution.py:375
  499.1 37.0 %collective-permute-start.33 = (bf16[64,1152]{1,0:T(8,128)(2,1)S(1)}, bf16[64,1152]{1,0:T(8,128)(2,1)S(1)}, u32[]{:S(2)}, u32[]{:S(2)}) collective-permute-start(bf16[64,1152]{1,0:T(8,128)(2,1)S(1)} %get-tuple-element.181), channel_id=1, source_target_pairs={{0,3},{1,0},{2,1},{3,2},{4,7},{5,4},{6,5},{7,6},{8,11},{9,8},{10,9... | collective-permute-start | bytes 442376 | tf_op jit(solution)/shard_map/ppermute | solution.py:375
  536.2 5.0 collective-permute-start.34
  537.2 12.5 %collective-permute-start.35 = (bf16[64,1152]{1,0:T(8,128)(2,1)S(1)}, bf16[64,1152]{1,0:T(8,128)(2,1)S(1)}, u32[]{:S(2)}, u32[]{:S(2)}) collective-permute-start(bf16[64,1152]{1,0:T(8,128)(2,1)S(1)} %get-tuple-element.148), channel_id=1, source_target_pairs={{0,2},{1,3},{2,0},{3,1},{4,6},{5,7},{6,4},{7,5},{8,10},{9,11},{10,... | collective-permute-start | bytes 442376 | tf_op jit(solution)/shard_map/ppermute | solution.py:375
  539.8 13.0 %collective-permute-start.36 = (bf16[64,1152]{1,0:T(8,128)(2,1)S(1)}, bf16[64,1152]{1,0:T(8,128)(2,1)S(1)}, u32[]{:S(2)}, u32[]{:S(2)}) collective-permute-start(bf16[64,1152]{1,0:T(8,128)(2,1)S(1)} %get-tuple-element.148), channel_id=1, source_target_pairs={{0,3},{1,0},{2,1},{3,2},{4,7},{5,4},{6,5},{7,6},{8,11},{9,8},{10,9... | collective-permute-start | bytes 442376 | tf_op jit(solution)/shard_map/ppermute | solution.py:375
  553.7 4.3 collective-permute-start.37
  (79 other events, 964.4 us)
Sparse Core Ops, SparseCore 0:
  12.4 33.3 all-gather.6
  47.7 24.3 all-gather.8
  74.0 38.7 all-gather.10
  143.9 45.5 all-gather.12

commit v4 on v3

--- a/solution.py
+++ b/solution.py
@@ -161,7 +161,7 @@
             pltpu.SemaphoreType.DMA((pairs, pieces)),
         ],
         compiler_params=pltpu.CompilerParams(vmem_limit_bytes=40 << 20),
-        cost_estimate=pl.CostEstimate(flops=50_000_000_000, bytes_accessed=8_000_000, transcendentals=0),
+        cost_estimate=pl.CostEstimate(flops=1_000_000_000, bytes_accessed=1_000_000, transcendentals=0),
         name="attend_forward",
     )(mask, ends, own, sib, seg_col, seg_row)
 
@@ -266,7 +266,7 @@
             pltpu.SemaphoreType.DMA((3, pieces)),
         ],
         compiler_params=pltpu.CompilerParams(vmem_limit_bytes=24 << 20),
-        cost_estimate=pl.CostEstimate(flops=20_000_000_000, bytes_accessed=8_000_000, transcendentals=0),
+        cost_estimate=pl.CostEstimate(flops=1_000_000_000, bytes_accessed=1_000_000, transcendentals=0),
         name=f"attend_backward_{pair}",
     )(mask, ends, own, sib, ctx_own, ctx_sib, dctx_own, dctx_sib, seg_col, seg_row, lse)
 
@@ -291,10 +291,147 @@
     )
 
 
-def gelu_slope(pre):
-    cdf = 0.5 * (1.0 + lax.erf(pre * (1.0 / math.sqrt(2.0))))
-    density = jnp.exp(-0.5 * pre * pre) * (1.0 / math.sqrt(2.0 * math.pi))
-    return cdf + pre * density
+ROWS = 256
+CHUNK = 768
+
+
+def fold(x):
+    return jnp.sum(x.reshape(-1, 8, x.shape[1]), axis=0)
+
+
+def middle_kernel(
+    core_ref, x_ref, near_ref, far_ref, cot_ref, vec_ref, in_bias_ref, w_out, w_in, w_down,
+    result_ref, low_ref, act_ref, grad_down_ref, grad_pre_ref, grad_one_ref, grad_attn_ref, dnear_ref, dfar_ref,
+    sums_ref, in_sums_ref, wo, wi, wd, slope, acc, sums, in_sums, sems
+):
+    f32, bf16 = jnp.float32, jnp.bfloat16
+    mine = near_ref.shape[1]
+    chunks = w_in.shape[1] // CHUNK
+    step = pl.program_id(0)
+    core = core_ref[0]
+    copies = []
+    for place in range(2):
+        which = core if place == 0 else 1 - core
+        rows = pl.multiple_of(which * mine, mine)
+        copies.append(pltpu.make_async_copy(w_out.at[pl.ds(rows, mine), :], wo.at[pl.ds(place * mine, mine), :], sems.at[place]))
+    for chunk in range(chunks):
+        columns = pl.ds(chunk * CHUNK, CHUNK)
+        copies.append(pltpu.make_async_copy(w_in.at[:, columns], wi.at[chunk], sems.at[2 + chunk]))
+    for chunk in range(chunks):
+        columns = pl.ds(chunk * CHUNK, CHUNK)
+        copies.append(pltpu.make_async_copy(w_down.at[columns, :], wd.at[chunk], sems.at[2 + chunks + chunk]))
+
+    @pl.when(step == 0)
+    def _():
+        for copy in copies:
+            copy.start()
+        sums[...] = jnp.zeros_like(sums)
+        in_sums[...] = jnp.zeros_like(in_sums)
+        for copy in copies[:2]:
+            copy.wait()
+
+    bias_out, gain_one, shift_one, bias_down, gain_two, shift_two = [vec_ref[i : i + 1, :] for i in range(6)]
+    near, far = near_ref[...], far_ref[...]
+    attn = mm(near, wo[:mine], NN) + mm(far, wo[mine:], NN) + bias_out
+    hidden, normed_one, inv_one = norm_forward(x_ref[...].astype(f32) + attn, gain_one, shift_one)
+    low_ref[...] = hidden.astype(bf16)
+    acc[...] = hidden + bias_down
+
+    @pl.when(step == 0)
+    def _():
+        for copy in copies[2:]:
+            copy.wait()
+
+    @pl.loop(0, chunks)
+    def _(chunk):
+        columns = pl.ds(pl.multiple_of(chunk * CHUNK, CHUNK), CHUNK)
+        pre = mm(low_ref[...], wi[chunk], NN) + in_bias_ref[:, columns]
+        cdf = 0.5 * (1.0 + lax.erf(pre * (1.0 / math.sqrt(2.0))))
+        density = jnp.exp(-0.5 * pre * pre) * (1.0 / math.sqrt(2.0 * math.pi))
+        act = (pre * cdf).astype(bf16)
+        act_ref[:, columns] = act
+        slope[:, columns] = cdf + pre * density
+        acc[...] += mm(act, wd[chunk], NN)
+
+    result, normed_two, inv_two = norm_forward(acc[...], gain_two, shift_two)
+    result_ref[...] = result.astype(bf16)
+    dy = cot_ref[...].astype(f32)
+    grad_two = norm_backward(dy, normed_two, inv_two, gain_two)
+    grad_down = grad_two.astype(bf16)
+    grad_down_ref[...] = grad_down
+    sums[3] += fold(grad_down.astype(f32))
+    sums[4] += fold(dy * normed_two)
+    sums[5] += fold(dy)
+    acc[...] = grad_two
+
+    @pl.loop(0, chunks)
+    def _(chunk):
+        columns = pl.ds(pl.multiple_of(chunk * CHUNK, CHUNK), CHUNK)
+        grad_pre = (mm(grad_down_ref[...], wd[chunk], NT) * slope[:, columns]).astype(bf16)
+        grad_pre_ref[:, columns] = grad_pre
+        in_sums[:, columns] += fold(grad_pre.astype(f32))
+        acc[...] += mm(grad_pre, wi[chunk], NT)
+
+    grad_hidden = acc[...]
+    sums[1] += fold(grad_hidden * normed_one)
+    sums[2] += fold(grad_hidden)
+    grad_one = norm_backward(grad_hidden, normed_one, inv_one, gain_one)
+    grad_one_ref[...] = grad_one
+    grad_attn = grad_one.astype(bf16)
+    grad_attn_ref[...] = grad_attn
+    sums[0] += fold(grad_attn.astype(f32))
+    dnear_ref[...] = mm(grad_attn, wo[:mine], NT).astype(bf16)
+    dfar_ref[...] = mm(grad_attn, wo[mine:], NT).astype(bf16)
+
+    @pl.when(step == pl.num_programs(0) - 1)
+    def _():
+        sums_ref[...] = jnp.zeros_like(sums_ref)
+        for i in range(6):
+            sums_ref[i : i + 1, :] = jnp.sum(sums[i], axis=0, keepdims=True)
+        in_sums_ref[...] = jnp.sum(in_sums[...], axis=0, keepdims=True)
+
+
+def middle(core, x, near, far, cot, vec, in_bias, w_out, w_in, w_down):
+    count, width = x.shape
+    hidden = w_in.shape[1]
+    mine = near.shape[1]
+    chunks = hidden // CHUNK
+    f32, bf16 = jnp.float32, jnp.bfloat16
+    any_spec = pl.BlockSpec(memory_space=pl.ANY)
+    block = lambda columns: pl.BlockSpec((ROWS, columns), lambda i: (i, 0))
+    whole = lambda rows, columns: pl.BlockSpec((rows, columns), lambda i: (0, 0))
+    shape = jax.ShapeDtypeStruct
+    return pl.pallas_call(
+        middle_kernel,
+        grid=(count // ROWS,),
+        out_shape=(
+            shape((count, width), bf16), shape((count, width), bf16), shape((count, hidden), bf16),
+            shape((count, width), bf16), shape((count, hidden), bf16), shape((count, width), f32),
+            shape((count, width), bf16), shape((count, mine), bf16), shape((count, mine), bf16),
+            shape((8, width), f32), shape((1, hidden), f32),
+        ),
+        in_specs=[
+            pl.BlockSpec(memory_space=pltpu.SMEM), block(width), block(mine), block(mine), block(width),
+            whole(8, width), whole(1, hidden), any_spec, any_spec, any_spec,
+        ],
+        out_specs=(
+            block(width), block(width), block(hidden), block(width), block(hidden), block(width), block(width),
+            block(mine), block(mine), whole(8, width), whole(1, hidden),
+        ),
+        scratch_shapes=[
+            pltpu.VMEM((width, width), bf16),
+            pltpu.VMEM((chunks, width, CHUNK), bf16),
+            pltpu.VMEM((chunks, CHUNK, width), bf16),
+            pltpu.VMEM((ROWS, hidden), f32),
+            pltpu.VMEM((ROWS, width), f32),
+            pltpu.VMEM((6, 8, width), f32),
+            pltpu.VMEM((8, hidden), f32),
+            pltpu.SemaphoreType.DMA((2 + 2 * chunks,)),
+        ],
+        compiler_params=pltpu.CompilerParams(vmem_limit_bytes=48 << 20),
+        cost_estimate=pl.CostEstimate(flops=20_000_000_000, bytes_accessed=30_000_000, transcendentals=0),
+        name="middle",
+    )(core, x, near, far, cot, vec, in_bias, w_out, w_in, w_down)
 
 
 def doc_ids(ends, count):
@@ -414,10 +551,6 @@
         halves = [lax.dynamic_index_in_dim(x[0], which, 0, keepdims=False) for which in (odd, 1 - odd)]
         return [lax.ppermute(h, ("core", "seq"), r) for h, r in zip(halves, (first, second))]
 
-    def collect(x):
-        got = [lax.ppermute(x[i * run : (i + 1) * run], ("core", "seq"), back[i]) for i in range(2)]
-        return jnp.where(odd == 0, jnp.stack(got), jnp.stack(got[::-1]))[None]
-
     pieces = spread(tokens)
     lengths = jnp.stack([doc_lengths[0], swap(doc_lengths[0])])
     z = lax.axis_index("seq")
@@ -434,12 +567,14 @@
     kept = pick(own_columns, core)
     w_mine = either(core, kept, swap(pick(own_columns, 1 - core)), 0)
     w_mine = lax.all_gather(w_mine, "xy", axis=0, tiled=True)
-    small = [q_bias, v_bias, out_bias, norm1_gain, norm1_bias, ff_out_bias, norm2_gain, norm2_bias, ff_in_bias]
-    vectors = lax.all_gather(jnp.concatenate(small)[None, None], fsdp, axis=0, tiled=True)[:, 0].astype(f32)
-    bias_q, bias_v, bias_out, gain_one, shift_one, bias_down, gain_two, shift_two = [
-        vectors[:, i * rows : (i + 1) * rows].reshape(width) for i in range(8)
-    ]
-    bias_in = vectors[:, 8 * rows :].reshape(-1)
+    small = [q_bias, v_bias, out_bias, norm1_gain, norm1_bias, ff_out_bias, norm2_gain, norm2_bias]
+    inner = ff_in_bias.shape[0] // rows
+    small = jnp.concatenate([jnp.stack(small), ff_in_bias.reshape(inner, rows)])
+    vectors = lax.all_gather(small, fsdp, axis=0, tiled=False).astype(f32)
+    bias_in = vectors[:, 8:].reshape(1, -1)
+    vectors = jnp.moveaxis(vectors[:, :8], 0, 1).reshape(8, width)
+    bias_q, bias_v = vectors[0], vectors[1]
+    norms = jnp.concatenate([vectors[2:], jnp.zeros((2, width), f32)])
     w_out = lax.all_gather(out_weight, fsdp, axis=0, tiled=True)
     w_in = lax.all_gather(ff_in_weight, fsdp, axis=0, tiled=True)
     w_down = lax.all_gather(ff_out_weight, fsdp, axis=0, tiled=True)
@@ -448,58 +583,35 @@
     one = jnp.ones((pairs, LANES), f32)
     bias_mine = jnp.stack([own_slice(bias_q), 0.0 * one, own_slice(bias_v)], axis=1).reshape(-1)
     scale = jnp.stack([HEAD_DIM**-0.5 * one, one, one], axis=1).reshape(-1)
-    x_own = jnp.concatenate(pieces)
+    x_own = after(jnp.concatenate(pieces), norms, bias_in)
     x_sib = jnp.concatenate([swap(p) for p in pieces])
     projected = [((mm(x, w_mine, NN) + bias_mine) * scale).astype(bf16) for x in (x_own, x_sib)]
     ctx_own, ctx_sib, lse = attend_forward(mask, ends, *projected, seg_col, seg_row, run)
     ctx_far = swap(ctx_sib)
 
-    wo_own = lax.dynamic_slice_in_dim(w_out, core * mine, mine, 0)
-    wo_far = lax.dynamic_slice_in_dim(w_out, (1 - core) * mine, mine, 0)
-    attn = mm(ctx_own, wo_own, NN) + mm(ctx_far, wo_far, NN) + bias_out
-    hidden, normed_one, inv_one = norm_forward(x_own.astype(f32) + attn, gain_one, shift_one)
-    hidden_low = hidden.astype(bf16)
-    pre = mm(hidden_low, w_in, NN) + bias_in
-    act_low = jax.nn.gelu(pre, approximate=False).astype(bf16)
-    resid_two = hidden + mm(act_low, w_down, NN) + bias_down
-    result, normed_two, inv_two = norm_forward(resid_two, gain_two, shift_two)
-    output = collect(result.astype(bf16))
-
-    grad_out = jnp.concatenate(spread(out_cotangent)).astype(f32)
-    gain_two_grad = jnp.sum(grad_out * normed_two, axis=0)
-    shift_two_grad = jnp.sum(grad_out, axis=0)
-    grad_two = norm_backward(grad_out, normed_two, inv_two, gain_two)
-    grad_down = grad_two.astype(bf16)
+    cot = jnp.concatenate(spread(out_cotangent))
+    result, hidden_low, act_low, grad_down, grad_pre, grad_one, grad_attn, dctx_own, dctx_far, sums, in_sums = middle(
+        core.astype(jnp.int32)[None], x_own, ctx_own, ctx_far, cot, norms, bias_in, w_out, w_in, w_down
+    )
+    dctx_far = swap(dctx_far)
+    output = [lax.ppermute(result[i * run : (i + 1) * run], ("core", "seq"), back[i]) for i in range(2)]
 
     def cores(blocks):
         return pick(blocks, core, 1), swap(pick(blocks, 1 - core, 1))
 
     down_grad = cores(mm(act_low, grad_down, TN).astype(bf16).reshape(planes, CORES, -1, width))
-    down_bias_grad = jnp.sum(grad_down.astype(f32), axis=0)
-    grad_pre = (mm(grad_down, w_down, NT) * gelu_slope(pre)).astype(bf16)
     in_grad = cores(mm(hidden_low, grad_pre, TN).astype(bf16).reshape(planes, CORES, rows, -1))
-    in_bias_grad = jnp.sum(grad_pre.astype(f32), axis=0)
-    grad_hidden = grad_two + mm(grad_pre, w_in, NT)
-    gain_one_grad = jnp.sum(grad_hidden * normed_one, axis=0)
-    shift_one_grad = jnp.sum(grad_hidden, axis=0)
-    grad_one = norm_backward(grad_hidden, normed_one, inv_one, gain_one)
-    grad_attn = grad_one.astype(bf16)
-    dctx_far = swap(mm(grad_attn, wo_far, NT).astype(bf16))
-    dctx_own = mm(grad_attn, wo_own, NT).astype(bf16)
-    out_bias_grad = jnp.sum(grad_attn.astype(f32), axis=0)
     out_grad = [mm(c, grad_attn, TN).astype(bf16) for c in (ctx_own, ctx_far)]
     out_grad = cores(either(core, *out_grad, 0).reshape(planes, CORES, rows, width))
-    small = [out_bias_grad, gain_one_grad, shift_one_grad, down_bias_grad, gain_two_grad, shift_two_grad, in_bias_grad]
-    vector = jnp.concatenate([v.reshape(shards, -1) for v in small], axis=1).astype(bf16)
-    lines = -(-vector.shape[1] // width)
-    vector = jnp.pad(vector, ((0, 0), (0, lines * width - vector.shape[1])))
-    vector = jnp.pad(vector.reshape(shards, lines, width), ((0, 0), (0, 32 - lines), (0, 0)))
+    vector = [jnp.moveaxis(sums[:6].reshape(6, shards, rows), 1, 0), in_sums.reshape(shards, inner, rows)]
+    vector = jnp.concatenate(vector, axis=1).astype(bf16)
+    vector = jnp.pad(vector, ((0, 0), (0, 32 - vector.shape[1]), (0, width - rows)))
     vector = cores(vector.reshape(planes, CORES, 32, width))
-    inner = in_grad[0].shape[2] // width
+    inner_blocks = in_grad[0].shape[2] // width
     joined = []
     for which in range(2):
         wide = in_grad[which]
-        wide = [wide[:, :, i * width : (i + 1) * width] for i in range(inner)]
+        wide = [wide[:, :, i * width : (i + 1) * width] for i in range(inner_blocks)]
         joined.append(jnp.concatenate([down_grad[which]] + wide + [out_grad[which], vector[which]], axis=1))
     early = Halving(total(*joined), planes)
     early.send(0)
@@ -538,7 +650,7 @@
             first_sums = Halving(weight_sums(grads), planes)
             first_sums.send(0)
             sent = sent + first_sums.sent
-        grads.append(attend(pair, *sent))
+        grads.append(attend(pair, *sent, *(output if pair == 1 else ())))
     while len(progress) == 1:
         advance(grads[-1][0])
     early_sum = progress[1]
@@ -564,14 +676,14 @@
 
     down_rows = down_grad[0].shape[1]
     down_final = early_total[:down_rows].astype(f32)
-    wide = [early_total[down_rows + i * rows : down_rows + (i + 1) * rows] for i in range(inner)]
+    wide = [early_total[down_rows + i * rows : down_rows + (i + 1) * rows] for i in range(inner_blocks)]
     in_final = jnp.concatenate(wide, axis=1).astype(f32)
-    at = down_rows + inner * rows
+    at = down_rows + inner_blocks * rows
     out_final = early_total[at : at + rows].astype(f32)
     at = at + rows
-    line = early_total[at : at + lines].reshape(-1).astype(f32)
-    out_bias_final, g1, b1, down_bias_final, g2, b2 = [line[i * rows : (i + 1) * rows] for i in range(6)]
-    in_bias_final = line[6 * rows : 6 * rows + ff_in_bias.shape[0]]
+    line = early_total[at : at + 32, :rows].astype(f32)
+    out_bias_final, g1, b1, down_bias_final, g2, b2 = [line[i] for i in range(6)]
+    in_bias_final = line[6 : 6 + inner].reshape(-1)
 
     part = qkv_total
     column = part[CORES * rows]
@@ -583,6 +695,7 @@
     shard = lax.axis_index("xy") * CORES + core
     q_final = lax.dynamic_slice_in_dim(sums[0], shard * rows, rows, 0).astype(f32)
     v_final = lax.dynamic_slice_in_dim(sums[2], shard * rows, rows, 0).astype(f32)
+    output = jnp.where(odd == 0, jnp.stack(output), jnp.stack(output[::-1]))[None]
     return (
         output, input_grad, qkv_final, q_final, v_final, out_final, out_bias_final, g1, b1, in_final,
         in_bias_final, down_final, down_bias_final, g2, b2,

time: 581 us -> 530 us (0.912)
  matrix products: 112 us -> 42.2 us
  Pallas kernels: 126 us -> 178 us
  starting transfers between devices: 64.1 us -> 42.8 us
  other arithmetic: 43 us -> 36.3 us
  local copies, waits for them, and re-layouts: 60.1 us -> 53.9 us
    dot_general x20 -> x12, matrix products: 112 us -> 42.2 us  [mm(): lax.dot_general(left, right, dims, preferred_element_type=jnp.float32)]
    pallas_call x0 -> x1, Pallas kernels: none -> 47.9 us  [middle(): pl.pallas_call(middle_kernel, grid=(count // ROWS,), out_shape=(shape((co...]
    ppermute x2, waiting for transfers between devices: 27.4 us -> 0.01 us  [per_device(): lax.ppermute(result[i * run:(i + 1) * run], ('core', 'seq'), back[i])]
    ppermute x12, starting transfers between devices: 25.4 us -> 7.54 us  [send(): lax.ppermute(out, 'xy', [(i, i ^ 1 << bit) for i in range(self.planes)])]
    ppermute x4, waiting for transfers between devices: 17.3 us -> 30.4 us  [spread(): lax.ppermute(h, ('core', 'seq'), r)]
    pallas_call x3, Pallas kernels: 58.9 us -> 69.5 us  [attend_backward(): pl.pallas_call(functools.partial(backward_kernel, run, pair), out_shape=(...]
    reduce_sum x8 -> x0, other arithmetic: 9.27 us -> none  [the longest x1 4.23 us: per_device(): out_bias_grad = jnp.sum(grad_attn.astype(f32), axis=0)]
    pallas_call x1, Pallas kernels: 66.7 us -> 60.3 us  [attend_forward(): pl.pallas_call(functools.partial(forward_kernel, run), out_shape=(jax.Sha...]
  transfers between devices with their start and end apart: 48 -> 48, of which waited for: 19 -> 16; matrix products, arithmetic and copies ran while one was open for 23% -> 13% of each run, Pallas kernels for 19% -> 20%
where the time goes in v4:
time: 530 us; the launch traced here: 523 us
  Pallas kernels  178 us (34%)
  waiting for transfers between devices  140 us (26%)
  local copies, waits for them, and re-layouts  53.9 us (10%)
  starting transfers between devices  42.8 us (8%)
  matrix products  42.2 us (8%)
  other arithmetic  36.3 us (7%)
  between operations  15.8 us (3%)
  blocking collectives  13.9 us (3%)
    ppermute x12, waiting for transfers between devices, shift(): lax.ppermute(value, 'seq', [(i, (i + distance) % self.nseq) for i in rang...  76.9 us
    pallas_call x3, Pallas kernels, attend_backward(): pl.pallas_call(functools.partial(backward_kernel, run, pair), out_shape=(...  69.5 us
    pallas_call x1, Pallas kernels, attend_forward(): pl.pallas_call(functools.partial(forward_kernel, run), out_shape=(jax.Sha...  60.3 us
    pallas_call x1, Pallas kernels, middle(): pl.pallas_call(middle_kernel, grid=(count // ROWS,), out_shape=(shape((co...  47.9 us
    dot_general x12, matrix products, mm(): lax.dot_general(left, right, dims, preferred_element_type=jnp.float32)  42.2 us
    ppermute x4, waiting for transfers between devices, spread(): lax.ppermute(h, ('core', 'seq'), r)  30.4 us
    unnamed x147, local copies, waits for them, and re-layouts  25.6 us
    ppermute x12, waiting for transfers between devices, send(): lax.ppermute(out, 'xy', [(i, i ^ 1 << bit) for i in range(self.planes)])  23.3 us
  transfers between devices with their start and end apart: 48, of which 16 were waited for; matrix products, arithmetic and copies ran while one was open for 13% of the time, Pallas kernels for 20%

profile of v4, /device:TPU:9, one launch (start us, length us, event | category | flops | bytes accessed | tf_op | source)
XLA Modules:
  0.0 522.6 jit_solution(5201967598820129322)
XLA Ops:
  15.6 4.5 collective-permute-start
  21.6 4.4 collective-permute-start.7
  26.5 13.9 %all-gather.1 = bf16[8,12,96]{2,1,0:T(8,128)(2,1)S(1)} all-gather(bf16[1,12,96]{2,1,0:T(8,128)(2,1)S(1)} %bitcast.215), channel_id=2, replica_groups=mesh['xy'=4,'core'=2,'seq'=4] {'xy','core'}, dimensions={0}, use_global_device_ids=true | all-gather | bytes 20736 | tf_op jit(solution)/shard_map/all_gather | solution.py:573
  41.0 30.4 %collective-permute-done.1 = bf16[512,768]{1,0:T(8,128)(2,1)S(1)} collective-permute-done((bf16[512,768]{1,0:T(8,128)(2,1)}, bf16[512,768]{1,0:T(8,128)(2,1)S(1)}, u32[]{:S(2)}, u32[]{:S(2)}) %collective-permute-start.1) | collective-permute-done | bytes 786464 | tf_op jit(solution)/shard_map/ppermute | solution.py:552
  75.3 4.3 multiply_convert_fusion.sib
  79.7 2.2 multiply_convert_fusion.1.own
  82.2 60.3 %attend_forward.1 = (bf16[1024,384]{1,0:T(8,128)(2,1)S(1)}, bf16[1024,384]{1,0:T(8,128)(2,1)}, f32[6,8,2048]{2,1,0:T(8,128)S(1)}) custom-call(s32[1]{0:T(128)} %bitcast.13.mask_ref, s32[8]{0:T(128)S(1)} %bitcast.183, bf16[1024,1152]{1,0:T(8,128)(2,1)S(1)} %multiply_convert_fusion.1.own, bf16[1024,1152]{1,0:T(8,128)(2,1)S(1)} %multiply_convert_fusion.sib, ...), custom_call_target="tpu_custom_call" | custom-call | flops 1000000000 | bytes 1000000 | tf_op jit(solution)/shard_map/attend_forward/pallas_call | solution.py:145
  144.7 2.6 pad_maximum_fusion.1.cot_ref
  147.4 6.3 %all-gather.13.cloned.1.call-done.w_down = bf16[3072,768]{1,0:T(8,128)(2,1)} async-done(((bf16[384,768]{1,0:T(8,128)(2,1)}), bf16[3072,768]{1,0:T(8,128)(2,1)}) %all-gather.13.cloned.1.call-update) | async-done | bytes 4718608 | tf_op jit(solution)/shard_map/all_gather | solution.py:580
  156.0 47.9 %middle.1 = (bf16[1024,768]{1,0:T(8,128)(2,1)S(1)}, bf16[1024,768]{1,0:T(8,128)(2,1)}, bf16[1024,3072]{1,0:T(8,128)(2,1)}, bf16[1024,768]{1,0:T(8,128)(2,1)}, bf...) custom-call(s32[1]{0:T(128)} %bitcast.core_ref, ...), custom_call_target="tpu_custom_call" | custom-call | flops 20000000000 | bytes 30000000 | tf_op jit(solution)/shard_map/middle/pallas_call | solution.py:404
  203.9 8.5 %convolution_convert_fusion = bf16[768,3072]{1,0:T(8,128)(2,1)S(1)} fusion(bf16[1024,768]{1,0:T(8,128)(2,1)} %get-tuple-element.57, bf16[1024,3072]{1,0:T(8,128)(2,1)} %get-tuple-element.58), kind=kOutput, calls=%fused_computation.1 | convolution fusion | flops 4834197504 | bytes 12582912 | tf_op jit(solution)/shard_map/dot_general | solution.py:25
  212.5 2.4 dynamic-slice_bitcast_fusion.2
  214.9 1.7 convolution_convert_fusion.3
  216.9 7.9 %convolution_convert_fusion.1 = bf16[3072,768]{1,0:T(8,128)(2,1)S(1)} fusion(bf16[1024,3072]{1,0:T(8,128)(2,1)} %get-tuple-element.55, bf16[1024,768]{1,0:T(8,128)(2,1)} %get-tuple-element.56), kind=kOutput, calls=%fused_computation.2 | convolution fusion | flops 4834197504 | bytes 12582912 | tf_op jit(solution)/shard_map/dot_general | solution.py:25
  224.8 1.7 dynamic-slice_bitcast_fusion.1
  228.7 1.9 reshape.413
  230.9 2.5 convolution_convert_fusion.2
  237.3 5.0 constant_dynamic-update-slice_fusion.4
  247.5 5.5 %add_convert_fusion = bf16[4,896,768]{2,1,0:T(8,128)(2,1)S(1)} fusion(bf16[4,896,768]{2,1,0:T(8,128)(2,1)} %constant_dynamic-update-slice_fusion.2, bf16[4,896,768]{2,1,0:T(8,128)(2,1)} %copy-done.23), kind=kLoop, calls=%fused_computation | loop fusion | flops 11010048 | bytes 16515072 | tf_op jit(solution)/shard_map/convert_element_type | solution.py:468
  261.1 3.4 collective-permute-start.9
  266.7 23.3 %attend_backward_0.1 = (bf16[1024,384]{1,0:T(8,128)(2,1)S(1)}, bf16[1024,384]{1,0:T(8,128)(2,1)S(1)}) custom-call(s32[1]{0:T(128)} %bitcast.13.mask_ref, s32[8]{0:T(128)S(1)} %bitcast.184, bf16[1024,1152]{1,0:T(8,128)(2,1)S(1)} %copy-done.1, bf16[1024,1152]{1,0:T(8,128)(2,1)S(1)} %multiply_convert_fusion.sib, bf16[1024,384]{1,0:T(8,128)(2,1)S(1)} %copy-done.5, ...), custom_call_target="tpu_custom_call" | custom-call | flops 1000000000 | bytes 1000000 | tf_op jit(solution)/shard_map/attend_backward_0/pallas_call | solution.py:249
  292.3 1.9 fusion
  295.2 1.7 fusion.1
  298.2 23.1 %attend_backward_1.1 = (bf16[1024,384]{1,0:T(8,128)(2,1)S(1)}, bf16[1024,384]{1,0:T(8,128)(2,1)S(1)}) custom-call(s32[1]{0:T(128)} %bitcast.13.mask_ref, s32[8]{0:T(128)S(1)} %bitcast.185, bf16[1024,1152]{1,0:T(8,128)(2,1)S(1)} %copy-done.1, bf16[1024,1152]{1,0:T(8,128)(2,1)S(1)} %multiply_convert_fusion.sib, bf16[1024,384]{1,0:T(8,128)(2,1)S(1)} %copy-done.5, ...), custom_call_target="tpu_custom_call" | custom-call | flops 1000000000 | bytes 1000000 | tf_op jit(solution)/shard_map/attend_backward_1/pallas_call | solution.py:249
  321.5 1.8 copy-done.42
  325.5 2.9 add_convert_fusion.2
  330.4 9.6 %collective-permute-done.23 = bf16[2,128,768]{2,1,0:T(8,128)(2,1)S(1)} collective-permute-done((bf16[2,128,768]{2,1,0:T(8,128)(2,1)S(1)}, bf16[2,128,768]{2,1,0:T(8,128)(2,1)S(1)}, u32[]{:S(2)}, u32[]{:S(2)}) %collective-permute-start.23) | collective-permute-done | bytes 393248 | tf_op jit(solution)/shard_map/ppermute | solution.py:493
  341.8 3.5 maximum_select_fusion
  346.8 9.9 %collective-permute-done.26 = bf16[128,768]{1,0:T(8,128)(2,1)} collective-permute-done((bf16[128,768]{1,0:T(8,128)(2,1)}, bf16[128,768]{1,0:T(8,128)(2,1)}, u32[]{:S(2)}, u32[]{:S(2)}) %collective-permute-start.26) | collective-permute-done | bytes 196640 | tf_op jit(solution)/shard_map/ppermute | solution.py:493
  363.3 2.0 collective-permute-start.39
  365.6 23.1 %attend_backward_2.1 = (bf16[1024,384]{1,0:T(8,128)(2,1)S(1)}, bf16[1024,384]{1,0:T(8,128)(2,1)S(1)}) custom-call(s32[1]{0:T(128)} %bitcast.13.mask_ref, s32[8]{0:T(128)S(1)} %bitcast.186, bf16[1024,1152]{1,0:T(8,128)(2,1)S(1)} %copy-done.2, bf16[1024,1152]{1,0:T(8,128)(2,1)S(1)} %multiply_convert_fusion.sib, bf16[1024,384]{1,0:T(8,128)(2,1)S(1)} %copy-done.6, ...), custom_call_target="tpu_custom_call" | custom-call | flops 1000000000 | bytes 1000000 | tf_op jit(solution)/shard_map/attend_backward_2/pallas_call | solution.py:249
  390.7 3.4 fusion.14
  394.1 3.9 fusion.2
  398.1 2.4 fusion.20
  401.2 3.2 collective-permute-start.42
  404.6 5.7 %collective-permute-done.41 = bf16[224,768]{1,0:T(8,128)(2,1)S(1)} collective-permute-done((bf16[224,768]{1,0:T(8,128)(2,1)S(1)}, bf16[224,768]{1,0:T(8,128)(2,1)S(1)}, u32[]{:S(2)}, u32[]{:S(2)}) %collective-permute-start.41) | collective-permute-done | bytes 344096 | tf_op jit(solution)/shard_map/ppermute | solution.py:512
  410.4 20.2 %collective-permute-done.42 = bf16[224,768]{1,0:T(8,128)(2,1)S(1)} collective-permute-done((bf16[224,768]{1,0:T(8,128)(2,1)S(1)}, bf16[224,768]{1,0:T(8,128)(2,1)S(1)}, u32[]{:S(2)}, u32[]{:S(2)}) %collective-permute-start.42) | collective-permute-done | bytes 344096 | tf_op jit(solution)/shard_map/ppermute | solution.py:512
  430.6 3.4 collective-permute-done.43
  437.1 3.0 add_convert_fusion.1
  441.7 2.9 collective-permute-start.21
  447.1 2.5 collective-permute-done.28
  450.0 4.3 collective-permute-start.32
  455.4 34.5 %collective-permute-done.31 = bf16[64,1152]{1,0:T(8,128)(2,1)S(1)} collective-permute-done((bf16[64,1152]{1,0:T(8,128)(2,1)S(1)}, bf16[64,1152]{1,0:T(8,128)(2,1)S(1)}, u32[]{:S(2)}, u32[]{:S(2)}) %collective-permute-start.31) | collective-permute-done | bytes 147488 | tf_op jit(solution)/shard_map/ppermute | solution.py:512
  492.6 2.5 collective-permute-start.35
  495.1 1.7 collective-permute-start.36
  496.8 7.2 %collective-permute-done.35 = bf16[64,1152]{1,0:T(8,128)(2,1)S(1)} collective-permute-done((bf16[64,1152]{1,0:T(8,128)(2,1)S(1)}, bf16[64,1152]{1,0:T(8,128)(2,1)S(1)}, u32[]{:S(2)}, u32[]{:S(2)}) %collective-permute-start.35) | collective-permute-done | bytes 147488 | tf_op jit(solution)/shard_map/ppermute | solution.py:512
  504.1 4.3 collective-permute-done.36
  509.0 1.9 fusion.17
  (357 shorter events, 79.8 us)
Async XLA Ops:
  7.2 68.2 %all-gather.7.cloned.1.call-start = ((), (), s32[]{:S(2)}) async-start(), calls=%async_computation | async-start | bytes 2211840 | tf_op jit(solution)/shard_map/all_gather | solution.py:569
  9.6 1.8 collective-permute-start.3
  12.3 135.1 %all-gather.9.cloned.1.call-start = ((), (), s32[]{:S(2)}) async-start(), calls=%async_computation.1 | async-start | bytes 1327104 | tf_op jit(solution)/shard_map/all_gather | solution.py:578
  13.0 134.3 %all-gather.11.cloned.1.call-start = ((), (), s32[]{:S(2)}) async-start(), calls=%async_computation.2 | async-start | bytes 5308416 | tf_op jit(solution)/shard_map/all_gather | solution.py:579
  13.7 139.9 %all-gather.13.cloned.1.call-start = ((), (), s32[]{:S(2)}) async-start(), calls=%async_computation.3 | async-start | bytes 5308416 | tf_op jit(solution)/shard_map/all_gather | solution.py:580
  15.6 25.2 %collective-permute-start = (bf16[512,768]{1,0:T(8,128)(2,1)}, bf16[512,768]{1,0:T(8,128)(2,1)S(1)}, u32[]{:S(2)}, u32[]{:S(2)}) collective-permute-start(bf16[512,768]{1,0:T(8,128)(2,1)} %get-tuple-element.103), channel_id=1, source_target_pairs={{0,0},{1,1},{2,4},{3,5},{4,2},{5,3},{6,6},{7,7},{8,8},{9,9},{10,12... | collective-permute-start | bytes 2359304 | tf_op jit(solution)/shard_map/ppermute | solution.py:552
  20.1 51.3 %collective-permute-start.1 = (bf16[512,768]{1,0:T(8,128)(2,1)}, bf16[512,768]{1,0:T(8,128)(2,1)S(1)}, u32[]{:S(2)}, u32[]{:S(2)}) collective-permute-start(bf16[512,768]{1,0:T(8,128)(2,1)} %get-tuple-element.104), channel_id=1, source_target_pairs={{0,1},{1,0},{2,5},{3,4},{4,3},{5,2},{6,7},{7,6},{8,9},{9,8},{10,13... | collective-permute-start | bytes 2359304 | tf_op jit(solution)/shard_map/ppermute | solution.py:552
  20.3 51.5 %collective-permute-start.2 = (s32[2,8]{1,0:T(2,128)S(1)}, s32[2,8]{1,0:T(2,128)S(1)}, u32[]{:S(2)}, u32[]{:S(2)}) collective-permute-start(s32[2,8]{1,0:T(2,128)S(1)} %bitcast.218), channel_id=1, source_target_pairs={{0,4},{4,0},{1,5},{5,1},{2,6},{6,2},{3,7},{7,3},{8,12},{12,8},{9,1... | collective-permute-start | bytes 200 | tf_op jit(solution)/shard_map/ppermute | solution.py:456
  21.6 123.1 %collective-permute-start.7 = (bf16[512,768]{1,0:T(8,128)(2,1)}, bf16[512,768]{1,0:T(8,128)(2,1)}, u32[]{:S(2)}, u32[]{:S(2)}) collective-permute-start(bf16[512,768]{1,0:T(8,128)(2,1)} %get-tuple-element.101), channel_id=1, source_target_pairs={{0,0},{1,1},{2,4},{3,5},{4,2},{5,3},{6,6},{7,7},{8,8},{9,9},{10,12... | collective-permute-start | bytes 2359304 | tf_op jit(solution)/shard_map/ppermute | solution.py:552
  26.0 118.7 %collective-permute-start.8 = (bf16[512,768]{1,0:T(8,128)(2,1)}, bf16[512,768]{1,0:T(8,128)(2,1)}, u32[]{:S(2)}, u32[]{:S(2)}) collective-permute-start(bf16[512,768]{1,0:T(8,128)(2,1)} %get-tuple-element.102), channel_id=1, source_target_pairs={{0,1},{1,0},{2,5},{3,4},{4,3},{5,2},{6,7},{7,6},{8,9},{9,8},{10,13... | collective-permute-start | bytes 2359304 | tf_op jit(solution)/shard_map/ppermute | solution.py:552
  40.9 32.5 %collective-permute-start.4 = (bf16[512,768]{1,0:T(8,128)(2,1)S(1)}, bf16[512,768]{1,0:T(8,128)(2,1)S(1)}, u32[]{:S(2)}, u32[]{:S(2)}) collective-permute-start(bf16[512,768]{1,0:T(8,128)(2,1)S(1)} %collective-permute-done), channel_id=1, source_target_pairs={{0,4},{4,0},{1,5},{5,1},{2,6},{6,2},{3,7},{7,3},{8,12},{12,8},{9,1... | collective-permute-start | bytes 2359304 | tf_op jit(solution)/shard_map/ppermute | solution.py:456
  71.4 2.9 collective-permute-start.5
  144.2 3.1 collective-permute-start.6
  227.7 9.7 %collective-permute-start.11 = (bf16[4,384,768]{2,1,0:T(8,128)(2,1)}, bf16[4,384,768]{2,1,0:T(8,128)(2,1)}, u32[]{:S(2)}, u32[]{:S(2)}) collective-permute-start(bf16[4,384,768]{2,1,0:T(8,128)(2,1)} %dynamic-slice_bitcast_fusion.1), channel_id=1, source_target_pairs={{0,4},{4,0},{1,5},{5,1},{2,6},{6,2},{3,7},{7,3},{8,12},{12,8},{9,1... | collective-permute-start | bytes 7077896 | tf_op jit(solution)/shard_map/ppermute | solution.py:456
  230.6 11.8 %collective-permute-start.12 = (bf16[4,96,3072]{2,1,0:T(8,128)(2,1)}, bf16[4,96,3072]{2,1,0:T(8,128)(2,1)S(1)}, u32[]{:S(2)}, u32[]{:S(2)}) collective-permute-start(bf16[4,96,3072]{2,1,0:T(8,128)(2,1)} %get-tuple-element.96), channel_id=1, source_target_pairs={{0,4},{4,0},{1,5},{5,1},{2,6},{6,2},{3,7},{7,3},{8,12},{12,8},{9,1... | collective-permute-start | bytes 7077896 | tf_op jit(solution)/shard_map/ppermute | solution.py:456
  233.9 12.0 %collective-permute-start.13 = (bf16[4,96,768]{2,1,0:T(8,128)(2,1)S(1)}, bf16[4,96,768]{2,1,0:T(8,128)(2,1)S(1)}, u32[]{:S(2)}, u32[]{:S(2)}) collective-permute-start(bf16[4,96,768]{2,1,0:T(8,128)(2,1)S(1)} %dynamic-slice_bitcast_fusion.11), channel_id=1, source_target_pairs={{0,4},{4,0},{1,5},{5,1},{2,6},{6,2},{3,7},{7,3},{8,12},{12,8},{9,1... | collective-permute-start | bytes 1769480 | tf_op jit(solution)/shard_map/ppermute | solution.py:456
  235.2 11.6 %collective-permute-start.14 = (bf16[4,32,768]{2,1,0:T(8,128)(2,1)S(1)}, bf16[4,32,768]{2,1,0:T(8,128)(2,1)S(1)}, u32[]{:S(2)}, u32[]{:S(2)}) collective-permute-start(bf16[4,32,768]{2,1,0:T(8,128)(2,1)S(1)} %bitcast.213), channel_id=1, source_target_pairs={{0,4},{4,0},{1,5},{5,1},{2,6},{6,2},{3,7},{7,3},{8,12},{12,8},{9,1... | collective-permute-start | bytes 589832 | tf_op jit(solution)/shard_map/ppermute | solution.py:456
  254.6 36.5 %collective-permute-start.17 = (bf16[2,448,768]{2,1,0:T(8,128)(2,1)}, bf16[2,448,768]{2,1,0:T(8,128)(2,1)}, u32[]{:S(2)}, u32[]{:S(2)}) collective-permute-start(bf16[2,448,768]{2,1,0:T(8,128)(2,1)} %dynamic-slice_bitcast_fusion.3), channel_id=1, source_target_pairs={{0,16},{8,24},{16,0},{24,8},{1,17},{9,25},{17,1},{25,9},{2,18},{10... | collective-permute-start | bytes 4128776 | tf_op jit(solution)/shard_map/ppermute | solution.py:493
  256.9 34.2 %collective-permute-start.16 = (bf16[2,448,768]{2,1,0:T(8,128)(2,1)}, bf16[2,448,768]{2,1,0:T(8,128)(2,1)}, u32[]{:S(2)}, u32[]{:S(2)}) collective-permute-start(bf16[2,448,768]{2,1,0:T(8,128)(2,1)} %dynamic-slice_bitcast_fusion.4), channel_id=1, source_target_pairs={{0,8},{8,0},{16,24},{24,16},{1,9},{9,1},{17,25},{25,17},{2,10},{10... | collective-permute-start | bytes 4128776 | tf_op jit(solution)/shard_map/ppermute | solution.py:493
  257.8 6.8 %collective-permute-start.15 = (bf16[1024,384]{1,0:T(8,128)(2,1)}, bf16[1024,384]{1,0:T(8,128)(2,1)}, u32[]{:S(2)}, u32[]{:S(2)}) collective-permute-start(bf16[1024,384]{1,0:T(8,128)(2,1)} %get-tuple-element.64), channel_id=1, source_target_pairs={{0,4},{4,0},{1,5},{5,1},{2,6},{6,2},{3,7},{7,3},{8,12},{12,8},{9,1... | collective-permute-start | bytes 2359304 | tf_op jit(solution)/shard_map/ppermute | solution.py:456
  259.9 38.0 %collective-permute-start.10 = (bf16[512,768]{1,0:T(8,128)(2,1)S(1)}, bf16[512,768]{1,0:T(8,128)(2,1)S(1)}, u32[]{:S(2)}, u32[]{:S(2)}) collective-permute-start(bf16[512,768]{1,0:T(8,128)(2,1)S(1)} %get-tuple-element.100), channel_id=1, source_target_pairs={{1,0},{0,1},{5,2},{4,3},{3,4},{2,5},{7,6},{6,7},{9,8},{8,9},{13,10... | collective-permute-start | bytes 2359304 | tf_op jit(solution)/shard_map/ppermute | solution.py:597
  261.1 37.1 %collective-permute-start.9 = (bf16[512,768]{1,0:T(8,128)(2,1)S(1)}, bf16[512,768]{1,0:T(8,128)(2,1)S(1)}, u32[]{:S(2)}, u32[]{:S(2)}) collective-permute-start(bf16[512,768]{1,0:T(8,128)(2,1)S(1)} %get-tuple-element.99), channel_id=1, source_target_pairs={{0,0},{1,1},{4,2},{5,3},{2,4},{3,5},{6,6},{7,7},{8,8},{9,9},{12,10... | collective-permute-start | bytes 2359304 | tf_op jit(solution)/shard_map/ppermute | solution.py:597
  328.7 11.3 %collective-permute-start.23 = (bf16[2,128,768]{2,1,0:T(8,128)(2,1)S(1)}, bf16[2,128,768]{2,1,0:T(8,128)(2,1)S(1)}, u32[]{:S(2)}, u32[]{:S(2)}) collective-permute-start(bf16[2,128,768]{2,1,0:T(8,128)(2,1)S(1)} %dynamic-slice_bitcast_fusion.13), channel_id=1, source_target_pairs={{0,8},{8,0},{16,24},{24,16},{1,9},{9,1},{17,25},{25,17},{2,10},{10... | collective-permute-start | bytes 1179656 | tf_op jit(solution)/shard_map/ppermute | solution.py:493
  328.8 12.1 %collective-permute-start.25 = (bf16[2,128,768]{2,1,0:T(8,128)(2,1)S(1)}, bf16[2,128,768]{2,1,0:T(8,128)(2,1)S(1)}, u32[]{:S(2)}, u32[]{:S(2)}) collective-permute-start(bf16[2,128,768]{2,1,0:T(8,128)(2,1)S(1)} %dynamic-slice_bitcast_fusion.12), channel_id=1, source_target_pairs={{0,16},{8,24},{16,0},{24,8},{1,17},{9,25},{17,1},{25,9},{2,18},{10... | collective-permute-start | bytes 1179656 | tf_op jit(solution)/shard_map/ppermute | solution.py:493
  328.9 31.2 %collective-permute-start.19 = (bf16[448,768]{1,0:T(8,128)(2,1)}, bf16[448,768]{1,0:T(8,128)(2,1)}, u32[]{:S(2)}, u32[]{:S(2)}) collective-permute-start(bf16[448,768]{1,0:T(8,128)(2,1)} %dynamic-slice_bitcast_fusion.9), channel_id=1, source_target_pairs={{0,8},{8,0},{16,24},{24,16},{1,9},{9,1},{17,25},{25,17},{2,10},{10... | collective-permute-start | bytes 2064392 | tf_op jit(solution)/shard_map/ppermute | solution.py:493
  340.8 6.0 %collective-permute-start.24 = (bf16[128,768]{1,0:T(8,128)(2,1)}, bf16[128,768]{1,0:T(8,128)(2,1)}, u32[]{:S(2)}, u32[]{:S(2)}) collective-permute-start(bf16[128,768]{1,0:T(8,128)(2,1)} %dynamic-slice_bitcast_fusion.19), channel_id=1, source_target_pairs={{0,16},{8,24},{16,0},{24,8},{1,17},{9,25},{17,1},{25,9},{2,18},{10... | collective-permute-start | bytes 589832 | tf_op jit(solution)/shard_map/ppermute | solution.py:493
  341.8 14.9 %collective-permute-start.26 = (bf16[128,768]{1,0:T(8,128)(2,1)}, bf16[128,768]{1,0:T(8,128)(2,1)}, u32[]{:S(2)}, u32[]{:S(2)}) collective-permute-start(bf16[128,768]{1,0:T(8,128)(2,1)} %dynamic-slice_bitcast_fusion.18), channel_id=1, source_target_pairs={{0,8},{8,0},{16,24},{24,16},{1,9},{9,1},{17,25},{25,17},{2,10},{10... | collective-permute-start | bytes 589832 | tf_op jit(solution)/shard_map/ppermute | solution.py:493
  345.3 16.3 %collective-permute-start.18 = (bf16[448,768]{1,0:T(8,128)(2,1)S(1)}, bf16[448,768]{1,0:T(8,128)(2,1)S(1)}, u32[]{:S(2)}, u32[]{:S(2)}) collective-permute-start(bf16[448,768]{1,0:T(8,128)(2,1)S(1)} %copy-done.52), channel_id=1, source_target_pairs={{0,16},{8,24},{16,0},{24,8},{1,17},{9,25},{17,1},{25,9},{2,18},{10... | collective-permute-start | bytes 2064392 | tf_op jit(solution)/shard_map/ppermute | solution.py:493
  363.3 37.3 %collective-permute-start.38 = (bf16[224,768]{1,0:T(8,128)(2,1)S(1)}, bf16[224,768]{1,0:T(8,128)(2,1)S(1)}, u32[]{:S(2)}, u32[]{:S(2)}) collective-permute-start(bf16[224,768]{1,0:T(8,128)(2,1)S(1)} %get-tuple-element.111), channel_id=1, source_target_pairs={{0,1},{1,2},{2,3},{3,0},{4,5},{5,6},{6,7},{7,4},{8,9},{9,10},{10,1... | collective-permute-start | bytes 1032200 | tf_op jit(solution)/shard_map/ppermute | solution.py:512
  363.3 37.2 %collective-permute-start.39 = (bf16[224,768]{1,0:T(8,128)(2,1)S(1)}, bf16[224,768]{1,0:T(8,128)(2,1)S(1)}, u32[]{:S(2)}, u32[]{:S(2)}) collective-permute-start(bf16[224,768]{1,0:T(8,128)(2,1)S(1)} %get-tuple-element.112), channel_id=1, source_target_pairs={{0,2},{1,3},{2,0},{3,1},{4,6},{5,7},{6,4},{7,5},{8,10},{9,11},{10,... | collective-permute-start | bytes 1032200 | tf_op jit(solution)/shard_map/ppermute | solution.py:512
  365.3 35.3 %collective-permute-start.40 = (bf16[224,768]{1,0:T(8,128)(2,1)S(1)}, bf16[224,768]{1,0:T(8,128)(2,1)S(1)}, u32[]{:S(2)}, u32[]{:S(2)}) collective-permute-start(bf16[224,768]{1,0:T(8,128)(2,1)S(1)} %get-tuple-element.110), channel_id=1, source_target_pairs={{0,3},{1,0},{2,1},{3,2},{4,7},{5,4},{6,5},{7,6},{8,11},{9,8},{10,9... | collective-permute-start | bytes 1032200 | tf_op jit(solution)/shard_map/ppermute | solution.py:512
  394.1 42.5 %collective-permute-start.20 = (bf16[1024,768]{1,0:T(8,128)(2,1)}, bf16[1024,768]{1,0:T(8,128)(2,1)}, u32[]{:S(2)}, u32[]{:S(2)}) collective-permute-start(bf16[1024,768]{1,0:T(8,128)(2,1)} %fusion.14), channel_id=1, source_target_pairs={{0,4},{4,0},{1,5},{5,1},{2,6},{6,2},{3,7},{7,3},{8,12},{12,8},{9,1... | collective-permute-start | bytes 4718600 | tf_op jit(solution)/shard_map/ppermute | solution.py:456
  401.2 9.2 %collective-permute-start.41 = (bf16[224,768]{1,0:T(8,128)(2,1)S(1)}, bf16[224,768]{1,0:T(8,128)(2,1)S(1)}, u32[]{:S(2)}, u32[]{:S(2)}) collective-permute-start(bf16[224,768]{1,0:T(8,128)(2,1)S(1)} %get-tuple-element.90), channel_id=1, source_target_pairs={{0,1},{1,2},{2,3},{3,0},{4,5},{5,6},{6,7},{7,4},{8,9},{9,10},{10,1... | collective-permute-start | bytes 1032200 | tf_op jit(solution)/shard_map/ppermute | solution.py:512
  401.2 29.3 %collective-permute-start.42 = (bf16[224,768]{1,0:T(8,128)(2,1)S(1)}, bf16[224,768]{1,0:T(8,128)(2,1)S(1)}, u32[]{:S(2)}, u32[]{:S(2)}) collective-permute-start(bf16[224,768]{1,0:T(8,128)(2,1)S(1)} %get-tuple-element.90), channel_id=1, source_target_pairs={{0,2},{1,3},{2,0},{3,1},{4,6},{5,7},{6,4},{7,5},{8,10},{9,11},{10,... | collective-permute-start | bytes 1032200 | tf_op jit(solution)/shard_map/ppermute | solution.py:512
  404.4 29.6 %collective-permute-start.43 = (bf16[224,768]{1,0:T(8,128)(2,1)S(1)}, bf16[224,768]{1,0:T(8,128)(2,1)S(1)}, u32[]{:S(2)}, u32[]{:S(2)}) collective-permute-start(bf16[224,768]{1,0:T(8,128)(2,1)S(1)} %get-tuple-element.90), channel_id=1, source_target_pairs={{0,3},{1,0},{2,1},{3,2},{4,7},{5,4},{6,5},{7,6},{8,11},{9,8},{10,9... | collective-permute-start | bytes 1032200 | tf_op jit(solution)/shard_map/ppermute | solution.py:512
  440.2 5.5 %collective-permute-start.27 = (bf16[2,128,384]{2,1,0:T(8,128)(2,1)S(1)}, bf16[2,128,384]{2,1,0:T(8,128)(2,1)S(1)}, u32[]{:S(2)}, u32[]{:S(2)}) collective-permute-start(bf16[2,128,384]{2,1,0:T(8,128)(2,1)S(1)} %dynamic-slice_bitcast_fusion.17), channel_id=1, source_target_pairs={{0,8},{8,0},{16,24},{24,16},{1,9},{9,1},{17,25},{25,17},{2,10},{10... | collective-permute-start | bytes 589832 | tf_op jit(solution)/shard_map/ppermute | solution.py:493
  440.3 5.5 %collective-permute-start.29 = (bf16[2,128,384]{2,1,0:T(8,128)(2,1)S(1)}, bf16[2,128,384]{2,1,0:T(8,128)(2,1)S(1)}, u32[]{:S(2)}, u32[]{:S(2)}) collective-permute-start(bf16[2,128,384]{2,1,0:T(8,128)(2,1)S(1)} %dynamic-slice_bitcast_fusion.16), channel_id=1, source_target_pairs={{0,16},{8,24},{16,0},{24,8},{1,17},{9,25},{17,1},{25,9},{2,18},{10... | collective-permute-start | bytes 589832 | tf_op jit(solution)/shard_map/ppermute | solution.py:493
  441.7 48.2 %collective-permute-start.21 = (bf16[512,768]{1,0:T(8,128)(2,1)S(1)}, bf16[512,768]{1,0:T(8,128)(2,1)S(1)}, u32[]{:S(2)}, u32[]{:S(2)}) collective-permute-start(bf16[512,768]{1,0:T(8,128)(2,1)S(1)} %get-tuple-element.97), channel_id=1, source_target_pairs={{0,0},{1,1},{4,2},{5,3},{2,4},{3,5},{6,6},{7,7},{8,8},{9,9},{12,10... | collective-permute-start | bytes 2359304 | tf_op jit(solution)/shard_map/ppermute | solution.py:663
  444.7 45.3 %collective-permute-start.22 = (bf16[512,768]{1,0:T(8,128)(2,1)S(1)}, bf16[512,768]{1,0:T(8,128)(2,1)S(1)}, u32[]{:S(2)}, u32[]{:S(2)}) collective-permute-start(bf16[512,768]{1,0:T(8,128)(2,1)S(1)} %get-tuple-element.98), channel_id=1, source_target_pairs={{1,0},{0,1},{5,2},{4,3},{3,4},{2,5},{7,6},{6,7},{9,8},{8,9},{13,10... | collective-permute-start | bytes 2359304 | tf_op jit(solution)/shard_map/ppermute | solution.py:663
  445.8 3.8 collective-permute-start.28
  446.0 3.8 collective-permute-start.30
  450.0 40.0 %collective-permute-start.31 = (bf16[64,1152]{1,0:T(8,128)(2,1)S(1)}, bf16[64,1152]{1,0:T(8,128)(2,1)S(1)}, u32[]{:S(2)}, u32[]{:S(2)}) collective-permute-start(bf16[64,1152]{1,0:T(8,128)(2,1)S(1)} %get-tuple-element.119), channel_id=1, source_target_pairs={{0,1},{1,2},{2,3},{3,0},{4,5},{5,6},{6,7},{7,4},{8,9},{9,10},{10,1... | collective-permute-start | bytes 442376 | tf_op jit(solution)/shard_map/ppermute | solution.py:512
  450.0 41.5 %collective-permute-start.32 = (bf16[64,1152]{1,0:T(8,128)(2,1)S(1)}, bf16[64,1152]{1,0:T(8,128)(2,1)S(1)}, u32[]{:S(2)}, u32[]{:S(2)}) collective-permute-start(bf16[64,1152]{1,0:T(8,128)(2,1)S(1)} %get-tuple-element.121), channel_id=1, source_target_pairs={{0,2},{1,3},{2,0},{3,1},{4,6},{5,7},{6,4},{7,5},{8,10},{9,11},{10,... | collective-permute-start | bytes 442376 | tf_op jit(solution)/shard_map/ppermute | solution.py:512
  454.3 37.2 %collective-permute-start.33 = (bf16[64,1152]{1,0:T(8,128)(2,1)S(1)}, bf16[64,1152]{1,0:T(8,128)(2,1)S(1)}, u32[]{:S(2)}, u32[]{:S(2)}) collective-permute-start(bf16[64,1152]{1,0:T(8,128)(2,1)S(1)} %get-tuple-element.120), channel_id=1, source_target_pairs={{0,3},{1,0},{2,1},{3,2},{4,7},{5,4},{6,5},{7,6},{8,11},{9,8},{10,9... | collective-permute-start | bytes 442376 | tf_op jit(solution)/shard_map/ppermute | solution.py:512
  491.7 5.1 collective-permute-start.34
  492.6 11.4 %collective-permute-start.35 = (bf16[64,1152]{1,0:T(8,128)(2,1)S(1)}, bf16[64,1152]{1,0:T(8,128)(2,1)S(1)}, u32[]{:S(2)}, u32[]{:S(2)}) collective-permute-start(bf16[64,1152]{1,0:T(8,128)(2,1)S(1)} %get-tuple-element.92), channel_id=1, source_target_pairs={{0,2},{1,3},{2,0},{3,1},{4,6},{5,7},{6,4},{7,5},{8,10},{9,11},{10,... | collective-permute-start | bytes 442376 | tf_op jit(solution)/shard_map/ppermute | solution.py:512
  495.1 13.2 %collective-permute-start.36 = (bf16[64,1152]{1,0:T(8,128)(2,1)S(1)}, bf16[64,1152]{1,0:T(8,128)(2,1)S(1)}, u32[]{:S(2)}, u32[]{:S(2)}) collective-permute-start(bf16[64,1152]{1,0:T(8,128)(2,1)S(1)} %get-tuple-element.92), channel_id=1, source_target_pairs={{0,3},{1,0},{2,1},{3,2},{4,7},{5,4},{6,5},{7,6},{8,11},{9,8},{10,9... | collective-permute-start | bytes 442376 | tf_op jit(solution)/shard_map/ppermute | solution.py:512
  508.4 3.0 collective-permute-start.37
  (66 other events, 418.2 us)
Sparse Core Ops, SparseCore 0:
  12.4 33.3 all-gather.6
  47.6 24.5 all-gather.8
  74.1 38.7 all-gather.10
  114.7 38.9 all-gather.12

commit v5 on v4

--- a/solution.py
+++ b/solution.py
@@ -266,7 +266,7 @@
             pltpu.SemaphoreType.DMA((3, pieces)),
         ],
         compiler_params=pltpu.CompilerParams(vmem_limit_bytes=24 << 20),
-        cost_estimate=pl.CostEstimate(flops=1_000_000_000, bytes_accessed=1_000_000, transcendentals=0),
+        cost_estimate=pl.CostEstimate(flops=20_000_000_000, bytes_accessed=8_000_000, transcendentals=0),
         name=f"attend_backward_{pair}",
     )(mask, ends, own, sib, ctx_own, ctx_sib, dctx_own, dctx_sib, seg_col, seg_row, lse)
 
@@ -434,6 +434,97 @@
     )(core, x, near, far, cot, vec, in_bias, w_out, w_in, w_down)
 
 
+def gradients_kernel(
+    rows, core_ref, act_ref, low_ref, down_ref, pre_ref, near_ref, far_ref, attn_ref, vec_ref,
+    keep_ref, send_ref, result, sems
+):
+    step = pl.program_id(0)
+    core = core_ref[0]
+    shards = low_ref.shape[1] // rows
+    chunks = (pl.num_programs(0) - 1) // 2
+    blocks = pre_ref.shape[1] * chunks // low_ref.shape[1]
+    slot = step % 2
+
+    def wait(which):
+        pltpu.make_async_copy(result.at[which], result.at[which], sems.at[which]).wait()
+
+    def put(source, shard_core, plane, at, count, sem):
+        target = pl.ds(at, count)
+
+        @pl.when(core == shard_core)
+        def _():
+            pltpu.make_async_copy(source, keep_ref.at[plane, target, :], sem).start()
+
+        @pl.when(core != shard_core)
+        def _():
+            pltpu.make_async_copy(source, send_ref.at[plane, target, :], sem).start()
+
+    @pl.when(step >= 2)
+    def _():
+        wait(slot)
+
+    @pl.when(step < chunks)
+    def _():
+        result[slot] = mm(act_ref[...], down_ref[...], TN).astype(jnp.bfloat16)
+        count = blocks * rows
+        here = result.shape[1] // count
+        for part in range(here):
+            put(result.at[slot, pl.ds(part * count, count), :], part % CORES, step * (here // CORES) + part // CORES, 0, count, sems.at[slot])
+
+    @pl.when(jnp.logical_and(step >= chunks, step < 2 * chunks))
+    def _():
+        result[slot] = mm(low_ref[...], pre_ref[...], TN).astype(jnp.bfloat16)
+        at = pl.multiple_of(blocks * rows + (step - chunks) * rows, 16)
+        for shard in range(shards):
+            put(result.at[slot, pl.ds(shard * rows, rows), :], shard % CORES, shard // CORES, at, rows, sems.at[slot])
+
+    @pl.when(step == 2 * chunks)
+    def _():
+        mine = near_ref.shape[1]
+        result[slot, :mine] = mm(near_ref[...], attn_ref[...], TN).astype(jnp.bfloat16)
+        result[slot, mine:] = mm(far_ref[...], attn_ref[...], TN).astype(jnp.bfloat16)
+        half = shards // 2
+        for shard in range(shards):
+            first = core if shard < half else 1 - core
+            plane = first * (half // CORES) + (shard % half) // CORES
+            put(result.at[slot, pl.ds(shard * rows, rows), :], shard % CORES, plane, 2 * blocks * rows, rows, sems.at[slot])
+        for shard in range(shards):
+            put(vec_ref.at[shard], shard % CORES, shard // CORES, (2 * blocks + 1) * rows, vec_ref.shape[1], sems.at[2 + shard])
+        wait(0)
+        wait(1)
+        for shard in range(shards):
+            pltpu.make_async_copy(vec_ref.at[shard], vec_ref.at[shard], sems.at[2 + shard]).wait()
+
+
+def gradients(core, act, low, down, pre, near, far, attn, vec, planes):
+    count, width = low.shape
+    rows = width // (planes * CORES)
+    chunks = pre.shape[1] // width
+    total_rows = (2 * chunks + 1) * rows + vec.shape[1]
+    whole = lambda x: pl.BlockSpec(x.shape, lambda i: (0,) * x.ndim)
+    out = jax.ShapeDtypeStruct((planes, total_rows, width), jnp.bfloat16)
+    return pl.pallas_call(
+        functools.partial(gradients_kernel, rows),
+        grid=(2 * chunks + 1,),
+        out_shape=(out, out),
+        in_specs=[
+            pl.BlockSpec(memory_space=pltpu.SMEM),
+            pl.BlockSpec((count, width), lambda i: (0, jnp.minimum(i, chunks - 1))),
+            whole(low), whole(down),
+            pl.BlockSpec((count, width), lambda i: (0, jnp.clip(i - chunks, 0, chunks - 1))),
+            whole(near), whole(far), whole(attn), whole(vec),
+        ],
+        out_specs=(pl.BlockSpec(memory_space=pl.ANY),) * 2,
+        scratch_shapes=[
+            pltpu.VMEM((2, width, width), jnp.bfloat16),
+            pltpu.SemaphoreType.DMA((2 + planes * CORES,)),
+        ],
+        compiler_params=pltpu.CompilerParams(vmem_limit_bytes=48 << 20),
+        cost_estimate=pl.CostEstimate(flops=11_000_000_000, bytes_accessed=30_000_000, transcendentals=0),
+        name="gradients",
+    )(core, act, low, down, pre, near, far, attn, vec)
+
+
 def doc_ids(ends, count):
     places = jnp.arange(count, dtype=jnp.int32)
     return jnp.sum((places[:, None] >= ends[None, :]).astype(jnp.int32), axis=1)
@@ -516,9 +607,9 @@
         self.keep = sum(p.astype(jnp.float32) for p in parts).astype(jnp.bfloat16)
         self.received = [self.shift(self.keep, d) for d in range(1, self.nseq)]
 
-    def result(self):
+    def result(self, *done):
         whole = jnp.zeros((self.nseq * self.rows,) + self.keep.shape[1:], jnp.bfloat16)
-        for d, part in enumerate([self.keep] + self.received):
+        for d, part in enumerate([self.keep] + [after(r, *done) for r in self.received]):
             start = ((self.me - d) % self.nseq) * self.rows
             whole = lax.dynamic_update_slice_in_dim(whole, part, start, 0)
         return whole
@@ -589,7 +680,7 @@
     ctx_own, ctx_sib, lse = attend_forward(mask, ends, *projected, seg_col, seg_row, run)
     ctx_far = swap(ctx_sib)
 
-    cot = jnp.concatenate(spread(out_cotangent))
+    cot = jnp.concatenate(spread(after(out_cotangent, x_own)))
     result, hidden_low, act_low, grad_down, grad_pre, grad_one, grad_attn, dctx_own, dctx_far, sums, in_sums = middle(
         core.astype(jnp.int32)[None], x_own, ctx_own, ctx_far, cot, norms, bias_in, w_out, w_in, w_down
     )
@@ -599,20 +690,27 @@
     def cores(blocks):
         return pick(blocks, core, 1), swap(pick(blocks, 1 - core, 1))
 
-    down_grad = cores(mm(act_low, grad_down, TN).astype(bf16).reshape(planes, CORES, -1, width))
-    in_grad = cores(mm(hidden_low, grad_pre, TN).astype(bf16).reshape(planes, CORES, rows, -1))
-    out_grad = [mm(c, grad_attn, TN).astype(bf16) for c in (ctx_own, ctx_far)]
-    out_grad = cores(either(core, *out_grad, 0).reshape(planes, CORES, rows, width))
+    inner_blocks = ff_in_bias.shape[0] * shards // width
+    down_rows = ff_out_weight.shape[0]
     vector = [jnp.moveaxis(sums[:6].reshape(6, shards, rows), 1, 0), in_sums.reshape(shards, inner, rows)]
     vector = jnp.concatenate(vector, axis=1).astype(bf16)
     vector = jnp.pad(vector, ((0, 0), (0, 32 - vector.shape[1]), (0, width - rows)))
-    vector = cores(vector.reshape(planes, CORES, 32, width))
-    inner_blocks = in_grad[0].shape[2] // width
-    joined = []
-    for which in range(2):
-        wide = in_grad[which]
-        wide = [wide[:, :, i * width : (i + 1) * width] for i in range(inner_blocks)]
-        joined.append(jnp.concatenate([down_grad[which]] + wide + [out_grad[which], vector[which]], axis=1))
+    if rows % 16 == 0:
+        kept, sent = gradients(
+            core.astype(jnp.int32)[None], act_low, hidden_low, grad_down, grad_pre, ctx_own, ctx_far, grad_attn, vector, planes
+        )
+        joined = kept, swap(sent)
+    else:
+        down_grad = cores(mm(act_low, grad_down, TN).astype(bf16).reshape(planes, CORES, -1, width))
+        in_grad = cores(mm(hidden_low, grad_pre, TN).astype(bf16).reshape(planes, CORES, rows, -1))
+        out_grad = [mm(c, grad_attn, TN).astype(bf16) for c in (ctx_own, ctx_far)]
+        out_grad = cores(either(core, *out_grad, 0).reshape(planes, CORES, rows, width))
+        vector = cores(vector.reshape(planes, CORES, 32, width))
+        joined = []
+        for which in range(2):
+            wide = in_grad[which]
+            wide = [wide[:, :, i * width : (i + 1) * width] for i in range(inner_blocks)]
+            joined.append(jnp.concatenate([down_grad[which]] + wide + [out_grad[which], vector[which]], axis=1))
     early = Halving(total(*joined), planes)
     early.send(0)
     progress = [early]
@@ -649,7 +747,7 @@
         if pair == pairs - 1:
             first_sums = Halving(weight_sums(grads), planes)
             first_sums.send(0)
-            sent = sent + first_sums.sent
+            sent = list(sent) + first_sums.sent
         grads.append(attend(pair, *sent, *(output if pair == 1 else ())))
     while len(progress) == 1:
         advance(grads[-1][0])
@@ -665,16 +763,15 @@
     last_sums.send(0)
     for step in range(last_sums.steps):
         for sums in (first_sums, last_sums):
-            sums.add()
+            sums.add(input_grad)
             if step + 1 < sums.steps:
                 sums.send(step + 1)
     qkv_sum = Spread(jnp.concatenate([first_sums.result(), last_sums.result()], axis=1), nseq)
     qkv_sum.add(*returned)
     input_grad = jnp.where(odd == 0, jnp.stack(returned), jnp.stack(returned[::-1]))[None].astype(f32)
-    early_total = early_sum.result()
+    early_total = early_sum.result(qkv_sum.keep)
     qkv_total = qkv_sum.result()
 
-    down_rows = down_grad[0].shape[1]
     down_final = early_total[:down_rows].astype(f32)
     wide = [early_total[down_rows + i * rows : down_rows + (i + 1) * rows] for i in range(inner_blocks)]
     in_final = jnp.concatenate(wide, axis=1).astype(f32)

time: 530 us -> 509 us (0.960)
  local copies, waits for them, and re-layouts: 53.9 us -> 27.4 us
  matrix products: 42.2 us -> 16 us
  waiting for transfers between devices: 140 us -> 160 us
  starting transfers between devices: 42.8 us -> 60.3 us
  other arithmetic: 36.3 us -> 27.1 us
  Pallas kernels: 178 us -> 186 us
    ppermute x2, waiting for transfers between devices: 0.01 us -> 27.6 us  [per_device(): lax.ppermute(result[i * run:(i + 1) * run], ('core', 'seq'), back[i])]
    dot_general x12 -> x8, matrix products: 42.2 us -> 16 us  [mm(): lax.dot_general(left, right, dims, preferred_element_type=jnp.float32)]
    pallas_call x0 -> x1, Pallas kernels: none -> 18.4 us  [gradients(): pl.pallas_call(functools.partial(gradients_kernel, rows), grid=(2 * chunk...]
    all_gather x1, waiting for transfers between devices: 6.28 us -> 20.5 us  [per_device(): w_down = lax.all_gather(ff_out_weight, fsdp, axis=0, tiled=True)]
    unnamed x147 -> x74, local copies, waits for them, and re-layouts: 25.6 us -> 14.9 us
    ppermute x12, waiting for transfers between devices: 76.9 us -> 66.8 us  [shift(): lax.ppermute(value, 'seq', [(i, (i + distance) % self.nseq) for i in rang...]
    squeeze x16 -> x13, local copies, waits for them, and re-layouts: 10.4 us -> 0.54 us  [pick(): return lax.dynamic_index_in_dim(value, which, axis, keepdims=False)]
    convert_element_type x13, other arithmetic: 14.1 us -> 7 us  [total(): (keep.astype(jnp.float32) + received.astype(jnp.float32)).astype(jnp.bflo...]
  transfers between devices with their start and end apart: 48 -> 45, of which waited for: 16 -> 18; matrix products, arithmetic and copies ran while one was open for 13% -> 9% of each run, Pallas kernels for 20% -> 20%
where the time goes in v5:
time: 509 us; the launch traced here: 501 us
  Pallas kernels  186 us (37%)
  waiting for transfers between devices  160 us (31%)
  starting transfers between devices  60.3 us (12%)
  local copies, waits for them, and re-layouts  27.4 us (5%)
  other arithmetic  27.1 us (5%)
  matrix products  16 us (3%)
  between operations  15.3 us (3%)
  blocking collectives  9.65 us (2%)
    ppermute x12, waiting for transfers between devices, shift(): lax.ppermute(value, 'seq', [(i, (i + distance) % self.nseq) for i in rang...  66.8 us
    pallas_call x3, Pallas kernels, attend_backward(): pl.pallas_call(functools.partial(backward_kernel, run, pair), out_shape=(...  64.6 us
    pallas_call x1, Pallas kernels, attend_forward(): pl.pallas_call(functools.partial(forward_kernel, run), out_shape=(jax.Sha...  55 us
    pallas_call x1, Pallas kernels, middle(): pl.pallas_call(middle_kernel, grid=(count // ROWS,), out_shape=(shape((co...  47.8 us
    ppermute x2, waiting for transfers between devices, per_device(): lax.ppermute(result[i * run:(i + 1) * run], ('core', 'seq'), back[i])  27.6 us
    ppermute x4, waiting for transfers between devices, spread(): lax.ppermute(h, ('core', 'seq'), r)  23.3 us
    all_gather x1, waiting for transfers between devices, per_device(): w_down = lax.all_gather(ff_out_weight, fsdp, axis=0, tiled=True)  20.5 us
    ppermute x12, waiting for transfers between devices, send(): lax.ppermute(out, 'xy', [(i, i ^ 1 << bit) for i in range(self.planes)])  18.4 us
  transfers between devices with their start and end apart: 45, of which 18 were waited for; matrix products, arithmetic and copies ran while one was open for 9% of the time, Pallas kernels for 20%

profile of v5, /device:TPU:9, one launch (start us, length us, event | category | flops | bytes accessed | tf_op | source)
XLA Modules:
  0.0 501.2 jit_solution(11023173132044241803)
XLA Ops:
  7.2 1.6 reshape.393
  14.6 4.5 collective-permute-start
  19.5 9.6 %all-gather.1 = bf16[8,12,96]{2,1,0:T(8,128)(2,1)S(1)} all-gather(bf16[1,12,96]{2,1,0:T(8,128)(2,1)S(1)} %bitcast.179), channel_id=2, replica_groups=mesh['xy'=4,'core'=2,'seq'=4] {'xy','core'}, dimensions={0}, use_global_device_ids=true | all-gather | bytes 20736 | tf_op jit(solution)/shard_map/all_gather | solution.py:664
  29.6 15.2 %collective-permute-done = bf16[512,768]{1,0:T(8,128)(2,1)} collective-permute-done((bf16[512,768]{1,0:T(8,128)(2,1)S(1)}, bf16[512,768]{1,0:T(8,128)(2,1)}, u32[]{:S(2)}, u32[]{:S(2)}) %collective-permute-start) | collective-permute-done | bytes 786464 | tf_op jit(solution)/shard_map/ppermute | solution.py:643
  45.1 8.1 %collective-permute-done.1 = bf16[512,768]{1,0:T(8,128)(2,1)} collective-permute-done((bf16[512,768]{1,0:T(8,128)(2,1)S(1)}, bf16[512,768]{1,0:T(8,128)(2,1)}, u32[]{:S(2)}, u32[]{:S(2)}) %collective-permute-start.1) | collective-permute-done | bytes 786464 | tf_op jit(solution)/shard_map/ppermute | solution.py:643
  53.5 2.8 pad_maximum_fusion.x_ref
  57.6 1.9 collective-permute-start.7
  59.5 2.7 collective-permute-start.8
  63.5 4.3 multiply_convert_fusion.1.own
  67.8 2.2 multiply_convert_fusion.sib
  70.4 55.0 %attend_forward.1 = (bf16[1024,384]{1,0:T(8,128)(2,1)S(1)}, bf16[1024,384]{1,0:T(8,128)(2,1)}, f32[6,8,2048]{2,1,0:T(8,128)S(1)}) custom-call(s32[1]{0:T(128)} %bitcast.13.mask_ref, s32[8]{0:T(128)S(1)} %bitcast.155, bf16[1024,1152]{1,0:T(8,128)(2,1)S(1)} %multiply_convert_fusion.1.own, bf16[1024,1152]{1,0:T(8,128)(2,1)S(1)} %multiply_convert_fusion.sib, ...), custom_call_target="tpu_custom_call" | custom-call | flops 1000000000 | bytes 1000000 | tf_op jit(solution)/shard_map/attend_forward/pallas_call | solution.py:145
  127.0 3.4 collective-permute-start.6
  130.4 2.6 pad_maximum_fusion.1.cot_ref
  133.0 20.5 %all-gather.13.cloned.1.call-done.w_down = bf16[3072,768]{1,0:T(8,128)(2,1)} async-done(((bf16[384,768]{1,0:T(8,128)(2,1)}), bf16[3072,768]{1,0:T(8,128)(2,1)}) %all-gather.13.cloned.1.call-update) | async-done | bytes 4718608 | tf_op jit(solution)/shard_map/all_gather | solution.py:671
  155.9 47.8 %middle.1 = (bf16[1024,768]{1,0:T(8,128)(2,1)S(1)}, bf16[1024,768]{1,0:T(8,128)(2,1)}, bf16[1024,3072]{1,0:T(8,128)(2,1)}, bf16[1024,768]{1,0:T(8,128)(2,1)}, bf...) custom-call(s32[1]{0:T(128)} %bitcast.core_ref, ...), custom_call_target="tpu_custom_call" | custom-call | flops 20000000000 | bytes 30000000 | tf_op jit(solution)/shard_map/middle/pallas_call | solution.py:404
  210.8 18.4 %gradients.1 = (bf16[4,896,768]{2,1,0:T(8,128)(2,1)}, bf16[4,896,768]{2,1,0:T(8,128)(2,1)}) custom-call(s32[1]{0:T(128)} %bitcast.core_ref, bf16[1024,3072]{1,0:T(8,128)(2,1)} %get-tuple-element.70.act_ref, bf16[1024,768]{1,0:T(8,128)(2,1)S(1)} %copy-done.12, bf16[1024,768]{1,0:T(8,128)(2,1)S(1)} %copy-done.13, ...), custom_call_target="tpu_custom_call" | custom-call | flops 11000000512 | bytes 30000000 | tf_op jit(solution)/shard_map/gradients/pallas_call | solution.py:506
  232.1 3.2 collective-permute-start.9
  235.5 3.5 collective-permute-start.12
  239.0 11.1 %collective-permute-done.10 = bf16[512,768]{1,0:T(8,128)(2,1)} collective-permute-done((bf16[512,768]{1,0:T(8,128)(2,1)}, bf16[512,768]{1,0:T(8,128)(2,1)}, u32[]{:S(2)}, u32[]{:S(2)}) %collective-permute-start.10) | collective-permute-done | bytes 786464 | tf_op jit(solution)/shard_map/ppermute | solution.py:688
  250.1 16.6 %collective-permute-done.9 = bf16[512,768]{1,0:T(8,128)(2,1)} collective-permute-done((bf16[512,768]{1,0:T(8,128)(2,1)}, bf16[512,768]{1,0:T(8,128)(2,1)}, u32[]{:S(2)}, u32[]{:S(2)}) %collective-permute-start.9) | collective-permute-done | bytes 786464 | tf_op jit(solution)/shard_map/ppermute | solution.py:688
  266.6 3.4 maximum_select_fusion
  270.0 5.5 %add_convert_fusion = bf16[4,896,768]{2,1,0:T(8,128)(2,1)S(1)} fusion(bf16[4,896,768]{2,1,0:T(8,128)(2,1)} %collective-permute-done.11, bf16[4,896,768]{2,1,0:T(8,128)(2,1)} %get-tuple-element.77), kind=kLoop, calls=%fused_computation | loop fusion | flops 11010048 | bytes 16515072 | tf_op jit(solution)/shard_map/convert_element_type | solution.py:559
  278.1 21.5 %attend_backward_0.1 = (bf16[1024,384]{1,0:T(8,128)(2,1)S(1)}, bf16[1024,384]{1,0:T(8,128)(2,1)S(1)}) custom-call(s32[1]{0:T(128)} %bitcast.13.mask_ref, s32[8]{0:T(128)S(1)} %bitcast.156, bf16[1024,1152]{1,0:T(8,128)(2,1)S(1)} %multiply_convert_fusion.1.own, bf16[1024,1152]{1,0:T(8,128)(2,1)S(1)} %copy-done.1, bf16[1024,384]{1,0:T(8,128)(2,1)S(1)} %copy-done.8, ...), custom_call_target="tpu_custom_call" | custom-call | flops 20000000000 | bytes 8000000 | tf_op jit(solution)/shard_map/attend_backward_0/pallas_call | solution.py:249
  300.6 21.3 %attend_backward_1.1 = (bf16[1024,384]{1,0:T(8,128)(2,1)S(1)}, bf16[1024,384]{1,0:T(8,128)(2,1)S(1)}) custom-call(s32[1]{0:T(128)} %bitcast.13.mask_ref, s32[8]{0:T(128)S(1)} %bitcast.157, bf16[1024,1152]{1,0:T(8,128)(2,1)S(1)} %multiply_convert_fusion.1.own, bf16[1024,1152]{1,0:T(8,128)(2,1)S(1)} %copy-done.1, bf16[1024,384]{1,0:T(8,128)(2,1)S(1)} %copy-done.8, ...), custom_call_target="tpu_custom_call" | custom-call | flops 20000000000 | bytes 8000000 | tf_op jit(solution)/shard_map/attend_backward_1/pallas_call | solution.py:249
  325.1 2.8 collective-permute-start.16
  332.5 3.8 collective-permute-done.16
  339.4 5.1 %collective-permute-start.36 = (bf16[224,768]{1,0:T(8,128)(2,1)S(1)}, bf16[224,768]{1,0:T(8,128)(2,1)S(1)}, u32[]{:S(2)}, u32[]{:S(2)}) collective-permute-start(bf16[224,768]{1,0:T(8,128)(2,1)S(1)} %get-tuple-element.138), channel_id=1, source_target_pairs={{0,2},{1,3},{2,0},{3,1},{4,6},{5,7},{6,4},{7,5},{8,10},{9,11},{10,... | collective-permute-start | bytes 1032200 | tf_op jit(solution)/shard_map/ppermute | solution.py:603
  344.5 21.7 %attend_backward_2.1 = (bf16[1024,384]{1,0:T(8,128)(2,1)S(1)}, bf16[1024,384]{1,0:T(8,128)(2,1)S(1)}) custom-call(s32[1]{0:T(128)} %bitcast.13.mask_ref, s32[8]{0:T(128)S(1)} %bitcast.158, bf16[1024,1152]{1,0:T(8,128)(2,1)S(1)} %multiply_convert_fusion.1.own, bf16[1024,1152]{1,0:T(8,128)(2,1)S(1)} %copy-done.1, bf16[1024,384]{1,0:T(8,128)(2,1)S(1)} %copy-done.8, ...), custom_call_target="tpu_custom_call" | custom-call | flops 20000000000 | bytes 8000000 | tf_op jit(solution)/shard_map/attend_backward_2/pallas_call | solution.py:249
  366.4 2.2 fusion.14
  368.6 2.7 collective-permute-start.17
  373.7 2.2 fusion.2
  375.9 2.6 collective-permute-start.22
  379.4 8.6 %collective-permute-done.22 = bf16[2,128,768]{2,1,0:T(8,128)(2,1)S(1)} collective-permute-done((bf16[2,128,768]{2,1,0:T(8,128)(2,1)S(1)}, bf16[2,128,768]{2,1,0:T(8,128)(2,1)S(1)}, u32[]{:S(2)}, u32[]{:S(2)}) %collective-permute-start.22) | collective-permute-done | bytes 393248 | tf_op jit(solution)/shard_map/ppermute | solution.py:584
  391.2 4.6 collective-permute-start.18
  396.0 2.1 collective-permute-done.24
  400.3 1.7 collective-permute-done.25
  403.1 2.6 collective-permute-start.29
  406.3 49.5 %collective-permute-done.28 = bf16[64,1152]{1,0:T(8,128)(2,1)S(1)} collective-permute-done((bf16[64,1152]{1,0:T(8,128)(2,1)S(1)}, bf16[64,1152]{1,0:T(8,128)(2,1)S(1)}, u32[]{:S(2)}, u32[]{:S(2)}) %collective-permute-start.28) | collective-permute-done | bytes 147488 | tf_op jit(solution)/shard_map/ppermute | solution.py:603
  455.8 3.1 collective-permute-start.39
  459.1 3.3 collective-permute-done.40
  462.3 6.5 %collective-permute-done.39 = bf16[224,768]{1,0:T(8,128)(2,1)S(1)} collective-permute-done((bf16[224,768]{1,0:T(8,128)(2,1)S(1)}, bf16[224,768]{1,0:T(8,128)(2,1)S(1)}, u32[]{:S(2)}, u32[]{:S(2)}) %collective-permute-start.39) | collective-permute-done | bytes 344096 | tf_op jit(solution)/shard_map/ppermute | solution.py:603
  468.8 3.7 collective-permute-done.38
  474.5 2.9 collective-permute-start.31
  477.4 4.0 collective-permute-start.32
  483.9 2.0 collective-permute-done.32
  485.9 1.9 collective-permute-done.33
  488.0 1.9 fusion.17
  492.9 1.6 reshape.422
  (267 shorter events, 56.3 us)
Async XLA Ops:
  7.2 56.3 %all-gather.7.cloned.1.call-start = ((), (), s32[]{:S(2)}) async-start(), calls=%async_computation | async-start | bytes 2211840 | tf_op jit(solution)/shard_map/all_gather | solution.py:660
  9.6 1.8 collective-permute-start.3
  12.3 120.7 %all-gather.9.cloned.1.call-start = ((), (), s32[]{:S(2)}) async-start(), calls=%async_computation.1 | async-start | bytes 1327104 | tf_op jit(solution)/shard_map/all_gather | solution.py:669
  13.0 120.0 %all-gather.11.cloned.1.call-start = ((), (), s32[]{:S(2)}) async-start(), calls=%async_computation.2 | async-start | bytes 5308416 | tf_op jit(solution)/shard_map/all_gather | solution.py:670
  13.7 139.7 %all-gather.13.cloned.1.call-start = ((), (), s32[]{:S(2)}) async-start(), calls=%async_computation.3 | async-start | bytes 5308416 | tf_op jit(solution)/shard_map/all_gather | solution.py:671
  14.6 30.2 %collective-permute-start = (bf16[512,768]{1,0:T(8,128)(2,1)S(1)}, bf16[512,768]{1,0:T(8,128)(2,1)}, u32[]{:S(2)}, u32[]{:S(2)}) collective-permute-start(bf16[512,768]{1,0:T(8,128)(2,1)S(1)} %get-tuple-element.129), channel_id=1, source_target_pairs={{0,0},{1,1},{2,4},{3,5},{4,2},{5,3},{6,6},{7,7},{8,8},{9,9},{10,12... | collective-permute-start | bytes 2359304 | tf_op jit(solution)/shard_map/ppermute | solution.py:643
  19.1 34.1 %collective-permute-start.1 = (bf16[512,768]{1,0:T(8,128)(2,1)S(1)}, bf16[512,768]{1,0:T(8,128)(2,1)}, u32[]{:S(2)}, u32[]{:S(2)}) collective-permute-start(bf16[512,768]{1,0:T(8,128)(2,1)S(1)} %get-tuple-element.130), channel_id=1, source_target_pairs={{0,1},{1,0},{2,5},{3,4},{4,3},{5,2},{6,7},{7,6},{8,9},{9,8},{10,13... | collective-permute-start | bytes 2359304 | tf_op jit(solution)/shard_map/ppermute | solution.py:643
  19.2 34.1 %collective-permute-start.2 = (s32[2,8]{1,0:T(2,128)S(1)}, s32[2,8]{1,0:T(2,128)S(1)}, u32[]{:S(2)}, u32[]{:S(2)}) collective-permute-start(s32[2,8]{1,0:T(2,128)S(1)} %bitcast.182), channel_id=1, source_target_pairs={{0,4},{4,0},{1,5},{5,1},{2,6},{6,2},{3,7},{7,3},{8,12},{12,8},{9,1... | collective-permute-start | bytes 200 | tf_op jit(solution)/shard_map/ppermute | solution.py:547
  44.8 17.4 %collective-permute-start.4 = (bf16[512,768]{1,0:T(8,128)(2,1)}, bf16[512,768]{1,0:T(8,128)(2,1)S(1)}, u32[]{:S(2)}, u32[]{:S(2)}) collective-permute-start(bf16[512,768]{1,0:T(8,128)(2,1)} %collective-permute-done), channel_id=1, source_target_pairs={{0,4},{4,0},{1,5},{5,1},{2,6},{6,2},{3,7},{7,3},{8,12},{12,8},{9,1... | collective-permute-start | bytes 2359304 | tf_op jit(solution)/shard_map/ppermute | solution.py:547
  53.2 9.1 %collective-permute-start.5 = (bf16[512,768]{1,0:T(8,128)(2,1)}, bf16[512,768]{1,0:T(8,128)(2,1)S(1)}, u32[]{:S(2)}, u32[]{:S(2)}) collective-permute-start(bf16[512,768]{1,0:T(8,128)(2,1)} %collective-permute-done.1), channel_id=1, source_target_pairs={{0,4},{4,0},{1,5},{5,1},{2,6},{6,2},{3,7},{7,3},{8,12},{12,8},{9,1... | collective-permute-start | bytes 2359304 | tf_op jit(solution)/shard_map/ppermute | solution.py:547
  57.6 72.7 %collective-permute-start.7 = (bf16[512,768]{1,0:T(8,128)(2,1)}, bf16[512,768]{1,0:T(8,128)(2,1)}, u32[]{:S(2)}, u32[]{:S(2)}) collective-permute-start(bf16[512,768]{1,0:T(8,128)(2,1)} %get-tuple-element.127), channel_id=1, source_target_pairs={{0,0},{1,1},{2,4},{3,5},{4,2},{5,3},{6,6},{7,7},{8,8},{9,9},{10,12... | collective-permute-start | bytes 2359304 | tf_op jit(solution)/shard_map/ppermute | solution.py:643
  59.5 70.8 %collective-permute-start.8 = (bf16[512,768]{1,0:T(8,128)(2,1)}, bf16[512,768]{1,0:T(8,128)(2,1)}, u32[]{:S(2)}, u32[]{:S(2)}) collective-permute-start(bf16[512,768]{1,0:T(8,128)(2,1)} %get-tuple-element.128), channel_id=1, source_target_pairs={{0,1},{1,0},{2,5},{3,4},{4,3},{5,2},{6,7},{7,6},{8,9},{9,8},{10,13... | collective-permute-start | bytes 2359304 | tf_op jit(solution)/shard_map/ppermute | solution.py:643
  70.1 55.3 %copy-start = (bf16[1024,1152]{1,0:T(8,128)(2,1)}, bf16[1024,1152]{1,0:T(8,128)(2,1)S(1)}, u32[]{:S(2)}) copy-start(bf16[1024,1152]{1,0:T(8,128)(2,1)S(1)} %multiply_convert_fusion.sib) | copy-start | bytes 7077892
  127.0 6.0 %collective-permute-start.6 = (bf16[1024,384]{1,0:T(8,128)(2,1)}, bf16[1024,384]{1,0:T(8,128)(2,1)}, u32[]{:S(2)}, u32[]{:S(2)}) collective-permute-start(bf16[1024,384]{1,0:T(8,128)(2,1)} %get-tuple-element.66.ctx_sib), channel_id=1, source_target_pairs={{0,4},{4,0},{1,5},{5,1},{2,6},{6,2},{3,7},{7,3},{8,12},{12,8},{9,1... | collective-permute-start | bytes 2359304 | tf_op jit(solution)/shard_map/ppermute | solution.py:547
  210.8 18.7 %copy-start.3 = (bf16[1024,768]{1,0:T(8,128)(2,1)S(1)}, bf16[1024,768]{1,0:T(8,128)(2,1)}, u32[]{:S(2)}) copy-start(bf16[1024,768]{1,0:T(8,128)(2,1)} %copy-done.2) | copy-start | bytes 4718596
  229.2 40.8 %collective-permute-start.11 = (bf16[4,896,768]{2,1,0:T(8,128)(2,1)}, bf16[4,896,768]{2,1,0:T(8,128)(2,1)}, u32[]{:S(2)}, u32[]{:S(2)}) collective-permute-start(bf16[4,896,768]{2,1,0:T(8,128)(2,1)} %get-tuple-element.78), channel_id=1, source_target_pairs={{0,4},{4,0},{1,5},{5,1},{2,6},{6,2},{3,7},{7,3},{8,12},{12,8},{9,1... | collective-permute-start | bytes 16515080 | tf_op jit(solution)/shard_map/ppermute | solution.py:547
  230.8 19.3 %collective-permute-start.10 = (bf16[512,768]{1,0:T(8,128)(2,1)}, bf16[512,768]{1,0:T(8,128)(2,1)}, u32[]{:S(2)}, u32[]{:S(2)}) collective-permute-start(bf16[512,768]{1,0:T(8,128)(2,1)} %get-tuple-element.126), channel_id=1, source_target_pairs={{1,0},{0,1},{5,2},{4,3},{3,4},{2,5},{7,6},{6,7},{9,8},{8,9},{13,10... | collective-permute-start | bytes 2359304 | tf_op jit(solution)/shard_map/ppermute | solution.py:688
  232.1 34.5 %collective-permute-start.9 = (bf16[512,768]{1,0:T(8,128)(2,1)}, bf16[512,768]{1,0:T(8,128)(2,1)}, u32[]{:S(2)}, u32[]{:S(2)}) collective-permute-start(bf16[512,768]{1,0:T(8,128)(2,1)} %get-tuple-element.125), channel_id=1, source_target_pairs={{0,0},{1,1},{4,2},{5,3},{2,4},{3,5},{6,6},{7,7},{8,8},{9,9},{12,10... | collective-permute-start | bytes 2359304 | tf_op jit(solution)/shard_map/ppermute | solution.py:688
  235.5 42.2 %collective-permute-start.12 = (bf16[1024,384]{1,0:T(8,128)(2,1)}, bf16[1024,384]{1,0:T(8,128)(2,1)S(1)}, u32[]{:S(2)}, u32[]{:S(2)}) collective-permute-start(bf16[1024,384]{1,0:T(8,128)(2,1)} %copy-done.9), channel_id=1, source_target_pairs={{0,4},{4,0},{1,5},{5,1},{2,6},{6,2},{3,7},{7,3},{8,12},{12,8},{9,1... | collective-permute-start | bytes 2359304 | tf_op jit(solution)/shard_map/ppermute | solution.py:547
  276.0 23.8 %collective-permute-start.14 = (bf16[2,448,768]{2,1,0:T(8,128)(2,1)S(1)}, bf16[2,448,768]{2,1,0:T(8,128)(2,1)S(1)}, u32[]{:S(2)}, u32[]{:S(2)}) collective-permute-start(bf16[2,448,768]{2,1,0:T(8,128)(2,1)S(1)} %dynamic-slice_bitcast_fusion), channel_id=1, source_target_pairs={{0,16},{8,24},{16,0},{24,8},{1,17},{9,25},{17,1},{25,9},{2,18},{10... | collective-permute-start | bytes 4128776 | tf_op jit(solution)/shard_map/ppermute | solution.py:584
  277.2 23.0 %collective-permute-start.13 = (bf16[2,448,768]{2,1,0:T(8,128)(2,1)S(1)}, bf16[2,448,768]{2,1,0:T(8,128)(2,1)S(1)}, u32[]{:S(2)}, u32[]{:S(2)}) collective-permute-start(bf16[2,448,768]{2,1,0:T(8,128)(2,1)S(1)} %dynamic-slice_bitcast_fusion.1), channel_id=1, source_target_pairs={{0,8},{8,0},{16,24},{24,16},{1,9},{9,1},{17,25},{25,17},{2,10},{10... | collective-permute-start | bytes 4128776 | tf_op jit(solution)/shard_map/ppermute | solution.py:584
  325.1 11.1 %collective-permute-start.16 = (bf16[448,768]{1,0:T(8,128)(2,1)S(1)}, bf16[448,768]{1,0:T(8,128)(2,1)S(1)}, u32[]{:S(2)}, u32[]{:S(2)}) collective-permute-start(bf16[448,768]{1,0:T(8,128)(2,1)S(1)} %dynamic-slice_bitcast_fusion.6), channel_id=1, source_target_pairs={{0,8},{8,0},{16,24},{24,16},{1,9},{9,1},{17,25},{25,17},{2,10},{10... | collective-permute-start | bytes 2064392 | tf_op jit(solution)/shard_map/ppermute | solution.py:584
  328.0 9.8 %collective-permute-start.15 = (bf16[448,768]{1,0:T(8,128)(2,1)S(1)}, bf16[448,768]{1,0:T(8,128)(2,1)S(1)}, u32[]{:S(2)}, u32[]{:S(2)}) collective-permute-start(bf16[448,768]{1,0:T(8,128)(2,1)S(1)} %dynamic-slice_bitcast_fusion.7), channel_id=1, source_target_pairs={{0,16},{8,24},{16,0},{24,8},{1,17},{9,25},{17,1},{25,9},{2,18},{10... | collective-permute-start | bytes 2064392 | tf_op jit(solution)/shard_map/ppermute | solution.py:584
  331.4 47.8 %collective-permute-start.20 = (bf16[2,128,768]{2,1,0:T(8,128)(2,1)S(1)}, bf16[2,128,768]{2,1,0:T(8,128)(2,1)S(1)}, u32[]{:S(2)}, u32[]{:S(2)}) collective-permute-start(bf16[2,128,768]{2,1,0:T(8,128)(2,1)S(1)} %dynamic-slice_bitcast_fusion.9), channel_id=1, source_target_pairs={{0,8},{8,0},{16,24},{24,16},{1,9},{9,1},{17,25},{25,17},{2,10},{10... | collective-permute-start | bytes 1179656 | tf_op jit(solution)/shard_map/ppermute | solution.py:584
  339.4 36.6 %collective-permute-start.35 = (bf16[224,768]{1,0:T(8,128)(2,1)S(1)}, bf16[224,768]{1,0:T(8,128)(2,1)S(1)}, u32[]{:S(2)}, u32[]{:S(2)}) collective-permute-start(bf16[224,768]{1,0:T(8,128)(2,1)S(1)} %get-tuple-element.137), channel_id=1, source_target_pairs={{0,1},{1,2},{2,3},{3,0},{4,5},{5,6},{6,7},{7,4},{8,9},{9,10},{10,1... | collective-permute-start | bytes 1032200 | tf_op jit(solution)/shard_map/ppermute | solution.py:603
  339.4 39.1 %collective-permute-start.36 = (bf16[224,768]{1,0:T(8,128)(2,1)S(1)}, bf16[224,768]{1,0:T(8,128)(2,1)S(1)}, u32[]{:S(2)}, u32[]{:S(2)}) collective-permute-start(bf16[224,768]{1,0:T(8,128)(2,1)S(1)} %get-tuple-element.138), channel_id=1, source_target_pairs={{0,2},{1,3},{2,0},{3,1},{4,6},{5,7},{6,4},{7,5},{8,10},{9,11},{10,... | collective-permute-start | bytes 1032200 | tf_op jit(solution)/shard_map/ppermute | solution.py:603
  344.5 21.9 %copy-start.34 = (bf16[768,1152]{1,0:T(8,128)(2,1)S(1)}, bf16[768,1152]{1,0:T(8,128)(2,1)}, u32[]{:S(2)}) copy-start(bf16[768,1152]{1,0:T(8,128)(2,1)} %all-gather.7.cloned.1.call-done) | copy-start | bytes 5308420
  344.5 34.0 %collective-permute-start.37 = (bf16[224,768]{1,0:T(8,128)(2,1)S(1)}, bf16[224,768]{1,0:T(8,128)(2,1)S(1)}, u32[]{:S(2)}, u32[]{:S(2)}) collective-permute-start(bf16[224,768]{1,0:T(8,128)(2,1)S(1)} %get-tuple-element.136), channel_id=1, source_target_pairs={{0,3},{1,0},{2,1},{3,2},{4,7},{5,4},{6,5},{7,6},{8,11},{9,8},{10,9... | collective-permute-start | bytes 1032200 | tf_op jit(solution)/shard_map/ppermute | solution.py:603
  368.6 9.9 %collective-permute-start.17 = (bf16[1024,768]{1,0:T(8,128)(2,1)S(1)}, bf16[1024,768]{1,0:T(8,128)(2,1)S(1)}, u32[]{:S(2)}, u32[]{:S(2)}) collective-permute-start(bf16[1024,768]{1,0:T(8,128)(2,1)S(1)} %fusion.14), channel_id=1, source_target_pairs={{0,4},{4,0},{1,5},{5,1},{2,6},{6,2},{3,7},{7,3},{8,12},{12,8},{9,1... | collective-permute-start | bytes 4718600 | tf_op jit(solution)/shard_map/ppermute | solution.py:547
  375.9 12.1 %collective-permute-start.22 = (bf16[2,128,768]{2,1,0:T(8,128)(2,1)S(1)}, bf16[2,128,768]{2,1,0:T(8,128)(2,1)S(1)}, u32[]{:S(2)}, u32[]{:S(2)}) collective-permute-start(bf16[2,128,768]{2,1,0:T(8,128)(2,1)S(1)} %dynamic-slice_bitcast_fusion.8), channel_id=1, source_target_pairs={{0,16},{8,24},{16,0},{24,8},{1,17},{9,25},{17,1},{25,9},{2,18},{10... | collective-permute-start | bytes 1179656 | tf_op jit(solution)/shard_map/ppermute | solution.py:584
  379.3 16.5 %collective-permute-start.21 = (bf16[128,768]{1,0:T(8,128)(2,1)S(1)}, bf16[128,768]{1,0:T(8,128)(2,1)S(1)}, u32[]{:S(2)}, u32[]{:S(2)}) collective-permute-start(bf16[128,768]{1,0:T(8,128)(2,1)S(1)} %dynamic-slice_bitcast_fusion.15), channel_id=1, source_target_pairs={{0,16},{8,24},{16,0},{24,8},{1,17},{9,25},{17,1},{25,9},{2,18},{10... | collective-permute-start | bytes 589832 | tf_op jit(solution)/shard_map/ppermute | solution.py:584
  388.1 7.7 %collective-permute-start.23 = (bf16[128,768]{1,0:T(8,128)(2,1)S(1)}, bf16[128,768]{1,0:T(8,128)(2,1)S(1)}, u32[]{:S(2)}, u32[]{:S(2)}) collective-permute-start(bf16[128,768]{1,0:T(8,128)(2,1)S(1)} %dynamic-slice_bitcast_fusion.14), channel_id=1, source_target_pairs={{0,8},{8,0},{16,24},{24,16},{1,9},{9,1},{17,25},{25,17},{2,10},{10... | collective-permute-start | bytes 589832 | tf_op jit(solution)/shard_map/ppermute | solution.py:584
  389.5 8.6 %collective-permute-start.24 = (bf16[2,128,384]{2,1,0:T(8,128)(2,1)S(1)}, bf16[2,128,384]{2,1,0:T(8,128)(2,1)S(1)}, u32[]{:S(2)}, u32[]{:S(2)}) collective-permute-start(bf16[2,128,384]{2,1,0:T(8,128)(2,1)S(1)} %dynamic-slice_bitcast_fusion.13), channel_id=1, source_target_pairs={{0,8},{8,0},{16,24},{24,16},{1,9},{9,1},{17,25},{25,17},{2,10},{10... | collective-permute-start | bytes 589832 | tf_op jit(solution)/shard_map/ppermute | solution.py:584
  389.9 9.0 %collective-permute-start.26 = (bf16[2,128,384]{2,1,0:T(8,128)(2,1)S(1)}, bf16[2,128,384]{2,1,0:T(8,128)(2,1)S(1)}, u32[]{:S(2)}, u32[]{:S(2)}) collective-permute-start(bf16[2,128,384]{2,1,0:T(8,128)(2,1)S(1)} %dynamic-slice_bitcast_fusion.12), channel_id=1, source_target_pairs={{0,16},{8,24},{16,0},{24,8},{1,17},{9,25},{17,1},{25,9},{2,18},{10... | collective-permute-start | bytes 589832 | tf_op jit(solution)/shard_map/ppermute | solution.py:584
  391.2 64.6 %collective-permute-start.18 = (bf16[512,768]{1,0:T(8,128)(2,1)S(1)}, bf16[512,768]{1,0:T(8,128)(2,1)S(1)}, u32[]{:S(2)}, u32[]{:S(2)}) collective-permute-start(bf16[512,768]{1,0:T(8,128)(2,1)S(1)} %get-tuple-element.123), channel_id=1, source_target_pairs={{0,0},{1,1},{4,2},{5,3},{2,4},{3,5},{6,6},{7,7},{8,8},{9,9},{12,10... | collective-permute-start | bytes 2359304 | tf_op jit(solution)/shard_map/ppermute | solution.py:761
  395.8 63.1 %collective-permute-start.19 = (bf16[512,768]{1,0:T(8,128)(2,1)S(1)}, bf16[512,768]{1,0:T(8,128)(2,1)S(1)}, u32[]{:S(2)}, u32[]{:S(2)}) collective-permute-start(bf16[512,768]{1,0:T(8,128)(2,1)S(1)} %get-tuple-element.124), channel_id=1, source_target_pairs={{1,0},{0,1},{5,2},{4,3},{3,4},{2,5},{7,6},{6,7},{9,8},{8,9},{13,10... | collective-permute-start | bytes 2359304 | tf_op jit(solution)/shard_map/ppermute | solution.py:761
  398.2 3.8 collective-permute-start.25
  399.0 3.8 collective-permute-start.27
  403.0 52.8 %collective-permute-start.28 = (bf16[64,1152]{1,0:T(8,128)(2,1)S(1)}, bf16[64,1152]{1,0:T(8,128)(2,1)S(1)}, u32[]{:S(2)}, u32[]{:S(2)}) collective-permute-start(bf16[64,1152]{1,0:T(8,128)(2,1)S(1)} %get-tuple-element.145), channel_id=1, source_target_pairs={{0,1},{1,2},{2,3},{3,0},{4,5},{5,6},{6,7},{7,4},{8,9},{9,10},{10,1... | collective-permute-start | bytes 442376 | tf_op jit(solution)/shard_map/ppermute | solution.py:603
  403.1 55.8 %collective-permute-start.29 = (bf16[64,1152]{1,0:T(8,128)(2,1)S(1)}, bf16[64,1152]{1,0:T(8,128)(2,1)S(1)}, u32[]{:S(2)}, u32[]{:S(2)}) collective-permute-start(bf16[64,1152]{1,0:T(8,128)(2,1)S(1)} %get-tuple-element.147), channel_id=1, source_target_pairs={{0,2},{1,3},{2,0},{3,1},{4,6},{5,7},{6,4},{7,5},{8,10},{9,11},{10,... | collective-permute-start | bytes 442376 | tf_op jit(solution)/shard_map/ppermute | solution.py:603
  405.7 53.2 %collective-permute-start.30 = (bf16[64,1152]{1,0:T(8,128)(2,1)S(1)}, bf16[64,1152]{1,0:T(8,128)(2,1)S(1)}, u32[]{:S(2)}, u32[]{:S(2)}) collective-permute-start(bf16[64,1152]{1,0:T(8,128)(2,1)S(1)} %get-tuple-element.146), channel_id=1, source_target_pairs={{0,3},{1,0},{2,1},{3,2},{4,7},{5,4},{6,5},{7,6},{8,11},{9,8},{10,9... | collective-permute-start | bytes 442376 | tf_op jit(solution)/shard_map/ppermute | solution.py:603
  455.8 6.5 %collective-permute-start.40 = (bf16[224,768]{1,0:T(8,128)(2,1)S(1)}, bf16[224,768]{1,0:T(8,128)(2,1)S(1)}, u32[]{:S(2)}, u32[]{:S(2)}) collective-permute-start(bf16[224,768]{1,0:T(8,128)(2,1)S(1)} %get-tuple-element.118), channel_id=1, source_target_pairs={{0,3},{1,0},{2,1},{3,2},{4,7},{5,4},{6,5},{7,6},{8,11},{9,8},{10,9... | collective-permute-start | bytes 1032200 | tf_op jit(solution)/shard_map/ppermute | solution.py:603
  455.8 13.0 %collective-permute-start.39 = (bf16[224,768]{1,0:T(8,128)(2,1)S(1)}, bf16[224,768]{1,0:T(8,128)(2,1)S(1)}, u32[]{:S(2)}, u32[]{:S(2)}) collective-permute-start(bf16[224,768]{1,0:T(8,128)(2,1)S(1)} %get-tuple-element.118), channel_id=1, source_target_pairs={{0,2},{1,3},{2,0},{3,1},{4,6},{5,7},{6,4},{7,5},{8,10},{9,11},{10,... | collective-permute-start | bytes 1032200 | tf_op jit(solution)/shard_map/ppermute | solution.py:603
  458.9 13.6 %collective-permute-start.38 = (bf16[224,768]{1,0:T(8,128)(2,1)S(1)}, bf16[224,768]{1,0:T(8,128)(2,1)S(1)}, u32[]{:S(2)}, u32[]{:S(2)}) collective-permute-start(bf16[224,768]{1,0:T(8,128)(2,1)S(1)} %get-tuple-element.118), channel_id=1, source_target_pairs={{0,1},{1,2},{2,3},{3,0},{4,5},{5,6},{6,7},{7,4},{8,9},{9,10},{10,1... | collective-permute-start | bytes 1032200 | tf_op jit(solution)/shard_map/ppermute | solution.py:603
  474.5 9.4 %collective-permute-start.31 = (bf16[64,1152]{1,0:T(8,128)(2,1)S(1)}, bf16[64,1152]{1,0:T(8,128)(2,1)S(1)}, u32[]{:S(2)}, u32[]{:S(2)}) collective-permute-start(bf16[64,1152]{1,0:T(8,128)(2,1)S(1)} %get-tuple-element.120), channel_id=1, source_target_pairs={{0,1},{1,2},{2,3},{3,0},{4,5},{5,6},{6,7},{7,4},{8,9},{9,10},{10,1... | collective-permute-start | bytes 442376 | tf_op jit(solution)/shard_map/ppermute | solution.py:603
  477.4 8.5 %collective-permute-start.32 = (bf16[64,1152]{1,0:T(8,128)(2,1)S(1)}, bf16[64,1152]{1,0:T(8,128)(2,1)S(1)}, u32[]{:S(2)}, u32[]{:S(2)}) collective-permute-start(bf16[64,1152]{1,0:T(8,128)(2,1)S(1)} %get-tuple-element.120), channel_id=1, source_target_pairs={{0,2},{1,3},{2,0},{3,1},{4,6},{5,7},{6,4},{7,5},{8,10},{9,11},{10,... | collective-permute-start | bytes 442376 | tf_op jit(solution)/shard_map/ppermute | solution.py:603
  481.4 6.4 %collective-permute-start.33 = (bf16[64,1152]{1,0:T(8,128)(2,1)S(1)}, bf16[64,1152]{1,0:T(8,128)(2,1)S(1)}, u32[]{:S(2)}, u32[]{:S(2)}) collective-permute-start(bf16[64,1152]{1,0:T(8,128)(2,1)S(1)} %get-tuple-element.120), channel_id=1, source_target_pairs={{0,3},{1,0},{2,1},{3,2},{4,7},{5,4},{6,5},{7,6},{8,11},{9,8},{10,9... | collective-permute-start | bytes 442376 | tf_op jit(solution)/shard_map/ppermute | solution.py:603
  487.9 2.5 collective-permute-start.34
  (33 other events, 97.1 us)
Sparse Core Ops, SparseCore 0:
  12.4 33.2 all-gather.6
  47.6 24.5 all-gather.8
  74.0 38.8 all-gather.10
  114.7 38.7 all-gather.12

commit v6 on v5

--- a/solution.py
+++ b/solution.py
@@ -300,26 +300,42 @@
 
 
 def middle_kernel(
-    core_ref, x_ref, near_ref, far_ref, cot_ref, vec_ref, in_bias_ref, w_out, w_in, w_down,
+    core_ref, x_ref, near_ref, far_ref, cot_ref, vec_ref, in_bias_ref, packed,
     result_ref, low_ref, act_ref, grad_down_ref, grad_pre_ref, grad_one_ref, grad_attn_ref, dnear_ref, dfar_ref,
     sums_ref, in_sums_ref, wo, wi, wd, slope, acc, sums, in_sums, sems
 ):
     f32, bf16 = jnp.float32, jnp.bfloat16
     mine = near_ref.shape[1]
-    chunks = w_in.shape[1] // CHUNK
+    chunks = wi.shape[0]
     step = pl.program_id(0)
     core = core_ref[0]
+    shards = packed.shape[0]
+    rows = packed.shape[1] // (2 * chunks + 1)
     copies = []
-    for place in range(2):
-        which = core if place == 0 else 1 - core
-        rows = pl.multiple_of(which * mine, mine)
-        copies.append(pltpu.make_async_copy(w_out.at[pl.ds(rows, mine), :], wo.at[pl.ds(place * mine, mine), :], sems.at[place]))
+
+    def load(shard, at, count, target):
+        copies.append(pltpu.make_async_copy(packed.at[shard, pl.ds(at, count), :], target, sems.at[len(copies)]))
+
+    if shards == 1:
+        for place in range(2):
+            which = core if place == 0 else 1 - core
+            load(0, pl.multiple_of(2 * chunks * rows + which * mine, 16), mine, wo.at[pl.ds(place * mine, mine), :])
+    else:
+        for place in range(2):
+            which = core if place == 0 else 1 - core
+            for part in range(shards // 2):
+                target = wo.at[pl.ds(place * mine + part * rows, rows), :]
+                load(which * (shards // 2) + part, 2 * chunks * rows, rows, target)
+    outs = len(copies)
     for chunk in range(chunks):
-        columns = pl.ds(chunk * CHUNK, CHUNK)
-        copies.append(pltpu.make_async_copy(w_in.at[:, columns], wi.at[chunk], sems.at[2 + chunk]))
+        for shard in range(shards):
+            load(shard, (chunks + chunk) * rows, rows, wi.at[chunk, pl.ds(shard * rows, rows), :])
     for chunk in range(chunks):
-        columns = pl.ds(chunk * CHUNK, CHUNK)
-        copies.append(pltpu.make_async_copy(w_down.at[columns, :], wd.at[chunk], sems.at[2 + chunks + chunk]))
+        for shard in range(shards):
+            first = shard * chunks * rows
+            low, high = max(first, chunk * CHUNK), min(first + chunks * rows, (chunk + 1) * CHUNK)
+            if low < high:
+                load(shard, low - first, high - low, wd.at[chunk, pl.ds(low - chunk * CHUNK, high - low), :])
 
     @pl.when(step == 0)
     def _():
@@ -327,7 +343,7 @@
             copy.start()
         sums[...] = jnp.zeros_like(sums)
         in_sums[...] = jnp.zeros_like(in_sums)
-        for copy in copies[:2]:
+        for copy in copies[:outs]:
             copy.wait()
 
     bias_out, gain_one, shift_one, bias_down, gain_two, shift_two = [vec_ref[i : i + 1, :] for i in range(6)]
@@ -339,7 +355,7 @@
 
     @pl.when(step == 0)
     def _():
-        for copy in copies[2:]:
+        for copy in copies[outs:]:
             copy.wait()
 
     @pl.loop(0, chunks)
@@ -391,9 +407,9 @@
         in_sums_ref[...] = jnp.sum(in_sums[...], axis=0, keepdims=True)
 
 
-def middle(core, x, near, far, cot, vec, in_bias, w_out, w_in, w_down):
+def middle(core, x, near, far, cot, vec, in_bias, packed):
     count, width = x.shape
-    hidden = w_in.shape[1]
+    hidden = in_bias.shape[1]
     mine = near.shape[1]
     chunks = hidden // CHUNK
     f32, bf16 = jnp.float32, jnp.bfloat16
@@ -412,7 +428,7 @@
         ),
         in_specs=[
             pl.BlockSpec(memory_space=pltpu.SMEM), block(width), block(mine), block(mine), block(width),
-            whole(8, width), whole(1, hidden), any_spec, any_spec, any_spec,
+            whole(8, width), whole(1, hidden), any_spec,
         ],
         out_specs=(
             block(width), block(width), block(hidden), block(width), block(hidden), block(width), block(width),
@@ -426,12 +442,12 @@
             pltpu.VMEM((ROWS, width), f32),
             pltpu.VMEM((6, 8, width), f32),
             pltpu.VMEM((8, hidden), f32),
-            pltpu.SemaphoreType.DMA((2 + 2 * chunks,)),
+            pltpu.SemaphoreType.DMA(((2 * chunks + 1) * max(packed.shape[0], 2),)),
         ],
         compiler_params=pltpu.CompilerParams(vmem_limit_bytes=48 << 20),
         cost_estimate=pl.CostEstimate(flops=20_000_000_000, bytes_accessed=30_000_000, transcendentals=0),
         name="middle",
-    )(core, x, near, far, cot, vec, in_bias, w_out, w_in, w_down)
+    )(core, x, near, far, cot, vec, in_bias, packed)
 
 
 def gradients_kernel(
@@ -666,9 +682,12 @@
     vectors = jnp.moveaxis(vectors[:, :8], 0, 1).reshape(8, width)
     bias_q, bias_v = vectors[0], vectors[1]
     norms = jnp.concatenate([vectors[2:], jnp.zeros((2, width), f32)])
-    w_out = lax.all_gather(out_weight, fsdp, axis=0, tiled=True)
-    w_in = lax.all_gather(ff_in_weight, fsdp, axis=0, tiled=True)
-    w_down = lax.all_gather(ff_out_weight, fsdp, axis=0, tiled=True)
+    wide = [ff_in_weight[:, i * width : (i + 1) * width] for i in range(inner)]
+    packed = lax.all_gather(jnp.concatenate([ff_out_weight] + wide + [out_weight]), fsdp, axis=0, tiled=False)
+    if rows % 16:
+        parts = [packed[:, : inner * rows].reshape(-1, width)]
+        parts += [packed[:, (inner + i) * rows : (inner + i + 1) * rows].reshape(width, width) for i in range(inner + 1)]
+        packed = jnp.concatenate(parts)[None]
 
     own_slice = lambda v: lax.dynamic_slice_in_dim(v, core * mine, mine, 0).reshape(pairs, LANES)
     one = jnp.ones((pairs, LANES), f32)
@@ -680,9 +699,9 @@
     ctx_own, ctx_sib, lse = attend_forward(mask, ends, *projected, seg_col, seg_row, run)
     ctx_far = swap(ctx_sib)
 
-    cot = jnp.concatenate(spread(after(out_cotangent, x_own)))
+    cot = jnp.concatenate(spread(after(out_cotangent, *projected)))
     result, hidden_low, act_low, grad_down, grad_pre, grad_one, grad_attn, dctx_own, dctx_far, sums, in_sums = middle(
-        core.astype(jnp.int32)[None], x_own, ctx_own, ctx_far, cot, norms, bias_in, w_out, w_in, w_down
+        core.astype(jnp.int32)[None], x_own, ctx_own, ctx_far, cot, norms, bias_in, packed
     )
     dctx_far = swap(dctx_far)
     output = [lax.ppermute(result[i * run : (i + 1) * run], ("core", "seq"), back[i]) for i in range(2)]
@@ -732,9 +751,7 @@
             pair, held, ends, *projected, ctx_own, ctx_sib, dctx_own, dctx_far, seg_col, seg_row, lse, run
         )
 
-    def weight_sums(grads):
-        near = jnp.concatenate([g[0] for g in grads], axis=1)
-        far = jnp.concatenate([g[1] for g in grads], axis=1)
+    def weight_sums(near, far):
         matrix = (mm(x_own, near, TN) + mm(x_sib, far, TN)).astype(bf16)
         column = (jnp.sum(near.astype(f32), axis=0) + jnp.sum(far.astype(f32), axis=0)).astype(bf16)
         column = jnp.pad(column[None], ((0, 63), (0, 0)))
@@ -744,10 +761,6 @@
     grads = [attend(0, *early.sent)]
     for pair in range(1, pairs):
         sent = advance(grads[-1][0])
-        if pair == pairs - 1:
-            first_sums = Halving(weight_sums(grads), planes)
-            first_sums.send(0)
-            sent = list(sent) + first_sums.sent
         grads.append(attend(pair, *sent, *(output if pair == 1 else ())))
     while len(progress) == 1:
         advance(grads[-1][0])
@@ -759,14 +772,11 @@
     early_sum.add(grads[-1][0])
     input_grad = (grad_one + mm(near, w_mine, NT) + grad_far.astype(f32)).astype(bf16)
     returned = [lax.ppermute(input_grad[i * run : (i + 1) * run], ("core", "seq"), back[i]) for i in range(2)]
-    last_sums = Halving(after(weight_sums(grads[-1:]), input_grad), planes)
-    last_sums.send(0)
-    for step in range(last_sums.steps):
-        for sums in (first_sums, last_sums):
-            sums.add(input_grad)
-            if step + 1 < sums.steps:
-                sums.send(step + 1)
-    qkv_sum = Spread(jnp.concatenate([first_sums.result(), last_sums.result()], axis=1), nseq)
+    qkv_halves = Halving(after(weight_sums(near, far), input_grad), planes)
+    for step in range(qkv_halves.steps):
+        qkv_halves.send(step)
+        qkv_halves.add(input_grad)
+    qkv_sum = Spread(qkv_halves.result(), nseq)
     qkv_sum.add(*returned)
     input_grad = jnp.where(odd == 0, jnp.stack(returned), jnp.stack(returned[::-1]))[None].astype(f32)
     early_total = early_sum.result(qkv_sum.keep)

time: 509 us -> 473 us (0.929)
  Pallas kernels: 186 us -> 157 us
  waiting for transfers between devices: 160 us -> 135 us
  starting transfers between devices: 60.3 us -> 74.3 us
  local copies, waits for them, and re-layouts: 27.4 us -> 33.5 us
    ppermute x12, waiting for transfers between devices: 66.8 us -> 16 us  [shift(): lax.ppermute(value, 'seq', [(i, (i + distance) % self.nseq) for i in rang...]
    ppermute x2, waiting for transfers between devices: 0.01 us -> 39.1 us  [per_device(): lax.ppermute(input_grad[i * run:(i + 1) * run], ('core', 'seq'), back[i])]
    all_gather x3 -> x1, waiting for transfers between devices: 20.5 us -> 0.01 us  [per_device(): lax.all_gather(jnp.concatenate([ff_out_weight] + wide + [out_weight]), fs...]
    ppermute x2, starting transfers between devices: 4.52 us -> 21.5 us  [per_device(): lax.ppermute(result[i * run:(i + 1) * run], ('core', 'seq'), back[i])]
    pallas_call x3, Pallas kernels: 64.6 us -> 49 us  [attend_backward(): pl.pallas_call(functools.partial(backward_kernel, run, pair), out_shape=(...]
    pallas_call x1, Pallas kernels: 55 us -> 41.4 us  [attend_forward(): pl.pallas_call(functools.partial(forward_kernel, run), out_shape=(jax.Sha...]
    ppermute x12 -> x8, waiting for transfers between devices: 18.4 us -> 23.1 us  [send(): lax.ppermute(out, 'xy', [(i, i ^ 1 << bit) for i in range(self.planes)])]
    unnamed x74 -> x91, local copies, waits for them, and re-layouts: 14.9 us -> 19.2 us
  transfers between devices with their start and end apart: 45 -> 39, of which waited for: 18 -> 19; matrix products, arithmetic and copies ran while one was open for 9% -> 10% of each run, Pallas kernels for 20% -> 19%
where the time goes in v6:
time: 473 us; the launch traced here: 467 us
  Pallas kernels  157 us (33%)
  waiting for transfers between devices  135 us (29%)
  starting transfers between devices  74.3 us (16%)
  local copies, waits for them, and re-layouts  33.5 us (7%)
  other arithmetic  24.6 us (5%)
  matrix products  17.1 us (4%)
  between operations  15.7 us (3%)
  blocking collectives  9.52 us (2%)
    pallas_call x3, Pallas kernels, attend_backward(): pl.pallas_call(functools.partial(backward_kernel, run, pair), out_shape=(...  49 us
    pallas_call x1, Pallas kernels, middle(): pl.pallas_call(middle_kernel, grid=(count // ROWS,), out_shape=(shape((co...  48.8 us
    pallas_call x1, Pallas kernels, attend_forward(): pl.pallas_call(functools.partial(forward_kernel, run), out_shape=(jax.Sha...  41.4 us
    ppermute x2, waiting for transfers between devices, per_device(): lax.ppermute(input_grad[i * run:(i + 1) * run], ('core', 'seq'), back[i])  39.1 us
    ppermute x2, waiting for transfers between devices, per_device(): lax.ppermute(result[i * run:(i + 1) * run], ('core', 'seq'), back[i])  30.8 us
    ppermute x4, waiting for transfers between devices, spread(): lax.ppermute(h, ('core', 'seq'), r)  23.8 us
    ppermute x8, waiting for transfers between devices, send(): lax.ppermute(out, 'xy', [(i, i ^ 1 << bit) for i in range(self.planes)])  23.1 us
    ppermute x2, starting transfers between devices, per_device(): lax.ppermute(result[i * run:(i + 1) * run], ('core', 'seq'), back[i])  21.5 us
  transfers between devices with their start and end apart: 39, of which 19 were waited for; matrix products, arithmetic and copies ran while one was open for 10% of the time, Pallas kernels for 19%

profile of v6, /device:TPU:9, one launch (start us, length us, event | category | flops | bytes accessed | tf_op | source)
XLA Modules:
  0.0 466.8 jit_solution(6166893834799280833)
XLA Ops:
  7.2 1.6 reshape.360
  15.8 4.5 collective-permute-start
  20.6 9.5 %all-gather.2 = bf16[8,12,96]{2,1,0:T(8,128)(2,1)S(1)} all-gather(bf16[1,12,96]{2,1,0:T(8,128)(2,1)S(1)} %bitcast.148), channel_id=2, replica_groups=mesh['xy'=4,'core'=2,'seq'=4] {'xy','core'}, dimensions={0}, use_global_device_ids=true | all-gather | bytes 20736 | tf_op jit(solution)/shard_map/all_gather | solution.py:680
  30.2 15.7 %collective-permute-done = bf16[512,768]{1,0:T(8,128)(2,1)S(1)} collective-permute-done((bf16[512,768]{1,0:T(8,128)(2,1)S(1)}, bf16[512,768]{1,0:T(8,128)(2,1)S(1)}, u32[]{:S(2)}, u32[]{:S(2)}) %collective-permute-start) | collective-permute-done | bytes 786464 | tf_op jit(solution)/shard_map/ppermute | solution.py:659
  46.4 8.1 %collective-permute-done.1 = bf16[512,768]{1,0:T(8,128)(2,1)S(1)} collective-permute-done((bf16[512,768]{1,0:T(8,128)(2,1)}, bf16[512,768]{1,0:T(8,128)(2,1)S(1)}, u32[]{:S(2)}, u32[]{:S(2)}) %collective-permute-start.1) | collective-permute-done | bytes 786464 | tf_op jit(solution)/shard_map/ppermute | solution.py:659
  58.2 4.5 multiply_convert_fusion.sib
  62.7 2.2 multiply_convert_fusion.1.own
  65.1 2.2 collective-permute-start.7
  67.3 2.2 collective-permute-start.8
  70.0 41.4 %attend_forward.1 = (bf16[1024,384]{1,0:T(8,128)(2,1)S(1)}, bf16[1024,384]{1,0:T(8,128)(2,1)S(1)}, f32[6,8,2048]{2,1,0:T(8,128)S(1)}) custom-call(s32[1]{0:T(128)} %bitcast.13.mask_ref, s32[8]{0:T(128)S(1)} %bitcast.129, bf16[1024,1152]{1,0:T(8,128)(2,1)S(1)} %multiply_convert_fusion.1.own, bf16[1024,1152]{1,0:T(8,128)(2,1)S(1)} %multiply_convert_fusion.sib, ...), custom_call_target="tpu_custom_call" | custom-call | flops 1000000000 | bytes 1000000 | tf_op jit(solution)/shard_map/attend_forward/pallas_call | solution.py:145
  117.6 48.8 %middle.1 = (bf16[1024,768]{1,0:T(8,128)(2,1)S(1)}, bf16[1024,768]{1,0:T(8,128)(2,1)}, bf16[1024,3072]{1,0:T(8,128)(2,1)}, bf16[1024,768]{1,0:T(8,128)(2,1)}, bf...) custom-call(s32[1]{0:T(128)} %bitcast.core_ref, ...), custom_call_target="tpu_custom_call" | custom-call | flops 20000000000 | bytes 30000000 | tf_op jit(solution)/shard_map/middle/pallas_call | solution.py:420
  174.7 18.1 %gradients.1 = (bf16[4,896,768]{2,1,0:T(8,128)(2,1)}, bf16[4,896,768]{2,1,0:T(8,128)(2,1)}) custom-call(s32[1]{0:T(128)} %bitcast.core_ref, bf16[1024,3072]{1,0:T(8,128)(2,1)} %get-tuple-element.66.act_ref, bf16[1024,768]{1,0:T(8,128)(2,1)S(1)} %copy-done.16, bf16[1024,768]{1,0:T(8,128)(2,1)S(1)} %copy-done.17, ...), custom_call_target="tpu_custom_call" | custom-call | flops 11000000512 | bytes 30000000 | tf_op jit(solution)/shard_map/gradients/pallas_call | solution.py:522
  194.3 18.1 %collective-permute-start.10 = (bf16[512,768]{1,0:T(8,128)(2,1)}, bf16[512,768]{1,0:T(8,128)(2,1)}, u32[]{:S(2)}, u32[]{:S(2)}) collective-permute-start(bf16[512,768]{1,0:T(8,128)(2,1)} %get-tuple-element.120), channel_id=1, source_target_pairs={{1,0},{0,1},{5,2},{4,3},{3,4},{2,5},{7,6},{6,7},{9,8},{8,9},{13,10... | collective-permute-start | bytes 2359304 | tf_op jit(solution)/shard_map/ppermute | solution.py:707
  212.4 3.4 collective-permute-start.9
  216.0 22.4 %collective-permute-done.10 = bf16[512,768]{1,0:T(8,128)(2,1)} collective-permute-done((bf16[512,768]{1,0:T(8,128)(2,1)}, bf16[512,768]{1,0:T(8,128)(2,1)}, u32[]{:S(2)}, u32[]{:S(2)}) %collective-permute-start.10) | collective-permute-done | bytes 786464 | tf_op jit(solution)/shard_map/ppermute | solution.py:707
  238.5 8.4 %collective-permute-done.9 = bf16[512,768]{1,0:T(8,128)(2,1)} collective-permute-done((bf16[512,768]{1,0:T(8,128)(2,1)}, bf16[512,768]{1,0:T(8,128)(2,1)}, u32[]{:S(2)}, u32[]{:S(2)}) %collective-permute-start.9) | collective-permute-done | bytes 786464 | tf_op jit(solution)/shard_map/ppermute | solution.py:707
  246.9 3.3 maximum_select_fusion
  250.2 5.5 %add_convert_fusion = bf16[4,896,768]{2,1,0:T(8,128)(2,1)S(1)} fusion(bf16[4,896,768]{2,1,0:T(8,128)(2,1)} %collective-permute-done.11, bf16[4,896,768]{2,1,0:T(8,128)(2,1)} %get-tuple-element.73), kind=kLoop, calls=%fused_computation | loop fusion | flops 11010048 | bytes 16515072 | tf_op jit(solution)/shard_map/convert_element_type | solution.py:575
  258.5 16.3 %attend_backward_0.1 = (bf16[1024,384]{1,0:T(8,128)(2,1)S(1)}, bf16[1024,384]{1,0:T(8,128)(2,1)S(1)}) custom-call(s32[1]{0:T(128)} %bitcast.13.mask_ref, s32[8]{0:T(128)S(1)} %bitcast.130, bf16[1024,1152]{1,0:T(8,128)(2,1)S(1)} %copy-done.1, bf16[1024,1152]{1,0:T(8,128)(2,1)S(1)} %multiply_convert_fusion.sib, bf16[1024,384]{1,0:T(8,128)(2,1)S(1)} %copy-done.7, ...), custom_call_target="tpu_custom_call" | custom-call | flops 20000000000 | bytes 8000000 | tf_op jit(solution)/shard_map/attend_backward_0/pallas_call | solution.py:249
  275.5 7.8 %collective-permute-done.13 = bf16[2,448,768]{2,1,0:T(8,128)(2,1)S(1)} collective-permute-done((bf16[2,448,768]{2,1,0:T(8,128)(2,1)S(1)}, bf16[2,448,768]{2,1,0:T(8,128)(2,1)S(1)}, u32[]{:S(2)}, u32[]{:S(2)}) %collective-permute-start.13) | collective-permute-done | bytes 1376288 | tf_op jit(solution)/shard_map/ppermute | solution.py:600
  283.8 1.8 collective-permute-start.16
  285.6 16.3 %attend_backward_1.1 = (bf16[1024,384]{1,0:T(8,128)(2,1)S(1)}, bf16[1024,384]{1,0:T(8,128)(2,1)S(1)}) custom-call(s32[1]{0:T(128)} %bitcast.13.mask_ref, s32[8]{0:T(128)S(1)} %bitcast.131, bf16[1024,1152]{1,0:T(8,128)(2,1)S(1)} %copy-done.1, bf16[1024,1152]{1,0:T(8,128)(2,1)S(1)} %multiply_convert_fusion.sib, bf16[1024,384]{1,0:T(8,128)(2,1)S(1)} %copy-done.7, ...), custom_call_target="tpu_custom_call" | custom-call | flops 20000000000 | bytes 8000000 | tf_op jit(solution)/shard_map/attend_backward_1/pallas_call | solution.py:249
  304.1 5.8 %collective-permute-start.32 = (bf16[224,768]{1,0:T(8,128)(2,1)S(1)}, bf16[224,768]{1,0:T(8,128)(2,1)S(1)}, u32[]{:S(2)}, u32[]{:S(2)}) collective-permute-start(bf16[224,768]{1,0:T(8,128)(2,1)S(1)} %get-tuple-element.132), channel_id=1, source_target_pairs={{0,2},{1,3},{2,0},{3,1},{4,6},{5,7},{6,4},{7,5},{8,10},{9,11},{10,... | collective-permute-start | bytes 1032200 | tf_op jit(solution)/shard_map/ppermute | solution.py:619
  310.1 16.3 %attend_backward_2.1 = (bf16[1024,384]{1,0:T(8,128)(2,1)S(1)}, bf16[1024,384]{1,0:T(8,128)(2,1)S(1)}) custom-call(s32[1]{0:T(128)} %bitcast.13.mask_ref, s32[8]{0:T(128)S(1)} %bitcast.132, bf16[1024,1152]{1,0:T(8,128)(2,1)S(1)} %copy-done.1, bf16[1024,1152]{1,0:T(8,128)(2,1)S(1)} %multiply_convert_fusion.sib, bf16[1024,384]{1,0:T(8,128)(2,1)S(1)} %copy-done.7, ...), custom_call_target="tpu_custom_call" | custom-call | flops 20000000000 | bytes 8000000 | tf_op jit(solution)/shard_map/attend_backward_2/pallas_call | solution.py:249
  328.7 2.2 convolution_convert_fusion
  330.9 7.1 %collective-permute-start.17 = (bf16[1024,768]{1,0:T(8,128)(2,1)S(1)}, bf16[1024,768]{1,0:T(8,128)(2,1)S(1)}, u32[]{:S(2)}, u32[]{:S(2)}) collective-permute-start(bf16[1024,768]{1,0:T(8,128)(2,1)S(1)} %convolution_convert_fusion), channel_id=1, source_target_pairs={{0,4},{4,0},{1,5},{5,1},{2,6},{6,2},{3,7},{7,3},{8,12},{12,8},{9,1... | collective-permute-start | bytes 4718600 | tf_op jit(solution)/shard_map/ppermute | solution.py:563
  338.0 2.2 fusion.31
  340.2 2.3 fusion.32
  342.5 3.7 fusion
  346.5 1.6 copy-done.22
  349.0 7.0 %collective-permute-start.22 = (bf16[2,128,1152]{2,1,0:T(8,128)(2,1)S(1)}, bf16[2,128,1152]{2,1,0:T(8,128)(2,1)S(1)}, u32[]{:S(2)}, u32[]{:S(2)}) collective-permute-start(bf16[2,128,1152]{2,1,0:T(8,128)(2,1)S(1)} %dynamic-slice_bitcast_fusion.8), channel_id=1, source_target_pairs={{0,16},{8,24},{16,0},{24,8},{1,17},{9,25},{17,1},{25,9},{2,18},{10... | collective-permute-start | bytes 1769480 | tf_op jit(solution)/shard_map/ppermute | solution.py:600
  358.5 5.4 %collective-permute-start.18 = (bf16[512,768]{1,0:T(8,128)(2,1)S(1)}, bf16[512,768]{1,0:T(8,128)(2,1)S(1)}, u32[]{:S(2)}, u32[]{:S(2)}) collective-permute-start(bf16[512,768]{1,0:T(8,128)(2,1)S(1)} %get-tuple-element.117), channel_id=1, source_target_pairs={{0,0},{1,1},{4,2},{5,3},{2,4},{3,5},{6,6},{7,7},{8,8},{9,9},{12,10... | collective-permute-start | bytes 2359304 | tf_op jit(solution)/shard_map/ppermute | solution.py:774
  363.9 5.8 %collective-permute-done.22 = bf16[2,128,1152]{2,1,0:T(8,128)(2,1)S(1)} collective-permute-done((bf16[2,128,1152]{2,1,0:T(8,128)(2,1)S(1)}, bf16[2,128,1152]{2,1,0:T(8,128)(2,1)S(1)}, u32[]{:S(2)}, u32[]{:S(2)}) %collective-permute-start.22) | collective-permute-done | bytes 589856 | tf_op jit(solution)/shard_map/ppermute | solution.py:600
  371.0 1.7 collective-permute-start.23
  372.9 4.9 %collective-permute-done.23 = bf16[128,1152]{1,0:T(8,128)(2,1)S(1)} collective-permute-done((bf16[128,1152]{1,0:T(8,128)(2,1)S(1)}, bf16[128,1152]{1,0:T(8,128)(2,1)S(1)}, u32[]{:S(2)}, u32[]{:S(2)}) %collective-permute-start.23) | collective-permute-done | bytes 294944 | tf_op jit(solution)/shard_map/ppermute | solution.py:600
  377.8 1.5 collective-permute-start.21
  379.3 4.3 collective-permute-done.21
  384.2 3.3 collective-permute-start.24
  387.4 18.7 %collective-permute-done.18 = bf16[512,768]{1,0:T(8,128)(2,1)S(1)} collective-permute-done((bf16[512,768]{1,0:T(8,128)(2,1)S(1)}, bf16[512,768]{1,0:T(8,128)(2,1)S(1)}, u32[]{:S(2)}, u32[]{:S(2)}) %collective-permute-start.18) | collective-permute-done | bytes 786464 | tf_op jit(solution)/shard_map/ppermute | solution.py:774
  406.1 20.4 %collective-permute-done.19 = bf16[512,768]{1,0:T(8,128)(2,1)S(1)} collective-permute-done((bf16[512,768]{1,0:T(8,128)(2,1)S(1)}, bf16[512,768]{1,0:T(8,128)(2,1)S(1)}, u32[]{:S(2)}, u32[]{:S(2)}) %collective-permute-start.19) | collective-permute-done | bytes 786464 | tf_op jit(solution)/shard_map/ppermute | solution.py:774
  426.5 2.0 fusion.3
  430.0 5.0 %collective-permute-done.26 = bf16[64,1152]{1,0:T(8,128)(2,1)S(1)} collective-permute-done((bf16[64,1152]{1,0:T(8,128)(2,1)S(1)}, bf16[64,1152]{1,0:T(8,128)(2,1)S(1)}, u32[]{:S(2)}, u32[]{:S(2)}) %collective-permute-start.26) | collective-permute-done | bytes 147488 | tf_op jit(solution)/shard_map/ppermute | solution.py:619
  435.2 1.6 collective-permute-done.34
  437.7 1.9 collective-permute-start.27
  440.0 1.5 collective-permute-start.29
  444.3 5.0 %collective-permute-done.27 = bf16[64,1152]{1,0:T(8,128)(2,1)S(1)} collective-permute-done((bf16[64,1152]{1,0:T(8,128)(2,1)S(1)}, bf16[64,1152]{1,0:T(8,128)(2,1)S(1)}, u32[]{:S(2)}, u32[]{:S(2)}) %collective-permute-start.27) | collective-permute-done | bytes 147488 | tf_op jit(solution)/shard_map/ppermute | solution.py:619
  449.4 3.3 collective-permute-done.28
  458.1 1.6 reshape.382
  (253 shorter events, 52.6 us)
Async XLA Ops:
  7.2 51.0 %all-gather.6.cloned.1.call-start = ((), (), s32[]{:S(2)}) async-start(), calls=%async_computation | async-start | bytes 2211840 | tf_op jit(solution)/shard_map/all_gather | solution.py:676
  9.6 1.8 collective-permute-start.3
  12.3 103.0 %all-gather.8.cloned.1.call-start = ((), (), s32[]{:S(2)}) async-start(), calls=%async_computation.1 | async-start | bytes 11943936 | tf_op jit(solution)/shard_map/all_gather | solution.py:686
  14.7 5.8 %copy-start.30 = (bf16[96]{0:T(256)(128)(2,1)S(1)}, bf16[96]{0:T(256)(128)(2,1)}, u32[]{:S(2)}) copy-start(bf16[96]{0:T(256)(128)(2,1)} %param.19) | copy-start | bytes 580
  14.7 5.8 %copy-start.31 = (bf16[96]{0:T(256)(128)(2,1)S(1)}, bf16[96]{0:T(256)(128)(2,1)}, u32[]{:S(2)}) copy-start(bf16[96]{0:T(256)(128)(2,1)} %param.20) | copy-start | bytes 580
  14.7 5.8 %copy-start.32 = (bf16[96]{0:T(256)(128)(2,1)S(1)}, bf16[96]{0:T(256)(128)(2,1)}, u32[]{:S(2)}) copy-start(bf16[96]{0:T(256)(128)(2,1)} %param.22) | copy-start | bytes 580
  14.7 5.8 %copy-start.33 = (bf16[96]{0:T(256)(128)(2,1)S(1)}, bf16[96]{0:T(256)(128)(2,1)}, u32[]{:S(2)}) copy-start(bf16[96]{0:T(256)(128)(2,1)} %param.23) | copy-start | bytes 580
  14.7 5.8 %copy-start.34 = (bf16[96]{0:T(256)(128)(2,1)S(1)}, bf16[96]{0:T(256)(128)(2,1)}, u32[]{:S(2)}) copy-start(bf16[96]{0:T(256)(128)(2,1)} %param.24) | copy-start | bytes 580
  14.7 5.8 %copy-start.35 = (bf16[96]{0:T(256)(128)(2,1)S(1)}, bf16[96]{0:T(256)(128)(2,1)}, u32[]{:S(2)}) copy-start(bf16[96]{0:T(256)(128)(2,1)} %param.28) | copy-start | bytes 580
  14.7 5.8 %copy-start.36 = (bf16[96]{0:T(256)(128)(2,1)S(1)}, bf16[96]{0:T(256)(128)(2,1)}, u32[]{:S(2)}) copy-start(bf16[96]{0:T(256)(128)(2,1)} %param.29) | copy-start | bytes 580
  15.8 30.2 %collective-permute-start = (bf16[512,768]{1,0:T(8,128)(2,1)S(1)}, bf16[512,768]{1,0:T(8,128)(2,1)S(1)}, u32[]{:S(2)}, u32[]{:S(2)}) collective-permute-start(bf16[512,768]{1,0:T(8,128)(2,1)S(1)} %get-tuple-element.123), channel_id=1, source_target_pairs={{0,0},{1,1},{2,4},{3,5},{4,2},{5,3},{6,6},{7,7},{8,8},{9,9},{10,12... | collective-permute-start | bytes 2359304 | tf_op jit(solution)/shard_map/ppermute | solution.py:659
  20.2 34.2 %collective-permute-start.1 = (bf16[512,768]{1,0:T(8,128)(2,1)}, bf16[512,768]{1,0:T(8,128)(2,1)S(1)}, u32[]{:S(2)}, u32[]{:S(2)}) collective-permute-start(bf16[512,768]{1,0:T(8,128)(2,1)} %get-tuple-element.124), channel_id=1, source_target_pairs={{0,1},{1,0},{2,5},{3,4},{4,3},{5,2},{6,7},{7,6},{8,9},{9,8},{10,13... | collective-permute-start | bytes 2359304 | tf_op jit(solution)/shard_map/ppermute | solution.py:659
  20.3 34.5 %collective-permute-start.2 = (s32[2,8]{1,0:T(2,128)S(1)}, s32[2,8]{1,0:T(2,128)S(1)}, u32[]{:S(2)}, u32[]{:S(2)}) collective-permute-start(s32[2,8]{1,0:T(2,128)S(1)} %bitcast.151), channel_id=1, source_target_pairs={{0,4},{4,0},{1,5},{5,1},{2,6},{6,2},{3,7},{7,3},{8,12},{12,8},{9,1... | collective-permute-start | bytes 200 | tf_op jit(solution)/shard_map/ppermute | solution.py:563
  45.9 10.3 %collective-permute-start.4 = (bf16[512,768]{1,0:T(8,128)(2,1)S(1)}, bf16[512,768]{1,0:T(8,128)(2,1)S(1)}, u32[]{:S(2)}, u32[]{:S(2)}) collective-permute-start(bf16[512,768]{1,0:T(8,128)(2,1)S(1)} %collective-permute-done), channel_id=1, source_target_pairs={{0,4},{4,0},{1,5},{5,1},{2,6},{6,2},{3,7},{7,3},{8,12},{12,8},{9,1... | collective-permute-start | bytes 2359304 | tf_op jit(solution)/shard_map/ppermute | solution.py:563
  54.5 2.7 collective-permute-start.5
  65.1 47.1 %collective-permute-start.7 = (bf16[512,768]{1,0:T(8,128)(2,1)S(1)}, bf16[512,768]{1,0:T(8,128)(2,1)S(1)}, u32[]{:S(2)}, u32[]{:S(2)}) collective-permute-start(bf16[512,768]{1,0:T(8,128)(2,1)S(1)} %get-tuple-element.121), channel_id=1, source_target_pairs={{0,0},{1,1},{2,4},{3,5},{4,2},{5,3},{6,6},{7,7},{8,8},{9,9},{10,12... | collective-permute-start | bytes 2359304 | tf_op jit(solution)/shard_map/ppermute | solution.py:659
  67.3 44.8 %collective-permute-start.8 = (bf16[512,768]{1,0:T(8,128)(2,1)S(1)}, bf16[512,768]{1,0:T(8,128)(2,1)S(1)}, u32[]{:S(2)}, u32[]{:S(2)}) collective-permute-start(bf16[512,768]{1,0:T(8,128)(2,1)S(1)} %get-tuple-element.122), channel_id=1, source_target_pairs={{0,1},{1,0},{2,5},{3,4},{4,3},{5,2},{6,7},{7,6},{8,9},{9,8},{10,13... | collective-permute-start | bytes 2359304 | tf_op jit(solution)/shard_map/ppermute | solution.py:659
  112.1 2.3 collective-permute-start.6
  174.7 18.4 %copy-start.3 = (bf16[1024,768]{1,0:T(8,128)(2,1)S(1)}, bf16[1024,768]{1,0:T(8,128)(2,1)}, u32[]{:S(2)}) copy-start(bf16[1024,768]{1,0:T(8,128)(2,1)} %copy-done.2) | copy-start | bytes 4718596
  192.8 57.4 %collective-permute-start.11 = (bf16[4,896,768]{2,1,0:T(8,128)(2,1)}, bf16[4,896,768]{2,1,0:T(8,128)(2,1)}, u32[]{:S(2)}, u32[]{:S(2)}) collective-permute-start(bf16[4,896,768]{2,1,0:T(8,128)(2,1)} %get-tuple-element.74), channel_id=1, source_target_pairs={{0,4},{4,0},{1,5},{5,1},{2,6},{6,2},{3,7},{7,3},{8,12},{12,8},{9,1... | collective-permute-start | bytes 16515080 | tf_op jit(solution)/shard_map/ppermute | solution.py:563
  194.3 44.2 %collective-permute-start.10 = (bf16[512,768]{1,0:T(8,128)(2,1)}, bf16[512,768]{1,0:T(8,128)(2,1)}, u32[]{:S(2)}, u32[]{:S(2)}) collective-permute-start(bf16[512,768]{1,0:T(8,128)(2,1)} %get-tuple-element.120), channel_id=1, source_target_pairs={{1,0},{0,1},{5,2},{4,3},{3,4},{2,5},{7,6},{6,7},{9,8},{8,9},{13,10... | collective-permute-start | bytes 2359304 | tf_op jit(solution)/shard_map/ppermute | solution.py:707
  212.4 34.5 %collective-permute-start.9 = (bf16[512,768]{1,0:T(8,128)(2,1)}, bf16[512,768]{1,0:T(8,128)(2,1)}, u32[]{:S(2)}, u32[]{:S(2)}) collective-permute-start(bf16[512,768]{1,0:T(8,128)(2,1)} %get-tuple-element.119), channel_id=1, source_target_pairs={{0,0},{1,1},{4,2},{5,3},{2,4},{3,5},{6,6},{7,7},{8,8},{9,9},{12,10... | collective-permute-start | bytes 2359304 | tf_op jit(solution)/shard_map/ppermute | solution.py:707
  216.0 41.0 %collective-permute-start.12 = (bf16[1024,384]{1,0:T(8,128)(2,1)}, bf16[1024,384]{1,0:T(8,128)(2,1)S(1)}, u32[]{:S(2)}, u32[]{:S(2)}) collective-permute-start(bf16[1024,384]{1,0:T(8,128)(2,1)} %copy-done.10), channel_id=1, source_target_pairs={{0,4},{4,0},{1,5},{5,1},{2,6},{6,2},{3,7},{7,3},{8,12},{12,8},{9,1... | collective-permute-start | bytes 2359304 | tf_op jit(solution)/shard_map/ppermute | solution.py:563
  256.2 18.8 %collective-permute-start.14 = (bf16[2,448,768]{2,1,0:T(8,128)(2,1)S(1)}, bf16[2,448,768]{2,1,0:T(8,128)(2,1)S(1)}, u32[]{:S(2)}, u32[]{:S(2)}) collective-permute-start(bf16[2,448,768]{2,1,0:T(8,128)(2,1)S(1)} %dynamic-slice_bitcast_fusion), channel_id=1, source_target_pairs={{0,16},{8,24},{16,0},{24,8},{1,17},{9,25},{17,1},{25,9},{2,18},{10... | collective-permute-start | bytes 4128776 | tf_op jit(solution)/shard_map/ppermute | solution.py:600
  256.9 26.4 %collective-permute-start.13 = (bf16[2,448,768]{2,1,0:T(8,128)(2,1)S(1)}, bf16[2,448,768]{2,1,0:T(8,128)(2,1)S(1)}, u32[]{:S(2)}, u32[]{:S(2)}) collective-permute-start(bf16[2,448,768]{2,1,0:T(8,128)(2,1)S(1)} %dynamic-slice_bitcast_fusion.1), channel_id=1, source_target_pairs={{0,8},{8,0},{16,24},{24,16},{1,9},{9,1},{17,25},{25,17},{2,10},{10... | collective-permute-start | bytes 4128776 | tf_op jit(solution)/shard_map/ppermute | solution.py:600
  283.8 18.5 %collective-permute-start.16 = (bf16[448,768]{1,0:T(8,128)(2,1)S(1)}, bf16[448,768]{1,0:T(8,128)(2,1)S(1)}, u32[]{:S(2)}, u32[]{:S(2)}) collective-permute-start(bf16[448,768]{1,0:T(8,128)(2,1)S(1)} %dynamic-slice_bitcast_fusion.6), channel_id=1, source_target_pairs={{0,8},{8,0},{16,24},{24,16},{1,9},{9,1},{17,25},{25,17},{2,10},{10... | collective-permute-start | bytes 2064392 | tf_op jit(solution)/shard_map/ppermute | solution.py:600
  285.6 16.9 %collective-permute-start.15 = (bf16[448,768]{1,0:T(8,128)(2,1)S(1)}, bf16[448,768]{1,0:T(8,128)(2,1)S(1)}, u32[]{:S(2)}, u32[]{:S(2)}) collective-permute-start(bf16[448,768]{1,0:T(8,128)(2,1)S(1)} %dynamic-slice_bitcast_fusion.7), channel_id=1, source_target_pairs={{0,16},{8,24},{16,0},{24,8},{1,17},{9,25},{17,1},{25,9},{2,18},{10... | collective-permute-start | bytes 2064392 | tf_op jit(solution)/shard_map/ppermute | solution.py:600
  304.1 42.4 %collective-permute-start.31 = (bf16[224,768]{1,0:T(8,128)(2,1)S(1)}, bf16[224,768]{1,0:T(8,128)(2,1)S(1)}, u32[]{:S(2)}, u32[]{:S(2)}) collective-permute-start(bf16[224,768]{1,0:T(8,128)(2,1)S(1)} %get-tuple-element.131), channel_id=1, source_target_pairs={{0,1},{1,2},{2,3},{3,0},{4,5},{5,6},{6,7},{7,4},{8,9},{9,10},{10,1... | collective-permute-start | bytes 1032200 | tf_op jit(solution)/shard_map/ppermute | solution.py:619
  304.1 42.4 %collective-permute-start.32 = (bf16[224,768]{1,0:T(8,128)(2,1)S(1)}, bf16[224,768]{1,0:T(8,128)(2,1)S(1)}, u32[]{:S(2)}, u32[]{:S(2)}) collective-permute-start(bf16[224,768]{1,0:T(8,128)(2,1)S(1)} %get-tuple-element.132), channel_id=1, source_target_pairs={{0,2},{1,3},{2,0},{3,1},{4,6},{5,7},{6,4},{7,5},{8,10},{9,11},{10,... | collective-permute-start | bytes 1032200 | tf_op jit(solution)/shard_map/ppermute | solution.py:619
  310.0 36.5 %collective-permute-start.33 = (bf16[224,768]{1,0:T(8,128)(2,1)S(1)}, bf16[224,768]{1,0:T(8,128)(2,1)S(1)}, u32[]{:S(2)}, u32[]{:S(2)}) collective-permute-start(bf16[224,768]{1,0:T(8,128)(2,1)S(1)} %get-tuple-element.130), channel_id=1, source_target_pairs={{0,3},{1,0},{2,1},{3,2},{4,7},{5,4},{6,5},{7,6},{8,11},{9,8},{10,9... | collective-permute-start | bytes 1032200 | tf_op jit(solution)/shard_map/ppermute | solution.py:619
  330.9 9.3 %copy-start.21 = (bf16[1024,768]{1,0:T(8,128)(2,1)S(1)}, bf16[1024,768]{1,0:T(8,128)(2,1)}, u32[]{:S(2)}) copy-start(bf16[1024,768]{1,0:T(8,128)(2,1)} %pad_maximum_fusion.1.x_ref) | copy-start | bytes 4718596
  330.9 15.6 %collective-permute-start.17 = (bf16[1024,768]{1,0:T(8,128)(2,1)S(1)}, bf16[1024,768]{1,0:T(8,128)(2,1)S(1)}, u32[]{:S(2)}, u32[]{:S(2)}) collective-permute-start(bf16[1024,768]{1,0:T(8,128)(2,1)S(1)} %convolution_convert_fusion), channel_id=1, source_target_pairs={{0,4},{4,0},{1,5},{5,1},{2,6},{6,2},{3,7},{7,3},{8,12},{12,8},{9,1... | collective-permute-start | bytes 4718600 | tf_op jit(solution)/shard_map/ppermute | solution.py:563
  349.0 20.7 %collective-permute-start.22 = (bf16[2,128,1152]{2,1,0:T(8,128)(2,1)S(1)}, bf16[2,128,1152]{2,1,0:T(8,128)(2,1)S(1)}, u32[]{:S(2)}, u32[]{:S(2)}) collective-permute-start(bf16[2,128,1152]{2,1,0:T(8,128)(2,1)S(1)} %dynamic-slice_bitcast_fusion.8), channel_id=1, source_target_pairs={{0,16},{8,24},{16,0},{24,8},{1,17},{9,25},{17,1},{25,9},{2,18},{10... | collective-permute-start | bytes 1769480 | tf_op jit(solution)/shard_map/ppermute | solution.py:600
  356.6 78.5 %collective-permute-start.36 = (bf16[224,768]{1,0:T(8,128)(2,1)S(1)}, bf16[224,768]{1,0:T(8,128)(2,1)S(1)}, u32[]{:S(2)}, u32[]{:S(2)}) collective-permute-start(bf16[224,768]{1,0:T(8,128)(2,1)S(1)} %get-tuple-element.110), channel_id=1, source_target_pairs={{0,3},{1,0},{2,1},{3,2},{4,7},{5,4},{6,5},{7,6},{8,11},{9,8},{10,9... | collective-permute-start | bytes 1032200 | tf_op jit(solution)/shard_map/ppermute | solution.py:619
  356.9 78.3 %collective-permute-start.35 = (bf16[224,768]{1,0:T(8,128)(2,1)S(1)}, bf16[224,768]{1,0:T(8,128)(2,1)S(1)}, u32[]{:S(2)}, u32[]{:S(2)}) collective-permute-start(bf16[224,768]{1,0:T(8,128)(2,1)S(1)} %get-tuple-element.110), channel_id=1, source_target_pairs={{0,2},{1,3},{2,0},{3,1},{4,6},{5,7},{6,4},{7,5},{8,10},{9,11},{10,... | collective-permute-start | bytes 1032200 | tf_op jit(solution)/shard_map/ppermute | solution.py:619
  357.4 13.6 %collective-permute-start.20 = (bf16[2,128,1152]{2,1,0:T(8,128)(2,1)S(1)}, bf16[2,128,1152]{2,1,0:T(8,128)(2,1)S(1)}, u32[]{:S(2)}, u32[]{:S(2)}) collective-permute-start(bf16[2,128,1152]{2,1,0:T(8,128)(2,1)S(1)} %dynamic-slice_bitcast_fusion.9), channel_id=1, source_target_pairs={{0,8},{8,0},{16,24},{24,16},{1,9},{9,1},{17,25},{25,17},{2,10},{10... | collective-permute-start | bytes 1769480 | tf_op jit(solution)/shard_map/ppermute | solution.py:600
  358.5 47.7 %collective-permute-start.18 = (bf16[512,768]{1,0:T(8,128)(2,1)S(1)}, bf16[512,768]{1,0:T(8,128)(2,1)S(1)}, u32[]{:S(2)}, u32[]{:S(2)}) collective-permute-start(bf16[512,768]{1,0:T(8,128)(2,1)S(1)} %get-tuple-element.117), channel_id=1, source_target_pairs={{0,0},{1,1},{4,2},{5,3},{2,4},{3,5},{6,6},{7,7},{8,8},{9,9},{12,10... | collective-permute-start | bytes 2359304 | tf_op jit(solution)/shard_map/ppermute | solution.py:774
  369.7 56.8 %collective-permute-start.19 = (bf16[512,768]{1,0:T(8,128)(2,1)S(1)}, bf16[512,768]{1,0:T(8,128)(2,1)S(1)}, u32[]{:S(2)}, u32[]{:S(2)}) collective-permute-start(bf16[512,768]{1,0:T(8,128)(2,1)S(1)} %get-tuple-element.118), channel_id=1, source_target_pairs={{1,0},{0,1},{5,2},{4,3},{3,4},{2,5},{7,6},{6,7},{9,8},{8,9},{13,10... | collective-permute-start | bytes 2359304 | tf_op jit(solution)/shard_map/ppermute | solution.py:774
  371.0 6.8 %collective-permute-start.23 = (bf16[128,1152]{1,0:T(8,128)(2,1)S(1)}, bf16[128,1152]{1,0:T(8,128)(2,1)S(1)}, u32[]{:S(2)}, u32[]{:S(2)}) collective-permute-start(bf16[128,1152]{1,0:T(8,128)(2,1)S(1)} %dynamic-slice_bitcast_fusion.10), channel_id=1, source_target_pairs={{0,8},{8,0},{16,24},{24,16},{1,9},{9,1},{17,25},{25,17},{2,10},{10... | collective-permute-start | bytes 884744 | tf_op jit(solution)/shard_map/ppermute | solution.py:600
  377.8 5.9 %collective-permute-start.21 = (bf16[128,1152]{1,0:T(8,128)(2,1)S(1)}, bf16[128,1152]{1,0:T(8,128)(2,1)S(1)}, u32[]{:S(2)}, u32[]{:S(2)}) collective-permute-start(bf16[128,1152]{1,0:T(8,128)(2,1)S(1)} %dynamic-slice_bitcast_fusion.11), channel_id=1, source_target_pairs={{0,16},{8,24},{16,0},{24,8},{1,17},{9,25},{17,1},{25,9},{2,18},{10... | collective-permute-start | bytes 884744 | tf_op jit(solution)/shard_map/ppermute | solution.py:600
  384.2 44.4 %collective-permute-start.24 = (bf16[64,1152]{1,0:T(8,128)(2,1)S(1)}, bf16[64,1152]{1,0:T(8,128)(2,1)S(1)}, u32[]{:S(2)}, u32[]{:S(2)}) collective-permute-start(bf16[64,1152]{1,0:T(8,128)(2,1)S(1)} %get-tuple-element.135), channel_id=1, source_target_pairs={{0,1},{1,2},{2,3},{3,0},{4,5},{5,6},{6,7},{7,4},{8,9},{9,10},{10,1... | collective-permute-start | bytes 442376 | tf_op jit(solution)/shard_map/ppermute | solution.py:619
  406.1 23.9 %collective-permute-start.25 = (bf16[64,1152]{1,0:T(8,128)(2,1)S(1)}, bf16[64,1152]{1,0:T(8,128)(2,1)S(1)}, u32[]{:S(2)}, u32[]{:S(2)}) collective-permute-start(bf16[64,1152]{1,0:T(8,128)(2,1)S(1)} %get-tuple-element.136), channel_id=1, source_target_pairs={{0,2},{1,3},{2,0},{3,1},{4,6},{5,7},{6,4},{7,5},{8,10},{9,11},{10,... | collective-permute-start | bytes 442376 | tf_op jit(solution)/shard_map/ppermute | solution.py:619
  426.5 8.4 %collective-permute-start.26 = (bf16[64,1152]{1,0:T(8,128)(2,1)S(1)}, bf16[64,1152]{1,0:T(8,128)(2,1)S(1)}, u32[]{:S(2)}, u32[]{:S(2)}) collective-permute-start(bf16[64,1152]{1,0:T(8,128)(2,1)S(1)} %get-tuple-element.137), channel_id=1, source_target_pairs={{0,3},{1,0},{2,1},{3,2},{4,7},{5,4},{6,5},{7,6},{8,11},{9,8},{10,9... | collective-permute-start | bytes 442376 | tf_op jit(solution)/shard_map/ppermute | solution.py:619
  428.5 8.3 %collective-permute-start.34 = (bf16[224,768]{1,0:T(8,128)(2,1)S(1)}, bf16[224,768]{1,0:T(8,128)(2,1)S(1)}, u32[]{:S(2)}, u32[]{:S(2)}) collective-permute-start(bf16[224,768]{1,0:T(8,128)(2,1)S(1)} %get-tuple-element.110), channel_id=1, source_target_pairs={{0,1},{1,2},{2,3},{3,0},{4,5},{5,6},{6,7},{7,4},{8,9},{9,10},{10,1... | collective-permute-start | bytes 1032200 | tf_op jit(solution)/shard_map/ppermute | solution.py:619
  437.7 11.7 %collective-permute-start.27 = (bf16[64,1152]{1,0:T(8,128)(2,1)S(1)}, bf16[64,1152]{1,0:T(8,128)(2,1)S(1)}, u32[]{:S(2)}, u32[]{:S(2)}) collective-permute-start(bf16[64,1152]{1,0:T(8,128)(2,1)S(1)} %get-tuple-element.112), channel_id=1, source_target_pairs={{0,1},{1,2},{2,3},{3,0},{4,5},{5,6},{6,7},{7,4},{8,9},{9,10},{10,1... | collective-permute-start | bytes 442376 | tf_op jit(solution)/shard_map/ppermute | solution.py:619
  439.6 13.0 %collective-permute-start.28 = (bf16[64,1152]{1,0:T(8,128)(2,1)S(1)}, bf16[64,1152]{1,0:T(8,128)(2,1)S(1)}, u32[]{:S(2)}, u32[]{:S(2)}) collective-permute-start(bf16[64,1152]{1,0:T(8,128)(2,1)S(1)} %get-tuple-element.112), channel_id=1, source_target_pairs={{0,2},{1,3},{2,0},{3,1},{4,6},{5,7},{6,4},{7,5},{8,10},{9,11},{10,... | collective-permute-start | bytes 442376 | tf_op jit(solution)/shard_map/ppermute | solution.py:619
  440.0 13.8 %collective-permute-start.29 = (bf16[64,1152]{1,0:T(8,128)(2,1)S(1)}, bf16[64,1152]{1,0:T(8,128)(2,1)S(1)}, u32[]{:S(2)}, u32[]{:S(2)}) collective-permute-start(bf16[64,1152]{1,0:T(8,128)(2,1)S(1)} %get-tuple-element.112), channel_id=1, source_target_pairs={{0,3},{1,0},{2,1},{3,2},{4,7},{5,4},{6,5},{7,6},{8,11},{9,8},{10,9... | collective-permute-start | bytes 442376 | tf_op jit(solution)/shard_map/ppermute | solution.py:619
  453.9 1.7 collective-permute-start.30
  (32 other events, 72.0 us)
Sparse Core Ops, SparseCore 0:
  12.4 33.2 all-gather.5
  48.1 64.2 all-gather.7

commit v7 on v6

--- a/solution.py
+++ b/solution.py
@@ -761,7 +761,10 @@
     grads = [attend(0, *early.sent)]
     for pair in range(1, pairs):
         sent = advance(grads[-1][0])
-        grads.append(attend(pair, *sent, *(output if pair == 1 else ())))
+        if pair == pairs - 1:
+            output = [after(o, grads[-1][0]) for o in output]
+            sent = list(sent) + output
+        grads.append(attend(pair, *sent))
     while len(progress) == 1:
         advance(grads[-1][0])
     early_sum = progress[1]
@@ -802,6 +805,7 @@
     shard = lax.axis_index("xy") * CORES + core
     q_final = lax.dynamic_slice_in_dim(sums[0], shard * rows, rows, 0).astype(f32)
     v_final = lax.dynamic_slice_in_dim(sums[2], shard * rows, rows, 0).astype(f32)
+    output = [after(o, qkv_sum.keep) for o in output]
     output = jnp.where(odd == 0, jnp.stack(output), jnp.stack(output[::-1]))[None]
     return (
         output, input_grad, qkv_final, q_final, v_final, out_final, out_bias_final, g1, b1, in_final,

time: 473 us -> 449 us (0.949)
  Pallas kernels: 157 us -> 187 us
  waiting for transfers between devices: 135 us -> 107 us
  starting transfers between devices: 74.3 us -> 46.8 us
    ppermute x2, waiting for transfers between devices: 30.8 us -> 0.01 us  [per_device(): lax.ppermute(result[i * run:(i + 1) * run], ('core', 'seq'), back[i])]
    ppermute x2, starting transfers between devices: 21.5 us -> 6.01 us  [per_device(): lax.ppermute(result[i * run:(i + 1) * run], ('core', 'seq'), back[i])]
    pallas_call x1, Pallas kernels: 41.4 us -> 56.6 us  [attend_forward(): pl.pallas_call(functools.partial(forward_kernel, run), out_shape=(jax.Sha...]
    pallas_call x3, Pallas kernels: 49 us -> 63.9 us  [attend_backward(): pl.pallas_call(functools.partial(backward_kernel, run, pair), out_shape=(...]
    ppermute x8, starting transfers between devices: 13.6 us -> 5.18 us  [send(): lax.ppermute(out, 'xy', [(i, i ^ 1 << bit) for i in range(self.planes)])]
    ppermute x8, waiting for transfers between devices: 23.1 us -> 29 us  [send(): lax.ppermute(out, 'xy', [(i, i ^ 1 << bit) for i in range(self.planes)])]
    ppermute x9, starting transfers between devices: 8.73 us -> 3.8 us  [swap(): return lax.ppermute(x, 'core', [(0, 1), (1, 0)])]
    unnamed x91 -> x89, local copies, waits for them, and re-layouts: 19.2 us -> 17.8 us
  transfers between devices with their start and end apart: 39 -> 39, of which waited for: 19 -> 16; matrix products, arithmetic and copies ran while one was open for 10% -> 11% of each run, Pallas kernels for 19% -> 27%
where the time goes in v7:
time: 449 us; the launch traced here: 441 us
  Pallas kernels  187 us (42%)
  waiting for transfers between devices  107 us (24%)
  starting transfers between devices  46.8 us (10%)
  local copies, waits for them, and re-layouts  33.3 us (7%)
  other arithmetic  24.5 us (5%)
  matrix products  17.3 us (4%)
  between operations  15.6 us (3%)
  blocking collectives  9.52 us (2%)
    pallas_call x3, Pallas kernels, attend_backward(): pl.pallas_call(functools.partial(backward_kernel, run, pair), out_shape=(...  63.9 us
    pallas_call x1, Pallas kernels, attend_forward(): pl.pallas_call(functools.partial(forward_kernel, run), out_shape=(jax.Sha...  56.6 us
    pallas_call x1, Pallas kernels, middle(): pl.pallas_call(middle_kernel, grid=(count // ROWS,), out_shape=(shape((co...  48.4 us
    ppermute x2, waiting for transfers between devices, per_device(): lax.ppermute(input_grad[i * run:(i + 1) * run], ('core', 'seq'), back[i])  36.8 us
    ppermute x8, waiting for transfers between devices, send(): lax.ppermute(out, 'xy', [(i, i ^ 1 << bit) for i in range(self.planes)])  29 us
    ppermute x4, waiting for transfers between devices, spread(): lax.ppermute(h, ('core', 'seq'), r)  23.8 us
    pallas_call x1, Pallas kernels, gradients(): pl.pallas_call(functools.partial(gradients_kernel, rows), grid=(2 * chunk...  18.1 us
    unnamed x89, local copies, waits for them, and re-layouts  17.8 us
  transfers between devices with their start and end apart: 39, of which 16 were waited for; matrix products, arithmetic and copies ran while one was open for 11% of the time, Pallas kernels for 27%

profile of v7, /device:TPU:9, one launch (start us, length us, event | category | flops | bytes accessed | tf_op | source)
XLA Modules:
  0.0 440.9 jit_solution(8987036148829569232)
XLA Ops:
  7.2 1.6 reshape.360
  15.8 4.5 %collective-permute-start = (bf16[512,768]{1,0:T(8,128)(2,1)S(1)}, bf16[512,768]{1,0:T(8,128)(2,1)S(1)}, u32[]{:S(2)}, u32[]{:S(2)}) collective-permute-start(bf16[512,768]{1,0:T(8,128)(2,1)S(1)} %get-tuple-element.131), channel_id=1, source_target_pairs={{0,0},{1,1},{2,4},{3,5},{4,2},{5,3},{6,6},{7,7},{8,8},{9,9},{10,12... | collective-permute-start | bytes 2359304 | tf_op jit(solution)/shard_map/ppermute | solution.py:659
  20.6 9.5 %all-gather.2 = bf16[8,12,96]{2,1,0:T(8,128)(2,1)S(1)} all-gather(bf16[1,12,96]{2,1,0:T(8,128)(2,1)S(1)} %bitcast.148), channel_id=2, replica_groups=mesh['xy'=4,'core'=2,'seq'=4] {'xy','core'}, dimensions={0}, use_global_device_ids=true | all-gather | bytes 20736 | tf_op jit(solution)/shard_map/all_gather | solution.py:680
  30.2 15.7 %collective-permute-done = bf16[512,768]{1,0:T(8,128)(2,1)S(1)} collective-permute-done((bf16[512,768]{1,0:T(8,128)(2,1)S(1)}, bf16[512,768]{1,0:T(8,128)(2,1)S(1)}, u32[]{:S(2)}, u32[]{:S(2)}) %collective-permute-start) | collective-permute-done | bytes 786464 | tf_op jit(solution)/shard_map/ppermute | solution.py:659
  46.4 8.1 %collective-permute-done.1 = bf16[512,768]{1,0:T(8,128)(2,1)S(1)} collective-permute-done((bf16[512,768]{1,0:T(8,128)(2,1)}, bf16[512,768]{1,0:T(8,128)(2,1)S(1)}, u32[]{:S(2)}, u32[]{:S(2)}) %collective-permute-start.1) | collective-permute-done | bytes 786464 | tf_op jit(solution)/shard_map/ppermute | solution.py:659
  58.1 4.6 %multiply_convert_fusion.sib = bf16[1024,1152]{1,0:T(8,128)(2,1)S(1)} fusion(bf16[1024,768]{1,0:T(8,128)(2,1)} %constant_dynamic-update-slice_fusion, bf16[768,1152]{1,0:T(8,128)(2,1)} %all-gather.6.cloned.1.call-done, f32[1152]{0:T(1024)S(1)} %copy-done.39, f32[1152]{0:T(1024)S(1)} %add.272), kind=kOutput, calls=%fused_computation.3 | convolution fusion | flops 1815478272 | bytes 5710848 | tf_op jit(solution)/shard_map/dot_general | solution.py:25
  62.7 2.2 multiply_convert_fusion.1.own
  65.1 2.2 collective-permute-start.7
  67.3 2.2 collective-permute-start.8
  69.9 56.6 %attend_forward.1 = (bf16[1024,384]{1,0:T(8,128)(2,1)S(1)}, bf16[1024,384]{1,0:T(8,128)(2,1)S(1)}, f32[6,8,2048]{2,1,0:T(8,128)S(1)}) custom-call(s32[1]{0:T(128)} %bitcast.13.mask_ref, s32[8]{0:T(128)S(1)} %bitcast.129, bf16[1024,1152]{1,0:T(8,128)(2,1)S(1)} %multiply_convert_fusion.1.own, bf16[1024,1152]{1,0:T(8,128)(2,1)S(1)} %multiply_convert_fusion.sib, ...), custom_call_target="tpu_custom_call" | custom-call | flops 1000000000 | bytes 1000000 | tf_op jit(solution)/shard_map/attend_forward/pallas_call | solution.py:145
  132.7 48.4 %middle.1 = (bf16[1024,768]{1,0:T(8,128)(2,1)S(1)}, bf16[1024,768]{1,0:T(8,128)(2,1)}, bf16[1024,3072]{1,0:T(8,128)(2,1)}, bf16[1024,768]{1,0:T(8,128)(2,1)}, bf...) custom-call(s32[1]{0:T(128)} %bitcast.core_ref, ...), custom_call_target="tpu_custom_call" | custom-call | flops 20000000000 | bytes 30000000 | tf_op jit(solution)/shard_map/middle/pallas_call | solution.py:420
  186.8 1.4 copy-done.15
  189.7 18.1 %gradients.1 = (bf16[4,896,768]{2,1,0:T(8,128)(2,1)}, bf16[4,896,768]{2,1,0:T(8,128)(2,1)}) custom-call(s32[1]{0:T(128)} %bitcast.core_ref, bf16[1024,3072]{1,0:T(8,128)(2,1)} %get-tuple-element.69.act_ref, bf16[1024,768]{1,0:T(8,128)(2,1)S(1)} %copy-done.15, bf16[1024,768]{1,0:T(8,128)(2,1)S(1)} %copy-done.16, ...), custom_call_target="tpu_custom_call" | custom-call | flops 11000000512 | bytes 30000000 | tf_op jit(solution)/shard_map/gradients/pallas_call | solution.py:522
  208.3 2.6 fusion.29
  211.0 5.9 %collective-permute-start.9 = (bf16[512,768]{1,0:T(8,128)(2,1)}, bf16[512,768]{1,0:T(8,128)(2,1)}, u32[]{:S(2)}, u32[]{:S(2)}) collective-permute-start(bf16[512,768]{1,0:T(8,128)(2,1)} %get-tuple-element.127), channel_id=1, source_target_pairs={{0,0},{1,1},{4,2},{5,3},{2,4},{3,5},{6,6},{7,7},{8,8},{9,9},{12,10... | collective-permute-start | bytes 2359304 | tf_op jit(solution)/shard_map/ppermute | solution.py:707
  217.2 5.5 %add_convert_fusion = bf16[4,896,768]{2,1,0:T(8,128)(2,1)S(1)} fusion(bf16[4,896,768]{2,1,0:T(8,128)(2,1)} %collective-permute-done.10, bf16[4,896,768]{2,1,0:T(8,128)(2,1)} %get-tuple-element.76), kind=kLoop, calls=%fused_computation | loop fusion | flops 11010048 | bytes 16515072 | tf_op jit(solution)/shard_map/convert_element_type | solution.py:575
  223.2 3.7 collective-permute-start.13
  227.1 21.3 %attend_backward_0.1 = (bf16[1024,384]{1,0:T(8,128)(2,1)S(1)}, bf16[1024,384]{1,0:T(8,128)(2,1)S(1)}) custom-call(s32[1]{0:T(128)} %bitcast.13.mask_ref, s32[8]{0:T(128)S(1)} %bitcast.130, bf16[1024,1152]{1,0:T(8,128)(2,1)S(1)} %copy-done.1, bf16[1024,1152]{1,0:T(8,128)(2,1)S(1)} %multiply_convert_fusion.sib, bf16[1024,384]{1,0:T(8,128)(2,1)S(1)} %copy-done.6, ...), custom_call_target="tpu_custom_call" | custom-call | flops 20000000000 | bytes 8000000 | tf_op jit(solution)/shard_map/attend_backward_0/pallas_call | solution.py:249
  248.6 6.7 %collective-permute-done.13 = bf16[2,448,768]{2,1,0:T(8,128)(2,1)S(1)} collective-permute-done((bf16[2,448,768]{2,1,0:T(8,128)(2,1)S(1)}, bf16[2,448,768]{2,1,0:T(8,128)(2,1)S(1)}, u32[]{:S(2)}, u32[]{:S(2)}) %collective-permute-start.13) | collective-permute-done | bytes 1376288 | tf_op jit(solution)/shard_map/ppermute | solution.py:600
  258.0 21.3 %attend_backward_1.1 = (bf16[1024,384]{1,0:T(8,128)(2,1)S(1)}, bf16[1024,384]{1,0:T(8,128)(2,1)S(1)}) custom-call(s32[1]{0:T(128)} %bitcast.13.mask_ref, s32[8]{0:T(128)S(1)} %bitcast.131, bf16[1024,1152]{1,0:T(8,128)(2,1)S(1)} %copy-done.1, bf16[1024,1152]{1,0:T(8,128)(2,1)S(1)} %multiply_convert_fusion.sib, bf16[1024,384]{1,0:T(8,128)(2,1)S(1)} %copy-done.6, ...), custom_call_target="tpu_custom_call" | custom-call | flops 20000000000 | bytes 8000000 | tf_op jit(solution)/shard_map/attend_backward_1/pallas_call | solution.py:249
  280.0 1.4 fusion.20
  281.4 3.4 collective-permute-start.31
  284.8 2.9 collective-permute-start.32
  287.7 1.5 collective-permute-start.33
  289.3 21.3 %attend_backward_2.1 = (bf16[1024,384]{1,0:T(8,128)(2,1)S(1)}, bf16[1024,384]{1,0:T(8,128)(2,1)S(1)}) custom-call(s32[1]{0:T(128)} %bitcast.13.mask_ref, s32[8]{0:T(128)S(1)} %bitcast.132, bf16[1024,1152]{1,0:T(8,128)(2,1)S(1)} %copy-done.1, bf16[1024,1152]{1,0:T(8,128)(2,1)S(1)} %multiply_convert_fusion.sib, bf16[1024,384]{1,0:T(8,128)(2,1)S(1)} %copy-done.6, ...), custom_call_target="tpu_custom_call" | custom-call | flops 20000000000 | bytes 8000000 | tf_op jit(solution)/shard_map/attend_backward_2/pallas_call | solution.py:249
  312.2 2.2 convolution_convert_fusion
  315.8 2.2 fusion.32
  318.0 2.3 fusion.31
  320.3 3.7 fusion
  324.4 1.6 copy-done.21
  327.6 2.4 collective-permute-start.36
  331.1 4.5 %collective-permute-start.23 = (bf16[512,768]{1,0:T(8,128)(2,1)S(1)}, bf16[512,768]{1,0:T(8,128)(2,1)S(1)}, u32[]{:S(2)}, u32[]{:S(2)}) collective-permute-start(bf16[512,768]{1,0:T(8,128)(2,1)S(1)} %get-tuple-element.126), channel_id=1, source_target_pairs={{0,0},{1,1},{4,2},{5,3},{2,4},{3,5},{6,6},{7,7},{8,8},{9,9},{12,10... | collective-permute-start | bytes 2359304 | tf_op jit(solution)/shard_map/ppermute | solution.py:777
  335.7 6.2 %collective-permute-done.20 = bf16[2,128,1152]{2,1,0:T(8,128)(2,1)S(1)} collective-permute-done((bf16[2,128,1152]{2,1,0:T(8,128)(2,1)S(1)}, bf16[2,128,1152]{2,1,0:T(8,128)(2,1)S(1)}, u32[]{:S(2)}, u32[]{:S(2)}) %collective-permute-start.20) | collective-permute-done | bytes 589856 | tf_op jit(solution)/shard_map/ppermute | solution.py:600
  342.9 2.4 collective-permute-done.18
  345.5 6.9 %collective-permute-done.21 = bf16[128,1152]{1,0:T(8,128)(2,1)S(1)} collective-permute-done((bf16[128,1152]{1,0:T(8,128)(2,1)S(1)}, bf16[128,1152]{1,0:T(8,128)(2,1)S(1)}, u32[]{:S(2)}, u32[]{:S(2)}) %collective-permute-start.21) | collective-permute-done | bytes 294944 | tf_op jit(solution)/shard_map/ppermute | solution.py:600
  353.1 5.6 %collective-permute-done.19 = bf16[128,1152]{1,0:T(8,128)(2,1)S(1)} collective-permute-done((bf16[128,1152]{1,0:T(8,128)(2,1)S(1)}, bf16[128,1152]{1,0:T(8,128)(2,1)S(1)}, u32[]{:S(2)}, u32[]{:S(2)}) %collective-permute-start.19) | collective-permute-done | bytes 294944 | tf_op jit(solution)/shard_map/ppermute | solution.py:600
  359.2 1.5 collective-permute-start.22
  360.7 19.7 %collective-permute-done.23 = bf16[512,768]{1,0:T(8,128)(2,1)S(1)} collective-permute-done((bf16[512,768]{1,0:T(8,128)(2,1)S(1)}, bf16[512,768]{1,0:T(8,128)(2,1)S(1)}, u32[]{:S(2)}, u32[]{:S(2)}) %collective-permute-start.23) | collective-permute-done | bytes 786464 | tf_op jit(solution)/shard_map/ppermute | solution.py:777
  380.4 17.1 %collective-permute-done.24 = bf16[512,768]{1,0:T(8,128)(2,1)S(1)} collective-permute-done((bf16[512,768]{1,0:T(8,128)(2,1)S(1)}, bf16[512,768]{1,0:T(8,128)(2,1)S(1)}, u32[]{:S(2)}, u32[]{:S(2)}) %collective-permute-start.24) | collective-permute-done | bytes 786464 | tf_op jit(solution)/shard_map/ppermute | solution.py:777
  397.5 1.9 fusion.3
  399.5 1.5 collective-permute-start.34
  400.9 1.9 collective-permute-done.26
  403.1 4.9 %collective-permute-done.34 = bf16[224,768]{1,0:T(8,128)(2,1)S(1)} collective-permute-done((bf16[224,768]{1,0:T(8,128)(2,1)S(1)}, bf16[224,768]{1,0:T(8,128)(2,1)S(1)}, u32[]{:S(2)}, u32[]{:S(2)}) %collective-permute-start.34) | collective-permute-done | bytes 344096 | tf_op jit(solution)/shard_map/ppermute | solution.py:619
  410.0 2.2 collective-permute-start.27
  415.7 8.3 %collective-permute-done.28 = bf16[64,1152]{1,0:T(8,128)(2,1)S(1)} collective-permute-done((bf16[64,1152]{1,0:T(8,128)(2,1)S(1)}, bf16[64,1152]{1,0:T(8,128)(2,1)S(1)}, u32[]{:S(2)}, u32[]{:S(2)}) %collective-permute-start.28) | collective-permute-done | bytes 147488 | tf_op jit(solution)/shard_map/ppermute | solution.py:619
  424.2 1.7 collective-permute-start.30
  426.0 3.3 maximum_select_fusion
  432.3 1.6 reshape.382
  (251 shorter events, 46.7 us)
Async XLA Ops:
  7.2 50.9 %all-gather.6.cloned.1.call-start = ((), (), s32[]{:S(2)}) async-start(), calls=%async_computation | async-start | bytes 2211840 | tf_op jit(solution)/shard_map/all_gather | solution.py:676
  9.6 1.8 collective-permute-start.3
  12.3 118.2 %all-gather.8.cloned.1.call-start = ((), (), s32[]{:S(2)}) async-start(), calls=%async_computation.1 | async-start | bytes 11943936 | tf_op jit(solution)/shard_map/all_gather | solution.py:686
  14.7 5.7 %copy-start.28 = (bf16[384]{0:T(512)(128)(2,1)S(1)}, bf16[384]{0:T(512)(128)(2,1)}, u32[]{:S(2)}) copy-start(bf16[384]{0:T(512)(128)(2,1)} %param.26) | copy-start | bytes 2308
  14.7 5.8 %copy-start.29 = (bf16[96]{0:T(256)(128)(2,1)S(1)}, bf16[96]{0:T(256)(128)(2,1)}, u32[]{:S(2)}) copy-start(bf16[96]{0:T(256)(128)(2,1)} %param.19) | copy-start | bytes 580
  14.7 5.8 %copy-start.30 = (bf16[96]{0:T(256)(128)(2,1)S(1)}, bf16[96]{0:T(256)(128)(2,1)}, u32[]{:S(2)}) copy-start(bf16[96]{0:T(256)(128)(2,1)} %param.20) | copy-start | bytes 580
  14.7 5.8 %copy-start.31 = (bf16[96]{0:T(256)(128)(2,1)S(1)}, bf16[96]{0:T(256)(128)(2,1)}, u32[]{:S(2)}) copy-start(bf16[96]{0:T(256)(128)(2,1)} %param.22) | copy-start | bytes 580
  14.7 5.8 %copy-start.32 = (bf16[96]{0:T(256)(128)(2,1)S(1)}, bf16[96]{0:T(256)(128)(2,1)}, u32[]{:S(2)}) copy-start(bf16[96]{0:T(256)(128)(2,1)} %param.23) | copy-start | bytes 580
  14.7 5.8 %copy-start.33 = (bf16[96]{0:T(256)(128)(2,1)S(1)}, bf16[96]{0:T(256)(128)(2,1)}, u32[]{:S(2)}) copy-start(bf16[96]{0:T(256)(128)(2,1)} %param.24) | copy-start | bytes 580
  14.7 5.8 %copy-start.34 = (bf16[96]{0:T(256)(128)(2,1)S(1)}, bf16[96]{0:T(256)(128)(2,1)}, u32[]{:S(2)}) copy-start(bf16[96]{0:T(256)(128)(2,1)} %param.28) | copy-start | bytes 580
  14.7 5.8 %copy-start.35 = (bf16[96]{0:T(256)(128)(2,1)S(1)}, bf16[96]{0:T(256)(128)(2,1)}, u32[]{:S(2)}) copy-start(bf16[96]{0:T(256)(128)(2,1)} %param.29) | copy-start | bytes 580
  14.7 5.8 %copy-start.36 = (bf16[96]{0:T(256)(128)(2,1)S(1)}, bf16[96]{0:T(256)(128)(2,1)}, u32[]{:S(2)}) copy-start(bf16[96]{0:T(256)(128)(2,1)} %param.30) | copy-start | bytes 580
  15.8 30.2 %collective-permute-start = (bf16[512,768]{1,0:T(8,128)(2,1)S(1)}, bf16[512,768]{1,0:T(8,128)(2,1)S(1)}, u32[]{:S(2)}, u32[]{:S(2)}) collective-permute-start(bf16[512,768]{1,0:T(8,128)(2,1)S(1)} %get-tuple-element.131), channel_id=1, source_target_pairs={{0,0},{1,1},{2,4},{3,5},{4,2},{5,3},{6,6},{7,7},{8,8},{9,9},{10,12... | collective-permute-start | bytes 2359304 | tf_op jit(solution)/shard_map/ppermute | solution.py:659
  20.2 34.2 %collective-permute-start.1 = (bf16[512,768]{1,0:T(8,128)(2,1)}, bf16[512,768]{1,0:T(8,128)(2,1)S(1)}, u32[]{:S(2)}, u32[]{:S(2)}) collective-permute-start(bf16[512,768]{1,0:T(8,128)(2,1)} %get-tuple-element.132), channel_id=1, source_target_pairs={{0,1},{1,0},{2,5},{3,4},{4,3},{5,2},{6,7},{7,6},{8,9},{9,8},{10,13... | collective-permute-start | bytes 2359304 | tf_op jit(solution)/shard_map/ppermute | solution.py:659
  20.3 34.5 %collective-permute-start.2 = (s32[2,8]{1,0:T(2,128)S(1)}, s32[2,8]{1,0:T(2,128)S(1)}, u32[]{:S(2)}, u32[]{:S(2)}) collective-permute-start(s32[2,8]{1,0:T(2,128)S(1)} %bitcast.151), channel_id=1, source_target_pairs={{0,4},{4,0},{1,5},{5,1},{2,6},{6,2},{3,7},{7,3},{8,12},{12,8},{9,1... | collective-permute-start | bytes 200 | tf_op jit(solution)/shard_map/ppermute | solution.py:563
  45.9 10.3 %collective-permute-start.4 = (bf16[512,768]{1,0:T(8,128)(2,1)S(1)}, bf16[512,768]{1,0:T(8,128)(2,1)S(1)}, u32[]{:S(2)}, u32[]{:S(2)}) collective-permute-start(bf16[512,768]{1,0:T(8,128)(2,1)S(1)} %collective-permute-done), channel_id=1, source_target_pairs={{0,4},{4,0},{1,5},{5,1},{2,6},{6,2},{3,7},{7,3},{8,12},{12,8},{9,1... | collective-permute-start | bytes 2359304 | tf_op jit(solution)/shard_map/ppermute | solution.py:563
  54.5 2.7 collective-permute-start.5
  65.1 62.2 %collective-permute-start.7 = (bf16[512,768]{1,0:T(8,128)(2,1)S(1)}, bf16[512,768]{1,0:T(8,128)(2,1)S(1)}, u32[]{:S(2)}, u32[]{:S(2)}) collective-permute-start(bf16[512,768]{1,0:T(8,128)(2,1)S(1)} %get-tuple-element.129), channel_id=1, source_target_pairs={{0,0},{1,1},{2,4},{3,5},{4,2},{5,3},{6,6},{7,7},{8,8},{9,9},{10,12... | collective-permute-start | bytes 2359304 | tf_op jit(solution)/shard_map/ppermute | solution.py:659
  67.3 60.0 %collective-permute-start.8 = (bf16[512,768]{1,0:T(8,128)(2,1)S(1)}, bf16[512,768]{1,0:T(8,128)(2,1)S(1)}, u32[]{:S(2)}, u32[]{:S(2)}) collective-permute-start(bf16[512,768]{1,0:T(8,128)(2,1)S(1)} %get-tuple-element.130), channel_id=1, source_target_pairs={{0,1},{1,0},{2,5},{3,4},{4,3},{5,2},{6,7},{7,6},{8,9},{9,8},{10,13... | collective-permute-start | bytes 2359304 | tf_op jit(solution)/shard_map/ppermute | solution.py:659
  127.3 2.3 collective-permute-start.6
  207.8 9.4 %collective-permute-start.10 = (bf16[4,896,768]{2,1,0:T(8,128)(2,1)}, bf16[4,896,768]{2,1,0:T(8,128)(2,1)}, u32[]{:S(2)}, u32[]{:S(2)}) collective-permute-start(bf16[4,896,768]{2,1,0:T(8,128)(2,1)} %get-tuple-element.77), channel_id=1, source_target_pairs={{0,4},{4,0},{1,5},{5,1},{2,6},{6,2},{3,7},{7,3},{8,12},{12,8},{9,1... | collective-permute-start | bytes 16515080 | tf_op jit(solution)/shard_map/ppermute | solution.py:563
  208.1 19.0 %collective-permute-start.12 = (bf16[1024,384]{1,0:T(8,128)(2,1)}, bf16[1024,384]{1,0:T(8,128)(2,1)S(1)}, u32[]{:S(2)}, u32[]{:S(2)}) collective-permute-start(bf16[1024,384]{1,0:T(8,128)(2,1)} %copy-done.9), channel_id=1, source_target_pairs={{0,4},{4,0},{1,5},{5,1},{2,6},{6,2},{3,7},{7,3},{8,12},{12,8},{9,1... | collective-permute-start | bytes 2359304 | tf_op jit(solution)/shard_map/ppermute | solution.py:563
  211.0 68.3 %collective-permute-start.9 = (bf16[512,768]{1,0:T(8,128)(2,1)}, bf16[512,768]{1,0:T(8,128)(2,1)}, u32[]{:S(2)}, u32[]{:S(2)}) collective-permute-start(bf16[512,768]{1,0:T(8,128)(2,1)} %get-tuple-element.127), channel_id=1, source_target_pairs={{0,0},{1,1},{4,2},{5,3},{2,4},{3,5},{6,6},{7,7},{8,8},{9,9},{12,10... | collective-permute-start | bytes 2359304 | tf_op jit(solution)/shard_map/ppermute | solution.py:707
  216.9 62.4 %collective-permute-start.16 = (bf16[512,768]{1,0:T(8,128)(2,1)}, bf16[512,768]{1,0:T(8,128)(2,1)}, u32[]{:S(2)}, u32[]{:S(2)}) collective-permute-start(bf16[512,768]{1,0:T(8,128)(2,1)} %get-tuple-element.128), channel_id=1, source_target_pairs={{1,0},{0,1},{5,2},{4,3},{3,4},{2,5},{7,6},{6,7},{9,8},{8,9},{13,10... | collective-permute-start | bytes 2359304 | tf_op jit(solution)/shard_map/ppermute | solution.py:707
  223.2 32.1 %collective-permute-start.13 = (bf16[2,448,768]{2,1,0:T(8,128)(2,1)S(1)}, bf16[2,448,768]{2,1,0:T(8,128)(2,1)S(1)}, u32[]{:S(2)}, u32[]{:S(2)}) collective-permute-start(bf16[2,448,768]{2,1,0:T(8,128)(2,1)S(1)} %dynamic-slice_bitcast_fusion), channel_id=1, source_target_pairs={{0,16},{8,24},{16,0},{24,8},{1,17},{9,25},{17,1},{25,9},{2,18},{10... | collective-permute-start | bytes 4128776 | tf_op jit(solution)/shard_map/ppermute | solution.py:600
  227.0 29.9 %collective-permute-start.11 = (bf16[2,448,768]{2,1,0:T(8,128)(2,1)S(1)}, bf16[2,448,768]{2,1,0:T(8,128)(2,1)S(1)}, u32[]{:S(2)}, u32[]{:S(2)}) collective-permute-start(bf16[2,448,768]{2,1,0:T(8,128)(2,1)S(1)} %dynamic-slice_bitcast_fusion.1), channel_id=1, source_target_pairs={{0,8},{8,0},{16,24},{24,16},{1,9},{9,1},{17,25},{25,17},{2,10},{10... | collective-permute-start | bytes 4128776 | tf_op jit(solution)/shard_map/ppermute | solution.py:600
  257.3 22.4 %collective-permute-start.15 = (bf16[448,768]{1,0:T(8,128)(2,1)S(1)}, bf16[448,768]{1,0:T(8,128)(2,1)S(1)}, u32[]{:S(2)}, u32[]{:S(2)}) collective-permute-start(bf16[448,768]{1,0:T(8,128)(2,1)S(1)} %dynamic-slice_bitcast_fusion.6), channel_id=1, source_target_pairs={{0,8},{8,0},{16,24},{24,16},{1,9},{9,1},{17,25},{25,17},{2,10},{10... | collective-permute-start | bytes 2064392 | tf_op jit(solution)/shard_map/ppermute | solution.py:600
  257.6 22.2 %collective-permute-start.14 = (bf16[448,768]{1,0:T(8,128)(2,1)S(1)}, bf16[448,768]{1,0:T(8,128)(2,1)S(1)}, u32[]{:S(2)}, u32[]{:S(2)}) collective-permute-start(bf16[448,768]{1,0:T(8,128)(2,1)S(1)} %dynamic-slice_bitcast_fusion.7), channel_id=1, source_target_pairs={{0,16},{8,24},{16,0},{24,8},{1,17},{9,25},{17,1},{25,9},{2,18},{10... | collective-permute-start | bytes 2064392 | tf_op jit(solution)/shard_map/ppermute | solution.py:600
  281.4 42.9 %collective-permute-start.31 = (bf16[224,768]{1,0:T(8,128)(2,1)S(1)}, bf16[224,768]{1,0:T(8,128)(2,1)S(1)}, u32[]{:S(2)}, u32[]{:S(2)}) collective-permute-start(bf16[224,768]{1,0:T(8,128)(2,1)S(1)} %get-tuple-element.139), channel_id=1, source_target_pairs={{0,1},{1,2},{2,3},{3,0},{4,5},{5,6},{6,7},{7,4},{8,9},{9,10},{10,1... | collective-permute-start | bytes 1032200 | tf_op jit(solution)/shard_map/ppermute | solution.py:619
  284.8 39.5 %collective-permute-start.32 = (bf16[224,768]{1,0:T(8,128)(2,1)S(1)}, bf16[224,768]{1,0:T(8,128)(2,1)S(1)}, u32[]{:S(2)}, u32[]{:S(2)}) collective-permute-start(bf16[224,768]{1,0:T(8,128)(2,1)S(1)} %get-tuple-element.140), channel_id=1, source_target_pairs={{0,2},{1,3},{2,0},{3,1},{4,6},{5,7},{6,4},{7,5},{8,10},{9,11},{10,... | collective-permute-start | bytes 1032200 | tf_op jit(solution)/shard_map/ppermute | solution.py:619
  287.7 36.7 %collective-permute-start.33 = (bf16[224,768]{1,0:T(8,128)(2,1)S(1)}, bf16[224,768]{1,0:T(8,128)(2,1)S(1)}, u32[]{:S(2)}, u32[]{:S(2)}) collective-permute-start(bf16[224,768]{1,0:T(8,128)(2,1)S(1)} %get-tuple-element.138), channel_id=1, source_target_pairs={{0,3},{1,0},{2,1},{3,2},{4,7},{5,4},{6,5},{7,6},{8,11},{9,8},{10,9... | collective-permute-start | bytes 1032200 | tf_op jit(solution)/shard_map/ppermute | solution.py:619
  314.4 10.0 %collective-permute-start.17 = (bf16[1024,768]{1,0:T(8,128)(2,1)S(1)}, bf16[1024,768]{1,0:T(8,128)(2,1)S(1)}, u32[]{:S(2)}, u32[]{:S(2)}) collective-permute-start(bf16[1024,768]{1,0:T(8,128)(2,1)S(1)} %convolution_convert_fusion), channel_id=1, source_target_pairs={{0,4},{4,0},{1,5},{5,1},{2,6},{6,2},{3,7},{7,3},{8,12},{12,8},{9,1... | collective-permute-start | bytes 4718600 | tf_op jit(solution)/shard_map/ppermute | solution.py:563
  326.9 14.9 %collective-permute-start.20 = (bf16[2,128,1152]{2,1,0:T(8,128)(2,1)S(1)}, bf16[2,128,1152]{2,1,0:T(8,128)(2,1)S(1)}, u32[]{:S(2)}, u32[]{:S(2)}) collective-permute-start(bf16[2,128,1152]{2,1,0:T(8,128)(2,1)S(1)} %dynamic-slice_bitcast_fusion.8), channel_id=1, source_target_pairs={{0,16},{8,24},{16,0},{24,8},{1,17},{9,25},{17,1},{25,9},{2,18},{10... | collective-permute-start | bytes 1769480 | tf_op jit(solution)/shard_map/ppermute | solution.py:600
  327.6 75.5 %collective-permute-start.36 = (bf16[224,768]{1,0:T(8,128)(2,1)S(1)}, bf16[224,768]{1,0:T(8,128)(2,1)S(1)}, u32[]{:S(2)}, u32[]{:S(2)}) collective-permute-start(bf16[224,768]{1,0:T(8,128)(2,1)S(1)} %get-tuple-element.118), channel_id=1, source_target_pairs={{0,3},{1,0},{2,1},{3,2},{4,7},{5,4},{6,5},{7,6},{8,11},{9,8},{10,9... | collective-permute-start | bytes 1032200 | tf_op jit(solution)/shard_map/ppermute | solution.py:619
  330.0 73.1 %collective-permute-start.35 = (bf16[224,768]{1,0:T(8,128)(2,1)S(1)}, bf16[224,768]{1,0:T(8,128)(2,1)S(1)}, u32[]{:S(2)}, u32[]{:S(2)}) collective-permute-start(bf16[224,768]{1,0:T(8,128)(2,1)S(1)} %get-tuple-element.118), channel_id=1, source_target_pairs={{0,2},{1,3},{2,0},{3,1},{4,6},{5,7},{6,4},{7,5},{8,10},{9,11},{10,... | collective-permute-start | bytes 1032200 | tf_op jit(solution)/shard_map/ppermute | solution.py:619
  330.9 14.4 %collective-permute-start.18 = (bf16[2,128,1152]{2,1,0:T(8,128)(2,1)S(1)}, bf16[2,128,1152]{2,1,0:T(8,128)(2,1)S(1)}, u32[]{:S(2)}, u32[]{:S(2)}) collective-permute-start(bf16[2,128,1152]{2,1,0:T(8,128)(2,1)S(1)} %dynamic-slice_bitcast_fusion.9), channel_id=1, source_target_pairs={{0,8},{8,0},{16,24},{24,16},{1,9},{9,1},{17,25},{25,17},{2,10},{10... | collective-permute-start | bytes 1769480 | tf_op jit(solution)/shard_map/ppermute | solution.py:600
  331.1 49.3 %collective-permute-start.23 = (bf16[512,768]{1,0:T(8,128)(2,1)S(1)}, bf16[512,768]{1,0:T(8,128)(2,1)S(1)}, u32[]{:S(2)}, u32[]{:S(2)}) collective-permute-start(bf16[512,768]{1,0:T(8,128)(2,1)S(1)} %get-tuple-element.126), channel_id=1, source_target_pairs={{0,0},{1,1},{4,2},{5,3},{2,4},{3,5},{6,6},{7,7},{8,8},{9,9},{12,10... | collective-permute-start | bytes 2359304 | tf_op jit(solution)/shard_map/ppermute | solution.py:777
  341.9 55.7 %collective-permute-start.24 = (bf16[512,768]{1,0:T(8,128)(2,1)S(1)}, bf16[512,768]{1,0:T(8,128)(2,1)S(1)}, u32[]{:S(2)}, u32[]{:S(2)}) collective-permute-start(bf16[512,768]{1,0:T(8,128)(2,1)S(1)} %get-tuple-element.125), channel_id=1, source_target_pairs={{1,0},{0,1},{5,2},{4,3},{3,4},{2,5},{7,6},{6,7},{9,8},{8,9},{13,10... | collective-permute-start | bytes 2359304 | tf_op jit(solution)/shard_map/ppermute | solution.py:777
  345.3 7.1 %collective-permute-start.21 = (bf16[128,1152]{1,0:T(8,128)(2,1)S(1)}, bf16[128,1152]{1,0:T(8,128)(2,1)S(1)}, u32[]{:S(2)}, u32[]{:S(2)}) collective-permute-start(bf16[128,1152]{1,0:T(8,128)(2,1)S(1)} %dynamic-slice_bitcast_fusion.10), channel_id=1, source_target_pairs={{0,8},{8,0},{16,24},{24,16},{1,9},{9,1},{17,25},{25,17},{2,10},{10... | collective-permute-start | bytes 884744 | tf_op jit(solution)/shard_map/ppermute | solution.py:600
  352.4 6.3 %collective-permute-start.19 = (bf16[128,1152]{1,0:T(8,128)(2,1)S(1)}, bf16[128,1152]{1,0:T(8,128)(2,1)S(1)}, u32[]{:S(2)}, u32[]{:S(2)}) collective-permute-start(bf16[128,1152]{1,0:T(8,128)(2,1)S(1)} %dynamic-slice_bitcast_fusion.11), channel_id=1, source_target_pairs={{0,16},{8,24},{16,0},{24,8},{1,17},{9,25},{17,1},{25,9},{2,18},{10... | collective-permute-start | bytes 884744 | tf_op jit(solution)/shard_map/ppermute | solution.py:600
  359.2 40.3 %collective-permute-start.22 = (bf16[64,1152]{1,0:T(8,128)(2,1)S(1)}, bf16[64,1152]{1,0:T(8,128)(2,1)S(1)}, u32[]{:S(2)}, u32[]{:S(2)}) collective-permute-start(bf16[64,1152]{1,0:T(8,128)(2,1)S(1)} %get-tuple-element.143), channel_id=1, source_target_pairs={{0,1},{1,2},{2,3},{3,0},{4,5},{5,6},{6,7},{7,4},{8,9},{9,10},{10,1... | collective-permute-start | bytes 442376 | tf_op jit(solution)/shard_map/ppermute | solution.py:619
  380.4 20.5 %collective-permute-start.25 = (bf16[64,1152]{1,0:T(8,128)(2,1)S(1)}, bf16[64,1152]{1,0:T(8,128)(2,1)S(1)}, u32[]{:S(2)}, u32[]{:S(2)}) collective-permute-start(bf16[64,1152]{1,0:T(8,128)(2,1)S(1)} %get-tuple-element.144), channel_id=1, source_target_pairs={{0,2},{1,3},{2,0},{3,1},{4,6},{5,7},{6,4},{7,5},{8,10},{9,11},{10,... | collective-permute-start | bytes 442376 | tf_op jit(solution)/shard_map/ppermute | solution.py:619
  397.5 5.4 %collective-permute-start.26 = (bf16[64,1152]{1,0:T(8,128)(2,1)S(1)}, bf16[64,1152]{1,0:T(8,128)(2,1)S(1)}, u32[]{:S(2)}, u32[]{:S(2)}) collective-permute-start(bf16[64,1152]{1,0:T(8,128)(2,1)S(1)} %get-tuple-element.145), channel_id=1, source_target_pairs={{0,3},{1,0},{2,1},{3,2},{4,7},{5,4},{6,5},{7,6},{8,11},{9,8},{10,9... | collective-permute-start | bytes 442376 | tf_op jit(solution)/shard_map/ppermute | solution.py:619
  399.5 8.5 %collective-permute-start.34 = (bf16[224,768]{1,0:T(8,128)(2,1)S(1)}, bf16[224,768]{1,0:T(8,128)(2,1)S(1)}, u32[]{:S(2)}, u32[]{:S(2)}) collective-permute-start(bf16[224,768]{1,0:T(8,128)(2,1)S(1)} %get-tuple-element.118), channel_id=1, source_target_pairs={{0,1},{1,2},{2,3},{3,0},{4,5},{5,6},{6,7},{7,4},{8,9},{9,10},{10,1... | collective-permute-start | bytes 1032200 | tf_op jit(solution)/shard_map/ppermute | solution.py:619
  410.0 5.7 %collective-permute-start.27 = (bf16[64,1152]{1,0:T(8,128)(2,1)S(1)}, bf16[64,1152]{1,0:T(8,128)(2,1)S(1)}, u32[]{:S(2)}, u32[]{:S(2)}) collective-permute-start(bf16[64,1152]{1,0:T(8,128)(2,1)S(1)} %get-tuple-element.120), channel_id=1, source_target_pairs={{0,1},{1,2},{2,3},{3,0},{4,5},{5,6},{6,7},{7,4},{8,9},{9,10},{10,1... | collective-permute-start | bytes 442376 | tf_op jit(solution)/shard_map/ppermute | solution.py:619
  412.2 11.9 %collective-permute-start.28 = (bf16[64,1152]{1,0:T(8,128)(2,1)S(1)}, bf16[64,1152]{1,0:T(8,128)(2,1)S(1)}, u32[]{:S(2)}, u32[]{:S(2)}) collective-permute-start(bf16[64,1152]{1,0:T(8,128)(2,1)S(1)} %get-tuple-element.120), channel_id=1, source_target_pairs={{0,2},{1,3},{2,0},{3,1},{4,6},{5,7},{6,4},{7,5},{8,10},{9,11},{10,... | collective-permute-start | bytes 442376 | tf_op jit(solution)/shard_map/ppermute | solution.py:619
  412.2 11.9 %collective-permute-start.29 = (bf16[64,1152]{1,0:T(8,128)(2,1)S(1)}, bf16[64,1152]{1,0:T(8,128)(2,1)S(1)}, u32[]{:S(2)}, u32[]{:S(2)}) collective-permute-start(bf16[64,1152]{1,0:T(8,128)(2,1)S(1)} %get-tuple-element.120), channel_id=1, source_target_pairs={{0,3},{1,0},{2,1},{3,2},{4,7},{5,4},{6,5},{7,6},{8,11},{9,8},{10,9... | collective-permute-start | bytes 442376 | tf_op jit(solution)/shard_map/ppermute | solution.py:619
  424.2 5.5 %collective-permute-start.30 = (bf16[112,1152]{1,0:T(8,128)(2,1)S(1)}, bf16[112,1152]{1,0:T(8,128)(2,1)S(1)}, u32[]{:S(2)}, u32[]{:S(2)}) collective-permute-start(bf16[112,1152]{1,0:T(8,128)(2,1)S(1)} %pad_maximum_fusion.3), channel_id=1, source_target_pairs={{0,4},{4,0},{1,5},{5,1},{2,6},{6,2},{3,7},{7,3},{8,12},{12,8},{9,1... | collective-permute-start | bytes 774152 | tf_op jit(solution)/shard_map/ppermute | solution.py:563
  (31 other events, 73.9 us)
Sparse Core Ops, SparseCore 0:
  12.4 33.2 all-gather.5
  48.1 64.3 all-gather.7

commit v8 on v7

--- a/solution.py
+++ b/solution.py
@@ -14,8 +14,8 @@
 NEG = -1e30
 TILE = 256
 VALUE_ROWS = HEAD_DIM + 16
-KEY_TILES = 2
-QUERY_TILES = 2
+KEY_TILES = 1
+QUERY_TILES = 1
 NT = (((1,), (1,)), ((), ()))
 NN = (((1,), (0,)), ((), ()))
 TN = (((0,), (0,)), ((), ()))
@@ -110,8 +110,14 @@
                 keys = [qkv[pairs + pair, pl.ds(at, KEY_TILES * TILE), :] for pair in range(pairs)]
                 segk = seg_col[pl.ds(at, KEY_TILES * TILE), :]
                 same = jnp.concatenate([segk] * (TILE // LANES), axis=1) == segq
+                def scores_of(head):
+                    return jnp.where(same, mm(keys[head // 2], q_heads[head], NT), NEG)
+
+                queue = [scores_of(head) for head in range(6)]
                 for head in range(2 * pairs):
-                    scores = jnp.where(same, mm(keys[head // 2], q_heads[head], NT), NEG)
+                    if head + 6 < 2 * pairs:
+                        queue.append(scores_of(head + 6))
+                    scores = queue.pop(0)
                     old = top[head, 0:1]
                     new = jnp.maximum(old, jnp.max(scores, axis=0, keepdims=True))
                     probs = jnp.exp(scores - new).astype(jnp.bfloat16)
@@ -215,15 +221,18 @@
             q_heads = lane_halves(queries, 0.0)
             g_heads = lane_halves(grads, 0.0)
             same = jnp.concatenate([segk] * QUERY_TILES, axis=1) == seg_row[:, span]
+            scores = [mm(k_heads[head], queries, NT) for head in range(2)]
+            dprobs = [mm(v_heads[head], grads, NT) for head in range(2)]
+            low, dscores = [], []
             for head in range(2):
-                scores = mm(k_heads[head], queries, NT)
-                probs = jnp.exp(jnp.where(same, scores - lse_ref[2 * pair + head, 0:1, span], NEG))
-                dprobs = mm(v_heads[head], grads, NT)
-                dscores = (probs * (dprobs - delta[head, 0:1, span])).astype(jnp.bfloat16)
-                dkv[1] += mm(probs.astype(jnp.bfloat16), g_heads[head], NN)
-                dkv[0] += mm(dscores, q_heads[head], NN)
+                probs = jnp.exp(jnp.where(same, scores[head] - lse_ref[2 * pair + head, 0:1, span], NEG))
+                low.append(probs.astype(jnp.bfloat16))
+                dscores.append((probs * (dprobs[head] - delta[head, 0:1, span])).astype(jnp.bfloat16))
+            dkv[1] += mm(low[0], g_heads[0], NN) + mm(low[1], g_heads[1], NN)
+            dkv[0] += mm(dscores[0], q_heads[0], NN) + mm(dscores[1], q_heads[1], NN)
+            for head in range(2):
                 lanes = slice(head * HEAD_DIM, (head + 1) * HEAD_DIM)
-                dq[lanes, span] += mm(turned[lanes, pl.ds(rows, TILE)], dscores, NN)
+                dq[lanes, span] += mm(turned[lanes, pl.ds(rows, TILE)], dscores[head], NN)
 
         out[1, pl.ds(rows, TILE), :] = dkv[0].astype(jnp.bfloat16)
         out[2, pl.ds(rows, TILE), :] = dkv[1].astype(jnp.bfloat16)

time: 449 us -> 427 us (0.951)
  Pallas kernels: 187 us -> 160 us
  waiting for transfers between devices: 107 us -> 112 us
    pallas_call x1, Pallas kernels: 56.6 us -> 32.5 us  [attend_forward(): pl.pallas_call(functools.partial(forward_kernel, run), out_shape=(jax.Sha...]
    all_gather x1, waiting for transfers between devices: 0.01 us -> 5.32 us  [per_device(): lax.all_gather(jnp.concatenate([ff_out_weight] + wide + [out_weight]), fs...]
    ppermute x8, waiting for transfers between devices: 29 us -> 24.4 us  [send(): lax.ppermute(out, 'xy', [(i, i ^ 1 << bit) for i in range(self.planes)])]
  transfers between devices with their start and end apart: 39 -> 39, of which waited for: 16 -> 20; matrix products, arithmetic and copies ran while one was open for 11% -> 11% of each run, Pallas kernels for 27% -> 22%
where the time goes in v8:
time: 427 us; the launch traced here: 419 us
  Pallas kernels  160 us (37%)
  waiting for transfers between devices  112 us (26%)
  starting transfers between devices  46.6 us (11%)
  local copies, waits for them, and re-layouts  33.7 us (8%)
  other arithmetic  24.4 us (6%)
  matrix products  17.3 us (4%)
  between operations  15.4 us (4%)
  blocking collectives  9.52 us (2%)
    pallas_call x3, Pallas kernels, attend_backward(): pl.pallas_call(functools.partial(backward_kernel, run, pair), out_shape=(...  61 us
    pallas_call x1, Pallas kernels, middle(): pl.pallas_call(middle_kernel, grid=(count // ROWS,), out_shape=(shape((co...  48.4 us
    ppermute x2, waiting for transfers between devices, per_device(): lax.ppermute(input_grad[i * run:(i + 1) * run], ('core', 'seq'), back[i])  37.8 us
    pallas_call x1, Pallas kernels, attend_forward(): pl.pallas_call(functools.partial(forward_kernel, run), out_shape=(jax.Sha...  32.5 us
    ppermute x4, waiting for transfers between devices, spread(): lax.ppermute(h, ('core', 'seq'), r)  25 us
    ppermute x8, waiting for transfers between devices, send(): lax.ppermute(out, 'xy', [(i, i ^ 1 << bit) for i in range(self.planes)])  24.4 us
    pallas_call x1, Pallas kernels, gradients(): pl.pallas_call(functools.partial(gradients_kernel, rows), grid=(2 * chunk...  18.1 us
    unnamed x89, local copies, waits for them, and re-layouts  18.1 us
  transfers between devices with their start and end apart: 39, of which 20 were waited for; matrix products, arithmetic and copies ran while one was open for 11% of the time, Pallas kernels for 22%

profile of v8, /device:TPU:9, one launch (start us, length us, event | category | flops | bytes accessed | tf_op | source)
XLA Modules:
  0.0 419.1 jit_solution(7960511182607659072)
XLA Ops:
  7.2 1.6 reshape.360
  15.8 4.5 %collective-permute-start = (bf16[512,768]{1,0:T(8,128)(2,1)S(1)}, bf16[512,768]{1,0:T(8,128)(2,1)S(1)}, u32[]{:S(2)}, u32[]{:S(2)}) collective-permute-start(bf16[512,768]{1,0:T(8,128)(2,1)S(1)} %get-tuple-element.131), channel_id=1, source_target_pairs={{0,0},{1,1},{2,4},{3,5},{4,2},{5,3},{6,6},{7,7},{8,8},{9,9},{10,12... | collective-permute-start | bytes 2359304 | tf_op jit(solution)/shard_map/ppermute | solution.py:668
  20.6 9.5 %all-gather.2 = bf16[8,12,96]{2,1,0:T(8,128)(2,1)S(1)} all-gather(bf16[1,12,96]{2,1,0:T(8,128)(2,1)S(1)} %bitcast.148), channel_id=2, replica_groups=mesh['xy'=4,'core'=2,'seq'=4] {'xy','core'}, dimensions={0}, use_global_device_ids=true | all-gather | bytes 20736 | tf_op jit(solution)/shard_map/all_gather | solution.py:689
  30.2 15.7 %collective-permute-done = bf16[512,768]{1,0:T(8,128)(2,1)S(1)} collective-permute-done((bf16[512,768]{1,0:T(8,128)(2,1)S(1)}, bf16[512,768]{1,0:T(8,128)(2,1)S(1)}, u32[]{:S(2)}, u32[]{:S(2)}) %collective-permute-start) | collective-permute-done | bytes 786464 | tf_op jit(solution)/shard_map/ppermute | solution.py:668
  46.4 8.1 %collective-permute-done.1 = bf16[512,768]{1,0:T(8,128)(2,1)S(1)} collective-permute-done((bf16[512,768]{1,0:T(8,128)(2,1)}, bf16[512,768]{1,0:T(8,128)(2,1)S(1)}, u32[]{:S(2)}, u32[]{:S(2)}) %collective-permute-start.1) | collective-permute-done | bytes 786464 | tf_op jit(solution)/shard_map/ppermute | solution.py:668
  58.1 4.6 %multiply_convert_fusion.sib = bf16[1024,1152]{1,0:T(8,128)(2,1)S(1)} fusion(bf16[1024,768]{1,0:T(8,128)(2,1)} %constant_dynamic-update-slice_fusion, bf16[768,1152]{1,0:T(8,128)(2,1)} %all-gather.6.cloned.1.call-done, f32[1152]{0:T(1024)S(1)} %copy-done.39, f32[1152]{0:T(1024)S(1)} %add.272), kind=kOutput, calls=%fused_computation.3 | convolution fusion | flops 1815478272 | bytes 5710848 | tf_op jit(solution)/shard_map/dot_general | solution.py:25
  62.7 2.2 multiply_convert_fusion.1.own
  65.1 2.2 collective-permute-start.7
  67.3 2.2 collective-permute-start.8
  69.9 32.5 %attend_forward.1 = (bf16[1024,384]{1,0:T(8,128)(2,1)S(1)}, bf16[1024,384]{1,0:T(8,128)(2,1)S(1)}, f32[6,8,2048]{2,1,0:T(8,128)S(1)}) custom-call(s32[1]{0:T(128)} %bitcast.13.mask_ref, s32[8]{0:T(128)S(1)} %bitcast.129, bf16[1024,1152]{1,0:T(8,128)(2,1)S(1)} %multiply_convert_fusion.1.own, bf16[1024,1152]{1,0:T(8,128)(2,1)S(1)} %multiply_convert_fusion.sib, ...), custom_call_target="tpu_custom_call" | custom-call | flops 1000000000 | bytes 1000000 | tf_op jit(solution)/shard_map/attend_forward/pallas_call | solution.py:151
  107.1 5.3 %all-gather.8.cloned.1.call-done = bf16[6912,768]{1,0:T(8,128)(2,1)} async-done(((bf16[864,768]{1,0:T(8,128)(2,1)}), bf16[6912,768]{1,0:T(8,128)(2,1)}) %all-gather.8.cloned.1.call-update) | async-done | bytes 10616848 | tf_op jit(solution)/shard_map/all_gather | solution.py:695
  114.7 48.4 %middle.1 = (bf16[1024,768]{1,0:T(8,128)(2,1)S(1)}, bf16[1024,768]{1,0:T(8,128)(2,1)}, bf16[1024,3072]{1,0:T(8,128)(2,1)}, bf16[1024,768]{1,0:T(8,128)(2,1)}, bf...) custom-call(s32[1]{0:T(128)} %bitcast.core_ref, ...), custom_call_target="tpu_custom_call" | custom-call | flops 20000000000 | bytes 30000000 | tf_op jit(solution)/shard_map/middle/pallas_call | solution.py:429
  171.6 18.1 %gradients.1 = (bf16[4,896,768]{2,1,0:T(8,128)(2,1)}, bf16[4,896,768]{2,1,0:T(8,128)(2,1)}) custom-call(s32[1]{0:T(128)} %bitcast.core_ref, bf16[1024,3072]{1,0:T(8,128)(2,1)} %get-tuple-element.69.act_ref, bf16[1024,768]{1,0:T(8,128)(2,1)S(1)} %copy-done.15, bf16[1024,768]{1,0:T(8,128)(2,1)S(1)} %copy-done.16, ...), custom_call_target="tpu_custom_call" | custom-call | flops 11000000512 | bytes 30000000 | tf_op jit(solution)/shard_map/gradients/pallas_call | solution.py:531
  190.3 2.6 fusion.29
  192.9 4.7 %collective-permute-start.9 = (bf16[512,768]{1,0:T(8,128)(2,1)}, bf16[512,768]{1,0:T(8,128)(2,1)}, u32[]{:S(2)}, u32[]{:S(2)}) collective-permute-start(bf16[512,768]{1,0:T(8,128)(2,1)} %get-tuple-element.127), channel_id=1, source_target_pairs={{0,0},{1,1},{4,2},{5,3},{2,4},{3,5},{6,6},{7,7},{8,8},{9,9},{12,10... | collective-permute-start | bytes 2359304 | tf_op jit(solution)/shard_map/ppermute | solution.py:716
  197.7 1.4 collective-permute-done.10
  199.2 5.5 %add_convert_fusion = bf16[4,896,768]{2,1,0:T(8,128)(2,1)S(1)} fusion(bf16[4,896,768]{2,1,0:T(8,128)(2,1)} %collective-permute-done.10, bf16[4,896,768]{2,1,0:T(8,128)(2,1)} %get-tuple-element.76), kind=kLoop, calls=%fused_computation | loop fusion | flops 11010048 | bytes 16515072 | tf_op jit(solution)/shard_map/convert_element_type | solution.py:584
  207.4 20.3 %attend_backward_0.1 = (bf16[1024,384]{1,0:T(8,128)(2,1)S(1)}, bf16[1024,384]{1,0:T(8,128)(2,1)S(1)}) custom-call(s32[1]{0:T(128)} %bitcast.13.mask_ref, s32[8]{0:T(128)S(1)} %bitcast.130, bf16[1024,1152]{1,0:T(8,128)(2,1)S(1)} %copy-done.1, bf16[1024,1152]{1,0:T(8,128)(2,1)S(1)} %multiply_convert_fusion.sib, bf16[1024,384]{1,0:T(8,128)(2,1)S(1)} %copy-done.6, ...), custom_call_target="tpu_custom_call" | custom-call | flops 20000000000 | bytes 8000000 | tf_op jit(solution)/shard_map/attend_backward_0/pallas_call | solution.py:258
  227.9 6.4 %collective-permute-done.13 = bf16[2,448,768]{2,1,0:T(8,128)(2,1)S(1)} collective-permute-done((bf16[2,448,768]{2,1,0:T(8,128)(2,1)S(1)}, bf16[2,448,768]{2,1,0:T(8,128)(2,1)S(1)}, u32[]{:S(2)}, u32[]{:S(2)}) %collective-permute-start.13) | collective-permute-done | bytes 1376288 | tf_op jit(solution)/shard_map/ppermute | solution.py:609
  237.4 20.3 %attend_backward_1.1 = (bf16[1024,384]{1,0:T(8,128)(2,1)S(1)}, bf16[1024,384]{1,0:T(8,128)(2,1)S(1)}) custom-call(s32[1]{0:T(128)} %bitcast.13.mask_ref, s32[8]{0:T(128)S(1)} %bitcast.131, bf16[1024,1152]{1,0:T(8,128)(2,1)S(1)} %copy-done.1, bf16[1024,1152]{1,0:T(8,128)(2,1)S(1)} %multiply_convert_fusion.sib, bf16[1024,384]{1,0:T(8,128)(2,1)S(1)} %copy-done.6, ...), custom_call_target="tpu_custom_call" | custom-call | flops 20000000000 | bytes 8000000 | tf_op jit(solution)/shard_map/attend_backward_1/pallas_call | solution.py:258
  258.4 1.4 fusion.20
  259.9 5.3 %collective-permute-start.31 = (bf16[224,768]{1,0:T(8,128)(2,1)S(1)}, bf16[224,768]{1,0:T(8,128)(2,1)S(1)}, u32[]{:S(2)}, u32[]{:S(2)}) collective-permute-start(bf16[224,768]{1,0:T(8,128)(2,1)S(1)} %get-tuple-element.139), channel_id=1, source_target_pairs={{0,1},{1,2},{2,3},{3,0},{4,5},{5,6},{6,7},{7,4},{8,9},{9,10},{10,1... | collective-permute-start | bytes 1032200 | tf_op jit(solution)/shard_map/ppermute | solution.py:628
  265.2 1.4 collective-permute-start.33
  266.6 20.3 %attend_backward_2.1 = (bf16[1024,384]{1,0:T(8,128)(2,1)S(1)}, bf16[1024,384]{1,0:T(8,128)(2,1)S(1)}) custom-call(s32[1]{0:T(128)} %bitcast.13.mask_ref, s32[8]{0:T(128)S(1)} %bitcast.132, bf16[1024,1152]{1,0:T(8,128)(2,1)S(1)} %copy-done.1, bf16[1024,1152]{1,0:T(8,128)(2,1)S(1)} %multiply_convert_fusion.sib, bf16[1024,384]{1,0:T(8,128)(2,1)S(1)} %copy-done.6, ...), custom_call_target="tpu_custom_call" | custom-call | flops 20000000000 | bytes 8000000 | tf_op jit(solution)/shard_map/attend_backward_2/pallas_call | solution.py:258
  288.6 2.2 convolution_convert_fusion
  290.8 1.8 collective-permute-start.17
  293.2 2.2 fusion.32
  295.4 2.3 fusion.31
  297.7 3.7 fusion
  301.8 1.6 copy-done.21
  306.2 1.7 collective-permute-start.35
  309.4 3.5 collective-permute-start.23
  313.0 6.3 %collective-permute-done.20 = bf16[2,128,1152]{2,1,0:T(8,128)(2,1)S(1)} collective-permute-done((bf16[2,128,1152]{2,1,0:T(8,128)(2,1)S(1)}, bf16[2,128,1152]{2,1,0:T(8,128)(2,1)S(1)}, u32[]{:S(2)}, u32[]{:S(2)}) %collective-permute-start.20) | collective-permute-done | bytes 589856 | tf_op jit(solution)/shard_map/ppermute | solution.py:609
  319.3 2.5 collective-permute-start.24
  323.8 5.8 %collective-permute-done.21 = bf16[128,1152]{1,0:T(8,128)(2,1)S(1)} collective-permute-done((bf16[128,1152]{1,0:T(8,128)(2,1)S(1)}, bf16[128,1152]{1,0:T(8,128)(2,1)S(1)}, u32[]{:S(2)}, u32[]{:S(2)}) %collective-permute-start.21) | collective-permute-done | bytes 294944 | tf_op jit(solution)/shard_map/ppermute | solution.py:609
  330.5 5.3 %collective-permute-done.19 = bf16[128,1152]{1,0:T(8,128)(2,1)S(1)} collective-permute-done((bf16[128,1152]{1,0:T(8,128)(2,1)S(1)}, bf16[128,1152]{1,0:T(8,128)(2,1)S(1)}, u32[]{:S(2)}, u32[]{:S(2)}) %collective-permute-start.19) | collective-permute-done | bytes 294944 | tf_op jit(solution)/shard_map/ppermute | solution.py:609
  337.4 18.1 %collective-permute-done.23 = bf16[512,768]{1,0:T(8,128)(2,1)S(1)} collective-permute-done((bf16[512,768]{1,0:T(8,128)(2,1)S(1)}, bf16[512,768]{1,0:T(8,128)(2,1)S(1)}, u32[]{:S(2)}, u32[]{:S(2)}) %collective-permute-start.23) | collective-permute-done | bytes 786464 | tf_op jit(solution)/shard_map/ppermute | solution.py:786
  355.5 19.7 %collective-permute-done.24 = bf16[512,768]{1,0:T(8,128)(2,1)S(1)} collective-permute-done((bf16[512,768]{1,0:T(8,128)(2,1)S(1)}, bf16[512,768]{1,0:T(8,128)(2,1)S(1)}, u32[]{:S(2)}, u32[]{:S(2)}) %collective-permute-start.24) | collective-permute-done | bytes 786464 | tf_op jit(solution)/shard_map/ppermute | solution.py:786
  375.2 1.9 fusion.3
  377.1 1.5 collective-permute-start.34
  378.6 5.0 %collective-permute-done.26 = bf16[64,1152]{1,0:T(8,128)(2,1)S(1)} collective-permute-done((bf16[64,1152]{1,0:T(8,128)(2,1)S(1)}, bf16[64,1152]{1,0:T(8,128)(2,1)S(1)}, u32[]{:S(2)}, u32[]{:S(2)}) %collective-permute-start.26) | collective-permute-done | bytes 147488 | tf_op jit(solution)/shard_map/ppermute | solution.py:628
  383.8 1.6 collective-permute-done.34
  387.4 1.9 collective-permute-start.27
  389.7 1.5 collective-permute-start.29
  393.5 5.6 %collective-permute-done.27 = bf16[64,1152]{1,0:T(8,128)(2,1)S(1)} collective-permute-done((bf16[64,1152]{1,0:T(8,128)(2,1)S(1)}, bf16[64,1152]{1,0:T(8,128)(2,1)S(1)}, u32[]{:S(2)}, u32[]{:S(2)}) %collective-permute-start.27) | collective-permute-done | bytes 147488 | tf_op jit(solution)/shard_map/ppermute | solution.py:628
  399.1 3.3 collective-permute-done.28
  404.1 3.3 maximum_select_fusion
  410.4 1.6 reshape.382
  (251 shorter events, 55.0 us)
Async XLA Ops:
  7.2 50.9 %all-gather.6.cloned.1.call-start = ((), (), s32[]{:S(2)}) async-start(), calls=%async_computation | async-start | bytes 2211840 | tf_op jit(solution)/shard_map/all_gather | solution.py:685
  9.6 1.8 collective-permute-start.3
  12.3 100.2 %all-gather.8.cloned.1.call-start = ((), (), s32[]{:S(2)}) async-start(), calls=%async_computation.1 | async-start | bytes 11943936 | tf_op jit(solution)/shard_map/all_gather | solution.py:695
  14.7 5.7 %copy-start.28 = (bf16[384]{0:T(512)(128)(2,1)S(1)}, bf16[384]{0:T(512)(128)(2,1)}, u32[]{:S(2)}) copy-start(bf16[384]{0:T(512)(128)(2,1)} %param.26) | copy-start | bytes 2308
  14.7 5.8 %copy-start.29 = (bf16[96]{0:T(256)(128)(2,1)S(1)}, bf16[96]{0:T(256)(128)(2,1)}, u32[]{:S(2)}) copy-start(bf16[96]{0:T(256)(128)(2,1)} %param.19) | copy-start | bytes 580
  14.7 5.8 %copy-start.30 = (bf16[96]{0:T(256)(128)(2,1)S(1)}, bf16[96]{0:T(256)(128)(2,1)}, u32[]{:S(2)}) copy-start(bf16[96]{0:T(256)(128)(2,1)} %param.20) | copy-start | bytes 580
  14.7 5.8 %copy-start.31 = (bf16[96]{0:T(256)(128)(2,1)S(1)}, bf16[96]{0:T(256)(128)(2,1)}, u32[]{:S(2)}) copy-start(bf16[96]{0:T(256)(128)(2,1)} %param.22) | copy-start | bytes 580
  14.7 5.8 %copy-start.32 = (bf16[96]{0:T(256)(128)(2,1)S(1)}, bf16[96]{0:T(256)(128)(2,1)}, u32[]{:S(2)}) copy-start(bf16[96]{0:T(256)(128)(2,1)} %param.23) | copy-start | bytes 580
  14.7 5.8 %copy-start.33 = (bf16[96]{0:T(256)(128)(2,1)S(1)}, bf16[96]{0:T(256)(128)(2,1)}, u32[]{:S(2)}) copy-start(bf16[96]{0:T(256)(128)(2,1)} %param.24) | copy-start | bytes 580
  14.7 5.8 %copy-start.34 = (bf16[96]{0:T(256)(128)(2,1)S(1)}, bf16[96]{0:T(256)(128)(2,1)}, u32[]{:S(2)}) copy-start(bf16[96]{0:T(256)(128)(2,1)} %param.28) | copy-start | bytes 580
  14.7 5.8 %copy-start.35 = (bf16[96]{0:T(256)(128)(2,1)S(1)}, bf16[96]{0:T(256)(128)(2,1)}, u32[]{:S(2)}) copy-start(bf16[96]{0:T(256)(128)(2,1)} %param.29) | copy-start | bytes 580
  14.7 5.8 %copy-start.36 = (bf16[96]{0:T(256)(128)(2,1)S(1)}, bf16[96]{0:T(256)(128)(2,1)}, u32[]{:S(2)}) copy-start(bf16[96]{0:T(256)(128)(2,1)} %param.30) | copy-start | bytes 580
  15.8 30.2 %collective-permute-start = (bf16[512,768]{1,0:T(8,128)(2,1)S(1)}, bf16[512,768]{1,0:T(8,128)(2,1)S(1)}, u32[]{:S(2)}, u32[]{:S(2)}) collective-permute-start(bf16[512,768]{1,0:T(8,128)(2,1)S(1)} %get-tuple-element.131), channel_id=1, source_target_pairs={{0,0},{1,1},{2,4},{3,5},{4,2},{5,3},{6,6},{7,7},{8,8},{9,9},{10,12... | collective-permute-start | bytes 2359304 | tf_op jit(solution)/shard_map/ppermute | solution.py:668
  20.2 34.2 %collective-permute-start.1 = (bf16[512,768]{1,0:T(8,128)(2,1)}, bf16[512,768]{1,0:T(8,128)(2,1)S(1)}, u32[]{:S(2)}, u32[]{:S(2)}) collective-permute-start(bf16[512,768]{1,0:T(8,128)(2,1)} %get-tuple-element.132), channel_id=1, source_target_pairs={{0,1},{1,0},{2,5},{3,4},{4,3},{5,2},{6,7},{7,6},{8,9},{9,8},{10,13... | collective-permute-start | bytes 2359304 | tf_op jit(solution)/shard_map/ppermute | solution.py:668
  20.3 34.5 %collective-permute-start.2 = (s32[2,8]{1,0:T(2,128)S(1)}, s32[2,8]{1,0:T(2,128)S(1)}, u32[]{:S(2)}, u32[]{:S(2)}) collective-permute-start(s32[2,8]{1,0:T(2,128)S(1)} %bitcast.151), channel_id=1, source_target_pairs={{0,4},{4,0},{1,5},{5,1},{2,6},{6,2},{3,7},{7,3},{8,12},{12,8},{9,1... | collective-permute-start | bytes 200 | tf_op jit(solution)/shard_map/ppermute | solution.py:572
  45.9 10.3 %collective-permute-start.4 = (bf16[512,768]{1,0:T(8,128)(2,1)S(1)}, bf16[512,768]{1,0:T(8,128)(2,1)S(1)}, u32[]{:S(2)}, u32[]{:S(2)}) collective-permute-start(bf16[512,768]{1,0:T(8,128)(2,1)S(1)} %collective-permute-done), channel_id=1, source_target_pairs={{0,4},{4,0},{1,5},{5,1},{2,6},{6,2},{3,7},{7,3},{8,12},{12,8},{9,1... | collective-permute-start | bytes 2359304 | tf_op jit(solution)/shard_map/ppermute | solution.py:572
  54.5 2.7 collective-permute-start.5
  65.1 38.2 %collective-permute-start.7 = (bf16[512,768]{1,0:T(8,128)(2,1)S(1)}, bf16[512,768]{1,0:T(8,128)(2,1)S(1)}, u32[]{:S(2)}, u32[]{:S(2)}) collective-permute-start(bf16[512,768]{1,0:T(8,128)(2,1)S(1)} %get-tuple-element.129), channel_id=1, source_target_pairs={{0,0},{1,1},{2,4},{3,5},{4,2},{5,3},{6,6},{7,7},{8,8},{9,9},{10,12... | collective-permute-start | bytes 2359304 | tf_op jit(solution)/shard_map/ppermute | solution.py:668
  67.3 37.2 %collective-permute-start.8 = (bf16[512,768]{1,0:T(8,128)(2,1)S(1)}, bf16[512,768]{1,0:T(8,128)(2,1)S(1)}, u32[]{:S(2)}, u32[]{:S(2)}) collective-permute-start(bf16[512,768]{1,0:T(8,128)(2,1)S(1)} %get-tuple-element.130), channel_id=1, source_target_pairs={{0,1},{1,0},{2,5},{3,4},{4,3},{5,2},{6,7},{7,6},{8,9},{9,8},{10,13... | collective-permute-start | bytes 2359304 | tf_op jit(solution)/shard_map/ppermute | solution.py:668
  103.2 3.0 collective-permute-start.6
  189.7 9.4 %collective-permute-start.10 = (bf16[4,896,768]{2,1,0:T(8,128)(2,1)}, bf16[4,896,768]{2,1,0:T(8,128)(2,1)}, u32[]{:S(2)}, u32[]{:S(2)}) collective-permute-start(bf16[4,896,768]{2,1,0:T(8,128)(2,1)} %get-tuple-element.77), channel_id=1, source_target_pairs={{0,4},{4,0},{1,5},{5,1},{2,6},{6,2},{3,7},{7,3},{8,12},{12,8},{9,1... | collective-permute-start | bytes 16515080 | tf_op jit(solution)/shard_map/ppermute | solution.py:572
  190.0 16.8 %collective-permute-start.12 = (bf16[1024,384]{1,0:T(8,128)(2,1)}, bf16[1024,384]{1,0:T(8,128)(2,1)S(1)}, u32[]{:S(2)}, u32[]{:S(2)}) collective-permute-start(bf16[1024,384]{1,0:T(8,128)(2,1)} %copy-done.9), channel_id=1, source_target_pairs={{0,4},{4,0},{1,5},{5,1},{2,6},{6,2},{3,7},{7,3},{8,12},{12,8},{9,1... | collective-permute-start | bytes 2359304 | tf_op jit(solution)/shard_map/ppermute | solution.py:572
  192.9 64.8 %collective-permute-start.9 = (bf16[512,768]{1,0:T(8,128)(2,1)}, bf16[512,768]{1,0:T(8,128)(2,1)}, u32[]{:S(2)}, u32[]{:S(2)}) collective-permute-start(bf16[512,768]{1,0:T(8,128)(2,1)} %get-tuple-element.127), channel_id=1, source_target_pairs={{0,0},{1,1},{4,2},{5,3},{2,4},{3,5},{6,6},{7,7},{8,8},{9,9},{12,10... | collective-permute-start | bytes 2359304 | tf_op jit(solution)/shard_map/ppermute | solution.py:716
  197.6 60.1 %collective-permute-start.16 = (bf16[512,768]{1,0:T(8,128)(2,1)}, bf16[512,768]{1,0:T(8,128)(2,1)}, u32[]{:S(2)}, u32[]{:S(2)}) collective-permute-start(bf16[512,768]{1,0:T(8,128)(2,1)} %get-tuple-element.128), channel_id=1, source_target_pairs={{1,0},{0,1},{5,2},{4,3},{3,4},{2,5},{7,6},{6,7},{9,8},{8,9},{13,10... | collective-permute-start | bytes 2359304 | tf_op jit(solution)/shard_map/ppermute | solution.py:716
  205.1 29.2 %collective-permute-start.13 = (bf16[2,448,768]{2,1,0:T(8,128)(2,1)S(1)}, bf16[2,448,768]{2,1,0:T(8,128)(2,1)S(1)}, u32[]{:S(2)}, u32[]{:S(2)}) collective-permute-start(bf16[2,448,768]{2,1,0:T(8,128)(2,1)S(1)} %dynamic-slice_bitcast_fusion), channel_id=1, source_target_pairs={{0,16},{8,24},{16,0},{24,8},{1,17},{9,25},{17,1},{25,9},{2,18},{10... | collective-permute-start | bytes 4128776 | tf_op jit(solution)/shard_map/ppermute | solution.py:609
  206.0 28.9 %collective-permute-start.11 = (bf16[2,448,768]{2,1,0:T(8,128)(2,1)S(1)}, bf16[2,448,768]{2,1,0:T(8,128)(2,1)S(1)}, u32[]{:S(2)}, u32[]{:S(2)}) collective-permute-start(bf16[2,448,768]{2,1,0:T(8,128)(2,1)S(1)} %dynamic-slice_bitcast_fusion.1), channel_id=1, source_target_pairs={{0,8},{8,0},{16,24},{24,16},{1,9},{9,1},{17,25},{25,17},{2,10},{10... | collective-permute-start | bytes 4128776 | tf_op jit(solution)/shard_map/ppermute | solution.py:609
  235.4 22.7 %collective-permute-start.15 = (bf16[448,768]{1,0:T(8,128)(2,1)S(1)}, bf16[448,768]{1,0:T(8,128)(2,1)S(1)}, u32[]{:S(2)}, u32[]{:S(2)}) collective-permute-start(bf16[448,768]{1,0:T(8,128)(2,1)S(1)} %dynamic-slice_bitcast_fusion.6), channel_id=1, source_target_pairs={{0,8},{8,0},{16,24},{24,16},{1,9},{9,1},{17,25},{25,17},{2,10},{10... | collective-permute-start | bytes 2064392 | tf_op jit(solution)/shard_map/ppermute | solution.py:609
  236.5 21.8 %collective-permute-start.14 = (bf16[448,768]{1,0:T(8,128)(2,1)S(1)}, bf16[448,768]{1,0:T(8,128)(2,1)S(1)}, u32[]{:S(2)}, u32[]{:S(2)}) collective-permute-start(bf16[448,768]{1,0:T(8,128)(2,1)S(1)} %dynamic-slice_bitcast_fusion.7), channel_id=1, source_target_pairs={{0,16},{8,24},{16,0},{24,8},{1,17},{9,25},{17,1},{25,9},{2,18},{10... | collective-permute-start | bytes 2064392 | tf_op jit(solution)/shard_map/ppermute | solution.py:609
  259.9 41.9 %collective-permute-start.31 = (bf16[224,768]{1,0:T(8,128)(2,1)S(1)}, bf16[224,768]{1,0:T(8,128)(2,1)S(1)}, u32[]{:S(2)}, u32[]{:S(2)}) collective-permute-start(bf16[224,768]{1,0:T(8,128)(2,1)S(1)} %get-tuple-element.139), channel_id=1, source_target_pairs={{0,1},{1,2},{2,3},{3,0},{4,5},{5,6},{6,7},{7,4},{8,9},{9,10},{10,1... | collective-permute-start | bytes 1032200 | tf_op jit(solution)/shard_map/ppermute | solution.py:628
  265.2 36.6 %collective-permute-start.32 = (bf16[224,768]{1,0:T(8,128)(2,1)S(1)}, bf16[224,768]{1,0:T(8,128)(2,1)S(1)}, u32[]{:S(2)}, u32[]{:S(2)}) collective-permute-start(bf16[224,768]{1,0:T(8,128)(2,1)S(1)} %get-tuple-element.140), channel_id=1, source_target_pairs={{0,2},{1,3},{2,0},{3,1},{4,6},{5,7},{6,4},{7,5},{8,10},{9,11},{10,... | collective-permute-start | bytes 1032200 | tf_op jit(solution)/shard_map/ppermute | solution.py:628
  265.2 36.6 %collective-permute-start.33 = (bf16[224,768]{1,0:T(8,128)(2,1)S(1)}, bf16[224,768]{1,0:T(8,128)(2,1)S(1)}, u32[]{:S(2)}, u32[]{:S(2)}) collective-permute-start(bf16[224,768]{1,0:T(8,128)(2,1)S(1)} %get-tuple-element.138), channel_id=1, source_target_pairs={{0,3},{1,0},{2,1},{3,2},{4,7},{5,4},{6,5},{7,6},{8,11},{9,8},{10,9... | collective-permute-start | bytes 1032200 | tf_op jit(solution)/shard_map/ppermute | solution.py:628
  290.8 11.0 %collective-permute-start.17 = (bf16[1024,768]{1,0:T(8,128)(2,1)S(1)}, bf16[1024,768]{1,0:T(8,128)(2,1)S(1)}, u32[]{:S(2)}, u32[]{:S(2)}) collective-permute-start(bf16[1024,768]{1,0:T(8,128)(2,1)S(1)} %convolution_convert_fusion), channel_id=1, source_target_pairs={{0,4},{4,0},{1,5},{5,1},{2,6},{6,2},{3,7},{7,3},{8,12},{12,8},{9,1... | collective-permute-start | bytes 4718600 | tf_op jit(solution)/shard_map/ppermute | solution.py:572
  304.3 14.9 %collective-permute-start.20 = (bf16[2,128,1152]{2,1,0:T(8,128)(2,1)S(1)}, bf16[2,128,1152]{2,1,0:T(8,128)(2,1)S(1)}, u32[]{:S(2)}, u32[]{:S(2)}) collective-permute-start(bf16[2,128,1152]{2,1,0:T(8,128)(2,1)S(1)} %dynamic-slice_bitcast_fusion.8), channel_id=1, source_target_pairs={{0,16},{8,24},{16,0},{24,8},{1,17},{9,25},{17,1},{25,9},{2,18},{10... | collective-permute-start | bytes 1769480 | tf_op jit(solution)/shard_map/ppermute | solution.py:609
  305.0 78.8 %collective-permute-start.36 = (bf16[224,768]{1,0:T(8,128)(2,1)S(1)}, bf16[224,768]{1,0:T(8,128)(2,1)S(1)}, u32[]{:S(2)}, u32[]{:S(2)}) collective-permute-start(bf16[224,768]{1,0:T(8,128)(2,1)S(1)} %get-tuple-element.118), channel_id=1, source_target_pairs={{0,3},{1,0},{2,1},{3,2},{4,7},{5,4},{6,5},{7,6},{8,11},{9,8},{10,9... | collective-permute-start | bytes 1032200 | tf_op jit(solution)/shard_map/ppermute | solution.py:628
  306.2 77.6 %collective-permute-start.35 = (bf16[224,768]{1,0:T(8,128)(2,1)S(1)}, bf16[224,768]{1,0:T(8,128)(2,1)S(1)}, u32[]{:S(2)}, u32[]{:S(2)}) collective-permute-start(bf16[224,768]{1,0:T(8,128)(2,1)S(1)} %get-tuple-element.118), channel_id=1, source_target_pairs={{0,2},{1,3},{2,0},{3,1},{4,6},{5,7},{6,4},{7,5},{8,10},{9,11},{10,... | collective-permute-start | bytes 1032200 | tf_op jit(solution)/shard_map/ppermute | solution.py:628
  308.0 14.4 %collective-permute-start.18 = (bf16[2,128,1152]{2,1,0:T(8,128)(2,1)S(1)}, bf16[2,128,1152]{2,1,0:T(8,128)(2,1)S(1)}, u32[]{:S(2)}, u32[]{:S(2)}) collective-permute-start(bf16[2,128,1152]{2,1,0:T(8,128)(2,1)S(1)} %dynamic-slice_bitcast_fusion.9), channel_id=1, source_target_pairs={{0,8},{8,0},{16,24},{24,16},{1,9},{9,1},{17,25},{25,17},{2,10},{10... | collective-permute-start | bytes 1769480 | tf_op jit(solution)/shard_map/ppermute | solution.py:609
  309.4 46.1 %collective-permute-start.23 = (bf16[512,768]{1,0:T(8,128)(2,1)S(1)}, bf16[512,768]{1,0:T(8,128)(2,1)S(1)}, u32[]{:S(2)}, u32[]{:S(2)}) collective-permute-start(bf16[512,768]{1,0:T(8,128)(2,1)S(1)} %get-tuple-element.126), channel_id=1, source_target_pairs={{0,0},{1,1},{4,2},{5,3},{2,4},{3,5},{6,6},{7,7},{8,8},{9,9},{12,10... | collective-permute-start | bytes 2359304 | tf_op jit(solution)/shard_map/ppermute | solution.py:786
  319.3 55.9 %collective-permute-start.24 = (bf16[512,768]{1,0:T(8,128)(2,1)S(1)}, bf16[512,768]{1,0:T(8,128)(2,1)S(1)}, u32[]{:S(2)}, u32[]{:S(2)}) collective-permute-start(bf16[512,768]{1,0:T(8,128)(2,1)S(1)} %get-tuple-element.125), channel_id=1, source_target_pairs={{1,0},{0,1},{5,2},{4,3},{3,4},{2,5},{7,6},{6,7},{9,8},{8,9},{13,10... | collective-permute-start | bytes 2359304 | tf_op jit(solution)/shard_map/ppermute | solution.py:786
  322.4 7.1 %collective-permute-start.21 = (bf16[128,1152]{1,0:T(8,128)(2,1)S(1)}, bf16[128,1152]{1,0:T(8,128)(2,1)S(1)}, u32[]{:S(2)}, u32[]{:S(2)}) collective-permute-start(bf16[128,1152]{1,0:T(8,128)(2,1)S(1)} %dynamic-slice_bitcast_fusion.10), channel_id=1, source_target_pairs={{0,8},{8,0},{16,24},{24,16},{1,9},{9,1},{17,25},{25,17},{2,10},{10... | collective-permute-start | bytes 884744 | tf_op jit(solution)/shard_map/ppermute | solution.py:609
  329.6 6.3 %collective-permute-start.19 = (bf16[128,1152]{1,0:T(8,128)(2,1)S(1)}, bf16[128,1152]{1,0:T(8,128)(2,1)S(1)}, u32[]{:S(2)}, u32[]{:S(2)}) collective-permute-start(bf16[128,1152]{1,0:T(8,128)(2,1)S(1)} %dynamic-slice_bitcast_fusion.11), channel_id=1, source_target_pairs={{0,16},{8,24},{16,0},{24,8},{1,17},{9,25},{17,1},{25,9},{2,18},{10... | collective-permute-start | bytes 884744 | tf_op jit(solution)/shard_map/ppermute | solution.py:609
  336.3 40.8 %collective-permute-start.22 = (bf16[64,1152]{1,0:T(8,128)(2,1)S(1)}, bf16[64,1152]{1,0:T(8,128)(2,1)S(1)}, u32[]{:S(2)}, u32[]{:S(2)}) collective-permute-start(bf16[64,1152]{1,0:T(8,128)(2,1)S(1)} %get-tuple-element.143), channel_id=1, source_target_pairs={{0,1},{1,2},{2,3},{3,0},{4,5},{5,6},{6,7},{7,4},{8,9},{9,10},{10,1... | collective-permute-start | bytes 442376 | tf_op jit(solution)/shard_map/ppermute | solution.py:628
  355.5 23.1 %collective-permute-start.25 = (bf16[64,1152]{1,0:T(8,128)(2,1)S(1)}, bf16[64,1152]{1,0:T(8,128)(2,1)S(1)}, u32[]{:S(2)}, u32[]{:S(2)}) collective-permute-start(bf16[64,1152]{1,0:T(8,128)(2,1)S(1)} %get-tuple-element.144), channel_id=1, source_target_pairs={{0,2},{1,3},{2,0},{3,1},{4,6},{5,7},{6,4},{7,5},{8,10},{9,11},{10,... | collective-permute-start | bytes 442376 | tf_op jit(solution)/shard_map/ppermute | solution.py:628
  375.2 8.4 %collective-permute-start.26 = (bf16[64,1152]{1,0:T(8,128)(2,1)S(1)}, bf16[64,1152]{1,0:T(8,128)(2,1)S(1)}, u32[]{:S(2)}, u32[]{:S(2)}) collective-permute-start(bf16[64,1152]{1,0:T(8,128)(2,1)S(1)} %get-tuple-element.145), channel_id=1, source_target_pairs={{0,3},{1,0},{2,1},{3,2},{4,7},{5,4},{6,5},{7,6},{8,11},{9,8},{10,9... | collective-permute-start | bytes 442376 | tf_op jit(solution)/shard_map/ppermute | solution.py:628
  377.1 8.3 %collective-permute-start.34 = (bf16[224,768]{1,0:T(8,128)(2,1)S(1)}, bf16[224,768]{1,0:T(8,128)(2,1)S(1)}, u32[]{:S(2)}, u32[]{:S(2)}) collective-permute-start(bf16[224,768]{1,0:T(8,128)(2,1)S(1)} %get-tuple-element.118), channel_id=1, source_target_pairs={{0,1},{1,2},{2,3},{3,0},{4,5},{5,6},{6,7},{7,4},{8,9},{9,10},{10,1... | collective-permute-start | bytes 1032200 | tf_op jit(solution)/shard_map/ppermute | solution.py:628
  387.4 11.7 %collective-permute-start.27 = (bf16[64,1152]{1,0:T(8,128)(2,1)S(1)}, bf16[64,1152]{1,0:T(8,128)(2,1)S(1)}, u32[]{:S(2)}, u32[]{:S(2)}) collective-permute-start(bf16[64,1152]{1,0:T(8,128)(2,1)S(1)} %get-tuple-element.120), channel_id=1, source_target_pairs={{0,1},{1,2},{2,3},{3,0},{4,5},{5,6},{6,7},{7,4},{8,9},{9,10},{10,1... | collective-permute-start | bytes 442376 | tf_op jit(solution)/shard_map/ppermute | solution.py:628
  389.3 13.0 %collective-permute-start.28 = (bf16[64,1152]{1,0:T(8,128)(2,1)S(1)}, bf16[64,1152]{1,0:T(8,128)(2,1)S(1)}, u32[]{:S(2)}, u32[]{:S(2)}) collective-permute-start(bf16[64,1152]{1,0:T(8,128)(2,1)S(1)} %get-tuple-element.120), channel_id=1, source_target_pairs={{0,2},{1,3},{2,0},{3,1},{4,6},{5,7},{6,4},{7,5},{8,10},{9,11},{10,... | collective-permute-start | bytes 442376 | tf_op jit(solution)/shard_map/ppermute | solution.py:628
  389.7 13.8 %collective-permute-start.29 = (bf16[64,1152]{1,0:T(8,128)(2,1)S(1)}, bf16[64,1152]{1,0:T(8,128)(2,1)S(1)}, u32[]{:S(2)}, u32[]{:S(2)}) collective-permute-start(bf16[64,1152]{1,0:T(8,128)(2,1)S(1)} %get-tuple-element.120), channel_id=1, source_target_pairs={{0,3},{1,0},{2,1},{3,2},{4,7},{5,4},{6,5},{7,6},{8,11},{9,8},{10,9... | collective-permute-start | bytes 442376 | tf_op jit(solution)/shard_map/ppermute | solution.py:628
  403.6 4.3 %collective-permute-start.30 = (bf16[112,1152]{1,0:T(8,128)(2,1)S(1)}, bf16[112,1152]{1,0:T(8,128)(2,1)S(1)}, u32[]{:S(2)}, u32[]{:S(2)}) collective-permute-start(bf16[112,1152]{1,0:T(8,128)(2,1)S(1)} %pad_maximum_fusion.3), channel_id=1, source_target_pairs={{0,4},{4,0},{1,5},{5,1},{2,6},{6,2},{3,7},{7,3},{8,12},{12,8},{9,1... | collective-permute-start | bytes 774152 | tf_op jit(solution)/shard_map/ppermute | solution.py:572
  (31 other events, 66.1 us)
Sparse Core Ops, SparseCore 0:
  12.4 33.2 all-gather.5
  48.1 64.2 all-gather.7

commit v9 on v8

--- a/solution.py
+++ b/solution.py
@@ -763,7 +763,7 @@
     def weight_sums(near, far):
         matrix = (mm(x_own, near, TN) + mm(x_sib, far, TN)).astype(bf16)
         column = (jnp.sum(near.astype(f32), axis=0) + jnp.sum(far.astype(f32), axis=0)).astype(bf16)
-        column = jnp.pad(column[None], ((0, 63), (0, 0)))
+        column = jnp.pad(column[None], ((0, 15), (0, 0)))
         column = jnp.broadcast_to(column, (planes,) + column.shape)
         return jnp.concatenate([matrix.reshape(planes, CORES * rows, -1), column], axis=1)
 
@@ -778,13 +778,14 @@
         advance(grads[-1][0])
     early_sum = progress[1]
 
+    early_sum.add(grads[-1][0])
     near = jnp.concatenate([g[0] for g in grads], axis=1)
-    far = jnp.concatenate([g[1] for g in grads], axis=1)
+    far = after(jnp.concatenate([g[1] for g in grads], axis=1), early_sum.keep)
     grad_far = swap(mm(far, w_mine, NT).astype(bf16))
-    early_sum.add(grads[-1][0])
     input_grad = (grad_one + mm(near, w_mine, NT) + grad_far.astype(f32)).astype(bf16)
     returned = [lax.ppermute(input_grad[i * run : (i + 1) * run], ("core", "seq"), back[i]) for i in range(2)]
-    qkv_halves = Halving(after(weight_sums(near, far), input_grad), planes)
+    near, far = after((near, far), input_grad)
+    qkv_halves = Halving(weight_sums(near, far), planes)
     for step in range(qkv_halves.steps):
         qkv_halves.send(step)
         qkv_halves.add(input_grad)

time: 427 us -> 427 us (level)
  waiting for transfers between devices: 112 us -> 106 us
  local copies, waits for them, and re-layouts: 33.7 us -> 38.4 us
    ppermute x2, waiting for transfers between devices: 37.8 us -> 31.6 us  [per_device(): lax.ppermute(input_grad[i * run:(i + 1) * run], ('core', 'seq'), back[i])]
    unnamed x89 -> x106, local copies, waits for them, and re-layouts: 18.1 us -> 19 us
  transfers between devices with their start and end apart: 39 -> 39, of which waited for: 20 -> 20; matrix products, arithmetic and copies ran while one was open for 11% -> 12% of each run, Pallas kernels for 22% -> 22%
where the time goes in v9:
time: 427 us; the launch traced here: 419 us
  Pallas kernels  160 us (37%)
  waiting for transfers between devices  106 us (25%)
  starting transfers between devices  45.4 us (11%)
  local copies, waits for them, and re-layouts  38.4 us (9%)
  other arithmetic  26.1 us (6%)
  matrix products  18.4 us (4%)
  between operations  15.5 us (4%)
  blocking collectives  9.52 us (2%)
    pallas_call x3, Pallas kernels, attend_backward(): pl.pallas_call(functools.partial(backward_kernel, run, pair), out_shape=(...  61 us
    pallas_call x1, Pallas kernels, middle(): pl.pallas_call(middle_kernel, grid=(count // ROWS,), out_shape=(shape((co...  48.4 us
    pallas_call x1, Pallas kernels, attend_forward(): pl.pallas_call(functools.partial(forward_kernel, run), out_shape=(jax.Sha...  32.6 us
    ppermute x2, waiting for transfers between devices, per_device(): lax.ppermute(input_grad[i * run:(i + 1) * run], ('core', 'seq'), back[i])  31.6 us
    ppermute x4, waiting for transfers between devices, spread(): lax.ppermute(h, ('core', 'seq'), r)  25 us
    ppermute x8, waiting for transfers between devices, send(): lax.ppermute(out, 'xy', [(i, i ^ 1 << bit) for i in range(self.planes)])  21.1 us
    ppermute x12, waiting for transfers between devices, shift(): lax.ppermute(value, 'seq', [(i, (i + distance) % self.nseq) for i in rang...  19.7 us
    unnamed x106, local copies, waits for them, and re-layouts  19 us
  transfers between devices with their start and end apart: 39, of which 20 were waited for; matrix products, arithmetic and copies ran while one was open for 12% of the time, Pallas kernels for 22%

profile of v9, /device:TPU:9, one launch (start us, length us, event | category | flops | bytes accessed | tf_op | source)
XLA Modules:
  0.0 419.1 jit_solution(17447153688727734312)
XLA Ops:
  7.2 1.6 reshape.360
  15.8 4.5 %collective-permute-start = (bf16[512,768]{1,0:T(8,128)(2,1)S(1)}, bf16[512,768]{1,0:T(8,128)(2,1)S(1)}, u32[]{:S(2)}, u32[]{:S(2)}) collective-permute-start(bf16[512,768]{1,0:T(8,128)(2,1)S(1)} %get-tuple-element.133), channel_id=1, source_target_pairs={{0,0},{1,1},{2,4},{3,5},{4,2},{5,3},{6,6},{7,7},{8,8},{9,9},{10,12... | collective-permute-start | bytes 2359304 | tf_op jit(solution)/shard_map/ppermute | solution.py:668
  20.6 9.5 %all-gather.2 = bf16[8,12,96]{2,1,0:T(8,128)(2,1)S(1)} all-gather(bf16[1,12,96]{2,1,0:T(8,128)(2,1)S(1)} %bitcast.148), channel_id=2, replica_groups=mesh['xy'=4,'core'=2,'seq'=4] {'xy','core'}, dimensions={0}, use_global_device_ids=true | all-gather | bytes 20736 | tf_op jit(solution)/shard_map/all_gather | solution.py:689
  30.2 15.7 %collective-permute-done = bf16[512,768]{1,0:T(8,128)(2,1)S(1)} collective-permute-done((bf16[512,768]{1,0:T(8,128)(2,1)S(1)}, bf16[512,768]{1,0:T(8,128)(2,1)S(1)}, u32[]{:S(2)}, u32[]{:S(2)}) %collective-permute-start) | collective-permute-done | bytes 786464 | tf_op jit(solution)/shard_map/ppermute | solution.py:668
  46.4 8.1 %collective-permute-done.1 = bf16[512,768]{1,0:T(8,128)(2,1)S(1)} collective-permute-done((bf16[512,768]{1,0:T(8,128)(2,1)}, bf16[512,768]{1,0:T(8,128)(2,1)S(1)}, u32[]{:S(2)}, u32[]{:S(2)}) %collective-permute-start.1) | collective-permute-done | bytes 786464 | tf_op jit(solution)/shard_map/ppermute | solution.py:668
  58.2 4.5 %multiply_convert_fusion.sib = bf16[1024,1152]{1,0:T(8,128)(2,1)S(1)} fusion(bf16[1024,768]{1,0:T(8,128)(2,1)} %constant_dynamic-update-slice_fusion, bf16[768,1152]{1,0:T(8,128)(2,1)} %all-gather.6.cloned.1.call-done, f32[1152]{0:T(1024)S(1)} %copy-done.48, f32[1152]{0:T(1024)S(1)} %add.272), kind=kOutput, calls=%fused_computation.3 | convolution fusion | flops 1815478272 | bytes 5710848 | tf_op jit(solution)/shard_map/dot_general | solution.py:25
  62.8 2.2 multiply_convert_fusion.1.own
  65.1 2.2 collective-permute-start.7
  67.3 2.2 collective-permute-start.8
  70.0 32.6 %attend_forward.1 = (bf16[1024,384]{1,0:T(8,128)(2,1)S(1)}, bf16[1024,384]{1,0:T(8,128)(2,1)S(1)}, f32[6,8,2048]{2,1,0:T(8,128)S(1)}) custom-call(s32[1]{0:T(128)} %bitcast.13.mask_ref, s32[8]{0:T(128)S(1)} %bitcast.129, bf16[1024,1152]{1,0:T(8,128)(2,1)S(1)} %multiply_convert_fusion.1.own, bf16[1024,1152]{1,0:T(8,128)(2,1)S(1)} %multiply_convert_fusion.sib, ...), custom_call_target="tpu_custom_call" | custom-call | flops 1000000000 | bytes 1000000 | tf_op jit(solution)/shard_map/attend_forward/pallas_call | solution.py:151
  107.2 5.2 %all-gather.8.cloned.1.call-done = bf16[6912,768]{1,0:T(8,128)(2,1)} async-done(((bf16[864,768]{1,0:T(8,128)(2,1)}), bf16[6912,768]{1,0:T(8,128)(2,1)}) %all-gather.8.cloned.1.call-update) | async-done | bytes 10616848 | tf_op jit(solution)/shard_map/all_gather | solution.py:695
  114.7 48.4 %middle.1 = (bf16[1024,768]{1,0:T(8,128)(2,1)S(1)}, bf16[1024,768]{1,0:T(8,128)(2,1)}, bf16[1024,3072]{1,0:T(8,128)(2,1)}, bf16[1024,768]{1,0:T(8,128)(2,1)}, bf...) custom-call(s32[1]{0:T(128)} %bitcast.core_ref, ...), custom_call_target="tpu_custom_call" | custom-call | flops 20000000000 | bytes 30000000 | tf_op jit(solution)/shard_map/middle/pallas_call | solution.py:429
  168.7 1.4 copy-done.21
  170.1 1.4 copy-done.22
  171.5 18.0 %gradients.1 = (bf16[4,896,768]{2,1,0:T(8,128)(2,1)}, bf16[4,896,768]{2,1,0:T(8,128)(2,1)}) custom-call(s32[1]{0:T(128)} %bitcast.core_ref, bf16[1024,3072]{1,0:T(8,128)(2,1)} %get-tuple-element.71.act_ref, bf16[1024,768]{1,0:T(8,128)(2,1)S(1)} %copy-done.21, bf16[1024,768]{1,0:T(8,128)(2,1)S(1)} %copy-done.22, ...), custom_call_target="tpu_custom_call" | custom-call | flops 11000000512 | bytes 30000000 | tf_op jit(solution)/shard_map/gradients/pallas_call | solution.py:531
  190.0 2.6 fusion.28
  192.6 4.7 %collective-permute-start.9 = (bf16[512,768]{1,0:T(8,128)(2,1)}, bf16[512,768]{1,0:T(8,128)(2,1)}, u32[]{:S(2)}, u32[]{:S(2)}) collective-permute-start(bf16[512,768]{1,0:T(8,128)(2,1)} %get-tuple-element.129), channel_id=1, source_target_pairs={{0,0},{1,1},{4,2},{5,3},{2,4},{3,5},{6,6},{7,7},{8,8},{9,9},{12,10... | collective-permute-start | bytes 2359304 | tf_op jit(solution)/shard_map/ppermute | solution.py:716
  197.4 1.5 collective-permute-done.10
  198.9 5.5 %add_convert_fusion = bf16[4,896,768]{2,1,0:T(8,128)(2,1)S(1)} fusion(bf16[4,896,768]{2,1,0:T(8,128)(2,1)} %collective-permute-done.10, bf16[4,896,768]{2,1,0:T(8,128)(2,1)} %get-tuple-element.78), kind=kLoop, calls=%fused_computation | loop fusion | flops 11010048 | bytes 16515072 | tf_op jit(solution)/shard_map/convert_element_type | solution.py:584
  207.2 20.3 %attend_backward_0.1 = (bf16[1024,384]{1,0:T(8,128)(2,1)S(1)}, bf16[1024,384]{1,0:T(8,128)(2,1)S(1)}) custom-call(s32[1]{0:T(128)} %bitcast.13.mask_ref, s32[8]{0:T(128)S(1)} %bitcast.130, bf16[1024,1152]{1,0:T(8,128)(2,1)S(1)} %copy-done.1, bf16[1024,1152]{1,0:T(8,128)(2,1)S(1)} %multiply_convert_fusion.sib, bf16[1024,384]{1,0:T(8,128)(2,1)S(1)} %copy-done.12, ...), custom_call_target="tpu_custom_call" | custom-call | flops 20000000000 | bytes 8000000 | tf_op jit(solution)/shard_map/attend_backward_0/pallas_call | solution.py:258
  227.5 6.6 %collective-permute-done.13 = bf16[2,448,768]{2,1,0:T(8,128)(2,1)S(1)} collective-permute-done((bf16[2,448,768]{2,1,0:T(8,128)(2,1)S(1)}, bf16[2,448,768]{2,1,0:T(8,128)(2,1)S(1)}, u32[]{:S(2)}, u32[]{:S(2)}) %collective-permute-start.13) | collective-permute-done | bytes 1376288 | tf_op jit(solution)/shard_map/ppermute | solution.py:609
  237.2 20.3 %attend_backward_1.1 = (bf16[1024,384]{1,0:T(8,128)(2,1)S(1)}, bf16[1024,384]{1,0:T(8,128)(2,1)S(1)}) custom-call(s32[1]{0:T(128)} %bitcast.13.mask_ref, s32[8]{0:T(128)S(1)} %bitcast.131, bf16[1024,1152]{1,0:T(8,128)(2,1)S(1)} %copy-done.1, bf16[1024,1152]{1,0:T(8,128)(2,1)S(1)} %multiply_convert_fusion.sib, bf16[1024,384]{1,0:T(8,128)(2,1)S(1)} %copy-done.12, ...), custom_call_target="tpu_custom_call" | custom-call | flops 20000000000 | bytes 8000000 | tf_op jit(solution)/shard_map/attend_backward_1/pallas_call | solution.py:258
  258.4 1.4 fusion.20
  261.2 4.8 %collective-permute-start.18 = (bf16[224,768]{1,0:T(8,128)(2,1)S(1)}, bf16[224,768]{1,0:T(8,128)(2,1)S(1)}, u32[]{:S(2)}, u32[]{:S(2)}) collective-permute-start(bf16[224,768]{1,0:T(8,128)(2,1)S(1)} %get-tuple-element.142), channel_id=1, source_target_pairs={{0,2},{1,3},{2,0},{3,1},{4,6},{5,7},{6,4},{7,5},{8,10},{9,11},{10,... | collective-permute-start | bytes 1032200 | tf_op jit(solution)/shard_map/ppermute | solution.py:628
  266.0 1.5 collective-permute-start.19
  267.5 20.3 %attend_backward_2.1 = (bf16[1024,384]{1,0:T(8,128)(2,1)S(1)}, bf16[1024,384]{1,0:T(8,128)(2,1)S(1)}) custom-call(s32[1]{0:T(128)} %bitcast.13.mask_ref, s32[8]{0:T(128)S(1)} %bitcast.132, bf16[1024,1152]{1,0:T(8,128)(2,1)S(1)} %copy-done.1, bf16[1024,1152]{1,0:T(8,128)(2,1)S(1)} %multiply_convert_fusion.sib, bf16[1024,384]{1,0:T(8,128)(2,1)S(1)} %copy-done.12, ...), custom_call_target="tpu_custom_call" | custom-call | flops 20000000000 | bytes 8000000 | tf_op jit(solution)/shard_map/attend_backward_2/pallas_call | solution.py:258
  288.8 7.8 %collective-permute-done.19 = bf16[224,768]{1,0:T(8,128)(2,1)S(1)} collective-permute-done((bf16[224,768]{1,0:T(8,128)(2,1)S(1)}, bf16[224,768]{1,0:T(8,128)(2,1)S(1)}, u32[]{:S(2)}, u32[]{:S(2)}) %collective-permute-start.19) | collective-permute-done | bytes 344096 | tf_op jit(solution)/shard_map/ppermute | solution.py:628
  298.2 3.4 convolution_convert_fusion
  304.2 2.2 fusion.30
  307.0 2.2 add_convert_fusion.1
  309.2 2.3 fusion.31
  312.2 3.7 fusion
  317.8 5.1 %collective-permute-start.26 = (bf16[512,768]{1,0:T(8,128)(2,1)S(1)}, bf16[512,768]{1,0:T(8,128)(2,1)S(1)}, u32[]{:S(2)}, u32[]{:S(2)}) collective-permute-start(bf16[512,768]{1,0:T(8,128)(2,1)S(1)} %get-tuple-element.128), channel_id=1, source_target_pairs={{0,0},{1,1},{4,2},{5,3},{2,4},{3,5},{6,6},{7,7},{8,8},{9,9},{12,10... | collective-permute-start | bytes 2359304 | tf_op jit(solution)/shard_map/ppermute | solution.py:786
  322.9 4.9 %collective-permute-done.23 = bf16[2,104,1152]{2,1,0:T(8,128)(2,1)S(1)} collective-permute-done((bf16[2,104,1152]{2,1,0:T(8,128)(2,1)S(1)}, bf16[2,104,1152]{2,1,0:T(8,128)(2,1)S(1)}, u32[]{:S(2)}, u32[]{:S(2)}) %collective-permute-start.23) | collective-permute-done | bytes 479264 | tf_op jit(solution)/shard_map/ppermute | solution.py:609
  327.7 2.9 collective-permute-start.27
  331.3 5.4 %collective-permute-done.24 = bf16[104,1152]{1,0:T(8,128)(2,1)S(1)} collective-permute-done((bf16[104,1152]{1,0:T(8,128)(2,1)S(1)}, bf16[104,1152]{1,0:T(8,128)(2,1)S(1)}, u32[]{:S(2)}, u32[]{:S(2)}) %collective-permute-start.24) | collective-permute-done | bytes 239648 | tf_op jit(solution)/shard_map/ppermute | solution.py:609
  337.9 4.0 collective-permute-done.22
  343.8 10.1 %collective-permute-done.26 = bf16[512,768]{1,0:T(8,128)(2,1)S(1)} collective-permute-done((bf16[512,768]{1,0:T(8,128)(2,1)S(1)}, bf16[512,768]{1,0:T(8,128)(2,1)S(1)}, u32[]{:S(2)}, u32[]{:S(2)}) %collective-permute-start.26) | collective-permute-done | bytes 786464 | tf_op jit(solution)/shard_map/ppermute | solution.py:786
  353.9 21.5 %collective-permute-done.27 = bf16[512,768]{1,0:T(8,128)(2,1)S(1)} collective-permute-done((bf16[512,768]{1,0:T(8,128)(2,1)S(1)}, bf16[512,768]{1,0:T(8,128)(2,1)S(1)}, u32[]{:S(2)}, u32[]{:S(2)}) %collective-permute-start.27) | collective-permute-done | bytes 786464 | tf_op jit(solution)/shard_map/ppermute | solution.py:786
  375.4 1.9 fusion.3
  377.4 1.5 collective-permute-start.34
  380.0 5.6 %collective-permute-done.34 = bf16[224,768]{1,0:T(8,128)(2,1)S(1)} collective-permute-done((bf16[224,768]{1,0:T(8,128)(2,1)S(1)}, bf16[224,768]{1,0:T(8,128)(2,1)S(1)}, u32[]{:S(2)}, u32[]{:S(2)}) %collective-permute-start.34) | collective-permute-done | bytes 344096 | tf_op jit(solution)/shard_map/ppermute | solution.py:628
  387.7 1.9 collective-permute-start.30
  389.9 1.5 collective-permute-start.32
  395.0 3.1 collective-permute-done.30
  399.3 1.7 collective-permute-done.31
  404.0 3.4 maximum_select_fusion
  410.4 1.6 reshape.382
  (267 shorter events, 58.7 us)
Async XLA Ops:
  7.2 51.0 %all-gather.6.cloned.1.call-start = ((), (), s32[]{:S(2)}) async-start(), calls=%async_computation | async-start | bytes 2211840 | tf_op jit(solution)/shard_map/all_gather | solution.py:685
  9.6 1.8 collective-permute-start.3
  12.3 100.2 %all-gather.8.cloned.1.call-start = ((), (), s32[]{:S(2)}) async-start(), calls=%async_computation.1 | async-start | bytes 11943936 | tf_op jit(solution)/shard_map/all_gather | solution.py:695
  14.7 5.8 %copy-start.37 = (bf16[96]{0:T(256)(128)(2,1)S(1)}, bf16[96]{0:T(256)(128)(2,1)}, u32[]{:S(2)}) copy-start(bf16[96]{0:T(256)(128)(2,1)} %param.19) | copy-start | bytes 580
  14.7 5.8 %copy-start.38 = (bf16[96]{0:T(256)(128)(2,1)S(1)}, bf16[96]{0:T(256)(128)(2,1)}, u32[]{:S(2)}) copy-start(bf16[96]{0:T(256)(128)(2,1)} %param.20) | copy-start | bytes 580
  14.7 5.8 %copy-start.39 = (bf16[96]{0:T(256)(128)(2,1)S(1)}, bf16[96]{0:T(256)(128)(2,1)}, u32[]{:S(2)}) copy-start(bf16[96]{0:T(256)(128)(2,1)} %param.22) | copy-start | bytes 580
  14.7 5.8 %copy-start.40 = (bf16[96]{0:T(256)(128)(2,1)S(1)}, bf16[96]{0:T(256)(128)(2,1)}, u32[]{:S(2)}) copy-start(bf16[96]{0:T(256)(128)(2,1)} %param.23) | copy-start | bytes 580
  14.7 5.8 %copy-start.41 = (bf16[96]{0:T(256)(128)(2,1)S(1)}, bf16[96]{0:T(256)(128)(2,1)}, u32[]{:S(2)}) copy-start(bf16[96]{0:T(256)(128)(2,1)} %param.24) | copy-start | bytes 580
  14.7 5.8 %copy-start.42 = (bf16[96]{0:T(256)(128)(2,1)S(1)}, bf16[96]{0:T(256)(128)(2,1)}, u32[]{:S(2)}) copy-start(bf16[96]{0:T(256)(128)(2,1)} %param.28) | copy-start | bytes 580
  14.7 5.8 %copy-start.43 = (bf16[96]{0:T(256)(128)(2,1)S(1)}, bf16[96]{0:T(256)(128)(2,1)}, u32[]{:S(2)}) copy-start(bf16[96]{0:T(256)(128)(2,1)} %param.29) | copy-start | bytes 580
  15.8 30.2 %collective-permute-start = (bf16[512,768]{1,0:T(8,128)(2,1)S(1)}, bf16[512,768]{1,0:T(8,128)(2,1)S(1)}, u32[]{:S(2)}, u32[]{:S(2)}) collective-permute-start(bf16[512,768]{1,0:T(8,128)(2,1)S(1)} %get-tuple-element.133), channel_id=1, source_target_pairs={{0,0},{1,1},{2,4},{3,5},{4,2},{5,3},{6,6},{7,7},{8,8},{9,9},{10,12... | collective-permute-start | bytes 2359304 | tf_op jit(solution)/shard_map/ppermute | solution.py:668
  20.2 34.2 %collective-permute-start.1 = (bf16[512,768]{1,0:T(8,128)(2,1)}, bf16[512,768]{1,0:T(8,128)(2,1)S(1)}, u32[]{:S(2)}, u32[]{:S(2)}) collective-permute-start(bf16[512,768]{1,0:T(8,128)(2,1)} %get-tuple-element.134), channel_id=1, source_target_pairs={{0,1},{1,0},{2,5},{3,4},{4,3},{5,2},{6,7},{7,6},{8,9},{9,8},{10,13... | collective-permute-start | bytes 2359304 | tf_op jit(solution)/shard_map/ppermute | solution.py:668
  20.3 34.5 %collective-permute-start.2 = (s32[2,8]{1,0:T(2,128)S(1)}, s32[2,8]{1,0:T(2,128)S(1)}, u32[]{:S(2)}, u32[]{:S(2)}) collective-permute-start(s32[2,8]{1,0:T(2,128)S(1)} %bitcast.151), channel_id=1, source_target_pairs={{0,4},{4,0},{1,5},{5,1},{2,6},{6,2},{3,7},{7,3},{8,12},{12,8},{9,1... | collective-permute-start | bytes 200 | tf_op jit(solution)/shard_map/ppermute | solution.py:572
  45.9 10.3 %collective-permute-start.4 = (bf16[512,768]{1,0:T(8,128)(2,1)S(1)}, bf16[512,768]{1,0:T(8,128)(2,1)S(1)}, u32[]{:S(2)}, u32[]{:S(2)}) collective-permute-start(bf16[512,768]{1,0:T(8,128)(2,1)S(1)} %collective-permute-done), channel_id=1, source_target_pairs={{0,4},{4,0},{1,5},{5,1},{2,6},{6,2},{3,7},{7,3},{8,12},{12,8},{9,1... | collective-permute-start | bytes 2359304 | tf_op jit(solution)/shard_map/ppermute | solution.py:572
  54.5 2.8 collective-permute-start.5
  65.1 38.2 %collective-permute-start.7 = (bf16[512,768]{1,0:T(8,128)(2,1)S(1)}, bf16[512,768]{1,0:T(8,128)(2,1)S(1)}, u32[]{:S(2)}, u32[]{:S(2)}) collective-permute-start(bf16[512,768]{1,0:T(8,128)(2,1)S(1)} %get-tuple-element.131), channel_id=1, source_target_pairs={{0,0},{1,1},{2,4},{3,5},{4,2},{5,3},{6,6},{7,7},{8,8},{9,9},{10,12... | collective-permute-start | bytes 2359304 | tf_op jit(solution)/shard_map/ppermute | solution.py:668
  67.3 37.2 %collective-permute-start.8 = (bf16[512,768]{1,0:T(8,128)(2,1)S(1)}, bf16[512,768]{1,0:T(8,128)(2,1)S(1)}, u32[]{:S(2)}, u32[]{:S(2)}) collective-permute-start(bf16[512,768]{1,0:T(8,128)(2,1)S(1)} %get-tuple-element.132), channel_id=1, source_target_pairs={{0,1},{1,0},{2,5},{3,4},{4,3},{5,2},{6,7},{7,6},{8,9},{9,8},{10,13... | collective-permute-start | bytes 2359304 | tf_op jit(solution)/shard_map/ppermute | solution.py:668
  103.3 3.0 collective-permute-start.6
  189.4 9.4 %collective-permute-start.10 = (bf16[4,896,768]{2,1,0:T(8,128)(2,1)}, bf16[4,896,768]{2,1,0:T(8,128)(2,1)}, u32[]{:S(2)}, u32[]{:S(2)}) collective-permute-start(bf16[4,896,768]{2,1,0:T(8,128)(2,1)} %get-tuple-element.79), channel_id=1, source_target_pairs={{0,4},{4,0},{1,5},{5,1},{2,6},{6,2},{3,7},{7,3},{8,12},{12,8},{9,1... | collective-permute-start | bytes 16515080 | tf_op jit(solution)/shard_map/ppermute | solution.py:572
  189.7 16.8 %collective-permute-start.12 = (bf16[1024,384]{1,0:T(8,128)(2,1)}, bf16[1024,384]{1,0:T(8,128)(2,1)S(1)}, u32[]{:S(2)}, u32[]{:S(2)}) collective-permute-start(bf16[1024,384]{1,0:T(8,128)(2,1)} %copy-done.15), channel_id=1, source_target_pairs={{0,4},{4,0},{1,5},{5,1},{2,6},{6,2},{3,7},{7,3},{8,12},{12,8},{9,1... | collective-permute-start | bytes 2359304 | tf_op jit(solution)/shard_map/ppermute | solution.py:572
  192.6 64.9 %collective-permute-start.9 = (bf16[512,768]{1,0:T(8,128)(2,1)}, bf16[512,768]{1,0:T(8,128)(2,1)}, u32[]{:S(2)}, u32[]{:S(2)}) collective-permute-start(bf16[512,768]{1,0:T(8,128)(2,1)} %get-tuple-element.129), channel_id=1, source_target_pairs={{0,0},{1,1},{4,2},{5,3},{2,4},{3,5},{6,6},{7,7},{8,8},{9,9},{12,10... | collective-permute-start | bytes 2359304 | tf_op jit(solution)/shard_map/ppermute | solution.py:716
  197.3 60.2 %collective-permute-start.16 = (bf16[512,768]{1,0:T(8,128)(2,1)}, bf16[512,768]{1,0:T(8,128)(2,1)}, u32[]{:S(2)}, u32[]{:S(2)}) collective-permute-start(bf16[512,768]{1,0:T(8,128)(2,1)} %get-tuple-element.130), channel_id=1, source_target_pairs={{1,0},{0,1},{5,2},{4,3},{3,4},{2,5},{7,6},{6,7},{9,8},{8,9},{13,10... | collective-permute-start | bytes 2359304 | tf_op jit(solution)/shard_map/ppermute | solution.py:716
  204.9 29.3 %collective-permute-start.13 = (bf16[2,448,768]{2,1,0:T(8,128)(2,1)S(1)}, bf16[2,448,768]{2,1,0:T(8,128)(2,1)S(1)}, u32[]{:S(2)}, u32[]{:S(2)}) collective-permute-start(bf16[2,448,768]{2,1,0:T(8,128)(2,1)S(1)} %dynamic-slice_bitcast_fusion), channel_id=1, source_target_pairs={{0,16},{8,24},{16,0},{24,8},{1,17},{9,25},{17,1},{25,9},{2,18},{10... | collective-permute-start | bytes 4128776 | tf_op jit(solution)/shard_map/ppermute | solution.py:609
  205.8 29.0 %collective-permute-start.11 = (bf16[2,448,768]{2,1,0:T(8,128)(2,1)S(1)}, bf16[2,448,768]{2,1,0:T(8,128)(2,1)S(1)}, u32[]{:S(2)}, u32[]{:S(2)}) collective-permute-start(bf16[2,448,768]{2,1,0:T(8,128)(2,1)S(1)} %dynamic-slice_bitcast_fusion.1), channel_id=1, source_target_pairs={{0,8},{8,0},{16,24},{24,16},{1,9},{9,1},{17,25},{25,17},{2,10},{10... | collective-permute-start | bytes 4128776 | tf_op jit(solution)/shard_map/ppermute | solution.py:609
  227.5 7.0 %copy-start.3 = (bf16[1024,384]{1,0:T(8,128)(2,1)}, bf16[1024,384]{1,0:T(8,128)(2,1)S(1)}, u32[]{:S(2)}) copy-start(bf16[1024,384]{1,0:T(8,128)(2,1)S(1)} %get-tuple-element.84) | copy-start | bytes 2359300
  235.2 22.4 %collective-permute-start.15 = (bf16[448,768]{1,0:T(8,128)(2,1)S(1)}, bf16[448,768]{1,0:T(8,128)(2,1)S(1)}, u32[]{:S(2)}, u32[]{:S(2)}) collective-permute-start(bf16[448,768]{1,0:T(8,128)(2,1)S(1)} %dynamic-slice_bitcast_fusion.6), channel_id=1, source_target_pairs={{0,8},{8,0},{16,24},{24,16},{1,9},{9,1},{17,25},{25,17},{2,10},{10... | collective-permute-start | bytes 2064392 | tf_op jit(solution)/shard_map/ppermute | solution.py:609
  236.3 21.4 %collective-permute-start.14 = (bf16[448,768]{1,0:T(8,128)(2,1)S(1)}, bf16[448,768]{1,0:T(8,128)(2,1)S(1)}, u32[]{:S(2)}, u32[]{:S(2)}) collective-permute-start(bf16[448,768]{1,0:T(8,128)(2,1)S(1)} %dynamic-slice_bitcast_fusion.7), channel_id=1, source_target_pairs={{0,16},{8,24},{16,0},{24,8},{1,17},{9,25},{17,1},{25,9},{2,18},{10... | collective-permute-start | bytes 2064392 | tf_op jit(solution)/shard_map/ppermute | solution.py:609
  259.8 29.0 %collective-permute-start.17 = (bf16[224,768]{1,0:T(8,128)(2,1)S(1)}, bf16[224,768]{1,0:T(8,128)(2,1)S(1)}, u32[]{:S(2)}, u32[]{:S(2)}) collective-permute-start(bf16[224,768]{1,0:T(8,128)(2,1)S(1)} %get-tuple-element.141), channel_id=1, source_target_pairs={{0,1},{1,2},{2,3},{3,0},{4,5},{5,6},{6,7},{7,4},{8,9},{9,10},{10,1... | collective-permute-start | bytes 1032200 | tf_op jit(solution)/shard_map/ppermute | solution.py:628
  261.2 27.6 %collective-permute-start.18 = (bf16[224,768]{1,0:T(8,128)(2,1)S(1)}, bf16[224,768]{1,0:T(8,128)(2,1)S(1)}, u32[]{:S(2)}, u32[]{:S(2)}) collective-permute-start(bf16[224,768]{1,0:T(8,128)(2,1)S(1)} %get-tuple-element.142), channel_id=1, source_target_pairs={{0,2},{1,3},{2,0},{3,1},{4,6},{5,7},{6,4},{7,5},{8,10},{9,11},{10,... | collective-permute-start | bytes 1032200 | tf_op jit(solution)/shard_map/ppermute | solution.py:628
  266.0 30.6 %collective-permute-start.19 = (bf16[224,768]{1,0:T(8,128)(2,1)S(1)}, bf16[224,768]{1,0:T(8,128)(2,1)S(1)}, u32[]{:S(2)}, u32[]{:S(2)}) collective-permute-start(bf16[224,768]{1,0:T(8,128)(2,1)S(1)} %get-tuple-element.140), channel_id=1, source_target_pairs={{0,3},{1,0},{2,1},{3,2},{4,7},{5,4},{6,5},{7,6},{8,11},{9,8},{10,9... | collective-permute-start | bytes 1032200 | tf_op jit(solution)/shard_map/ppermute | solution.py:628
  288.7 8.4 %copy-start.25 = (bf16[1024,1152]{1,0:T(8,128)(2,1)}, bf16[1024,1152]{1,0:T(8,128)(2,1)S(1)}, u32[]{:S(2)}) copy-start(bf16[1024,1152]{1,0:T(8,128)(2,1)S(1)} %pad_maximum_fusion) | copy-start | bytes 7077892
  301.6 5.4 %collective-permute-start.20 = (bf16[1024,768]{1,0:T(8,128)(2,1)}, bf16[1024,768]{1,0:T(8,128)(2,1)}, u32[]{:S(2)}, u32[]{:S(2)}) collective-permute-start(bf16[1024,768]{1,0:T(8,128)(2,1)} %convolution_convert_fusion), channel_id=1, source_target_pairs={{0,4},{4,0},{1,5},{5,1},{2,6},{6,2},{3,7},{7,3},{8,12},{12,8},{9,1... | collective-permute-start | bytes 4718600 | tf_op jit(solution)/shard_map/ppermute | solution.py:572
  306.5 73.6 %collective-permute-start.36 = (bf16[224,768]{1,0:T(8,128)(2,1)S(1)}, bf16[224,768]{1,0:T(8,128)(2,1)S(1)}, u32[]{:S(2)}, u32[]{:S(2)}) collective-permute-start(bf16[224,768]{1,0:T(8,128)(2,1)S(1)} %get-tuple-element.122), channel_id=1, source_target_pairs={{0,3},{1,0},{2,1},{3,2},{4,7},{5,4},{6,5},{7,6},{8,11},{9,8},{10,9... | collective-permute-start | bytes 1032200 | tf_op jit(solution)/shard_map/ppermute | solution.py:628
  306.5 73.5 %collective-permute-start.35 = (bf16[224,768]{1,0:T(8,128)(2,1)S(1)}, bf16[224,768]{1,0:T(8,128)(2,1)S(1)}, u32[]{:S(2)}, u32[]{:S(2)}) collective-permute-start(bf16[224,768]{1,0:T(8,128)(2,1)S(1)} %get-tuple-element.122), channel_id=1, source_target_pairs={{0,2},{1,3},{2,0},{3,1},{4,6},{5,7},{6,4},{7,5},{8,10},{9,11},{10,... | collective-permute-start | bytes 1032200 | tf_op jit(solution)/shard_map/ppermute | solution.py:628
  316.2 11.5 %collective-permute-start.23 = (bf16[2,104,1152]{2,1,0:T(8,128)(2,1)S(1)}, bf16[2,104,1152]{2,1,0:T(8,128)(2,1)S(1)}, u32[]{:S(2)}, u32[]{:S(2)}) collective-permute-start(bf16[2,104,1152]{2,1,0:T(8,128)(2,1)S(1)} %dynamic-slice_bitcast_fusion.8), channel_id=1, source_target_pairs={{0,16},{8,24},{16,0},{24,8},{1,17},{9,25},{17,1},{25,9},{2,18},{10... | collective-permute-start | bytes 1437704 | tf_op jit(solution)/shard_map/ppermute | solution.py:609
  317.6 13.2 %collective-permute-start.21 = (bf16[2,104,1152]{2,1,0:T(8,128)(2,1)S(1)}, bf16[2,104,1152]{2,1,0:T(8,128)(2,1)S(1)}, u32[]{:S(2)}, u32[]{:S(2)}) collective-permute-start(bf16[2,104,1152]{2,1,0:T(8,128)(2,1)S(1)} %dynamic-slice_bitcast_fusion.9), channel_id=1, source_target_pairs={{0,8},{8,0},{16,24},{24,16},{1,9},{9,1},{17,25},{25,17},{2,10},{10... | collective-permute-start | bytes 1437704 | tf_op jit(solution)/shard_map/ppermute | solution.py:609
  317.8 36.1 %collective-permute-start.26 = (bf16[512,768]{1,0:T(8,128)(2,1)S(1)}, bf16[512,768]{1,0:T(8,128)(2,1)S(1)}, u32[]{:S(2)}, u32[]{:S(2)}) collective-permute-start(bf16[512,768]{1,0:T(8,128)(2,1)S(1)} %get-tuple-element.128), channel_id=1, source_target_pairs={{0,0},{1,1},{4,2},{5,3},{2,4},{3,5},{6,6},{7,7},{8,8},{9,9},{12,10... | collective-permute-start | bytes 2359304 | tf_op jit(solution)/shard_map/ppermute | solution.py:786
  327.7 47.7 %collective-permute-start.27 = (bf16[512,768]{1,0:T(8,128)(2,1)S(1)}, bf16[512,768]{1,0:T(8,128)(2,1)S(1)}, u32[]{:S(2)}, u32[]{:S(2)}) collective-permute-start(bf16[512,768]{1,0:T(8,128)(2,1)S(1)} %get-tuple-element.127), channel_id=1, source_target_pairs={{1,0},{0,1},{5,2},{4,3},{3,4},{2,5},{7,6},{6,7},{9,8},{8,9},{13,10... | collective-permute-start | bytes 2359304 | tf_op jit(solution)/shard_map/ppermute | solution.py:786
  330.8 5.9 %collective-permute-start.24 = (bf16[104,1152]{1,0:T(8,128)(2,1)S(1)}, bf16[104,1152]{1,0:T(8,128)(2,1)S(1)}, u32[]{:S(2)}, u32[]{:S(2)}) collective-permute-start(bf16[104,1152]{1,0:T(8,128)(2,1)S(1)} %dynamic-slice_bitcast_fusion.10), channel_id=1, source_target_pairs={{0,8},{8,0},{16,24},{24,16},{1,9},{9,1},{17,25},{25,17},{2,10},{10... | collective-permute-start | bytes 718856 | tf_op jit(solution)/shard_map/ppermute | solution.py:609
  336.6 5.3 %collective-permute-start.22 = (bf16[104,1152]{1,0:T(8,128)(2,1)S(1)}, bf16[104,1152]{1,0:T(8,128)(2,1)S(1)}, u32[]{:S(2)}, u32[]{:S(2)}) collective-permute-start(bf16[104,1152]{1,0:T(8,128)(2,1)S(1)} %dynamic-slice_bitcast_fusion.11), channel_id=1, source_target_pairs={{0,16},{8,24},{16,0},{24,8},{1,17},{9,25},{17,1},{25,9},{2,18},{10... | collective-permute-start | bytes 718856 | tf_op jit(solution)/shard_map/ppermute | solution.py:609
  342.5 34.9 %collective-permute-start.25 = (bf16[52,1152]{1,0:T(8,128)(2,1)S(1)}, bf16[52,1152]{1,0:T(8,128)(2,1)S(1)}, u32[]{:S(2)}, u32[]{:S(2)}) collective-permute-start(bf16[52,1152]{1,0:T(8,128)(2,1)S(1)} %get-tuple-element.145), channel_id=1, source_target_pairs={{0,1},{1,2},{2,3},{3,0},{4,5},{5,6},{6,7},{7,4},{8,9},{9,10},{10,1... | collective-permute-start | bytes 359432 | tf_op jit(solution)/shard_map/ppermute | solution.py:628
  353.9 25.0 %collective-permute-start.28 = (bf16[52,1152]{1,0:T(8,128)(2,1)S(1)}, bf16[52,1152]{1,0:T(8,128)(2,1)S(1)}, u32[]{:S(2)}, u32[]{:S(2)}) collective-permute-start(bf16[52,1152]{1,0:T(8,128)(2,1)S(1)} %get-tuple-element.146), channel_id=1, source_target_pairs={{0,2},{1,3},{2,0},{3,1},{4,6},{5,7},{6,4},{7,5},{8,10},{9,11},{10,... | collective-permute-start | bytes 359432 | tf_op jit(solution)/shard_map/ppermute | solution.py:628
  375.4 4.4 %collective-permute-start.29 = (bf16[52,1152]{1,0:T(8,128)(2,1)S(1)}, bf16[52,1152]{1,0:T(8,128)(2,1)S(1)}, u32[]{:S(2)}, u32[]{:S(2)}) collective-permute-start(bf16[52,1152]{1,0:T(8,128)(2,1)S(1)} %get-tuple-element.147), channel_id=1, source_target_pairs={{0,3},{1,0},{2,1},{3,2},{4,7},{5,4},{6,5},{7,6},{8,11},{9,8},{10,9... | collective-permute-start | bytes 359432 | tf_op jit(solution)/shard_map/ppermute | solution.py:628
  377.4 8.3 %collective-permute-start.34 = (bf16[224,768]{1,0:T(8,128)(2,1)S(1)}, bf16[224,768]{1,0:T(8,128)(2,1)S(1)}, u32[]{:S(2)}, u32[]{:S(2)}) collective-permute-start(bf16[224,768]{1,0:T(8,128)(2,1)S(1)} %get-tuple-element.122), channel_id=1, source_target_pairs={{0,1},{1,2},{2,3},{3,0},{4,5},{5,6},{6,7},{7,4},{8,9},{9,10},{10,1... | collective-permute-start | bytes 1032200 | tf_op jit(solution)/shard_map/ppermute | solution.py:628
  387.7 10.5 %collective-permute-start.30 = (bf16[52,1152]{1,0:T(8,128)(2,1)S(1)}, bf16[52,1152]{1,0:T(8,128)(2,1)S(1)}, u32[]{:S(2)}, u32[]{:S(2)}) collective-permute-start(bf16[52,1152]{1,0:T(8,128)(2,1)S(1)} %add_convert_fusion.3), channel_id=1, source_target_pairs={{0,1},{1,2},{2,3},{3,0},{4,5},{5,6},{6,7},{7,4},{8,9},{9,10},{10,1... | collective-permute-start | bytes 359432 | tf_op jit(solution)/shard_map/ppermute | solution.py:628
  389.6 11.5 %collective-permute-start.31 = (bf16[52,1152]{1,0:T(8,128)(2,1)S(1)}, bf16[52,1152]{1,0:T(8,128)(2,1)S(1)}, u32[]{:S(2)}, u32[]{:S(2)}) collective-permute-start(bf16[52,1152]{1,0:T(8,128)(2,1)S(1)} %add_convert_fusion.3), channel_id=1, source_target_pairs={{0,2},{1,3},{2,0},{3,1},{4,6},{5,7},{6,4},{7,5},{8,10},{9,11},{10,... | collective-permute-start | bytes 359432 | tf_op jit(solution)/shard_map/ppermute | solution.py:628
  389.9 12.2 %collective-permute-start.32 = (bf16[52,1152]{1,0:T(8,128)(2,1)S(1)}, bf16[52,1152]{1,0:T(8,128)(2,1)S(1)}, u32[]{:S(2)}, u32[]{:S(2)}) collective-permute-start(bf16[52,1152]{1,0:T(8,128)(2,1)S(1)} %add_convert_fusion.3), channel_id=1, source_target_pairs={{0,3},{1,0},{2,1},{3,2},{4,7},{5,4},{6,5},{7,6},{8,11},{9,8},{10,9... | collective-permute-start | bytes 359432 | tf_op jit(solution)/shard_map/ppermute | solution.py:628
  403.4 4.5 %collective-permute-start.33 = (bf16[112,1152]{1,0:T(8,128)(2,1)S(1)}, bf16[112,1152]{1,0:T(8,128)(2,1)S(1)}, u32[]{:S(2)}, u32[]{:S(2)}) collective-permute-start(bf16[112,1152]{1,0:T(8,128)(2,1)S(1)} %pad_maximum_fusion.4), channel_id=1, source_target_pairs={{0,4},{4,0},{1,5},{5,1},{2,6},{6,2},{3,7},{7,3},{8,12},{12,8},{9,1... | collective-permute-start | bytes 774152 | tf_op jit(solution)/shard_map/ppermute | solution.py:572
  (40 other events, 90.1 us)
Sparse Core Ops, SparseCore 0:
  12.4 33.2 all-gather.5
  48.1 64.2 all-gather.7

commit v10 on v9

--- a/solution.py
+++ b/solution.py
@@ -82,55 +82,54 @@
     for pair in range(pairs):
         for copy in loads(pair):
             copy.wait()
-    heads = [(pair, head) for pair in range(pairs) for head in range(2)]
-    if True:
-
-        @pl.loop(0, total // TILE)
-        def _(block):
-            rows = pl.multiple_of(block * TILE, TILE)
-            for pair in range(pairs):
-                values = qkv[2 * pairs + pair, pl.ds(rows, TILE), :].astype(jnp.float32).T.astype(jnp.bfloat16)
-                for head in range(2):
-                    turned[2 * pair + head, :HEAD_DIM, pl.ds(rows, TILE)] = values[head * HEAD_DIM : (head + 1) * HEAD_DIM]
-
-        @pl.loop(0, total // TILE)
-        def _(block):
-            rows = pl.multiple_of(block * TILE, TILE)
-            q_heads = sum([list(lane_halves(qkv[pair, pl.ds(rows, TILE), :], 0.0)) for pair in range(pairs)], [])
-            segq = seg_row[:, pl.ds(rows, TILE)]
-            first, after = key_tiles(ends_ref, rows, rows + TILE - 1, TILE, total)
-            acc[...] = jnp.zeros_like(acc)
-            top[...] = jnp.full_like(top, NEG)
-
-            first, steps = spans(first, after, KEY_TILES, total // TILE)
-
-            @pl.loop(0, steps)
-            def _(step):
-                at = pl.multiple_of((first + step * KEY_TILES) * TILE, TILE)
-                keys = [qkv[pairs + pair, pl.ds(at, KEY_TILES * TILE), :] for pair in range(pairs)]
-                segk = seg_col[pl.ds(at, KEY_TILES * TILE), :]
-                same = jnp.concatenate([segk] * (TILE // LANES), axis=1) == segq
-                def scores_of(head):
-                    return jnp.where(same, mm(keys[head // 2], q_heads[head], NT), NEG)
-
-                queue = [scores_of(head) for head in range(6)]
-                for head in range(2 * pairs):
-                    if head + 6 < 2 * pairs:
-                        queue.append(scores_of(head + 6))
-                    scores = queue.pop(0)
-                    old = top[head, 0:1]
-                    new = jnp.maximum(old, jnp.max(scores, axis=0, keepdims=True))
-                    probs = jnp.exp(scores - new).astype(jnp.bfloat16)
-                    acc[head] = acc[head] * jnp.exp(old - new) + mm(turned[head, :, pl.ds(at, KEY_TILES * TILE)], probs, NN)
-                    top[head] = jnp.broadcast_to(new, (8, TILE))
-
-            for pair in range(pairs):
-                parts = []
-                for head in (2 * pair, 2 * pair + 1):
-                    weight = acc[head, HEAD_DIM : HEAD_DIM + 1]
-                    parts.append(acc[head, :HEAD_DIM] / weight)
-                    lse_ref[head, :, pl.ds(rows, TILE)] = top[head] + jnp.log(acc[head, HEAD_DIM : HEAD_DIM + 8])
-                out[pair, pl.ds(rows, TILE), :] = jnp.concatenate(parts, axis=0).T.astype(jnp.bfloat16)
+
+    @pl.loop(0, total // TILE)
+    def _(block):
+        rows = pl.multiple_of(block * TILE, TILE)
+        for pair in range(pairs):
+            values = qkv[2 * pairs + pair, pl.ds(rows, TILE), :].astype(jnp.float32).T.astype(jnp.bfloat16)
+            for head in range(2):
+                turned[2 * pair + head, :HEAD_DIM, pl.ds(rows, TILE)] = values[head * HEAD_DIM : (head + 1) * HEAD_DIM]
+
+    @pl.loop(0, total // TILE)
+    def _(block):
+        rows = pl.multiple_of(block * TILE, TILE)
+        q_heads = sum([list(lane_halves(qkv[pair, pl.ds(rows, TILE), :], 0.0)) for pair in range(pairs)], [])
+        segq = seg_row[:, pl.ds(rows, TILE)]
+        first, after = key_tiles(ends_ref, rows, rows + TILE - 1, TILE, total)
+        acc[...] = jnp.zeros_like(acc)
+        top[...] = jnp.full_like(top, NEG)
+
+        first, steps = spans(first, after, KEY_TILES, total // TILE)
+
+        @pl.loop(0, steps)
+        def _(step):
+            at = pl.multiple_of((first + step * KEY_TILES) * TILE, TILE)
+            keys = [qkv[pairs + pair, pl.ds(at, KEY_TILES * TILE), :] for pair in range(pairs)]
+            segk = seg_col[pl.ds(at, KEY_TILES * TILE), :]
+            same = jnp.concatenate([segk] * (TILE // LANES), axis=1) == segq
+
+            def scores_of(head):
+                return jnp.where(same, mm(keys[head // 2], q_heads[head], NT), NEG)
+
+            queue = [scores_of(head) for head in range(6)]
+            for head in range(2 * pairs):
+                if head + 6 < 2 * pairs:
+                    queue.append(scores_of(head + 6))
+                scores = queue.pop(0)
+                old = top[head, 0:1]
+                new = jnp.maximum(old, jnp.max(scores, axis=0, keepdims=True))
+                probs = jnp.exp(scores - new).astype(jnp.bfloat16)
+                acc[head] = acc[head] * jnp.exp(old - new) + mm(turned[head, :, pl.ds(at, KEY_TILES * TILE)], probs, NN)
+                top[head] = jnp.broadcast_to(new, (8, TILE))
+
+        for pair in range(pairs):
+            parts = []
+            for head in (2 * pair, 2 * pair + 1):
+                weight = acc[head, HEAD_DIM : HEAD_DIM + 1]
+                parts.append(acc[head, :HEAD_DIM] / weight)
+                lse_ref[head, :, pl.ds(rows, TILE)] = top[head] + jnp.log(acc[head, HEAD_DIM : HEAD_DIM + 8])
+            out[pair, pl.ds(rows, TILE), :] = jnp.concatenate(parts, axis=0).T.astype(jnp.bfloat16)
 
     for pair in range(pairs):
         for copy in piece_copies((ctx_own, ctx_sib), pair * LANES, pair, out, pair, out_sems, run, mask, False):
@@ -276,7 +275,6 @@
         ],
         compiler_params=pltpu.CompilerParams(vmem_limit_bytes=24 << 20),
         cost_estimate=pl.CostEstimate(flops=20_000_000_000, bytes_accessed=8_000_000, transcendentals=0),
-        name=f"attend_backward_{pair}",
     )(mask, ends, own, sib, ctx_own, ctx_sib, dctx_own, dctx_sib, seg_col, seg_row, lse)
 
 
@@ -781,11 +779,13 @@
     early_sum.add(grads[-1][0])
     near = jnp.concatenate([g[0] for g in grads], axis=1)
     far = after(jnp.concatenate([g[1] for g in grads], axis=1), early_sum.keep)
-    grad_far = swap(mm(far, w_mine, NT).astype(bf16))
+    grad_far = mm(far, w_mine, NT).astype(bf16)
+    grad_far = swap(grad_far)
     input_grad = (grad_one + mm(near, w_mine, NT) + grad_far.astype(f32)).astype(bf16)
     returned = [lax.ppermute(input_grad[i * run : (i + 1) * run], ("core", "seq"), back[i]) for i in range(2)]
     near, far = after((near, far), input_grad)
-    qkv_halves = Halving(weight_sums(near, far), planes)
+    blocks = weight_sums(near, far)
+    qkv_halves = Halving(blocks, planes)
     for step in range(qkv_halves.steps):
         qkv_halves.send(step)
         qkv_halves.add(input_grad)

time: 427 us -> 427 us (level)
    ppermute x2, waiting for transfers between devices: 31.6 us -> 27 us  [per_device(): lax.ppermute(input_grad[i * run:(i + 1) * run], ('core', 'seq'), back[i])]
    ppermute x8, waiting for transfers between devices: 21.1 us -> 25.6 us  [send(): lax.ppermute(out, 'xy', [(i, i ^ 1 << bit) for i in range(self.planes)])]
  transfers between devices with their start and end apart: 39 -> 39, of which waited for: 20 -> 21; matrix products, arithmetic and copies ran while one was open for 12% -> 12% of each run, Pallas kernels for 22% -> 22%
where the time goes in v10:
time: 427 us; the launch traced here: 419 us
  Pallas kernels  160 us (37%)
  waiting for transfers between devices  106 us (25%)
  starting transfers between devices  45.3 us (11%)
  local copies, waits for them, and re-layouts  38.4 us (9%)
  other arithmetic  26.1 us (6%)
  matrix products  18.4 us (4%)
  between operations  15.4 us (4%)
  blocking collectives  9.52 us (2%)
    pallas_call x3, Pallas kernels, attend_backward(): pl.pallas_call(functools.partial(backward_kernel, run, pair), out_shape=(...  61 us
    pallas_call x1, Pallas kernels, middle(): pl.pallas_call(middle_kernel, grid=(count // ROWS,), out_shape=(shape((co...  48.4 us
    pallas_call x1, Pallas kernels, attend_forward(): pl.pallas_call(functools.partial(forward_kernel, run), out_shape=(jax.Sha...  32.6 us
    ppermute x2, waiting for transfers between devices, per_device(): lax.ppermute(input_grad[i * run:(i + 1) * run], ('core', 'seq'), back[i])  27 us
    ppermute x8, waiting for transfers between devices, send(): lax.ppermute(out, 'xy', [(i, i ^ 1 << bit) for i in range(self.planes)])  25.6 us
    ppermute x4, waiting for transfers between devices, spread(): lax.ppermute(h, ('core', 'seq'), r)  25.1 us
    ppermute x12, waiting for transfers between devices, shift(): lax.ppermute(value, 'seq', [(i, (i + distance) % self.nseq) for i in rang...  19.5 us
    unnamed x106, local copies, waits for them, and re-layouts  18.9 us
  transfers between devices with their start and end apart: 39, of which 21 were waited for; matrix products, arithmetic and copies ran while one was open for 12% of the time, Pallas kernels for 22%

profile of v10, /device:TPU:9, one launch (start us, length us, event | category | flops | bytes accessed | tf_op | source)
XLA Modules:
  0.0 419.0 jit_solution(17447153688727734312)
XLA Ops:
  7.2 1.6 reshape.360
  15.8 4.5 %collective-permute-start = (bf16[512,768]{1,0:T(8,128)(2,1)S(1)}, bf16[512,768]{1,0:T(8,128)(2,1)S(1)}, u32[]{:S(2)}, u32[]{:S(2)}) collective-permute-start(bf16[512,768]{1,0:T(8,128)(2,1)S(1)} %get-tuple-element.133), channel_id=1, source_target_pairs={{0,0},{1,1},{2,4},{3,5},{4,2},{5,3},{6,6},{7,7},{8,8},{9,9},{10,12... | collective-permute-start | bytes 2359304 | tf_op jit(solution)/shard_map/ppermute | solution.py:666
  20.6 9.5 %all-gather.2 = bf16[8,12,96]{2,1,0:T(8,128)(2,1)S(1)} all-gather(bf16[1,12,96]{2,1,0:T(8,128)(2,1)S(1)} %bitcast.148), channel_id=2, replica_groups=mesh['xy'=4,'core'=2,'seq'=4] {'xy','core'}, dimensions={0}, use_global_device_ids=true | all-gather | bytes 20736 | tf_op jit(solution)/shard_map/all_gather | solution.py:687
  30.2 15.7 %collective-permute-done = bf16[512,768]{1,0:T(8,128)(2,1)S(1)} collective-permute-done((bf16[512,768]{1,0:T(8,128)(2,1)S(1)}, bf16[512,768]{1,0:T(8,128)(2,1)S(1)}, u32[]{:S(2)}, u32[]{:S(2)}) %collective-permute-start) | collective-permute-done | bytes 786464 | tf_op jit(solution)/shard_map/ppermute | solution.py:666
  46.4 8.1 %collective-permute-done.1 = bf16[512,768]{1,0:T(8,128)(2,1)S(1)} collective-permute-done((bf16[512,768]{1,0:T(8,128)(2,1)}, bf16[512,768]{1,0:T(8,128)(2,1)S(1)}, u32[]{:S(2)}, u32[]{:S(2)}) %collective-permute-start.1) | collective-permute-done | bytes 786464 | tf_op jit(solution)/shard_map/ppermute | solution.py:666
  58.2 4.5 %multiply_convert_fusion.sib = bf16[1024,1152]{1,0:T(8,128)(2,1)S(1)} fusion(bf16[1024,768]{1,0:T(8,128)(2,1)} %constant_dynamic-update-slice_fusion, bf16[768,1152]{1,0:T(8,128)(2,1)} %all-gather.6.cloned.1.call-done, f32[1152]{0:T(1024)S(1)} %copy-done.48, f32[1152]{0:T(1024)S(1)} %add.272), kind=kOutput, calls=%fused_computation.3 | convolution fusion | flops 1815478272 | bytes 5710848 | tf_op jit(solution)/shard_map/dot_general | solution.py:25
  62.8 2.2 multiply_convert_fusion.1.own
  65.1 2.1 collective-permute-start.7
  67.2 2.2 collective-permute-start.8
  69.9 32.6 %attend_forward.1 = (bf16[1024,384]{1,0:T(8,128)(2,1)S(1)}, bf16[1024,384]{1,0:T(8,128)(2,1)S(1)}, f32[6,8,2048]{2,1,0:T(8,128)S(1)}) custom-call(s32[1]{0:T(128)} %bitcast.13.mask_ref, s32[8]{0:T(128)S(1)} %bitcast.129, bf16[1024,1152]{1,0:T(8,128)(2,1)S(1)} %multiply_convert_fusion.1.own, bf16[1024,1152]{1,0:T(8,128)(2,1)S(1)} %multiply_convert_fusion.sib, ...), custom_call_target="tpu_custom_call" | custom-call | flops 1000000000 | bytes 1000000 | tf_op jit(solution)/shard_map/attend_forward/pallas_call | solution.py:150
  107.1 5.3 %all-gather.8.cloned.1.call-done = bf16[6912,768]{1,0:T(8,128)(2,1)} async-done(((bf16[864,768]{1,0:T(8,128)(2,1)}), bf16[6912,768]{1,0:T(8,128)(2,1)}) %all-gather.8.cloned.1.call-update) | async-done | bytes 10616848 | tf_op jit(solution)/shard_map/all_gather | solution.py:693
  114.7 48.4 %middle.1 = (bf16[1024,768]{1,0:T(8,128)(2,1)S(1)}, bf16[1024,768]{1,0:T(8,128)(2,1)}, bf16[1024,3072]{1,0:T(8,128)(2,1)}, bf16[1024,768]{1,0:T(8,128)(2,1)}, bf...) custom-call(s32[1]{0:T(128)} %bitcast.core_ref, ...), custom_call_target="tpu_custom_call" | custom-call | flops 20000000000 | bytes 30000000 | tf_op jit(solution)/shard_map/middle/pallas_call | solution.py:427
  168.7 1.4 copy-done.21
  171.5 18.0 %gradients.1 = (bf16[4,896,768]{2,1,0:T(8,128)(2,1)}, bf16[4,896,768]{2,1,0:T(8,128)(2,1)}) custom-call(s32[1]{0:T(128)} %bitcast.core_ref, bf16[1024,3072]{1,0:T(8,128)(2,1)} %get-tuple-element.71.act_ref, bf16[1024,768]{1,0:T(8,128)(2,1)S(1)} %copy-done.21, bf16[1024,768]{1,0:T(8,128)(2,1)S(1)} %copy-done.22, ...), custom_call_target="tpu_custom_call" | custom-call | flops 11000000512 | bytes 30000000 | tf_op jit(solution)/shard_map/gradients/pallas_call | solution.py:529
  190.0 2.6 fusion.28
  192.6 4.4 %collective-permute-start.9 = (bf16[512,768]{1,0:T(8,128)(2,1)}, bf16[512,768]{1,0:T(8,128)(2,1)}, u32[]{:S(2)}, u32[]{:S(2)}) collective-permute-start(bf16[512,768]{1,0:T(8,128)(2,1)} %get-tuple-element.129), channel_id=1, source_target_pairs={{0,0},{1,1},{4,2},{5,3},{2,4},{3,5},{6,6},{7,7},{8,8},{9,9},{12,10... | collective-permute-start | bytes 2359304 | tf_op jit(solution)/shard_map/ppermute | solution.py:714
  197.1 1.8 collective-permute-done.10
  198.9 5.5 %add_convert_fusion = bf16[4,896,768]{2,1,0:T(8,128)(2,1)S(1)} fusion(bf16[4,896,768]{2,1,0:T(8,128)(2,1)} %collective-permute-done.10, bf16[4,896,768]{2,1,0:T(8,128)(2,1)} %get-tuple-element.78), kind=kLoop, calls=%fused_computation | loop fusion | flops 11010048 | bytes 16515072 | tf_op jit(solution)/shard_map/convert_element_type | solution.py:582
  207.2 20.3 %shard_map.271 = (bf16[1024,384]{1,0:T(8,128)(2,1)S(1)}, bf16[1024,384]{1,0:T(8,128)(2,1)S(1)}) custom-call(s32[1]{0:T(128)} %bitcast.13.mask_ref, s32[8]{0:T(128)S(1)} %bitcast.130, bf16[1024,1152]{1,0:T(8,128)(2,1)S(1)} %copy-done.1, bf16[1024,1152]{1,0:T(8,128)(2,1)S(1)} %multiply_convert_fusion.sib, bf16[1024,384]{1,0:T(8,128)(2,1)S(1)} %copy-done.12, ...), custom_call_target="tpu_custom_call" | custom-call | flops 20000000000 | bytes 8000000 | tf_op jit(solution)/shard_map/pallas_call | solution.py:257
  227.5 7.0 %collective-permute-done.13 = bf16[2,448,768]{2,1,0:T(8,128)(2,1)S(1)} collective-permute-done((bf16[2,448,768]{2,1,0:T(8,128)(2,1)S(1)}, bf16[2,448,768]{2,1,0:T(8,128)(2,1)S(1)}, u32[]{:S(2)}, u32[]{:S(2)}) %collective-permute-start.13) | collective-permute-done | bytes 1376288 | tf_op jit(solution)/shard_map/ppermute | solution.py:607
  237.5 20.3 %shard_map.272 = (bf16[1024,384]{1,0:T(8,128)(2,1)S(1)}, bf16[1024,384]{1,0:T(8,128)(2,1)S(1)}) custom-call(s32[1]{0:T(128)} %bitcast.13.mask_ref, s32[8]{0:T(128)S(1)} %bitcast.131, bf16[1024,1152]{1,0:T(8,128)(2,1)S(1)} %copy-done.1, bf16[1024,1152]{1,0:T(8,128)(2,1)S(1)} %multiply_convert_fusion.sib, bf16[1024,384]{1,0:T(8,128)(2,1)S(1)} %copy-done.12, ...), custom_call_target="tpu_custom_call" | custom-call | flops 20000000000 | bytes 8000000 | tf_op jit(solution)/shard_map/pallas_call | solution.py:257
  260.1 2.0 collective-permute-start.17
  262.1 3.8 collective-permute-start.18
  265.9 1.8 collective-permute-start.19
  267.7 20.3 %shard_map.273 = (bf16[1024,384]{1,0:T(8,128)(2,1)S(1)}, bf16[1024,384]{1,0:T(8,128)(2,1)S(1)}) custom-call(s32[1]{0:T(128)} %bitcast.13.mask_ref, s32[8]{0:T(128)S(1)} %bitcast.132, bf16[1024,1152]{1,0:T(8,128)(2,1)S(1)} %copy-done.1, bf16[1024,1152]{1,0:T(8,128)(2,1)S(1)} %multiply_convert_fusion.sib, bf16[1024,384]{1,0:T(8,128)(2,1)S(1)} %copy-done.12, ...), custom_call_target="tpu_custom_call" | custom-call | flops 20000000000 | bytes 8000000 | tf_op jit(solution)/shard_map/pallas_call | solution.py:257
  290.0 6.5 %collective-permute-done.19 = bf16[224,768]{1,0:T(8,128)(2,1)S(1)} collective-permute-done((bf16[224,768]{1,0:T(8,128)(2,1)S(1)}, bf16[224,768]{1,0:T(8,128)(2,1)S(1)}, u32[]{:S(2)}, u32[]{:S(2)}) %collective-permute-start.19) | collective-permute-done | bytes 344096 | tf_op jit(solution)/shard_map/ppermute | solution.py:626
  298.1 3.4 convolution_convert_fusion
  304.2 2.2 fusion.30
  306.9 2.2 add_convert_fusion.1
  309.1 2.3 fusion.31
  312.2 3.7 fusion
  316.2 2.4 collective-permute-start.23
  318.8 4.9 %collective-permute-start.26 = (bf16[512,768]{1,0:T(8,128)(2,1)S(1)}, bf16[512,768]{1,0:T(8,128)(2,1)S(1)}, u32[]{:S(2)}, u32[]{:S(2)}) collective-permute-start(bf16[512,768]{1,0:T(8,128)(2,1)S(1)} %get-tuple-element.128), channel_id=1, source_target_pairs={{0,0},{1,1},{4,2},{5,3},{2,4},{3,5},{6,6},{7,7},{8,8},{9,9},{12,10... | collective-permute-start | bytes 2359304 | tf_op jit(solution)/shard_map/ppermute | solution.py:785
  323.7 5.5 %collective-permute-done.23 = bf16[2,104,1152]{2,1,0:T(8,128)(2,1)S(1)} collective-permute-done((bf16[2,104,1152]{2,1,0:T(8,128)(2,1)S(1)}, bf16[2,104,1152]{2,1,0:T(8,128)(2,1)S(1)}, u32[]{:S(2)}, u32[]{:S(2)}) %collective-permute-start.23) | collective-permute-done | bytes 479264 | tf_op jit(solution)/shard_map/ppermute | solution.py:607
  329.2 3.5 collective-permute-start.27
  333.4 7.3 %collective-permute-done.24 = bf16[104,1152]{1,0:T(8,128)(2,1)S(1)} collective-permute-done((bf16[104,1152]{1,0:T(8,128)(2,1)S(1)}, bf16[104,1152]{1,0:T(8,128)(2,1)S(1)}, u32[]{:S(2)}, u32[]{:S(2)}) %collective-permute-start.24) | collective-permute-done | bytes 239648 | tf_op jit(solution)/shard_map/ppermute | solution.py:607
  342.0 5.8 %collective-permute-done.22 = bf16[104,1152]{1,0:T(8,128)(2,1)S(1)} collective-permute-done((bf16[104,1152]{1,0:T(8,128)(2,1)S(1)}, bf16[104,1152]{1,0:T(8,128)(2,1)S(1)}, u32[]{:S(2)}, u32[]{:S(2)}) %collective-permute-start.22) | collective-permute-done | bytes 239648 | tf_op jit(solution)/shard_map/ppermute | solution.py:607
  348.4 6.5 %collective-permute-done.26 = bf16[512,768]{1,0:T(8,128)(2,1)S(1)} collective-permute-done((bf16[512,768]{1,0:T(8,128)(2,1)S(1)}, bf16[512,768]{1,0:T(8,128)(2,1)S(1)}, u32[]{:S(2)}, u32[]{:S(2)}) %collective-permute-start.26) | collective-permute-done | bytes 786464 | tf_op jit(solution)/shard_map/ppermute | solution.py:785
  354.9 20.5 %collective-permute-done.27 = bf16[512,768]{1,0:T(8,128)(2,1)S(1)} collective-permute-done((bf16[512,768]{1,0:T(8,128)(2,1)S(1)}, bf16[512,768]{1,0:T(8,128)(2,1)S(1)}, u32[]{:S(2)}, u32[]{:S(2)}) %collective-permute-start.27) | collective-permute-done | bytes 786464 | tf_op jit(solution)/shard_map/ppermute | solution.py:785
  375.4 1.9 fusion.3
  377.3 1.5 collective-permute-start.34
  380.0 5.6 %collective-permute-done.34 = bf16[224,768]{1,0:T(8,128)(2,1)S(1)} collective-permute-done((bf16[224,768]{1,0:T(8,128)(2,1)S(1)}, bf16[224,768]{1,0:T(8,128)(2,1)S(1)}, u32[]{:S(2)}, u32[]{:S(2)}) %collective-permute-start.34) | collective-permute-done | bytes 344096 | tf_op jit(solution)/shard_map/ppermute | solution.py:626
  387.6 1.9 collective-permute-start.30
  389.9 1.5 collective-permute-start.32
  394.9 3.1 collective-permute-done.30
  399.2 1.7 collective-permute-done.31
  403.9 3.4 maximum_select_fusion
  410.3 1.6 reshape.382
  (267 shorter events, 58.7 us)
Async XLA Ops:
  7.2 51.0 %all-gather.6.cloned.1.call-start = ((), (), s32[]{:S(2)}) async-start(), calls=%async_computation | async-start | bytes 2211840 | tf_op jit(solution)/shard_map/all_gather | solution.py:683
  9.6 1.8 collective-permute-start.3
  12.3 100.1 %all-gather.8.cloned.1.call-start = ((), (), s32[]{:S(2)}) async-start(), calls=%async_computation.1 | async-start | bytes 11943936 | tf_op jit(solution)/shard_map/all_gather | solution.py:693
  14.7 5.8 %copy-start.37 = (bf16[96]{0:T(256)(128)(2,1)S(1)}, bf16[96]{0:T(256)(128)(2,1)}, u32[]{:S(2)}) copy-start(bf16[96]{0:T(256)(128)(2,1)} %param.19) | copy-start | bytes 580
  14.7 5.8 %copy-start.38 = (bf16[96]{0:T(256)(128)(2,1)S(1)}, bf16[96]{0:T(256)(128)(2,1)}, u32[]{:S(2)}) copy-start(bf16[96]{0:T(256)(128)(2,1)} %param.20) | copy-start | bytes 580
  14.7 5.8 %copy-start.39 = (bf16[96]{0:T(256)(128)(2,1)S(1)}, bf16[96]{0:T(256)(128)(2,1)}, u32[]{:S(2)}) copy-start(bf16[96]{0:T(256)(128)(2,1)} %param.22) | copy-start | bytes 580
  14.7 5.8 %copy-start.40 = (bf16[96]{0:T(256)(128)(2,1)S(1)}, bf16[96]{0:T(256)(128)(2,1)}, u32[]{:S(2)}) copy-start(bf16[96]{0:T(256)(128)(2,1)} %param.23) | copy-start | bytes 580
  14.7 5.8 %copy-start.41 = (bf16[96]{0:T(256)(128)(2,1)S(1)}, bf16[96]{0:T(256)(128)(2,1)}, u32[]{:S(2)}) copy-start(bf16[96]{0:T(256)(128)(2,1)} %param.24) | copy-start | bytes 580
  14.7 5.8 %copy-start.42 = (bf16[96]{0:T(256)(128)(2,1)S(1)}, bf16[96]{0:T(256)(128)(2,1)}, u32[]{:S(2)}) copy-start(bf16[96]{0:T(256)(128)(2,1)} %param.28) | copy-start | bytes 580
  14.7 5.8 %copy-start.43 = (bf16[96]{0:T(256)(128)(2,1)S(1)}, bf16[96]{0:T(256)(128)(2,1)}, u32[]{:S(2)}) copy-start(bf16[96]{0:T(256)(128)(2,1)} %param.29) | copy-start | bytes 580
  15.8 30.2 %collective-permute-start = (bf16[512,768]{1,0:T(8,128)(2,1)S(1)}, bf16[512,768]{1,0:T(8,128)(2,1)S(1)}, u32[]{:S(2)}, u32[]{:S(2)}) collective-permute-start(bf16[512,768]{1,0:T(8,128)(2,1)S(1)} %get-tuple-element.133), channel_id=1, source_target_pairs={{0,0},{1,1},{2,4},{3,5},{4,2},{5,3},{6,6},{7,7},{8,8},{9,9},{10,12... | collective-permute-start | bytes 2359304 | tf_op jit(solution)/shard_map/ppermute | solution.py:666
  20.2 34.2 %collective-permute-start.1 = (bf16[512,768]{1,0:T(8,128)(2,1)}, bf16[512,768]{1,0:T(8,128)(2,1)S(1)}, u32[]{:S(2)}, u32[]{:S(2)}) collective-permute-start(bf16[512,768]{1,0:T(8,128)(2,1)} %get-tuple-element.134), channel_id=1, source_target_pairs={{0,1},{1,0},{2,5},{3,4},{4,3},{5,2},{6,7},{7,6},{8,9},{9,8},{10,13... | collective-permute-start | bytes 2359304 | tf_op jit(solution)/shard_map/ppermute | solution.py:666
  20.3 34.5 %collective-permute-start.2 = (s32[2,8]{1,0:T(2,128)S(1)}, s32[2,8]{1,0:T(2,128)S(1)}, u32[]{:S(2)}, u32[]{:S(2)}) collective-permute-start(s32[2,8]{1,0:T(2,128)S(1)} %bitcast.151), channel_id=1, source_target_pairs={{0,4},{4,0},{1,5},{5,1},{2,6},{6,2},{3,7},{7,3},{8,12},{12,8},{9,1... | collective-permute-start | bytes 200 | tf_op jit(solution)/shard_map/ppermute | solution.py:570
  45.9 10.3 %collective-permute-start.4 = (bf16[512,768]{1,0:T(8,128)(2,1)S(1)}, bf16[512,768]{1,0:T(8,128)(2,1)S(1)}, u32[]{:S(2)}, u32[]{:S(2)}) collective-permute-start(bf16[512,768]{1,0:T(8,128)(2,1)S(1)} %collective-permute-done), channel_id=1, source_target_pairs={{0,4},{4,0},{1,5},{5,1},{2,6},{6,2},{3,7},{7,3},{8,12},{12,8},{9,1... | collective-permute-start | bytes 2359304 | tf_op jit(solution)/shard_map/ppermute | solution.py:570
  54.5 2.8 collective-permute-start.5
  65.1 38.1 %collective-permute-start.7 = (bf16[512,768]{1,0:T(8,128)(2,1)S(1)}, bf16[512,768]{1,0:T(8,128)(2,1)S(1)}, u32[]{:S(2)}, u32[]{:S(2)}) collective-permute-start(bf16[512,768]{1,0:T(8,128)(2,1)S(1)} %get-tuple-element.131), channel_id=1, source_target_pairs={{0,0},{1,1},{2,4},{3,5},{4,2},{5,3},{6,6},{7,7},{8,8},{9,9},{10,12... | collective-permute-start | bytes 2359304 | tf_op jit(solution)/shard_map/ppermute | solution.py:666
  67.2 37.3 %collective-permute-start.8 = (bf16[512,768]{1,0:T(8,128)(2,1)S(1)}, bf16[512,768]{1,0:T(8,128)(2,1)S(1)}, u32[]{:S(2)}, u32[]{:S(2)}) collective-permute-start(bf16[512,768]{1,0:T(8,128)(2,1)S(1)} %get-tuple-element.132), channel_id=1, source_target_pairs={{0,1},{1,0},{2,5},{3,4},{4,3},{5,2},{6,7},{7,6},{8,9},{9,8},{10,13... | collective-permute-start | bytes 2359304 | tf_op jit(solution)/shard_map/ppermute | solution.py:666
  103.2 3.0 collective-permute-start.6
  189.4 9.4 %collective-permute-start.10 = (bf16[4,896,768]{2,1,0:T(8,128)(2,1)}, bf16[4,896,768]{2,1,0:T(8,128)(2,1)}, u32[]{:S(2)}, u32[]{:S(2)}) collective-permute-start(bf16[4,896,768]{2,1,0:T(8,128)(2,1)} %get-tuple-element.79), channel_id=1, source_target_pairs={{0,4},{4,0},{1,5},{5,1},{2,6},{6,2},{3,7},{7,3},{8,12},{12,8},{9,1... | collective-permute-start | bytes 16515080 | tf_op jit(solution)/shard_map/ppermute | solution.py:570
  189.7 16.8 %collective-permute-start.12 = (bf16[1024,384]{1,0:T(8,128)(2,1)}, bf16[1024,384]{1,0:T(8,128)(2,1)S(1)}, u32[]{:S(2)}, u32[]{:S(2)}) collective-permute-start(bf16[1024,384]{1,0:T(8,128)(2,1)} %copy-done.15), channel_id=1, source_target_pairs={{0,4},{4,0},{1,5},{5,1},{2,6},{6,2},{3,7},{7,3},{8,12},{12,8},{9,1... | collective-permute-start | bytes 2359304 | tf_op jit(solution)/shard_map/ppermute | solution.py:570
  192.6 65.2 %collective-permute-start.9 = (bf16[512,768]{1,0:T(8,128)(2,1)}, bf16[512,768]{1,0:T(8,128)(2,1)}, u32[]{:S(2)}, u32[]{:S(2)}) collective-permute-start(bf16[512,768]{1,0:T(8,128)(2,1)} %get-tuple-element.129), channel_id=1, source_target_pairs={{0,0},{1,1},{4,2},{5,3},{2,4},{3,5},{6,6},{7,7},{8,8},{9,9},{12,10... | collective-permute-start | bytes 2359304 | tf_op jit(solution)/shard_map/ppermute | solution.py:714
  197.0 60.8 %collective-permute-start.16 = (bf16[512,768]{1,0:T(8,128)(2,1)}, bf16[512,768]{1,0:T(8,128)(2,1)}, u32[]{:S(2)}, u32[]{:S(2)}) collective-permute-start(bf16[512,768]{1,0:T(8,128)(2,1)} %get-tuple-element.130), channel_id=1, source_target_pairs={{1,0},{0,1},{5,2},{4,3},{3,4},{2,5},{7,6},{6,7},{9,8},{8,9},{13,10... | collective-permute-start | bytes 2359304 | tf_op jit(solution)/shard_map/ppermute | solution.py:714
  204.9 29.6 %collective-permute-start.13 = (bf16[2,448,768]{2,1,0:T(8,128)(2,1)S(1)}, bf16[2,448,768]{2,1,0:T(8,128)(2,1)S(1)}, u32[]{:S(2)}, u32[]{:S(2)}) collective-permute-start(bf16[2,448,768]{2,1,0:T(8,128)(2,1)S(1)} %dynamic-slice_bitcast_fusion), channel_id=1, source_target_pairs={{0,16},{8,24},{16,0},{24,8},{1,17},{9,25},{17,1},{25,9},{2,18},{10... | collective-permute-start | bytes 4128776 | tf_op jit(solution)/shard_map/ppermute | solution.py:607
  205.8 29.3 %collective-permute-start.11 = (bf16[2,448,768]{2,1,0:T(8,128)(2,1)S(1)}, bf16[2,448,768]{2,1,0:T(8,128)(2,1)S(1)}, u32[]{:S(2)}, u32[]{:S(2)}) collective-permute-start(bf16[2,448,768]{2,1,0:T(8,128)(2,1)S(1)} %dynamic-slice_bitcast_fusion.1), channel_id=1, source_target_pairs={{0,8},{8,0},{16,24},{24,16},{1,9},{9,1},{17,25},{25,17},{2,10},{10... | collective-permute-start | bytes 4128776 | tf_op jit(solution)/shard_map/ppermute | solution.py:607
  227.5 7.3 %copy-start.3 = (bf16[1024,384]{1,0:T(8,128)(2,1)}, bf16[1024,384]{1,0:T(8,128)(2,1)S(1)}, u32[]{:S(2)}) copy-start(bf16[1024,384]{1,0:T(8,128)(2,1)S(1)} %get-tuple-element.84) | copy-start | bytes 2359300
  235.5 22.4 %collective-permute-start.15 = (bf16[448,768]{1,0:T(8,128)(2,1)S(1)}, bf16[448,768]{1,0:T(8,128)(2,1)S(1)}, u32[]{:S(2)}, u32[]{:S(2)}) collective-permute-start(bf16[448,768]{1,0:T(8,128)(2,1)S(1)} %dynamic-slice_bitcast_fusion.6), channel_id=1, source_target_pairs={{0,8},{8,0},{16,24},{24,16},{1,9},{9,1},{17,25},{25,17},{2,10},{10... | collective-permute-start | bytes 2064392 | tf_op jit(solution)/shard_map/ppermute | solution.py:607
  236.6 21.4 %collective-permute-start.14 = (bf16[448,768]{1,0:T(8,128)(2,1)S(1)}, bf16[448,768]{1,0:T(8,128)(2,1)S(1)}, u32[]{:S(2)}, u32[]{:S(2)}) collective-permute-start(bf16[448,768]{1,0:T(8,128)(2,1)S(1)} %dynamic-slice_bitcast_fusion.7), channel_id=1, source_target_pairs={{0,16},{8,24},{16,0},{24,8},{1,17},{9,25},{17,1},{25,9},{2,18},{10... | collective-permute-start | bytes 2064392 | tf_op jit(solution)/shard_map/ppermute | solution.py:607
  260.1 28.9 %collective-permute-start.17 = (bf16[224,768]{1,0:T(8,128)(2,1)S(1)}, bf16[224,768]{1,0:T(8,128)(2,1)S(1)}, u32[]{:S(2)}, u32[]{:S(2)}) collective-permute-start(bf16[224,768]{1,0:T(8,128)(2,1)S(1)} %get-tuple-element.141), channel_id=1, source_target_pairs={{0,1},{1,2},{2,3},{3,0},{4,5},{5,6},{6,7},{7,4},{8,9},{9,10},{10,1... | collective-permute-start | bytes 1032200 | tf_op jit(solution)/shard_map/ppermute | solution.py:626
  262.1 27.9 %collective-permute-start.18 = (bf16[224,768]{1,0:T(8,128)(2,1)S(1)}, bf16[224,768]{1,0:T(8,128)(2,1)S(1)}, u32[]{:S(2)}, u32[]{:S(2)}) collective-permute-start(bf16[224,768]{1,0:T(8,128)(2,1)S(1)} %get-tuple-element.142), channel_id=1, source_target_pairs={{0,2},{1,3},{2,0},{3,1},{4,6},{5,7},{6,4},{7,5},{8,10},{9,11},{10,... | collective-permute-start | bytes 1032200 | tf_op jit(solution)/shard_map/ppermute | solution.py:626
  265.9 30.6 %collective-permute-start.19 = (bf16[224,768]{1,0:T(8,128)(2,1)S(1)}, bf16[224,768]{1,0:T(8,128)(2,1)S(1)}, u32[]{:S(2)}, u32[]{:S(2)}) collective-permute-start(bf16[224,768]{1,0:T(8,128)(2,1)S(1)} %get-tuple-element.140), channel_id=1, source_target_pairs={{0,3},{1,0},{2,1},{3,2},{4,7},{5,4},{6,5},{7,6},{8,11},{9,8},{10,9... | collective-permute-start | bytes 1032200 | tf_op jit(solution)/shard_map/ppermute | solution.py:626
  288.9 8.2 %copy-start.25 = (bf16[1024,1152]{1,0:T(8,128)(2,1)}, bf16[1024,1152]{1,0:T(8,128)(2,1)S(1)}, u32[]{:S(2)}) copy-start(bf16[1024,1152]{1,0:T(8,128)(2,1)S(1)} %pad_maximum_fusion) | copy-start | bytes 7077892
  301.5 5.4 %collective-permute-start.20 = (bf16[1024,768]{1,0:T(8,128)(2,1)}, bf16[1024,768]{1,0:T(8,128)(2,1)}, u32[]{:S(2)}, u32[]{:S(2)}) collective-permute-start(bf16[1024,768]{1,0:T(8,128)(2,1)} %convolution_convert_fusion), channel_id=1, source_target_pairs={{0,4},{4,0},{1,5},{5,1},{2,6},{6,2},{3,7},{7,3},{8,12},{12,8},{9,1... | collective-permute-start | bytes 4718600 | tf_op jit(solution)/shard_map/ppermute | solution.py:570
  306.4 73.5 %collective-permute-start.36 = (bf16[224,768]{1,0:T(8,128)(2,1)S(1)}, bf16[224,768]{1,0:T(8,128)(2,1)S(1)}, u32[]{:S(2)}, u32[]{:S(2)}) collective-permute-start(bf16[224,768]{1,0:T(8,128)(2,1)S(1)} %get-tuple-element.122), channel_id=1, source_target_pairs={{0,3},{1,0},{2,1},{3,2},{4,7},{5,4},{6,5},{7,6},{8,11},{9,8},{10,9... | collective-permute-start | bytes 1032200 | tf_op jit(solution)/shard_map/ppermute | solution.py:626
  306.5 73.5 %collective-permute-start.35 = (bf16[224,768]{1,0:T(8,128)(2,1)S(1)}, bf16[224,768]{1,0:T(8,128)(2,1)S(1)}, u32[]{:S(2)}, u32[]{:S(2)}) collective-permute-start(bf16[224,768]{1,0:T(8,128)(2,1)S(1)} %get-tuple-element.122), channel_id=1, source_target_pairs={{0,2},{1,3},{2,0},{3,1},{4,6},{5,7},{6,4},{7,5},{8,10},{9,11},{10,... | collective-permute-start | bytes 1032200 | tf_op jit(solution)/shard_map/ppermute | solution.py:626
  316.2 13.0 %collective-permute-start.23 = (bf16[2,104,1152]{2,1,0:T(8,128)(2,1)S(1)}, bf16[2,104,1152]{2,1,0:T(8,128)(2,1)S(1)}, u32[]{:S(2)}, u32[]{:S(2)}) collective-permute-start(bf16[2,104,1152]{2,1,0:T(8,128)(2,1)S(1)} %dynamic-slice_bitcast_fusion.8), channel_id=1, source_target_pairs={{0,16},{8,24},{16,0},{24,8},{1,17},{9,25},{17,1},{25,9},{2,18},{10... | collective-permute-start | bytes 1437704 | tf_op jit(solution)/shard_map/ppermute | solution.py:607
  318.6 14.2 %collective-permute-start.21 = (bf16[2,104,1152]{2,1,0:T(8,128)(2,1)S(1)}, bf16[2,104,1152]{2,1,0:T(8,128)(2,1)S(1)}, u32[]{:S(2)}, u32[]{:S(2)}) collective-permute-start(bf16[2,104,1152]{2,1,0:T(8,128)(2,1)S(1)} %dynamic-slice_bitcast_fusion.9), channel_id=1, source_target_pairs={{0,8},{8,0},{16,24},{24,16},{1,9},{9,1},{17,25},{25,17},{2,10},{10... | collective-permute-start | bytes 1437704 | tf_op jit(solution)/shard_map/ppermute | solution.py:607
  318.8 36.0 %collective-permute-start.26 = (bf16[512,768]{1,0:T(8,128)(2,1)S(1)}, bf16[512,768]{1,0:T(8,128)(2,1)S(1)}, u32[]{:S(2)}, u32[]{:S(2)}) collective-permute-start(bf16[512,768]{1,0:T(8,128)(2,1)S(1)} %get-tuple-element.128), channel_id=1, source_target_pairs={{0,0},{1,1},{4,2},{5,3},{2,4},{3,5},{6,6},{7,7},{8,8},{9,9},{12,10... | collective-permute-start | bytes 2359304 | tf_op jit(solution)/shard_map/ppermute | solution.py:785
  329.2 46.1 %collective-permute-start.27 = (bf16[512,768]{1,0:T(8,128)(2,1)S(1)}, bf16[512,768]{1,0:T(8,128)(2,1)S(1)}, u32[]{:S(2)}, u32[]{:S(2)}) collective-permute-start(bf16[512,768]{1,0:T(8,128)(2,1)S(1)} %get-tuple-element.127), channel_id=1, source_target_pairs={{1,0},{0,1},{5,2},{4,3},{3,4},{2,5},{7,6},{6,7},{9,8},{8,9},{13,10... | collective-permute-start | bytes 2359304 | tf_op jit(solution)/shard_map/ppermute | solution.py:785
  332.8 7.8 %collective-permute-start.24 = (bf16[104,1152]{1,0:T(8,128)(2,1)S(1)}, bf16[104,1152]{1,0:T(8,128)(2,1)S(1)}, u32[]{:S(2)}, u32[]{:S(2)}) collective-permute-start(bf16[104,1152]{1,0:T(8,128)(2,1)S(1)} %dynamic-slice_bitcast_fusion.10), channel_id=1, source_target_pairs={{0,8},{8,0},{16,24},{24,16},{1,9},{9,1},{17,25},{25,17},{2,10},{10... | collective-permute-start | bytes 718856 | tf_op jit(solution)/shard_map/ppermute | solution.py:607
  340.6 7.1 %collective-permute-start.22 = (bf16[104,1152]{1,0:T(8,128)(2,1)S(1)}, bf16[104,1152]{1,0:T(8,128)(2,1)S(1)}, u32[]{:S(2)}, u32[]{:S(2)}) collective-permute-start(bf16[104,1152]{1,0:T(8,128)(2,1)S(1)} %dynamic-slice_bitcast_fusion.11), channel_id=1, source_target_pairs={{0,16},{8,24},{16,0},{24,8},{1,17},{9,25},{17,1},{25,9},{2,18},{10... | collective-permute-start | bytes 718856 | tf_op jit(solution)/shard_map/ppermute | solution.py:607
  348.3 29.0 %collective-permute-start.25 = (bf16[52,1152]{1,0:T(8,128)(2,1)S(1)}, bf16[52,1152]{1,0:T(8,128)(2,1)S(1)}, u32[]{:S(2)}, u32[]{:S(2)}) collective-permute-start(bf16[52,1152]{1,0:T(8,128)(2,1)S(1)} %get-tuple-element.145), channel_id=1, source_target_pairs={{0,1},{1,2},{2,3},{3,0},{4,5},{5,6},{6,7},{7,4},{8,9},{9,10},{10,1... | collective-permute-start | bytes 359432 | tf_op jit(solution)/shard_map/ppermute | solution.py:626
  354.9 23.9 %collective-permute-start.28 = (bf16[52,1152]{1,0:T(8,128)(2,1)S(1)}, bf16[52,1152]{1,0:T(8,128)(2,1)S(1)}, u32[]{:S(2)}, u32[]{:S(2)}) collective-permute-start(bf16[52,1152]{1,0:T(8,128)(2,1)S(1)} %get-tuple-element.146), channel_id=1, source_target_pairs={{0,2},{1,3},{2,0},{3,1},{4,6},{5,7},{6,4},{7,5},{8,10},{9,11},{10,... | collective-permute-start | bytes 359432 | tf_op jit(solution)/shard_map/ppermute | solution.py:626
  375.4 4.4 %collective-permute-start.29 = (bf16[52,1152]{1,0:T(8,128)(2,1)S(1)}, bf16[52,1152]{1,0:T(8,128)(2,1)S(1)}, u32[]{:S(2)}, u32[]{:S(2)}) collective-permute-start(bf16[52,1152]{1,0:T(8,128)(2,1)S(1)} %get-tuple-element.147), channel_id=1, source_target_pairs={{0,3},{1,0},{2,1},{3,2},{4,7},{5,4},{6,5},{7,6},{8,11},{9,8},{10,9... | collective-permute-start | bytes 359432 | tf_op jit(solution)/shard_map/ppermute | solution.py:626
  377.3 8.3 %collective-permute-start.34 = (bf16[224,768]{1,0:T(8,128)(2,1)S(1)}, bf16[224,768]{1,0:T(8,128)(2,1)S(1)}, u32[]{:S(2)}, u32[]{:S(2)}) collective-permute-start(bf16[224,768]{1,0:T(8,128)(2,1)S(1)} %get-tuple-element.122), channel_id=1, source_target_pairs={{0,1},{1,2},{2,3},{3,0},{4,5},{5,6},{6,7},{7,4},{8,9},{9,10},{10,1... | collective-permute-start | bytes 1032200 | tf_op jit(solution)/shard_map/ppermute | solution.py:626
  387.6 10.5 %collective-permute-start.30 = (bf16[52,1152]{1,0:T(8,128)(2,1)S(1)}, bf16[52,1152]{1,0:T(8,128)(2,1)S(1)}, u32[]{:S(2)}, u32[]{:S(2)}) collective-permute-start(bf16[52,1152]{1,0:T(8,128)(2,1)S(1)} %add_convert_fusion.3), channel_id=1, source_target_pairs={{0,1},{1,2},{2,3},{3,0},{4,5},{5,6},{6,7},{7,4},{8,9},{9,10},{10,1... | collective-permute-start | bytes 359432 | tf_op jit(solution)/shard_map/ppermute | solution.py:626
  389.5 11.5 %collective-permute-start.31 = (bf16[52,1152]{1,0:T(8,128)(2,1)S(1)}, bf16[52,1152]{1,0:T(8,128)(2,1)S(1)}, u32[]{:S(2)}, u32[]{:S(2)}) collective-permute-start(bf16[52,1152]{1,0:T(8,128)(2,1)S(1)} %add_convert_fusion.3), channel_id=1, source_target_pairs={{0,2},{1,3},{2,0},{3,1},{4,6},{5,7},{6,4},{7,5},{8,10},{9,11},{10,... | collective-permute-start | bytes 359432 | tf_op jit(solution)/shard_map/ppermute | solution.py:626
  389.9 12.2 %collective-permute-start.32 = (bf16[52,1152]{1,0:T(8,128)(2,1)S(1)}, bf16[52,1152]{1,0:T(8,128)(2,1)S(1)}, u32[]{:S(2)}, u32[]{:S(2)}) collective-permute-start(bf16[52,1152]{1,0:T(8,128)(2,1)S(1)} %add_convert_fusion.3), channel_id=1, source_target_pairs={{0,3},{1,0},{2,1},{3,2},{4,7},{5,4},{6,5},{7,6},{8,11},{9,8},{10,9... | collective-permute-start | bytes 359432 | tf_op jit(solution)/shard_map/ppermute | solution.py:626
  403.3 4.5 %collective-permute-start.33 = (bf16[112,1152]{1,0:T(8,128)(2,1)S(1)}, bf16[112,1152]{1,0:T(8,128)(2,1)S(1)}, u32[]{:S(2)}, u32[]{:S(2)}) collective-permute-start(bf16[112,1152]{1,0:T(8,128)(2,1)S(1)} %pad_maximum_fusion.4), channel_id=1, source_target_pairs={{0,4},{4,0},{1,5},{5,1},{2,6},{6,2},{3,7},{7,3},{8,12},{12,8},{9,1... | collective-permute-start | bytes 774152 | tf_op jit(solution)/shard_map/ppermute | solution.py:570
  (40 other events, 90.2 us)
Sparse Core Ops, SparseCore 0:
  12.4 33.2 all-gather.5
  48.1 64.2 all-gather.7
